TPU v7x, 32 devices: a whole 2x2x4 slice. The times are simulated.
32 devices in a mesh: dp: 4 (over y, x), expert: 8 (over z, core).
Axes of the slice: x: 2, y: 2, z: 4, core: 2. Of those that a mesh axis runs over, the one named last changes fastest.
Arguments:
- tokens_in: bfloat16 [32768, 768], P(('dp', 'expert')), may hold values from -6 to 6
- cont_ids: int32 [32, 512], P(('dp', 'expert')), may hold values from 0 to 3, never falling along the last dimension, each value on 1 to 256 neighbouring positions
- expert_ids: int32 [32768, 2], P(('dp', 'expert')), may hold values from 0 to 7, all different within a row; in each aligned block of 1024 rows (0 to 1023, 1024 to 2047, ...) at most 512 rows name the same one
- priority: int32 [32768, 2], P(('dp', 'expert')), may hold values from 0 to 3
- gain_attn: float32 [768], replicated, may hold values from 0.5 to 1.5
- w_qkv: bfloat16 [768, 2304], P(('dp', 'expert')), may hold values from -0.21875 to 0.21875
- rel_table: float32 [31, 12], replicated, may hold values from -4 to 4
- w_out: bfloat16 [768, 768], P(('dp', 'expert')), may hold values from -0.875 to 0.875
- gain_ffn: float32 [768], replicated, may hold values from 0.5 to 1.5
- w_router: bfloat16 [768, 8], P(('dp', 'expert')), may hold values from -0.21875 to 0.21875
- w_in: bfloat16 [8, 768, 3072], P('expert'), may hold values from -0.21875 to 0.21875
- w_down: bfloat16 [8, 3072, 768], P('expert'), may hold values from -0.109375 to 0.109375
- cotangent: bfloat16 [32768, 768], P(('dp', 'expert')), may hold values from -6 to 6
Outputs:
- out: bfloat16 [32768, 768], P(('dp', 'expert'))
- d_tokens: float32 [32768, 768], P(('dp', 'expert'))
- d_gain_attn: float32 [768], replicated
- d_w_qkv: float32 [768, 2304], P(('dp', 'expert'))
- d_rel_table: float32 [31, 12], replicated
- d_w_out: float32 [768, 768], P(('dp', 'expert'))
- d_gain_ffn: float32 [768], replicated
- d_w_router: float32 [768, 8], P(('dp', 'expert'))
- d_w_in: float32 [8, 768, 3072], P('expert', 'dp')
- d_w_down: float32 [8, 3072, 768], P('expert', 'dp')
Inputs may be any that keep to these rules, and one draw needn't show every extreme that they name: `expert_ids`: each token names 2 different experts. Within the rows of one device no expert is named more than 512 times, a bound that some block reaches. `cont_ids`: along each device's row the ids never fall; each run of one id is 1 to 256 tokens long, and some run is exactly 256.
All inputs are finite; a program needn't handle non-finite values.
Results may differ from a plain program's by a relative error of at most 0.015.
Values may be sent and summed in bfloat16 or wider, within the bound.
A program may use at most 320 MiB of HBM per device.

v0:
```python
import jax
import jax.numpy as jnp
from jax import lax
from jax.sharding import PartitionSpec as P

PRIO = 4
BLOCK = 512
PROMPT = 2048


BORDERS = (16, 24, 32, 48, 64, 96, 128, 192, 256, 384, 512, 768, 1024, 1536, 2048)
EPSILON = 1e-06
MASKED = -1e30


def bucket_of(distance):
    distance = jnp.maximum(distance, 0)
    counted = jnp.minimum(distance, 15)
    for border in BORDERS:
        counted = counted + (distance >= border).astype(jnp.int32)
    return counted


def normed(values, gain):
    return values * lax.rsqrt(jnp.mean(values * values, axis=-1, keepdims=True) + EPSILON) * gain


def dense_gather(w_qkv, w_out, w_router):
    return (
        lax.all_gather(w_qkv, ("dp", "expert"), axis=0, tiled=True),
        lax.all_gather(w_out, ("dp", "expert"), axis=0, tiled=True),
        lax.all_gather(w_router, ("dp", "expert"), axis=0, tiled=True),
    )


def dense_regather(w_qkv, w_out, w_router):
    return (
        lax.all_gather(w_qkv, ("dp", "expert"), axis=0, tiled=True),
        lax.all_gather(w_out, ("dp", "expert"), axis=0, tiled=True),
        lax.all_gather(w_router, ("dp", "expert"), axis=0, tiled=True),
    )


def prompt_gather(own_keys, own_values):
    return (
        lax.all_gather(own_keys, "dp", axis=0, tiled=True),
        lax.all_gather(own_values, "dp", axis=0, tiled=True),
    )


def bias_of(buckets, table_heads):
    bias = jnp.zeros((table_heads.shape[0],) + buckets.shape, jnp.float32)
    for bucket in range(table_heads.shape[1]):
        bias = bias + jnp.where(buckets[None] == bucket, table_heads[:, bucket][:, None, None], 0.0)
    return bias


def block_scores(
    query, key_block, key_position, key_sequence, query_position, query_sequence, table_heads, scale
):
    scores = (
        jnp.einsum("qhd,khd->hqk", query, key_block, preferred_element_type=jnp.float32) * scale
    )
    distance = query_position[:, None] - key_position[None, :]
    seen = (distance >= 0) & (
        (key_sequence[None, :] < 0) | (key_sequence[None, :] == query_sequence[:, None])
    )
    buckets = bucket_of(distance)
    scores = scores + bias_of(buckets, table_heads)
    return (scores, seen[None], buckets)


def attention_forward(
    query,
    all_keys,
    all_values,
    key_position,
    key_sequence,
    query_position,
    query_sequence,
    table_heads,
    scale,
):
    rows, heads, head_size = query.shape
    blocks = all_keys.shape[0] // BLOCK
    key_blocks = all_keys.reshape(blocks, BLOCK, heads, head_size)
    value_blocks = all_values.reshape(blocks, BLOCK, heads, head_size)
    position_blocks = key_position.reshape(blocks, BLOCK)
    sequence_blocks = key_sequence.reshape(blocks, BLOCK)

    def stats_step(carry, block_in):
        running_max, running_sum = carry
        key_block, position_block, sequence_block = block_in
        scores, seen, _ = block_scores(
            query,
            key_block,
            position_block,
            sequence_block,
            query_position,
            query_sequence,
            table_heads,
            scale,
        )
        scores = jnp.where(seen, scores, MASKED)
        new_max = jnp.maximum(running_max, jnp.max(scores, axis=-1))
        shifted = jnp.where(seen, jnp.exp(scores - new_max[..., None]), 0.0)
        running_sum = running_sum * jnp.exp(running_max - new_max) + jnp.sum(shifted, axis=-1)
        return ((new_max, running_sum), None)

    start = (jnp.full((heads, rows), MASKED, jnp.float32), jnp.zeros((heads, rows), jnp.float32))
    (largest, summed), _ = lax.scan(
        stats_step, start, (key_blocks, position_blocks, sequence_blocks)
    )
    log_total = largest + jnp.log(summed)

    def value_step(carry, block_in):
        rounded_sum, leftover_sum = carry
        key_block, value_block, position_block, sequence_block = block_in
        scores, seen, _ = block_scores(
            query,
            key_block,
            position_block,
            sequence_block,
            query_position,
            query_sequence,
            table_heads,
            scale,
        )
        weights = jnp.where(seen, jnp.exp(scores - log_total[..., None]), 0.0)
        rounded = weights.astype(jnp.bfloat16)
        leftover = (weights - rounded.astype(jnp.float32)).astype(jnp.bfloat16)
        rounded_sum = rounded_sum + jnp.einsum(
            "hqk,khd->qhd", rounded, value_block, preferred_element_type=jnp.float32
        )
        leftover_sum = leftover_sum + jnp.einsum(
            "hqk,khd->qhd", leftover, value_block, preferred_element_type=jnp.float32
        )
        return ((rounded_sum, leftover_sum), None)

    empty = jnp.zeros((rows, heads, head_size), jnp.float32)
    (rounded_sum, leftover_sum), _ = lax.scan(
        value_step, (empty, empty), (key_blocks, value_blocks, position_blocks, sequence_blocks)
    )
    return (rounded_sum, rounded_sum + leftover_sum, log_total)


def attention_backward(
    query,
    all_keys,
    all_values,
    key_position,
    key_sequence,
    query_position,
    query_sequence,
    table_heads,
    scale,
    log_total,
    grad_attended,
    delta,
):
    rows, heads, head_size = query.shape
    buckets_count = table_heads.shape[1]
    blocks = all_keys.shape[0] // BLOCK
    key_blocks = all_keys.reshape(blocks, BLOCK, heads, head_size)
    value_blocks = all_values.reshape(blocks, BLOCK, heads, head_size)
    position_blocks = key_position.reshape(blocks, BLOCK)
    sequence_blocks = key_sequence.reshape(blocks, BLOCK)

    def grad_step(carry, block_in):
        grad_query, grad_table = carry
        key_block, value_block, position_block, sequence_block = block_in
        scores, seen, buckets = block_scores(
            query,
            key_block,
            position_block,
            sequence_block,
            query_position,
            query_sequence,
            table_heads,
            scale,
        )
        weights = jnp.where(seen, jnp.exp(scores - log_total[..., None]), 0.0)
        rounded = weights.astype(jnp.bfloat16)
        grad_weights = jnp.einsum(
            "qhd,khd->hqk", grad_attended, value_block, preferred_element_type=jnp.float32
        )
        grad_scores = (weights * (grad_weights - delta[..., None])).astype(jnp.bfloat16)
        grad_query = grad_query + jnp.einsum(
            "hqk,khd->qhd", grad_scores, key_block, preferred_element_type=jnp.float32
        )
        grad_key = (
            jnp.einsum("hqk,qhd->khd", grad_scores, query, preferred_element_type=jnp.float32)
            * scale
        )
        grad_value = jnp.einsum(
            "hqk,qhd->khd", rounded, grad_attended, preferred_element_type=jnp.float32
        )
        grad_float = grad_scores.astype(jnp.float32)
        columns = [
            jnp.sum(jnp.where(buckets[None] == bucket, grad_float, 0.0), axis=(1, 2))
            for bucket in range(buckets_count)
        ]
        grad_table = grad_table + jnp.stack(columns, axis=1)
        return ((grad_query, grad_table), (grad_key, grad_value))

    start = (
        jnp.zeros((rows, heads, head_size), jnp.float32),
        jnp.zeros((heads, buckets_count), jnp.float32),
    )
    (grad_query, grad_table), (grad_keys, grad_values) = lax.scan(
        grad_step, start, (key_blocks, value_blocks, position_blocks, sequence_blocks)
    )
    return (
        grad_query * scale,
        grad_table,
        grad_keys.reshape(-1, heads * head_size),
        grad_values.reshape(-1, heads * head_size),
    )


def per_device(
    tokens_in,
    cont_ids,
    expert_ids,
    priority,
    gain_attn,
    w_qkv,
    rel_table,
    w_out,
    gain_ffn,
    w_router,
    w_in,
    w_down,
    cotangent,
):
    rows, width = tokens_in.shape
    heads = rel_table.shape[1]
    head_size = width // heads
    scale = head_size ** (-0.5)
    dp_count = lax.axis_size("dp")
    dp_index = lax.axis_index("dp")
    prompt_rows = PROMPT // dp_count
    cont_rows = rows - prompt_rows
    local_ids = cont_ids[0]
    same = local_ids[:, None] == local_ids[None, :]
    earlier = jnp.arange(cont_rows)[None, :] < jnp.arange(cont_rows)[:, None]
    offset = jnp.sum((same & earlier).astype(jnp.int32), axis=1)
    prompt_position = dp_index * prompt_rows + jnp.arange(prompt_rows, dtype=jnp.int32)
    query_position = jnp.concatenate([prompt_position, PROMPT + offset])
    query_sequence = jnp.concatenate([jnp.full((prompt_rows,), -1, jnp.int32), local_ids])
    key_position = jnp.concatenate([jnp.arange(PROMPT, dtype=jnp.int32), PROMPT + offset])
    key_sequence = jnp.concatenate([jnp.full((PROMPT,), -1, jnp.int32), local_ids])
    table_heads = rel_table.T
    whole_qkv, whole_out, whole_router = dense_gather(w_qkv, w_out, w_router)
    inputs = tokens_in.astype(jnp.float32)
    normed_attn = normed(inputs, gain_attn).astype(jnp.bfloat16)
    projected = jnp.dot(normed_attn, whole_qkv, preferred_element_type=jnp.float32).astype(
        jnp.bfloat16
    )
    query = projected[:, :width].reshape(rows, heads, head_size)
    own_keys = projected[:, width : 2 * width]
    own_values = projected[:, 2 * width :]
    prompt_keys, prompt_values = prompt_gather(own_keys[:prompt_rows], own_values[:prompt_rows])
    all_keys = jnp.concatenate([prompt_keys, own_keys[prompt_rows:]], axis=0).reshape(
        -1, heads, head_size
    )
    all_values = jnp.concatenate([prompt_values, own_values[prompt_rows:]], axis=0).reshape(
        -1, heads, head_size
    )
    rounded_sum, exact_sum, log_total = attention_forward(
        query,
        all_keys,
        all_values,
        key_position,
        key_sequence,
        query_position,
        query_sequence,
        table_heads,
        scale,
    )
    attended = rounded_sum.reshape(rows, width).astype(jnp.bfloat16)
    middle = inputs + jnp.dot(attended, whole_out, preferred_element_type=jnp.float32)
    normed_ffn = normed(middle, gain_ffn).astype(jnp.bfloat16)
    logits = jnp.dot(normed_ffn, whole_router, preferred_element_type=jnp.float32)
    experts_total = whole_router.shape[1]
    top = expert_ids.shape[1]
    picks = expert_ids[:, :, None] == jnp.arange(experts_total)[None, None, :]
    chosen = jnp.sum(jnp.where(picks, logits[:, None, :], 0.0), axis=2)
    gates = jax.nn.softmax(chosen, axis=-1)
    levels = PRIO
    local_experts = w_in.shape[0]
    capacity = rows * top // local_experts
    send = max(2, 2 * rows * top // experts_total)
    flat_expert = expert_ids.reshape(-1)
    code = priority.reshape(-1) * experts_total + flat_expert
    onehot = (code[:, None] == jnp.arange(levels * experts_total)[None, :]).astype(jnp.int32)
    rank = jnp.sum((jnp.cumsum(onehot, axis=0) - onehot) * onehot, axis=1)
    counts = jnp.sum(onehot, axis=0)
    every = lax.all_gather(counts[None, :], "expert", axis=0, tiled=True).reshape(
        -1, levels, experts_total
    )
    expert_index = lax.axis_index("expert")
    totals = jnp.sum(every, axis=0)
    lower = jnp.cumsum(totals, axis=0) - totals
    earlier_sources = jnp.cumsum(every, axis=0) - every
    mine_prefix = lax.dynamic_index_in_dim(earlier_sources, expert_index, 0, keepdims=False)
    base = (lower + mine_prefix).reshape(-1)
    slot = rank + jnp.sum(onehot * base[None, :], axis=1)
    kept = slot < capacity
    own_counts = counts.reshape(levels, experts_total)
    own_lower = (jnp.cumsum(own_counts, axis=0) - own_counts).reshape(-1)
    place = rank + jnp.sum(onehot * own_lower[None, :], axis=1)
    target = flat_expert * send + place
    first_mine = expert_index * local_experts
    counts_mine = lax.dynamic_slice_in_dim(every, first_mine, local_experts, 2)
    base_mine = lax.dynamic_slice_in_dim(
        lower[None] + earlier_sources, first_mine, local_experts, 2
    )
    band_end = jnp.cumsum(counts_mine, axis=1)
    band_start = band_end - counts_mine
    place_index = jnp.arange(send, dtype=jnp.int32)
    level = jnp.sum(
        (place_index[None, None, None, :] >= band_end[:, :, :, None]).astype(jnp.int32), axis=1
    )
    level_hot = level[:, None, :, :] == jnp.arange(levels)[None, :, None, None]
    start_of = jnp.sum(jnp.where(level_hot, band_start[:, :, :, None], 0), axis=1)
    base_of = jnp.sum(jnp.where(level_hot, base_mine[:, :, :, None], 0), axis=1)
    arrived_slot = base_of + place_index[None, None, :] - start_of
    usable = (level < levels) & (arrived_slot < capacity)
    landing = jnp.where(
        usable,
        jnp.arange(local_experts)[None, :, None] * capacity + arrived_slot,
        local_experts * capacity,
    ).reshape(-1)
    live = landing < local_experts * capacity
    safe = jnp.minimum(landing, local_experts * capacity - 1)
    pair_inputs = jnp.repeat(normed_ffn, top, axis=0)
    outgoing = (
        jnp.zeros((experts_total * send, width), jnp.bfloat16)
        .at[target]
        .set(pair_inputs)
        .reshape(experts_total, send, width)
    )
    arrived = lax.all_to_all(outgoing, "expert", split_axis=0, concat_axis=0, tiled=True)
    expert_inputs = (
        jnp.zeros((local_experts * capacity, width), jnp.bfloat16)
        .at[landing]
        .set(arrived.reshape(-1, width), mode="drop")
        .reshape(local_experts, capacity, width)
    )
    hidden = jnp.einsum("ecd,edf->ecf", expert_inputs, w_in, preferred_element_type=jnp.float32)
    activated = jax.nn.gelu(hidden).astype(jnp.bfloat16)
    expert_out = jnp.einsum(
        "ecf,efd->ecd", activated, w_down, preferred_element_type=jnp.float32
    ).astype(jnp.bfloat16)
    returning = jnp.where(
        live[:, None],
        jnp.take(expert_out.reshape(-1, width), safe, axis=0),
        jnp.zeros((), jnp.bfloat16),
    ).reshape(experts_total, send, width)
    returned = lax.all_to_all(returning, "expert", split_axis=0, concat_axis=0, tiled=True)
    pair_out = jnp.where(
        kept[:, None],
        jnp.take(returned.reshape(-1, width), target, axis=0).astype(jnp.float32),
        0.0,
    ).reshape(rows, top, width)
    mixed = jnp.sum(gates[:, :, None] * pair_out, axis=1)
    output = (middle + mixed).astype(jnp.bfloat16)
    grad_out = cotangent.astype(jnp.float32)
    grad_gates = jnp.sum(grad_out[:, None, :] * pair_out, axis=2)
    pair_grads = (gates[:, :, None] * grad_out[:, None, :]).astype(jnp.bfloat16).reshape(-1, width)
    outgoing_grads = (
        jnp.zeros((experts_total * send, width), jnp.bfloat16)
        .at[target]
        .set(pair_grads)
        .reshape(experts_total, send, width)
    )
    arrived_grads = lax.all_to_all(
        outgoing_grads, "expert", split_axis=0, concat_axis=0, tiled=True
    )
    grad_expert_out = (
        jnp.zeros((local_experts * capacity, width), jnp.bfloat16)
        .at[landing]
        .set(arrived_grads.reshape(-1, width), mode="drop")
        .reshape(local_experts, capacity, width)
    )
    hidden_again = jnp.einsum(
        "ecd,edf->ecf", expert_inputs, w_in, preferred_element_type=jnp.float32
    )
    activated_again, gelu_back = jax.vjp(jax.nn.gelu, hidden_again)
    grad_activated = jnp.einsum(
        "ecd,efd->ecf", grad_expert_out, w_down, preferred_element_type=jnp.float32
    )
    grad_hidden = gelu_back(grad_activated)[0].astype(jnp.bfloat16)
    grad_w_down = jnp.einsum(
        "ecf,ecd->efd",
        activated_again.astype(jnp.bfloat16),
        grad_expert_out,
        preferred_element_type=jnp.float32,
    )
    grad_w_in = jnp.einsum(
        "ecd,ecf->edf", expert_inputs, grad_hidden, preferred_element_type=jnp.float32
    )
    grad_inputs = jnp.einsum(
        "ecf,edf->ecd", grad_hidden, w_in, preferred_element_type=jnp.float32
    ).astype(jnp.bfloat16)
    back_rows = jnp.where(
        live[:, None],
        jnp.take(grad_inputs.reshape(-1, width), safe, axis=0),
        jnp.zeros((), jnp.bfloat16),
    ).reshape(experts_total, send, width)
    came_back = lax.all_to_all(back_rows, "expert", split_axis=0, concat_axis=0, tiled=True)
    pair_back = jnp.where(
        kept[:, None],
        jnp.take(came_back.reshape(-1, width), target, axis=0).astype(jnp.float32),
        0.0,
    )
    grad_normed_ffn = jnp.sum(pair_back.reshape(rows, top, width), axis=1)
    grad_chosen = gates * (grad_gates - jnp.sum(gates * grad_gates, axis=-1, keepdims=True))
    grad_logits = jnp.sum(jnp.where(picks, grad_chosen[:, :, None], 0.0), axis=1).astype(
        jnp.bfloat16
    )
    back_qkv, back_out, back_router = dense_regather(w_qkv, w_out, w_router)
    grad_normed_ffn = grad_normed_ffn + jnp.dot(
        grad_logits, back_router.T, preferred_element_type=jnp.float32
    )
    grad_router = jnp.dot(normed_ffn.T, grad_logits, preferred_element_type=jnp.float32)
    _, ffn_norm_back = jax.vjp(normed, middle, gain_ffn)
    grad_middle_part, grad_gain_ffn = ffn_norm_back(grad_normed_ffn)
    grad_middle = grad_out + grad_middle_part
    grad_branch = grad_middle.astype(jnp.bfloat16)
    grad_out_weight = jnp.dot(attended.T, grad_branch, preferred_element_type=jnp.float32)
    grad_attended = (
        jnp.dot(grad_branch, back_out.T, preferred_element_type=jnp.float32)
        .astype(jnp.bfloat16)
        .reshape(rows, heads, head_size)
    )
    delta = jnp.sum(grad_attended.astype(jnp.float32) * exact_sum, axis=-1).T
    back_keys, back_values = prompt_gather(own_keys[:prompt_rows], own_values[:prompt_rows])
    keys_again = jnp.concatenate([back_keys, own_keys[prompt_rows:]], axis=0).reshape(
        -1, heads, head_size
    )
    values_again = jnp.concatenate([back_values, own_values[prompt_rows:]], axis=0).reshape(
        -1, heads, head_size
    )
    grad_query, grad_table, grad_keys, grad_values = attention_backward(
        query,
        keys_again,
        values_again,
        key_position,
        key_sequence,
        query_position,
        query_sequence,
        table_heads,
        scale,
        log_total,
        grad_attended,
        delta,
    )
    prompt_grad_keys, prompt_grad_values = (
        lax.psum_scatter(
            grad_keys[:PROMPT].astype(jnp.bfloat16), "dp", scatter_dimension=0, tiled=True
        ).astype(jnp.float32),
        lax.psum_scatter(
            grad_values[:PROMPT].astype(jnp.bfloat16), "dp", scatter_dimension=0, tiled=True
        ).astype(jnp.float32),
    )
    grad_projected = jnp.concatenate(
        [
            grad_query.reshape(rows, width),
            jnp.concatenate([prompt_grad_keys, grad_keys[PROMPT:]], axis=0),
            jnp.concatenate([prompt_grad_values, grad_values[PROMPT:]], axis=0),
        ],
        axis=1,
    ).astype(jnp.bfloat16)
    grad_normed_attn = jnp.dot(grad_projected, back_qkv.T, preferred_element_type=jnp.float32)
    grad_qkv = jnp.dot(normed_attn.T, grad_projected, preferred_element_type=jnp.float32)
    _, attn_norm_back = jax.vjp(normed, inputs, gain_attn)
    grad_inputs_part, grad_gain_attn = attn_norm_back(grad_normed_attn)
    grad_tokens = grad_middle + grad_inputs_part
    dense_parts = (
        lax.psum_scatter(grad_qkv, ("dp", "expert"), scatter_dimension=0, tiled=True),
        lax.psum_scatter(grad_out_weight, ("dp", "expert"), scatter_dimension=0, tiled=True),
        lax.psum_scatter(grad_router, ("dp", "expert"), scatter_dimension=0, tiled=True),
    )
    expert_parts = (
        lax.psum_scatter(
            grad_w_in.astype(jnp.bfloat16), "dp", scatter_dimension=1, tiled=True
        ).astype(jnp.float32),
        lax.psum_scatter(
            grad_w_down.astype(jnp.bfloat16), "dp", scatter_dimension=1, tiled=True
        ).astype(jnp.float32),
    )
    small_parts = lax.psum((grad_gain_attn, grad_gain_ffn, grad_table.T), ("dp", "expert"))
    return (
        output,
        grad_tokens,
        small_parts[0],
        dense_parts[0],
        small_parts[2],
        dense_parts[1],
        small_parts[1],
        dense_parts[2],
        expert_parts[0],
        expert_parts[1],
    )


def solution(mesh):
    return jax.shard_map(
        per_device,
        mesh=mesh,
        in_specs=(
            P(("dp", "expert"), None),
            P(("dp", "expert"), None),
            P(("dp", "expert"), None),
            P(("dp", "expert"), None),
            P(),
            P(("dp", "expert"), None),
            P(),
            P(("dp", "expert"), None),
            P(),
            P(("dp", "expert"), None),
            P("expert", None, None),
            P("expert", None, None),
            P(("dp", "expert"), None),
        ),
        out_specs=(
            P(("dp", "expert"), None),
            P(("dp", "expert"), None),
            P(),
            P(("dp", "expert"), None),
            P(),
            P(("dp", "expert"), None),
            P(),
            P(("dp", "expert"), None),
            P("expert", "dp", None),
            P("expert", "dp", None),
        ),
        check_vma=False,
    )
```

profile of v0, /device:TPU:0, one launch (start us, length us, event | category | flops | bytes accessed | tf_op | source)
XLA Modules:
  0.0 4156.2 jit_solution(13130902549774050308)
XLA Ops:
  10.8 63.2 %all-gather.7.cloned.1.call-done = bf16[768,2304]{1,0:T(8,128)(2,1)} async-done(((bf16[24,2304]{1,0:T(8,128)(2,1)}), bf16[768,2304]{1,0:T(8,128)(2,1)}) %all-gather.7.cloned.1.call-update) | async-done | bytes 3538960 | tf_op jit(solution)/shard_map/all_gather | solution.py:30
  154.9 17.9 all-gather.11.cloned.1.call-done
  201.0 630.0 %while.43 = (s32[]{:T(128)}, f32[12,1024]{1,0:T(8,128)}, f32[12,1024]{1,0:T(8,128)}, s32[1024]{0:T(1024)}, s32[5,512]{1,0:T(8,128)}, /*index=5*/s32[5,512]{1,0:T...) while((s32[]{:T(128)}, f32[12,1024]{1,0:T(8,128)}, ...), condition=%wide.region_5.6_spmd.clone, body=%wide.region_2.5_spmd.clone.sunk | while | flops 1276703232 | bytes 88024656 | solution.py:111
  204.6 16.9 fusion.290
  221.5 94.2 %fusion.291 = (f32[12,1024]{1,0:T(8,128)S(1)}, f32[12,1024,512]{1,2,0:T(8,128)}) fusion(f32[12]{0:T(128)S(1)} %get-tuple-element.1313, pred[1024,512]{0,1:T(8,128)(4,1)} %get-tuple-element.1316, f32[12]{0:T(128)S(1)} %get-tuple-element.1317, pred[1024,512]{0,1:T(8,128)(4,1)} %get-tuple-element.1318, f32[12]{0:T(128)S(1)} %get-tuple-element.1319, ...), kind=kOutput, calls=%fused_computation.555.clone.2 | convolution fusion | flops 1214238720 | bytes 44352980 | tf_op jit(solution)/shard_map/while/body/eval_jaxpr/qhd,khd->hqk/dot_general | solution.py:62
  330.6 16.9 fusion.290
  347.5 94.2 %fusion.291 = (f32[12,1024]{1,0:T(8,128)S(1)}, f32[12,1024,512]{1,2,0:T(8,128)}) fusion(f32[12]{0:T(128)S(1)} %get-tuple-element.1313, pred[1024,512]{0,1:T(8,128)(4,1)} %get-tuple-element.1316, f32[12]{0:T(128)S(1)} %get-tuple-element.1317, pred[1024,512]{0,1:T(8,128)(4,1)} %get-tuple-element.1318, f32[12]{0:T(128)S(1)} %get-tuple-element.1319, ...), kind=kOutput, calls=%fused_computation.555.clone.2 | convolution fusion | flops 1214238720 | bytes 44352980 | tf_op jit(solution)/shard_map/while/body/eval_jaxpr/qhd,khd->hqk/dot_general | solution.py:62
  456.6 16.9 fusion.290
  473.5 94.2 %fusion.291 = (f32[12,1024]{1,0:T(8,128)S(1)}, f32[12,1024,512]{1,2,0:T(8,128)}) fusion(f32[12]{0:T(128)S(1)} %get-tuple-element.1313, pred[1024,512]{0,1:T(8,128)(4,1)} %get-tuple-element.1316, f32[12]{0:T(128)S(1)} %get-tuple-element.1317, pred[1024,512]{0,1:T(8,128)(4,1)} %get-tuple-element.1318, f32[12]{0:T(128)S(1)} %get-tuple-element.1319, ...), kind=kOutput, calls=%fused_computation.555.clone.2 | convolution fusion | flops 1214238720 | bytes 44352980 | tf_op jit(solution)/shard_map/while/body/eval_jaxpr/qhd,khd->hqk/dot_general | solution.py:62
  582.5 16.9 fusion.290
  599.4 94.2 %fusion.291 = (f32[12,1024]{1,0:T(8,128)S(1)}, f32[12,1024,512]{1,2,0:T(8,128)}) fusion(f32[12]{0:T(128)S(1)} %get-tuple-element.1313, pred[1024,512]{0,1:T(8,128)(4,1)} %get-tuple-element.1316, f32[12]{0:T(128)S(1)} %get-tuple-element.1317, pred[1024,512]{0,1:T(8,128)(4,1)} %get-tuple-element.1318, f32[12]{0:T(128)S(1)} %get-tuple-element.1319, ...), kind=kOutput, calls=%fused_computation.555.clone.2 | convolution fusion | flops 1214238720 | bytes 44352980 | tf_op jit(solution)/shard_map/while/body/eval_jaxpr/qhd,khd->hqk/dot_general | solution.py:62
  708.5 16.9 fusion.290
  725.4 94.2 %fusion.291 = (f32[12,1024]{1,0:T(8,128)S(1)}, f32[12,1024,512]{1,2,0:T(8,128)}) fusion(f32[12]{0:T(128)S(1)} %get-tuple-element.1313, pred[1024,512]{0,1:T(8,128)(4,1)} %get-tuple-element.1316, f32[12]{0:T(128)S(1)} %get-tuple-element.1317, pred[1024,512]{0,1:T(8,128)(4,1)} %get-tuple-element.1318, f32[12]{0:T(128)S(1)} %get-tuple-element.1319, ...), kind=kOutput, calls=%fused_computation.555.clone.2 | convolution fusion | flops 1214238720 | bytes 44352980 | tf_op jit(solution)/shard_map/while/body/eval_jaxpr/qhd,khd->hqk/dot_general | solution.py:62
  832.0 720.3 %while.44 = (s32[]{:T(128)}, f32[1024,12,64]{0,2,1:T(8,128)}, f32[1024,12,64]{0,2,1:T(8,128)}, bf16[5,512,12,64]{1,3,2,0:T(8,128)(2,1)}, s32[1024]{0:T(1024)}, /...) while((s32[]{:T(128)}, f32[1024,12,64]{0,2,1:T(8,128)}, ...), condition=%wide.region_7.8_spmd.clone, body=%wide.region_6.7_spmd.clone.sunk | while | flops 2902983168 | bytes 175974048 | solution.py:141
  853.8 16.3 fusion.298
  870.1 87.7 %fusion.299 = f32[12,1024,512]{1,2,0:T(8,128)} fusion(f32[12,1024]{1,0:T(8,128)S(1)} %get-tuple-element.1645, f32[12]{0:T(128)S(1)} %get-tuple-element.1392, f32[12]{0:T(128)S(1)} %get-tuple-element.1393, f32[12]{0:T(128)S(1)} %get-tuple-element.1394, f32[12]{0:T(128)S(1)} %get-tuple-element.1395, f32[12]{0:T(128)S(1)} %get-tuple-element.1396, ...), kind=kOutput, calls=%fused_computation.119.clone.2 | convolution fusion | flops 1214251008 | bytes 44352980 | tf_op jit(solution)/shard_map/while/body/eval_jaxpr/qhd,khd->hqk/dot_general | solution.py:62
  957.9 17.3 bitcast_add_fusion.10
  992.6 16.3 fusion.298
  1008.9 87.7 %fusion.299 = f32[12,1024,512]{1,2,0:T(8,128)} fusion(f32[12,1024]{1,0:T(8,128)S(1)} %get-tuple-element.1645, f32[12]{0:T(128)S(1)} %get-tuple-element.1392, f32[12]{0:T(128)S(1)} %get-tuple-element.1393, f32[12]{0:T(128)S(1)} %get-tuple-element.1394, f32[12]{0:T(128)S(1)} %get-tuple-element.1395, f32[12]{0:T(128)S(1)} %get-tuple-element.1396, ...), kind=kOutput, calls=%fused_computation.119.clone.2 | convolution fusion | flops 1214251008 | bytes 44352980 | tf_op jit(solution)/shard_map/while/body/eval_jaxpr/qhd,khd->hqk/dot_general | solution.py:62
  1096.6 17.3 bitcast_add_fusion.10
  1131.3 16.3 fusion.298
  1147.6 87.7 %fusion.299 = f32[12,1024,512]{1,2,0:T(8,128)} fusion(f32[12,1024]{1,0:T(8,128)S(1)} %get-tuple-element.1645, f32[12]{0:T(128)S(1)} %get-tuple-element.1392, f32[12]{0:T(128)S(1)} %get-tuple-element.1393, f32[12]{0:T(128)S(1)} %get-tuple-element.1394, f32[12]{0:T(128)S(1)} %get-tuple-element.1395, f32[12]{0:T(128)S(1)} %get-tuple-element.1396, ...), kind=kOutput, calls=%fused_computation.119.clone.2 | convolution fusion | flops 1214251008 | bytes 44352980 | tf_op jit(solution)/shard_map/while/body/eval_jaxpr/qhd,khd->hqk/dot_general | solution.py:62
  1235.4 17.3 bitcast_add_fusion.10
  1270.1 16.3 fusion.298
  1286.4 87.7 %fusion.299 = f32[12,1024,512]{1,2,0:T(8,128)} fusion(f32[12,1024]{1,0:T(8,128)S(1)} %get-tuple-element.1645, f32[12]{0:T(128)S(1)} %get-tuple-element.1392, f32[12]{0:T(128)S(1)} %get-tuple-element.1393, f32[12]{0:T(128)S(1)} %get-tuple-element.1394, f32[12]{0:T(128)S(1)} %get-tuple-element.1395, f32[12]{0:T(128)S(1)} %get-tuple-element.1396, ...), kind=kOutput, calls=%fused_computation.119.clone.2 | convolution fusion | flops 1214251008 | bytes 44352980 | tf_op jit(solution)/shard_map/while/body/eval_jaxpr/qhd,khd->hqk/dot_general | solution.py:62
  1374.1 17.3 bitcast_add_fusion.10
  1408.8 16.3 fusion.298
  1425.1 87.7 %fusion.299 = f32[12,1024,512]{1,2,0:T(8,128)} fusion(f32[12,1024]{1,0:T(8,128)S(1)} %get-tuple-element.1645, f32[12]{0:T(128)S(1)} %get-tuple-element.1392, f32[12]{0:T(128)S(1)} %get-tuple-element.1393, f32[12]{0:T(128)S(1)} %get-tuple-element.1394, f32[12]{0:T(128)S(1)} %get-tuple-element.1395, f32[12]{0:T(128)S(1)} %get-tuple-element.1396, ...), kind=kOutput, calls=%fused_computation.119.clone.2 | convolution fusion | flops 1214251008 | bytes 44352980 | tf_op jit(solution)/shard_map/while/body/eval_jaxpr/qhd,khd->hqk/dot_general | solution.py:62
  1512.9 17.3 bitcast_add_fusion.10
  1592.0 137.9 %all-to-all-done = bf16[8,512,768]{2,1,0:T(8,128)(2,1)} async-done(((bf16[8,512,768]{2,1,0:T(8,128)(2,1)}), bf16[8,512,768]{2,1,0:T(8,128)(2,1)}, u32[]{:S(2)}, u32[]{:S(2)}) %all-to-all-start) | async-done | bytes 6291488 | tf_op jit(solution)/shard_map/all_to_all | solution.py:344
  1729.9 20.0 scatter_custom_fusion.1
  1749.9 22.9 multiply_convert_fusion
  1787.0 17.8 gather_fusion
  1817.7 168.2 %all-gather.1 = bf16[32,24,8]{1,2,0:T(8,128)(2,1)S(1)} all-gather(bf16[1,24,8]{1,2,0:T(8,128)(2,1)S(1)} %bitcast.640), channel_id=1, replica_groups=mesh['dp'=4,'expert'=8] {'dp','expert'}, dimensions={0}, use_global_device_ids=true | all-gather | bytes 12672 | tf_op jit(solution)/shard_map/all_gather | solution.py:32
  2038.5 144.7 %all_to_all.20 = bf16[8,512,768]{2,1,0:T(8,128)(2,1)} all-to-all(bf16[8,512,768]{2,1,0:T(8,128)(2,1)} %bitcast.560), channel_id=1, replica_groups=mesh['dp'=4,'expert'=8] {'expert'}, dimensions={0} | all-to-all | bytes 12582912 | tf_op jit(solution)/shard_map/all_to_all | solution.py:378
  2183.1 20.0 scatter_custom_fusion.3
  2204.9 27.1 fusion.170
  2246.4 17.9 gather_fusion.2
  2285.7 31.3 multiply_reduce_fusion.1
  2319.4 96.6 %all-to-all-done.3 = bf16[8,512,768]{2,1,0:T(8,128)(2,1)} async-done(((bf16[8,512,768]{2,1,0:T(8,128)(2,1)}), bf16[8,512,768]{2,1,0:T(8,128)(2,1)}, u32[]{:S(2)}, u32[]{:S(2)}) %all-to-all-start.3) | async-done | bytes 6291488 | tf_op jit(solution)/shard_map/all_to_all | solution.py:412
  2468.5 1233.8 %while.45 = (s32[]{:T(128)}, f32[1024,12,64]{0,2,1:T(8,128)}, f32[12,31]{0,1:T(8,128)}, bf16[5,512,12,64]{1,3,2,0:T(8,128)(2,1)}, bf16[5,512,12,64]{1,3,2,0:T(8,...) while((s32[]{:T(128)}, f32[1024,12,64]{0,2,1:T(8,128)}, ...), condition=%wide.region_69.72_spmd.clone, body=%wide.region_37.71_spmd.clone.sunk | while | flops 4908778496 | bytes 294730048 | solution.py:210
  2478.4 16.3 fusion.309
  2494.7 95.8 %fusion.310 = f32[12,1024,512]{1,2,0:T(8,128)} fusion(f32[12,1024]{1,0:T(8,128)S(1)} %get-tuple-element.1696, f32[12]{0:T(128)S(1)} %get-tuple-element.1488, f32[12]{0:T(128)S(1)} %get-tuple-element.1489, f32[12]{0:T(128)S(1)} %get-tuple-element.1490, f32[12]{0:T(128)S(1)} %get-tuple-element.1491, f32[12]{0:T(128)S(1)} %get-tuple-element.1492, ...), kind=kOutput, calls=%fused_computation.302.clone.1 | convolution fusion | flops 1214251008 | bytes 44352980 | tf_op jit(solution)/shard_map/while/body/eval_jaxpr/qhd,khd->hqk/dot_general | solution.py:62
  2601.9 43.8 %fusion.311 = (f32[12]{0:T(128)S(1)}, f32[12]{0:T(128)S(1)}, f32[12]{0:T(128)S(1)}, f32[12]{0:T(128)S(1)}, f32[12]{0:T(128)S(1)}, /*index=5*/f32[12]{0:T(128)S(1...) fusion(pred[1024,512]{0,1:T(8,128)(4,1)} %get-tuple-element.147, ...), kind=kOutput, calls=%fused_computation.295.clone.1 | convolution fusion | flops 994050048 | bytes 46973556 | tf_op jit(solution)/shard_map/while/body/eval_jaxpr/qhd,khd->hqk/dot_general | solution.py:184
  2645.8 56.0 %fusion.312 = (f32[12]{0:T(128)S(1)}, f32[12]{0:T(128)S(1)}, f32[12]{0:T(128)S(1)}, f32[12]{0:T(128)S(1)}, f32[12]{0:T(128)S(1)}, /*index=5*/f32[12]{0:T(128)S(1...) fusion(bf16[12,1024,512]{1,2,0:T(8,128)(2,1)S(1)} %get-tuple-el, ...), kind=kLoop, calls=%fused_computation.296.clone.1 | loop fusion | flops 232783600 | bytes 22020960 | tf_op jit(solution)/shard_map/while/body/eval_jaxpr/reduce_sum | solution.py:200
  2740.1 95.8 %fusion.310 = f32[12,1024,512]{1,2,0:T(8,128)} fusion(f32[12,1024]{1,0:T(8,128)S(1)} %get-tuple-element.1696, f32[12]{0:T(128)S(1)} %get-tuple-element.1488, f32[12]{0:T(128)S(1)} %get-tuple-element.1489, f32[12]{0:T(128)S(1)} %get-tuple-element.1490, f32[12]{0:T(128)S(1)} %get-tuple-element.1491, f32[12]{0:T(128)S(1)} %get-tuple-element.1492, ...), kind=kOutput, calls=%fused_computation.302.clone.1 | convolution fusion | flops 1214251008 | bytes 44352980 | tf_op jit(solution)/shard_map/while/body/eval_jaxpr/qhd,khd->hqk/dot_general | solution.py:62
  2847.4 43.8 %fusion.311 = (f32[12]{0:T(128)S(1)}, f32[12]{0:T(128)S(1)}, f32[12]{0:T(128)S(1)}, f32[12]{0:T(128)S(1)}, f32[12]{0:T(128)S(1)}, /*index=5*/f32[12]{0:T(128)S(1...) fusion(pred[1024,512]{0,1:T(8,128)(4,1)} %get-tuple-element.147, ...), kind=kOutput, calls=%fused_computation.295.clone.1 | convolution fusion | flops 994050048 | bytes 46973556 | tf_op jit(solution)/shard_map/while/body/eval_jaxpr/qhd,khd->hqk/dot_general | solution.py:184
  2891.2 56.0 %fusion.312 = (f32[12]{0:T(128)S(1)}, f32[12]{0:T(128)S(1)}, f32[12]{0:T(128)S(1)}, f32[12]{0:T(128)S(1)}, f32[12]{0:T(128)S(1)}, /*index=5*/f32[12]{0:T(128)S(1...) fusion(bf16[12,1024,512]{1,2,0:T(8,128)(2,1)S(1)} %get-tuple-el, ...), kind=kLoop, calls=%fused_computation.296.clone.1 | loop fusion | flops 232783600 | bytes 22020960 | tf_op jit(solution)/shard_map/while/body/eval_jaxpr/reduce_sum | solution.py:200
  2985.5 95.8 %fusion.310 = f32[12,1024,512]{1,2,0:T(8,128)} fusion(f32[12,1024]{1,0:T(8,128)S(1)} %get-tuple-element.1696, f32[12]{0:T(128)S(1)} %get-tuple-element.1488, f32[12]{0:T(128)S(1)} %get-tuple-element.1489, f32[12]{0:T(128)S(1)} %get-tuple-element.1490, f32[12]{0:T(128)S(1)} %get-tuple-element.1491, f32[12]{0:T(128)S(1)} %get-tuple-element.1492, ...), kind=kOutput, calls=%fused_computation.302.clone.1 | convolution fusion | flops 1214251008 | bytes 44352980 | tf_op jit(solution)/shard_map/while/body/eval_jaxpr/qhd,khd->hqk/dot_general | solution.py:62
  3092.7 43.8 %fusion.311 = (f32[12]{0:T(128)S(1)}, f32[12]{0:T(128)S(1)}, f32[12]{0:T(128)S(1)}, f32[12]{0:T(128)S(1)}, f32[12]{0:T(128)S(1)}, /*index=5*/f32[12]{0:T(128)S(1...) fusion(pred[1024,512]{0,1:T(8,128)(4,1)} %get-tuple-element.147, ...), kind=kOutput, calls=%fused_computation.295.clone.1 | convolution fusion | flops 994050048 | bytes 46973556 | tf_op jit(solution)/shard_map/while/body/eval_jaxpr/qhd,khd->hqk/dot_general | solution.py:184
  3136.6 56.0 %fusion.312 = (f32[12]{0:T(128)S(1)}, f32[12]{0:T(128)S(1)}, f32[12]{0:T(128)S(1)}, f32[12]{0:T(128)S(1)}, f32[12]{0:T(128)S(1)}, /*index=5*/f32[12]{0:T(128)S(1...) fusion(bf16[12,1024,512]{1,2,0:T(8,128)(2,1)S(1)} %get-tuple-el, ...), kind=kLoop, calls=%fused_computation.296.clone.1 | loop fusion | flops 232783600 | bytes 22020960 | tf_op jit(solution)/shard_map/while/body/eval_jaxpr/reduce_sum | solution.py:200
  3214.6 16.3 fusion.309
  3230.9 95.8 %fusion.310 = f32[12,1024,512]{1,2,0:T(8,128)} fusion(f32[12,1024]{1,0:T(8,128)S(1)} %get-tuple-element.1696, f32[12]{0:T(128)S(1)} %get-tuple-element.1488, f32[12]{0:T(128)S(1)} %get-tuple-element.1489, f32[12]{0:T(128)S(1)} %get-tuple-element.1490, f32[12]{0:T(128)S(1)} %get-tuple-element.1491, f32[12]{0:T(128)S(1)} %get-tuple-element.1492, ...), kind=kOutput, calls=%fused_computation.302.clone.1 | convolution fusion | flops 1214251008 | bytes 44352980 | tf_op jit(solution)/shard_map/while/body/eval_jaxpr/qhd,khd->hqk/dot_general | solution.py:62
  3338.1 43.8 %fusion.311 = (f32[12]{0:T(128)S(1)}, f32[12]{0:T(128)S(1)}, f32[12]{0:T(128)S(1)}, f32[12]{0:T(128)S(1)}, f32[12]{0:T(128)S(1)}, /*index=5*/f32[12]{0:T(128)S(1...) fusion(pred[1024,512]{0,1:T(8,128)(4,1)} %get-tuple-element.147, ...), kind=kOutput, calls=%fused_computation.295.clone.1 | convolution fusion | flops 994050048 | bytes 46973556 | tf_op jit(solution)/shard_map/while/body/eval_jaxpr/qhd,khd->hqk/dot_general | solution.py:184
  3382.0 56.0 %fusion.312 = (f32[12]{0:T(128)S(1)}, f32[12]{0:T(128)S(1)}, f32[12]{0:T(128)S(1)}, f32[12]{0:T(128)S(1)}, f32[12]{0:T(128)S(1)}, /*index=5*/f32[12]{0:T(128)S(1...) fusion(bf16[12,1024,512]{1,2,0:T(8,128)(2,1)S(1)} %get-tuple-el, ...), kind=kLoop, calls=%fused_computation.296.clone.1 | loop fusion | flops 232783600 | bytes 22020960 | tf_op jit(solution)/shard_map/while/body/eval_jaxpr/reduce_sum | solution.py:200
  3476.3 95.8 %fusion.310 = f32[12,1024,512]{1,2,0:T(8,128)} fusion(f32[12,1024]{1,0:T(8,128)S(1)} %get-tuple-element.1696, f32[12]{0:T(128)S(1)} %get-tuple-element.1488, f32[12]{0:T(128)S(1)} %get-tuple-element.1489, f32[12]{0:T(128)S(1)} %get-tuple-element.1490, f32[12]{0:T(128)S(1)} %get-tuple-element.1491, f32[12]{0:T(128)S(1)} %get-tuple-element.1492, ...), kind=kOutput, calls=%fused_computation.302.clone.1 | convolution fusion | flops 1214251008 | bytes 44352980 | tf_op jit(solution)/shard_map/while/body/eval_jaxpr/qhd,khd->hqk/dot_general | solution.py:62
  3583.5 43.8 %fusion.311 = (f32[12]{0:T(128)S(1)}, f32[12]{0:T(128)S(1)}, f32[12]{0:T(128)S(1)}, f32[12]{0:T(128)S(1)}, f32[12]{0:T(128)S(1)}, /*index=5*/f32[12]{0:T(128)S(1...) fusion(pred[1024,512]{0,1:T(8,128)(4,1)} %get-tuple-element.147, ...), kind=kOutput, calls=%fused_computation.295.clone.1 | convolution fusion | flops 994050048 | bytes 46973556 | tf_op jit(solution)/shard_map/while/body/eval_jaxpr/qhd,khd->hqk/dot_general | solution.py:184
  3627.3 56.0 %fusion.312 = (f32[12]{0:T(128)S(1)}, f32[12]{0:T(128)S(1)}, f32[12]{0:T(128)S(1)}, f32[12]{0:T(128)S(1)}, f32[12]{0:T(128)S(1)}, /*index=5*/f32[12]{0:T(128)S(1...) fusion(bf16[12,1024,512]{1,2,0:T(8,128)(2,1)S(1)} %get-tuple-el, ...), kind=kLoop, calls=%fused_computation.296.clone.1 | loop fusion | flops 232783600 | bytes 22020960 | tf_op jit(solution)/shard_map/while/body/eval_jaxpr/reduce_sum | solution.py:200
  3759.5 39.1 reduce-scatter.8.cloned.1.call-done
  3810.4 48.3 %reduce-scatter.18.cloned.1.call-done = bf16[1,768,768]{2,1,0:T(8,128)(2,1)} async-done(((bf16[1,3072,768]{2,1,0:T(8,128)(2,1)}), bf16[1,768,768]{2,1,0:T(8,128)(2,1)}) %reduce-scatter.18.cloned.1.call-update) | async-done | bytes 1179664 | tf_op jit(solution)/shard_map/reduce_scatter | solution.py:490
  3861.5 57.3 %reduce-scatter.16.cloned.1.call-done = bf16[1,192,3072]{2,1,0:T(8,128)(2,1)} async-done(((bf16[1,768,3072]{2,1,0:T(8,128)(2,1)}), bf16[1,192,3072]{2,1,0:T(8,128)(2,1)}) %reduce-scatter.16.cloned.1.call-update) | async-done | bytes 1179664 | tf_op jit(solution)/shard_map/reduce_scatter | solution.py:487
  3938.2 40.4 all-reduce.4
  3979.3 44.7 %reduce-scatter.14.cloned.1.call-done = f32[24,768]{1,0:T(8,128)} async-done(((f32[768,768]{1,0:T(8,128)}), f32[24,768]{1,0:T(8,128)}) %reduce-scatter.14.cloned.1.call-update) | async-done | bytes 73744 | tf_op jit(solution)/shard_map/reduce_scatter | solution.py:483
  4024.0 125.2 %reduce-scatter.12.cloned.1.call-done = f32[24,2304]{1,0:T(8,128)} async-done(((f32[768,2304]{1,0:T(8,128)}), f32[24,2304]{1,0:T(8,128)}) %reduce-scatter.12.cloned.1.call-update) | async-done | bytes 221200 | tf_op jit(solution)/shard_map/reduce_scatter | solution.py:482
  (659 shorter events, 791.7 us)
Async XLA Ops:
  7.2 66.8 %all-gather.7.cloned.1.call-start = ((), (), s32[]{:S(2)}) async-start(), calls=%async_computation.10 | async-start | bytes 3649536 | tf_op jit(solution)/shard_map/all_gather | solution.py:30
  7.9 118.4 %all-gather.9.cloned.1.call-start = ((), (), s32[]{:S(2)}) async-start(), calls=%async_computation.11 | async-start | bytes 3932160 | tf_op jit(solution)/shard_map/all_gather | solution.py:47
  9.7 70.7 %copy-start.23 = (bf16[1024,768]{0,1:T(8,128)(2,1)}, bf16[1024,768]{0,1:T(8,128)(2,1)S(1)}, u32[]{:S(2)}) copy-start(bf16[1024,768]{0,1:T(8,128)(2,1)S(1)} %copy.143) | copy-start | bytes 4718596
  10.8 63.2 %copy-start.77 = (f32[1024]{0:T(1024)}, f32[1024]{0:T(1024)S(1)}, u32[]{:S(2)}) copy-start(f32[1024]{0:T(1024)S(1)} %fusion.222) | copy-start | bytes 12292
  83.3 89.4 %all-gather.11.cloned.1.call-start = ((), (), s32[]{:S(2)}) async-start(), calls=%async_computation.12 | async-start | bytes 3932160 | tf_op jit(solution)/shard_map/all_gather | solution.py:46
  84.1 1470.5 %all-gather.13.cloned.1.call-start = ((), (), s32[]{:S(2)}) async-start(), calls=%async_computation.13 | async-start | bytes 1216512 | tf_op jit(solution)/shard_map/all_gather | solution.py:31
  221.5 94.2 %copy-start.34 = (f32[12,1024]{1,0:T(8,128)S(1)}, f32[12,1024]{1,0:T(8,128)}, u32[]{:S(2)}) copy-start(f32[12,1024]{1,0:T(8,128)} %get-tuple-element.1583) | copy-start | bytes 147460 | tf_op jit(solution)/shard_map/while
  347.5 94.2 %copy-start.34 = (f32[12,1024]{1,0:T(8,128)S(1)}, f32[12,1024]{1,0:T(8,128)}, u32[]{:S(2)}) copy-start(f32[12,1024]{1,0:T(8,128)} %get-tuple-element.1583) | copy-start | bytes 147460 | tf_op jit(solution)/shard_map/while
  473.5 94.2 %copy-start.34 = (f32[12,1024]{1,0:T(8,128)S(1)}, f32[12,1024]{1,0:T(8,128)}, u32[]{:S(2)}) copy-start(f32[12,1024]{1,0:T(8,128)} %get-tuple-element.1583) | copy-start | bytes 147460 | tf_op jit(solution)/shard_map/while
  599.4 94.2 %copy-start.34 = (f32[12,1024]{1,0:T(8,128)S(1)}, f32[12,1024]{1,0:T(8,128)}, u32[]{:S(2)}) copy-start(f32[12,1024]{1,0:T(8,128)} %get-tuple-element.1583) | copy-start | bytes 147460 | tf_op jit(solution)/shard_map/while
  725.4 94.2 %copy-start.34 = (f32[12,1024]{1,0:T(8,128)S(1)}, f32[12,1024]{1,0:T(8,128)}, u32[]{:S(2)}) copy-start(f32[12,1024]{1,0:T(8,128)} %get-tuple-element.1583) | copy-start | bytes 147460 | tf_op jit(solution)/shard_map/while
  832.0 722.6 %copy-start.24 = (bf16[1024,768]{0,1:T(8,128)(2,1)S(1)}, bf16[1024,768]{0,1:T(8,128)(2,1)}, u32[]{:S(2)}) copy-start(bf16[1024,768]{0,1:T(8,128)(2,1)} %copy-done.23) | copy-start | bytes 4718596
  870.1 87.7 %copy-start.7 = (f32[1024,12,64]{0,2,1:T(8,128)S(1)}, f32[1024,12,64]{0,2,1:T(8,128)}, u32[]{:S(2)}) copy-start(f32[1024,12,64]{0,2,1:T(8,128)} %get-tuple-element.1622) | copy-start | bytes 9437188 | tf_op jit(solution)/shard_map/while
  1008.9 87.7 %copy-start.7 = (f32[1024,12,64]{0,2,1:T(8,128)S(1)}, f32[1024,12,64]{0,2,1:T(8,128)}, u32[]{:S(2)}) copy-start(f32[1024,12,64]{0,2,1:T(8,128)} %get-tuple-element.1622) | copy-start | bytes 9437188 | tf_op jit(solution)/shard_map/while
  1147.6 87.7 %copy-start.7 = (f32[1024,12,64]{0,2,1:T(8,128)S(1)}, f32[1024,12,64]{0,2,1:T(8,128)}, u32[]{:S(2)}) copy-start(f32[1024,12,64]{0,2,1:T(8,128)} %get-tuple-element.1622) | copy-start | bytes 9437188 | tf_op jit(solution)/shard_map/while
  1286.4 87.7 %copy-start.7 = (f32[1024,12,64]{0,2,1:T(8,128)S(1)}, f32[1024,12,64]{0,2,1:T(8,128)}, u32[]{:S(2)}) copy-start(f32[1024,12,64]{0,2,1:T(8,128)} %get-tuple-element.1622) | copy-start | bytes 9437188 | tf_op jit(solution)/shard_map/while
  1425.1 87.7 %copy-start.7 = (f32[1024,12,64]{0,2,1:T(8,128)S(1)}, f32[1024,12,64]{0,2,1:T(8,128)}, u32[]{:S(2)}) copy-start(f32[1024,12,64]{0,2,1:T(8,128)} %get-tuple-element.1622) | copy-start | bytes 9437188 | tf_op jit(solution)/shard_map/while
  1585.5 144.3 %all-to-all-start = ((bf16[8,512,768]{2,1,0:T(8,128)(2,1)}), bf16[8,512,768]{2,1,0:T(8,128)(2,1)}, u32[]{:S(2)}, u32[]{:S(2)}) async-start(bf16[8,512,768]{2,1,0:T(8,128)(2,1)} %bitcast.557), calls=%async_computation | async-start | bytes 12582912 | tf_op jit(solution)/shard_map/all_to_all | solution.py:344
  1812.7 173.3 %copy-start.43 = (bf16[1024,768]{1,0:T(8,128)(2,1)S(1)}, bf16[1024,768]{1,0:T(8,128)(2,1)}, u32[]{:S(2)}) copy-start(bf16[1024,768]{1,0:T(8,128)(2,1)} %param.35) | copy-start | bytes 4718596
  1812.8 192.2 %all-to-all-start.1 = ((bf16[8,512,768]{2,1,0:T(8,128)(2,1)}), bf16[8,512,768]{2,1,0:T(8,128)(2,1)}, u32[]{:S(2)}, u32[]{:S(2)}) async-start(bf16[8,512,768]{2,1,0:T(8,128)(2,1)} %bitcast.559), calls=%async_computation.1 | async-start | bytes 12582912 | tf_op jit(solution)/shard_map/all_to_all | solution.py:361
  2272.3 143.7 %all-to-all-start.3 = ((bf16[8,512,768]{2,1,0:T(8,128)(2,1)}), bf16[8,512,768]{2,1,0:T(8,128)(2,1)}, u32[]{:S(2)}, u32[]{:S(2)}) async-start(bf16[8,512,768]{2,1,0:T(8,128)(2,1)} %bitcast.558), calls=%async_computation.3 | async-start | bytes 12582912 | tf_op jit(solution)/shard_map/all_to_all | solution.py:412
  2277.0 1482.5 %reduce-scatter.10.cloned.1.call-start = ((), (), s32[]{:S(2)}) async-start(), calls=%async_computation.15 | async-start | bytes 3932160 | tf_op jit(solution)/shard_map/reduce_scatter | solution.py:464
  2319.4 137.0 %copy-start.50 = (bf16[1024,8]{0,1:T(8,128)(2,1)}, bf16[1024,8]{0,1:T(8,128)(2,1)S(1)}, u32[]{:S(2)}) copy-start(bf16[1024,8]{0,1:T(8,128)(2,1)S(1)} %select_reduce_fusion.3) | copy-start | bytes 49156
  2494.7 95.8 %copy-start.12 = (pred[1024,512]{0,1:T(8,128)(4,1)}, pred[1024,512]{0,1:T(8,128)(4,1)S(1)}, u32[]{:S(2)}) copy-start(pred[1024,512]{0,1:T(8,128)(4,1)S(1)} %get-tuple-element.1521) | copy-start | bytes 1572868 | tf_op jit(solution)/shard_map/while
  2494.7 95.8 %copy-start.14 = (pred[1024,512]{0,1:T(8,128)(4,1)}, pred[1024,512]{0,1:T(8,128)(4,1)S(1)}, u32[]{:S(2)}) copy-start(pred[1024,512]{0,1:T(8,128)(4,1)S(1)} %get-tuple-element.1520) | copy-start | bytes 1572868 | tf_op jit(solution)/shard_map/while
  2494.7 95.8 %copy-start.16 = (pred[1024,512]{0,1:T(8,128)(4,1)}, pred[1024,512]{0,1:T(8,128)(4,1)S(1)}, u32[]{:S(2)}) copy-start(pred[1024,512]{0,1:T(8,128)(4,1)S(1)} %get-tuple-element.1519) | copy-start | bytes 1572868 | tf_op jit(solution)/shard_map/while
  2494.7 95.8 %copy-start.11 = (bf16[1024,12,64]{0,2,1:T(8,128)(2,1)S(1)}, bf16[1024,12,64]{0,2,1:T(8,128)(2,1)}, u32[]{:S(2)}) copy-start(bf16[1024,12,64]{0,2,1:T(8,128)(2,1)} %get-tuple-element.1698) | copy-start | bytes 4718596 | tf_op jit(solution)/shard_map/while
  2645.7 56.1 %copy-start = (bf16[12,1024,512]{1,2,0:T(8,128)(2,1)}, bf16[12,1024,512]{1,2,0:T(8,128)(2,1)S(1)}, u32[]{:S(2)}) copy-start(bf16[12,1024,512]{1,2,0:T(8,128)(2,1)S(1)} %get-tuple-element.1538) | copy-start | bytes 37748740 | tf_op jit(solution)/shard_map/while
  2645.7 56.1 %copy-start.45 = (f32[12,31]{0,1:T(8,128)S(1)}, f32[12,31]{0,1:T(8,128)}, u32[]{:S(2)}) copy-start(f32[12,31]{0,1:T(8,128)} %get-tuple-element.1668) | copy-start | bytes 4468 | tf_op jit(solution)/shard_map/while
  2645.8 56.2 %copy-start.1 = (f32[1024,12,64]{0,2,1:T(8,128)S(1)}, f32[1024,12,64]{0,2,1:T(8,128)}, u32[]{:S(2)}) copy-start(f32[1024,12,64]{0,2,1:T(8,128)} %get-tuple-element.1667) | copy-start | bytes 9437188 | tf_op jit(solution)/shard_map/while
  2740.1 95.8 %copy-start.12 = (pred[1024,512]{0,1:T(8,128)(4,1)}, pred[1024,512]{0,1:T(8,128)(4,1)S(1)}, u32[]{:S(2)}) copy-start(pred[1024,512]{0,1:T(8,128)(4,1)S(1)} %get-tuple-element.1521) | copy-start | bytes 1572868 | tf_op jit(solution)/shard_map/while
  2740.1 95.8 %copy-start.14 = (pred[1024,512]{0,1:T(8,128)(4,1)}, pred[1024,512]{0,1:T(8,128)(4,1)S(1)}, u32[]{:S(2)}) copy-start(pred[1024,512]{0,1:T(8,128)(4,1)S(1)} %get-tuple-element.1520) | copy-start | bytes 1572868 | tf_op jit(solution)/shard_map/while
  2740.1 95.8 %copy-start.16 = (pred[1024,512]{0,1:T(8,128)(4,1)}, pred[1024,512]{0,1:T(8,128)(4,1)S(1)}, u32[]{:S(2)}) copy-start(pred[1024,512]{0,1:T(8,128)(4,1)S(1)} %get-tuple-element.1519) | copy-start | bytes 1572868 | tf_op jit(solution)/shard_map/while
  2740.1 95.8 %copy-start.11 = (bf16[1024,12,64]{0,2,1:T(8,128)(2,1)S(1)}, bf16[1024,12,64]{0,2,1:T(8,128)(2,1)}, u32[]{:S(2)}) copy-start(bf16[1024,12,64]{0,2,1:T(8,128)(2,1)} %get-tuple-element.1698) | copy-start | bytes 4718596 | tf_op jit(solution)/shard_map/while
  2891.1 56.1 %copy-start = (bf16[12,1024,512]{1,2,0:T(8,128)(2,1)}, bf16[12,1024,512]{1,2,0:T(8,128)(2,1)S(1)}, u32[]{:S(2)}) copy-start(bf16[12,1024,512]{1,2,0:T(8,128)(2,1)S(1)} %get-tuple-element.1538) | copy-start | bytes 37748740 | tf_op jit(solution)/shard_map/while
  2891.2 56.1 %copy-start.45 = (f32[12,31]{0,1:T(8,128)S(1)}, f32[12,31]{0,1:T(8,128)}, u32[]{:S(2)}) copy-start(f32[12,31]{0,1:T(8,128)} %get-tuple-element.1668) | copy-start | bytes 4468 | tf_op jit(solution)/shard_map/while
  2891.2 56.2 %copy-start.1 = (f32[1024,12,64]{0,2,1:T(8,128)S(1)}, f32[1024,12,64]{0,2,1:T(8,128)}, u32[]{:S(2)}) copy-start(f32[1024,12,64]{0,2,1:T(8,128)} %get-tuple-element.1667) | copy-start | bytes 9437188 | tf_op jit(solution)/shard_map/while
  2985.5 95.8 %copy-start.12 = (pred[1024,512]{0,1:T(8,128)(4,1)}, pred[1024,512]{0,1:T(8,128)(4,1)S(1)}, u32[]{:S(2)}) copy-start(pred[1024,512]{0,1:T(8,128)(4,1)S(1)} %get-tuple-element.1521) | copy-start | bytes 1572868 | tf_op jit(solution)/shard_map/while
  2985.5 95.8 %copy-start.14 = (pred[1024,512]{0,1:T(8,128)(4,1)}, pred[1024,512]{0,1:T(8,128)(4,1)S(1)}, u32[]{:S(2)}) copy-start(pred[1024,512]{0,1:T(8,128)(4,1)S(1)} %get-tuple-element.1520) | copy-start | bytes 1572868 | tf_op jit(solution)/shard_map/while
  2985.5 95.8 %copy-start.16 = (pred[1024,512]{0,1:T(8,128)(4,1)}, pred[1024,512]{0,1:T(8,128)(4,1)S(1)}, u32[]{:S(2)}) copy-start(pred[1024,512]{0,1:T(8,128)(4,1)S(1)} %get-tuple-element.1519) | copy-start | bytes 1572868 | tf_op jit(solution)/shard_map/while
  2985.5 95.8 %copy-start.11 = (bf16[1024,12,64]{0,2,1:T(8,128)(2,1)S(1)}, bf16[1024,12,64]{0,2,1:T(8,128)(2,1)}, u32[]{:S(2)}) copy-start(bf16[1024,12,64]{0,2,1:T(8,128)(2,1)} %get-tuple-element.1698) | copy-start | bytes 4718596 | tf_op jit(solution)/shard_map/while
  3136.5 56.1 %copy-start = (bf16[12,1024,512]{1,2,0:T(8,128)(2,1)}, bf16[12,1024,512]{1,2,0:T(8,128)(2,1)S(1)}, u32[]{:S(2)}) copy-start(bf16[12,1024,512]{1,2,0:T(8,128)(2,1)S(1)} %get-tuple-element.1538) | copy-start | bytes 37748740 | tf_op jit(solution)/shard_map/while
  3136.5 56.1 %copy-start.45 = (f32[12,31]{0,1:T(8,128)S(1)}, f32[12,31]{0,1:T(8,128)}, u32[]{:S(2)}) copy-start(f32[12,31]{0,1:T(8,128)} %get-tuple-element.1668) | copy-start | bytes 4468 | tf_op jit(solution)/shard_map/while
  3136.6 56.2 %copy-start.1 = (f32[1024,12,64]{0,2,1:T(8,128)S(1)}, f32[1024,12,64]{0,2,1:T(8,128)}, u32[]{:S(2)}) copy-start(f32[1024,12,64]{0,2,1:T(8,128)} %get-tuple-element.1667) | copy-start | bytes 9437188 | tf_op jit(solution)/shard_map/while
  3230.9 95.8 %copy-start.12 = (pred[1024,512]{0,1:T(8,128)(4,1)}, pred[1024,512]{0,1:T(8,128)(4,1)S(1)}, u32[]{:S(2)}) copy-start(pred[1024,512]{0,1:T(8,128)(4,1)S(1)} %get-tuple-element.1521) | copy-start | bytes 1572868 | tf_op jit(solution)/shard_map/while
  3230.9 95.8 %copy-start.14 = (pred[1024,512]{0,1:T(8,128)(4,1)}, pred[1024,512]{0,1:T(8,128)(4,1)S(1)}, u32[]{:S(2)}) copy-start(pred[1024,512]{0,1:T(8,128)(4,1)S(1)} %get-tuple-element.1520) | copy-start | bytes 1572868 | tf_op jit(solution)/shard_map/while
  3230.9 95.8 %copy-start.16 = (pred[1024,512]{0,1:T(8,128)(4,1)}, pred[1024,512]{0,1:T(8,128)(4,1)S(1)}, u32[]{:S(2)}) copy-start(pred[1024,512]{0,1:T(8,128)(4,1)S(1)} %get-tuple-element.1519) | copy-start | bytes 1572868 | tf_op jit(solution)/shard_map/while
  3230.9 95.8 %copy-start.11 = (bf16[1024,12,64]{0,2,1:T(8,128)(2,1)S(1)}, bf16[1024,12,64]{0,2,1:T(8,128)(2,1)}, u32[]{:S(2)}) copy-start(bf16[1024,12,64]{0,2,1:T(8,128)(2,1)} %get-tuple-element.1698) | copy-start | bytes 4718596 | tf_op jit(solution)/shard_map/while
  3381.9 56.1 %copy-start.45 = (f32[12,31]{0,1:T(8,128)S(1)}, f32[12,31]{0,1:T(8,128)}, u32[]{:S(2)}) copy-start(f32[12,31]{0,1:T(8,128)} %get-tuple-element.1668) | copy-start | bytes 4468 | tf_op jit(solution)/shard_map/while
  3382.0 56.2 %copy-start.1 = (f32[1024,12,64]{0,2,1:T(8,128)S(1)}, f32[1024,12,64]{0,2,1:T(8,128)}, u32[]{:S(2)}) copy-start(f32[1024,12,64]{0,2,1:T(8,128)} %get-tuple-element.1667) | copy-start | bytes 9437188 | tf_op jit(solution)/shard_map/while
  3476.2 95.8 %copy-start.12 = (pred[1024,512]{0,1:T(8,128)(4,1)}, pred[1024,512]{0,1:T(8,128)(4,1)S(1)}, u32[]{:S(2)}) copy-start(pred[1024,512]{0,1:T(8,128)(4,1)S(1)} %get-tuple-element.1521) | copy-start | bytes 1572868 | tf_op jit(solution)/shard_map/while
  3476.2 95.8 %copy-start.14 = (pred[1024,512]{0,1:T(8,128)(4,1)}, pred[1024,512]{0,1:T(8,128)(4,1)S(1)}, u32[]{:S(2)}) copy-start(pred[1024,512]{0,1:T(8,128)(4,1)S(1)} %get-tuple-element.1520) | copy-start | bytes 1572868 | tf_op jit(solution)/shard_map/while
  3476.2 95.8 %copy-start.16 = (pred[1024,512]{0,1:T(8,128)(4,1)}, pred[1024,512]{0,1:T(8,128)(4,1)S(1)}, u32[]{:S(2)}) copy-start(pred[1024,512]{0,1:T(8,128)(4,1)S(1)} %get-tuple-element.1519) | copy-start | bytes 1572868 | tf_op jit(solution)/shard_map/while
  3476.2 95.8 %copy-start.11 = (bf16[1024,12,64]{0,2,1:T(8,128)(2,1)S(1)}, bf16[1024,12,64]{0,2,1:T(8,128)(2,1)}, u32[]{:S(2)}) copy-start(bf16[1024,12,64]{0,2,1:T(8,128)(2,1)} %get-tuple-element.1698) | copy-start | bytes 4718596 | tf_op jit(solution)/shard_map/while
  3627.3 56.1 %copy-start.45 = (f32[12,31]{0,1:T(8,128)S(1)}, f32[12,31]{0,1:T(8,128)}, u32[]{:S(2)}) copy-start(f32[12,31]{0,1:T(8,128)} %get-tuple-element.1668) | copy-start | bytes 4468 | tf_op jit(solution)/shard_map/while
  3627.3 56.2 %copy-start.1 = (f32[1024,12,64]{0,2,1:T(8,128)S(1)}, f32[1024,12,64]{0,2,1:T(8,128)}, u32[]{:S(2)}) copy-start(f32[1024,12,64]{0,2,1:T(8,128)} %get-tuple-element.1667) | copy-start | bytes 9437188 | tf_op jit(solution)/shard_map/while
  3709.7 88.9 %reduce-scatter.8.cloned.1.call-start = ((), (), s32[]{:S(2)}) async-start(), calls=%async_computation.14 | async-start | bytes 3932160 | tf_op jit(solution)/shard_map/reduce_scatter | solution.py:461
  3717.3 141.4 %reduce-scatter.18.cloned.1.call-start = ((), (), s32[]{:S(2)}) async-start(), calls=%async_computation.19 | async-start | bytes 5898240 | tf_op jit(solution)/shard_map/reduce_scatter | solution.py:490
  3733.3 185.5 %reduce-scatter.16.cloned.1.call-start = ((), (), s32[]{:S(2)}) async-start(), calls=%async_computation.18 | async-start | bytes 5898240 | tf_op jit(solution)/shard_map/reduce_scatter | solution.py:487
  3748.0 276.0 %reduce-scatter.14.cloned.1.call-start = ((), (), s32[]{:S(2)}) async-start(), calls=%async_computation.17 | async-start | bytes 2433024 | tf_op jit(solution)/shard_map/reduce_scatter | solution.py:483
  3753.6 395.6 %reduce-scatter.12.cloned.1.call-start = ((), (), s32[]{:S(2)}) async-start(), calls=%async_computation.16 | async-start | bytes 7299072 | tf_op jit(solution)/shard_map/reduce_scatter | solution.py:482
  3808.3 115.1 %copy-start.47 = (f32[12,31]{0,1:T(8,128)S(1)}, f32[12,31]{0,1:T(8,128)}, u32[]{:S(2)}) copy-start(f32[12,31]{0,1:T(8,128)} %get-tuple-element.220) | copy-start | bytes 4468
  3808.3 115.2 %copy-start.25 = (bf16[1024,768]{0,1:T(8,128)(2,1)S(1)}, bf16[1024,768]{0,1:T(8,128)(2,1)}, u32[]{:S(2)}) copy-start(bf16[1024,768]{0,1:T(8,128)(2,1)} %copy-done.23) | copy-start | bytes 4718596
  3810.4 111.4 %copy-start.36 = (bf16[1024,768]{0,1:T(8,128)(2,1)S(1)}, bf16[1024,768]{0,1:T(8,128)(2,1)}, u32[]{:S(2)}) copy-start(bf16[1024,768]{0,1:T(8,128)(2,1)} %get-tuple-element.867) | copy-start | bytes 4718596
  (129 other events, 1847.2 us)
Sparse Core Ops, SparseCore 0:
  11.0 62.9 all-gather.6
  83.4 42.7 all-gather.8
  128.7 43.9 all-gather.10
  175.6 54.2 all-gather.12
  3709.9 41.8 reduce-scatter.9
  3754.6 43.9 reduce-scatter.7
  3801.6 57.0 reduce-scatter.17
  3861.7 57.0 reduce-scatter.15
  3924.7 99.2 reduce-scatter.13
  4031.0 118.0 reduce-scatter.11
where the time goes:
time: 4170 us; the launch traced here: 4160 us
  matrix products  2050 us (49%)
  other arithmetic  714 us (17%)
  waiting for transfers between devices  645 us (15%)
  blocking collectives  361 us (9%)
  local copies, waits for them, and re-layouts  316 us (8%)
    dot_general x15, matrix products, block_scores(): jnp.einsum('qhd,khd->hqk', query, key_block, preferred_element_type=jnp.f...  1390 us
    reduce_sum x5, other arithmetic, grad_step(): jnp.sum(jnp.where(buckets[None] == bucket, grad_float, 0.0), axis=(1, 2))  280 us
    and x15, other arithmetic, block_scores(): (distance >= 0) & ((key_sequence[None, :] < 0) | (key_sequence[None, :] =...  247 us
    dot_general x5, matrix products, grad_step(): jnp.einsum('qhd,khd->hqk', grad_attended, value_block, preferred_element_...  219 us
    all_gather x1, blocking collectives, dense_gather(): lax.all_gather(w_router, ('dp', 'expert'), axis=0, tiled=True)  168 us
    all_to_all x1, blocking collectives, per_device(): lax.all_to_all(outgoing_grads, 'expert', split_axis=0, concat_axis=0, til...  145 us
    all_to_all x1, waiting for transfers between devices, per_device(): lax.all_to_all(outgoing, 'expert', split_axis=0, concat_axis=0, tiled=True)  138 us
    reduce_scatter x1, waiting for transfers between devices, per_device(): lax.psum_scatter(grad_qkv, ('dp', 'expert'), scatter_dimension=0, tiled=T...  125 us
  transfers between devices with their start and end apart: 13, of which 10 were waited for; matrix products, arithmetic and copies ran while one was open for 37% of the time, Pallas kernels for 0%

commit v1 on v0

--- a/solution.py
+++ b/solution.py
@@ -1,10 +1,13 @@
+import functools
+import math
 import jax
 import jax.numpy as jnp
 from jax import lax
+from jax.experimental import pallas as pl
+from jax.experimental.pallas import tpu as pltpu
 from jax.sharding import PartitionSpec as P
 
 PRIO = 4
-BLOCK = 512
 PROMPT = 2048
 
 
@@ -48,174 +51,290 @@
     )
 
 
-def bias_of(buckets, table_heads):
-    bias = jnp.zeros((table_heads.shape[0],) + buckets.shape, jnp.float32)
-    for bucket in range(table_heads.shape[1]):
-        bias = bias + jnp.where(buckets[None] == bucket, table_heads[:, bucket][:, None, None], 0.0)
-    return bias
-
-
-def block_scores(
-    query, key_block, key_position, key_sequence, query_position, query_sequence, table_heads, scale
-):
-    scores = (
-        jnp.einsum("qhd,khd->hqk", query, key_block, preferred_element_type=jnp.float32) * scale
-    )
-    distance = query_position[:, None] - key_position[None, :]
-    seen = (distance >= 0) & (
-        (key_sequence[None, :] < 0) | (key_sequence[None, :] == query_sequence[:, None])
-    )
-    buckets = bucket_of(distance)
-    scores = scores + bias_of(buckets, table_heads)
-    return (scores, seen[None], buckets)
-
-
-def attention_forward(
-    query,
-    all_keys,
-    all_values,
-    key_position,
-    key_sequence,
-    query_position,
-    query_sequence,
-    table_heads,
-    scale,
-):
-    rows, heads, head_size = query.shape
-    blocks = all_keys.shape[0] // BLOCK
-    key_blocks = all_keys.reshape(blocks, BLOCK, heads, head_size)
-    value_blocks = all_values.reshape(blocks, BLOCK, heads, head_size)
-    position_blocks = key_position.reshape(blocks, BLOCK)
-    sequence_blocks = key_sequence.reshape(blocks, BLOCK)
-
-    def stats_step(carry, block_in):
-        running_max, running_sum = carry
-        key_block, position_block, sequence_block = block_in
-        scores, seen, _ = block_scores(
-            query,
-            key_block,
-            position_block,
-            sequence_block,
-            query_position,
-            query_sequence,
-            table_heads,
-            scale,
-        )
-        scores = jnp.where(seen, scores, MASKED)
-        new_max = jnp.maximum(running_max, jnp.max(scores, axis=-1))
-        shifted = jnp.where(seen, jnp.exp(scores - new_max[..., None]), 0.0)
-        running_sum = running_sum * jnp.exp(running_max - new_max) + jnp.sum(shifted, axis=-1)
-        return ((new_max, running_sum), None)
-
-    start = (jnp.full((heads, rows), MASKED, jnp.float32), jnp.zeros((heads, rows), jnp.float32))
-    (largest, summed), _ = lax.scan(
-        stats_step, start, (key_blocks, position_blocks, sequence_blocks)
-    )
-    log_total = largest + jnp.log(summed)
-
-    def value_step(carry, block_in):
-        rounded_sum, leftover_sum = carry
-        key_block, value_block, position_block, sequence_block = block_in
-        scores, seen, _ = block_scores(
-            query,
-            key_block,
-            position_block,
-            sequence_block,
-            query_position,
-            query_sequence,
-            table_heads,
-            scale,
-        )
-        weights = jnp.where(seen, jnp.exp(scores - log_total[..., None]), 0.0)
-        rounded = weights.astype(jnp.bfloat16)
-        leftover = (weights - rounded.astype(jnp.float32)).astype(jnp.bfloat16)
-        rounded_sum = rounded_sum + jnp.einsum(
-            "hqk,khd->qhd", rounded, value_block, preferred_element_type=jnp.float32
-        )
-        leftover_sum = leftover_sum + jnp.einsum(
-            "hqk,khd->qhd", leftover, value_block, preferred_element_type=jnp.float32
-        )
-        return ((rounded_sum, leftover_sum), None)
-
-    empty = jnp.zeros((rows, heads, head_size), jnp.float32)
-    (rounded_sum, leftover_sum), _ = lax.scan(
-        value_step, (empty, empty), (key_blocks, value_blocks, position_blocks, sequence_blocks)
-    )
-    return (rounded_sum, rounded_sum + leftover_sum, log_total)
-
-
-def attention_backward(
-    query,
-    all_keys,
-    all_values,
-    key_position,
-    key_sequence,
-    query_position,
-    query_sequence,
-    table_heads,
-    scale,
-    log_total,
-    grad_attended,
-    delta,
-):
-    rows, heads, head_size = query.shape
-    buckets_count = table_heads.shape[1]
-    blocks = all_keys.shape[0] // BLOCK
-    key_blocks = all_keys.reshape(blocks, BLOCK, heads, head_size)
-    value_blocks = all_values.reshape(blocks, BLOCK, heads, head_size)
-    position_blocks = key_position.reshape(blocks, BLOCK)
-    sequence_blocks = key_sequence.reshape(blocks, BLOCK)
-
-    def grad_step(carry, block_in):
-        grad_query, grad_table = carry
-        key_block, value_block, position_block, sequence_block = block_in
-        scores, seen, buckets = block_scores(
-            query,
-            key_block,
-            position_block,
-            sequence_block,
-            query_position,
-            query_sequence,
-            table_heads,
-            scale,
-        )
-        weights = jnp.where(seen, jnp.exp(scores - log_total[..., None]), 0.0)
-        rounded = weights.astype(jnp.bfloat16)
-        grad_weights = jnp.einsum(
-            "qhd,khd->hqk", grad_attended, value_block, preferred_element_type=jnp.float32
-        )
-        grad_scores = (weights * (grad_weights - delta[..., None])).astype(jnp.bfloat16)
-        grad_query = grad_query + jnp.einsum(
-            "hqk,khd->qhd", grad_scores, key_block, preferred_element_type=jnp.float32
-        )
-        grad_key = (
-            jnp.einsum("hqk,qhd->khd", grad_scores, query, preferred_element_type=jnp.float32)
-            * scale
-        )
-        grad_value = jnp.einsum(
-            "hqk,qhd->khd", rounded, grad_attended, preferred_element_type=jnp.float32
-        )
-        grad_float = grad_scores.astype(jnp.float32)
-        columns = [
-            jnp.sum(jnp.where(buckets[None] == bucket, grad_float, 0.0), axis=(1, 2))
-            for bucket in range(buckets_count)
-        ]
-        grad_table = grad_table + jnp.stack(columns, axis=1)
-        return ((grad_query, grad_table), (grad_key, grad_value))
-
-    start = (
-        jnp.zeros((rows, heads, head_size), jnp.float32),
-        jnp.zeros((heads, buckets_count), jnp.float32),
-    )
-    (grad_query, grad_table), (grad_keys, grad_values) = lax.scan(
-        grad_step, start, (key_blocks, value_blocks, position_blocks, sequence_blocks)
-    )
-    return (
-        grad_query * scale,
-        grad_table,
-        grad_keys.reshape(-1, heads * head_size),
-        grad_values.reshape(-1, heads * head_size),
-    )
+LOG2E = math.log2(math.e)
+F32, BF16 = jnp.float32, jnp.bfloat16
+QT = 256
+KT = 512
+RUN = 256
+ROWS = 32
+NT = (((1,), (1,)), ((), ()))
+NN = (((1,), (0,)), ((), ()))
+
+def dot(a, b, dims=NN):
+    return lax.dot_general(a, b, dims, preferred_element_type=F32)
+
+def bias_rows(rel_table):
+    width = PROMPT + 512 + RUN
+    distance = PROMPT + RUN - jnp.arange(width)[None, :] + jnp.arange(8)[:, None]
+    bucket = bucket_of(distance)
+    table = rel_table.T[:, None, None, :] * LOG2E
+    hot = (bucket[..., None] == jnp.arange(rel_table.shape[0])).astype(F32)
+    rows = jnp.sum(hot[None] * table, axis=-1)
+    return jnp.where(distance[None] >= 0, rows, MASKED)
+
+def build_bias(info, base, row_start, t_scr, b_scr):
+    width = base.shape[-1]
+    for a in range(16):
+        t_scr[8 * a:8 * a + 8, :] = pltpu.roll(base, 8 * a, 1) if a else base
+    lane = lax.broadcasted_iota(jnp.int32, (ROWS, 128), 1)
+    sub = lax.broadcasted_iota(jnp.int32, (ROWS, 128), 0)
+    for s in range(4):
+        start, end = info[s], info[s + 1]
+        turn = start % 128
+        left = (128 - turn) % 128
+        here = (lane < left) | (left == 0)
+        def place(g, _):
+            at = pl.ds(pl.multiple_of(ROWS * g, ROWS), ROWS)
+            first = start - turn + RUN - 128 * (g // (128 // ROWS))
+            of = pl.ds(pl.multiple_of(ROWS * (g % (128 // ROWS)), ROWS), ROWS)
+            mine = sub + ROWS * g >= start
+            turned = None
+            for b in range(PROMPT // 128 + 1):
+                after = pltpu.roll(t_scr[of, pl.ds(pl.multiple_of(first + 128 * b, 128), 128)], left, 1)
+                if b:
+                    cols = slice(128 * b - 128, 128 * b)
+                    b_scr[at, cols] = jnp.where(mine, jnp.where(here, turned, after), b_scr[at, cols])
+                turned = after
+            return 0
+        lax.fori_loop(start // ROWS, (end + ROWS - 1) // ROWS, place, 0)
+    lane = lax.broadcasted_iota(jnp.int32, (128, 128), 1)
+    for i in range(KT // 128):
+        rows = slice(128 * i, 128 * i + 128)
+        own = row_start[rows, :]
+        for b in range(KT // 128):
+            first = PROMPT + RUN - 128 * i + 128 * b
+            b_scr[rows, PROMPT + 128 * b:PROMPT + 128 * b + 128] = jnp.where(
+                lane + 128 * b >= own, t_scr[:, first:first + 128], MASKED)
+
+def own_lanes(h, rows):
+    lane = lax.broadcasted_iota(jnp.int32, (rows, 128), 1)
+    return lane // 64 == h % 2
+
+def fwd_kernel(scale2, info, q_ref, k_ref, v_ref, r_ref, st_ref, o_ref, lse_ref, t_scr, b_scr):
+    h = pl.program_id(0)
+    dp = info[5]
+    build_bias(info, r_ref[0], st_ref, t_scr, b_scr)
+    own = own_lanes(h, QT)
+    head_lane = lax.broadcasted_iota(jnp.int32, (QT, 128), 1) == h
+
+    def tile(first, key_tiles, bias_of, block):
+        rows = pl.ds(first, QT)
+        q = jnp.where(own, q_ref[rows, :], jnp.zeros((), BF16))
+        def step(t, carry):
+            m, l, acc = carry
+            cols = pl.ds(pl.multiple_of(block(t) * KT, KT), KT)
+            s = dot(q, k_ref[cols, :], NT) * scale2 + bias_of(t)
+            new = jnp.maximum(m, jnp.max(s, axis=1, keepdims=True))
+            keep = jnp.exp2(m - new)
+            p = jnp.exp2(s - new[:, :1])
+            part = p[:, :128]
+            for c in range(1, KT // 128):
+                part = part + p[:, 128 * c:128 * (c + 1)]
+            return new, l * keep + part, acc * keep + dot(p.astype(BF16), v_ref[cols, :])
+        zero = jnp.zeros((QT, 128), F32)
+        m, l, acc = lax.fori_loop(0, key_tiles, step, (jnp.full((QT, 128), MASKED, F32), zero, zero))
+        l = jnp.sum(l, axis=1, keepdims=True)
+        o_ref[rows, :] = jnp.where(own, acc / l, o_ref[rows, :])
+        lse_ref[rows, :] = jnp.where(head_lane, m + jnp.log2(l), lse_ref[rows, :])
+
+    for j in range(2):
+        shift = PROMPT - KT * dp - QT * j + RUN
+        def bias(t, shift=shift):
+            first = (dp - t) * KT + shift
+            return jnp.concatenate([t_scr[:, pl.ds(pl.multiple_of(first - 128 * x, 128), KT)] for x in range(QT // 128)], axis=0)
+        tile(QT * j, dp + 1, bias, lambda t: dp - t)
+    for j in range(2):
+        tile(KT + QT * j, PROMPT // KT + 1,
+             lambda t: b_scr[pl.ds(QT * j, QT), pl.ds(pl.multiple_of(t * KT, KT), KT)], lambda t: t)
+
+def attention_forward(info, q, k, v, rows_bias, row_start, heads):
+    n, width = q.shape
+    keys = k.shape[0]
+    pair = lambda r: pl.BlockSpec((r, 128), lambda h, *_: (0, h // 2))
+    whole = pl.BlockSpec((n, 128), lambda h, *_: (0, 0))
+    scale2 = (width // heads) ** -0.5 * LOG2E
+    return pl.pallas_call(
+        functools.partial(fwd_kernel, scale2),
+        grid_spec=pltpu.PrefetchScalarGridSpec(
+            num_scalar_prefetch=1, grid=(heads,),
+            in_specs=[pair(n), pair(keys), pair(keys),
+                      pl.BlockSpec((1, 8, rows_bias.shape[2]), lambda h, *_: (h, 0, 0)),
+                      pl.BlockSpec((KT, 128), lambda h, *_: (0, 0))],
+            out_specs=[pair(n), whole],
+            scratch_shapes=[pltpu.VMEM((128, rows_bias.shape[2]), F32), pltpu.VMEM((KT, PROMPT + KT), F32)]),
+        out_shape=[jax.ShapeDtypeStruct((n, width), F32), jax.ShapeDtypeStruct((n, 128), F32)],
+        compiler_params=pltpu.CompilerParams(vmem_limit_bytes=60 << 20),
+        name="attention_forward",
+    )(info, q, k, v, rows_bias, row_start)
+
+def split3(x):
+    hi = x.astype(BF16)
+    rest = x - hi.astype(F32)
+    mid = rest.astype(BF16)
+    return hi, mid, (rest - mid.astype(F32)).astype(BF16)
+
+def bwd_kernel(scale, info, q_ref, do_ref, o_ref, lse_ref, k_ref, v_ref, r_ref, st_ref,
+               dq_ref, dk_ref, dv_ref, dd_ref,
+               t_scr, b_scr, e_scr, db_scr, qa, da, ka, va, qt, dot_t, dkt, dvt):
+    h = pl.program_id(0)
+    dp = info[5]
+    n, keys = q_ref.shape[0], k_ref.shape[0]
+    half = h % 2
+    build_bias(info, r_ref[0], st_ref, t_scr, b_scr)
+    base = pl.multiple_of(64 * half, 64)
+    other = 64 - 64 * half
+
+    @pl.when(half == 0)
+    def _():
+        qt[...] = q_ref[...].T
+        dot_t[...] = do_ref[...].T
+        dq_ref[...] = jnp.zeros_like(dq_ref)
+
+    lane_n = lax.broadcasted_iota(jnp.int32, (QT, 128), 1)
+    own_n = lane_n // 64 == half
+    def augment(i, _):
+        rows = pl.ds(pl.multiple_of(i * QT, QT), QT)
+        lse = jnp.sum(jnp.where(lane_n == h, lse_ref[rows, :], 0.0), axis=1, keepdims=True)
+        parts = split3(-lse / (scale * LOG2E))
+        aug = jnp.zeros((QT, 128), BF16)
+        for x in range(3):
+            aug = jnp.where(lane_n == other + x, jnp.broadcast_to(parts[x], (QT, 128)), aug)
+        qa[rows, :] = jnp.where(own_n, q_ref[rows, :], aug)
+        do = do_ref[rows, :]
+        delta = jnp.sum(jnp.where(own_n, do.astype(F32) * o_ref[rows, :], 0.0), axis=1, keepdims=True)
+        parts = split3(-delta)
+        aug = jnp.zeros((QT, 128), BF16)
+        for x in range(3):
+            aug = jnp.where(lane_n == other + x, jnp.broadcast_to(parts[x], (QT, 128)), aug)
+        da[rows, :] = jnp.where(own_n, do, aug)
+        return 0
+    lax.fori_loop(0, n // QT, augment, 0)
+    lane_k = lax.broadcasted_iota(jnp.int32, (KT, 128), 1)
+    ones = jnp.where((lane_k >= other) & (lane_k < other + 3), 1.0, 0.0).astype(BF16)
+    own_k = lane_k // 64 == half
+    def augment_keys(i, _):
+        rows = pl.ds(pl.multiple_of(i * KT, KT), KT)
+        ka[rows, :] = jnp.where(own_k, k_ref[rows, :], ones)
+        va[rows, :] = jnp.where(own_k, v_ref[rows, :], ones)
+        return 0
+    lax.fori_loop(0, keys // KT, augment_keys, 0)
+    head_rows = pl.ds(base, 64)
+    dkt[head_rows, :] = jnp.zeros((64, keys), F32)
+    dvt[head_rows, :] = jnp.zeros((64, keys), F32)
+    e_scr[...] = jnp.zeros_like(e_scr)
+
+    def tile(first, key_tiles, bias_of, grad_bias):
+        rows = pl.ds(first, QT)
+        q, do = qa[rows, :], da[rows, :]
+        q_t, do_t = qt[head_rows, rows], dot_t[head_rows, rows]
+        def step(t, dq):
+            cols = pl.ds(pl.multiple_of(t * KT, KT), KT)
+            kk = ka[cols, :]
+            p = jnp.exp2(dot(q, kk, NT) * (scale * LOG2E) + bias_of(t))
+            ds = p * dot(do, va[cols, :], NT)
+            grad_bias(t, ds)
+            low = ds.astype(BF16)
+            dvt[head_rows, cols] += dot(do_t, p.astype(BF16))
+            dkt[head_rows, cols] += dot(q_t, low)
+            return dq + dot(low, kk)
+        dq = lax.fori_loop(0, key_tiles, step, jnp.zeros((QT, 128), F32))
+        dq_ref[rows, :] = jnp.where(own_n, dq * scale, dq_ref[rows, :].astype(F32)).astype(BF16)
+
+    for j in range(2):
+        shift = PROMPT - KT * dp - QT * j + RUN
+        def part(t, x, shift=shift):
+            return (slice(None), pl.ds(pl.multiple_of(t * KT + shift - 128 * x, 128), KT))
+        def bias(t):
+            return jnp.concatenate([t_scr[part(t, x)] for x in range(QT // 128)], axis=0)
+        def add(t, ds):
+            for x in range(QT // 128):
+                e_scr[part(t, x)] += ds[128 * x:128 * x + 128, :]
+        tile(QT * j, dp + 1, bias, add)
+    for j in range(2):
+        def where(t):
+            return (pl.ds(QT * j, QT), pl.ds(pl.multiple_of(t * KT, KT), KT))
+        def put(t, ds):
+            db_scr[where(t)] = ds
+        tile(KT + QT * j, PROMPT // KT + 1, lambda t: b_scr[where(t)], put)
+
+    lane = lax.broadcasted_iota(jnp.int32, (ROWS, 128), 1)
+    sub = lax.broadcasted_iota(jnp.int32, (ROWS, 128), 0)
+    for s in range(4):
+        start, end = info[s], info[s + 1]
+        turn = start % 128
+        def fold(g, _):
+            at = pl.ds(pl.multiple_of(ROWS * g, ROWS), ROWS)
+            first = start - turn + RUN - 128 * (g // (128 // ROWS))
+            to = pl.ds(pl.multiple_of(ROWS * (g % (128 // ROWS)), ROWS), ROWS)
+            mine = (sub + ROWS * g >= start) & (sub + ROWS * g < end)
+            before = jnp.zeros((ROWS, 128), F32)
+            for b in range(PROMPT // 128 + 1):
+                if b < PROMPT // 128:
+                    turned = pltpu.roll(jnp.where(mine, db_scr[at, 128 * b:128 * b + 128], 0.0), turn, 1)
+                else:
+                    turned = jnp.zeros((ROWS, 128), F32)
+                e_scr[to, pl.ds(pl.multiple_of(first + 128 * b, 128), 128)] += jnp.where(lane >= turn, turned, before)
+                before = turned
+            return 0
+        lax.fori_loop(start // ROWS, (end + ROWS - 1) // ROWS, fold, 0)
+    for i in range(KT // 128):
+        first = PROMPT + RUN - 128 * i
+        e_scr[:, first:first + KT] += db_scr[128 * i:128 * i + 128, PROMPT:]
+    width = r_ref.shape[2]
+    acc = e_scr[0:8, :]
+    for a in range(1, 16):
+        acc = acc + pltpu.roll(e_scr[8 * a:8 * a + 8, :], width - 8 * a, 1)
+    total = acc[0:1, :]
+    for i in range(1, 8):
+        total = total + pltpu.roll(acc, width - i, 1)[i:i + 1, :]
+    dd_ref[0] = total
+
+    @pl.when(half == 1)
+    def _():
+        dk_ref[...] = (dkt[...] * scale).T.astype(BF16)
+        dv_ref[...] = dvt[...].T.astype(BF16)
+
+def attention_backward(info, q, do, o32, lse, k, v, rows_bias, row_start, heads):
+    n, width = q.shape
+    keys = k.shape[0]
+    wide = rows_bias.shape[2]
+    pair = lambda r: pl.BlockSpec((r, 128), lambda h, *_: (0, h // 2))
+    whole = pl.BlockSpec((n, 128), lambda h, *_: (0, 0))
+    line = pl.BlockSpec((1, 1, wide), lambda h, *_: (h, 0, 0))
+    scale = (width // heads) ** -0.5
+    cols = PROMPT + KT
+    return pl.pallas_call(
+        functools.partial(bwd_kernel, scale),
+        grid_spec=pltpu.PrefetchScalarGridSpec(
+            num_scalar_prefetch=1, grid=(heads,),
+            in_specs=[pair(n), pair(n), pair(n), whole, pair(keys), pair(keys),
+                      pl.BlockSpec((1, 8, wide), lambda h, *_: (h, 0, 0)), pl.BlockSpec((KT, 128), lambda h, *_: (0, 0))],
+            out_specs=[pair(n), pair(keys), pair(keys), line],
+            scratch_shapes=[pltpu.VMEM((128, wide), F32), pltpu.VMEM((KT, cols), F32),
+                            pltpu.VMEM((128, wide), F32), pltpu.VMEM((KT, cols), F32),
+                            pltpu.VMEM((n, 128), BF16), pltpu.VMEM((n, 128), BF16),
+                            pltpu.VMEM((keys, 128), BF16), pltpu.VMEM((keys, 128), BF16),
+                            pltpu.VMEM((128, n), BF16), pltpu.VMEM((128, n), BF16),
+                            pltpu.VMEM((128, keys), F32), pltpu.VMEM((128, keys), F32)]),
+        out_shape=[jax.ShapeDtypeStruct((n, width), BF16), jax.ShapeDtypeStruct((keys, width), BF16),
+                   jax.ShapeDtypeStruct((keys, width), BF16), jax.ShapeDtypeStruct((heads, 1, wide), F32)],
+        compiler_params=pltpu.CompilerParams(vmem_limit_bytes=60 << 20),
+        name="attention_backward",
+    )(info, q, do, o32, lse, k, v, rows_bias, row_start)
+
+def info_of(ids, dp):
+    starts = jnp.sum((ids[None, :] < jnp.arange(5)[:, None]).astype(jnp.int32), axis=1)
+    return jnp.concatenate([starts, jnp.reshape(dp, (1,)).astype(jnp.int32)])
+
+def table_grad(dd, buckets):
+    width = dd.shape[2]
+    distance = PROMPT + RUN - jnp.arange(width)
+    hot = ((bucket_of(distance)[:, None] == jnp.arange(buckets)[None, :]) & (distance >= 0)[:, None]).astype(F32)
+    return jnp.dot(dd[:, 0, :], hot, precision=lax.Precision.HIGHEST)
+
+def row_start_of(ids):
+    starts = jnp.sum((ids[None, :] < ids[:, None]).astype(jnp.int32), axis=1)
+    return jnp.broadcast_to(starts[:, None], (ids.shape[0], 128))
 
 
 def per_device(
@@ -235,50 +354,30 @@
 ):
     rows, width = tokens_in.shape
     heads = rel_table.shape[1]
-    head_size = width // heads
-    scale = head_size ** (-0.5)
     dp_count = lax.axis_size("dp")
     dp_index = lax.axis_index("dp")
     prompt_rows = PROMPT // dp_count
     cont_rows = rows - prompt_rows
     local_ids = cont_ids[0]
-    same = local_ids[:, None] == local_ids[None, :]
-    earlier = jnp.arange(cont_rows)[None, :] < jnp.arange(cont_rows)[:, None]
-    offset = jnp.sum((same & earlier).astype(jnp.int32), axis=1)
-    prompt_position = dp_index * prompt_rows + jnp.arange(prompt_rows, dtype=jnp.int32)
-    query_position = jnp.concatenate([prompt_position, PROMPT + offset])
-    query_sequence = jnp.concatenate([jnp.full((prompt_rows,), -1, jnp.int32), local_ids])
-    key_position = jnp.concatenate([jnp.arange(PROMPT, dtype=jnp.int32), PROMPT + offset])
-    key_sequence = jnp.concatenate([jnp.full((PROMPT,), -1, jnp.int32), local_ids])
-    table_heads = rel_table.T
+    info = info_of(local_ids, dp_index)
+    row_start = row_start_of(local_ids)
+    rows_bias = bias_rows(rel_table)
     whole_qkv, whole_out, whole_router = dense_gather(w_qkv, w_out, w_router)
     inputs = tokens_in.astype(jnp.float32)
     normed_attn = normed(inputs, gain_attn).astype(jnp.bfloat16)
     projected = jnp.dot(normed_attn, whole_qkv, preferred_element_type=jnp.float32).astype(
         jnp.bfloat16
     )
-    query = projected[:, :width].reshape(rows, heads, head_size)
+    query = projected[:, :width]
     own_keys = projected[:, width : 2 * width]
     own_values = projected[:, 2 * width :]
     prompt_keys, prompt_values = prompt_gather(own_keys[:prompt_rows], own_values[:prompt_rows])
-    all_keys = jnp.concatenate([prompt_keys, own_keys[prompt_rows:]], axis=0).reshape(
-        -1, heads, head_size
-    )
-    all_values = jnp.concatenate([prompt_values, own_values[prompt_rows:]], axis=0).reshape(
-        -1, heads, head_size
-    )
-    rounded_sum, exact_sum, log_total = attention_forward(
-        query,
-        all_keys,
-        all_values,
-        key_position,
-        key_sequence,
-        query_position,
-        query_sequence,
-        table_heads,
-        scale,
-    )
-    attended = rounded_sum.reshape(rows, width).astype(jnp.bfloat16)
+    all_keys = jnp.concatenate([prompt_keys, own_keys[prompt_rows:]], axis=0)
+    all_values = jnp.concatenate([prompt_values, own_values[prompt_rows:]], axis=0)
+    exact, log_total = attention_forward(
+        info, query, all_keys, all_values, rows_bias, row_start, heads
+    )
+    attended = exact.astype(jnp.bfloat16)
     middle = inputs + jnp.dot(attended, whole_out, preferred_element_type=jnp.float32)
     normed_ffn = normed(middle, gain_ffn).astype(jnp.bfloat16)
     logits = jnp.dot(normed_ffn, whole_router, preferred_element_type=jnp.float32)
@@ -430,44 +529,24 @@
     grad_middle = grad_out + grad_middle_part
     grad_branch = grad_middle.astype(jnp.bfloat16)
     grad_out_weight = jnp.dot(attended.T, grad_branch, preferred_element_type=jnp.float32)
-    grad_attended = (
-        jnp.dot(grad_branch, back_out.T, preferred_element_type=jnp.float32)
-        .astype(jnp.bfloat16)
-        .reshape(rows, heads, head_size)
-    )
-    delta = jnp.sum(grad_attended.astype(jnp.float32) * exact_sum, axis=-1).T
-    back_keys, back_values = prompt_gather(own_keys[:prompt_rows], own_values[:prompt_rows])
-    keys_again = jnp.concatenate([back_keys, own_keys[prompt_rows:]], axis=0).reshape(
-        -1, heads, head_size
-    )
-    values_again = jnp.concatenate([back_values, own_values[prompt_rows:]], axis=0).reshape(
-        -1, heads, head_size
-    )
-    grad_query, grad_table, grad_keys, grad_values = attention_backward(
-        query,
-        keys_again,
-        values_again,
-        key_position,
-        key_sequence,
-        query_position,
-        query_sequence,
-        table_heads,
-        scale,
-        log_total,
-        grad_attended,
-        delta,
-    )
+    grad_attended = jnp.dot(
+        grad_branch, back_out.T, preferred_element_type=jnp.float32
+    ).astype(jnp.bfloat16)
+    grad_query, grad_keys, grad_values, grad_lines = attention_backward(
+        info, query, grad_attended, exact, log_total, all_keys, all_values, rows_bias, row_start, heads
+    )
+    grad_table = table_grad(grad_lines, rel_table.shape[0])
     prompt_grad_keys, prompt_grad_values = (
         lax.psum_scatter(
-            grad_keys[:PROMPT].astype(jnp.bfloat16), "dp", scatter_dimension=0, tiled=True
-        ).astype(jnp.float32),
+            grad_keys[:PROMPT], "dp", scatter_dimension=0, tiled=True
+        ),
         lax.psum_scatter(
-            grad_values[:PROMPT].astype(jnp.bfloat16), "dp", scatter_dimension=0, tiled=True
-        ).astype(jnp.float32),
+            grad_values[:PROMPT], "dp", scatter_dimension=0, tiled=True
+        ),
     )
     grad_projected = jnp.concatenate(
         [
-            grad_query.reshape(rows, width),
+            grad_query,
             jnp.concatenate([prompt_grad_keys, grad_keys[PROMPT:]], axis=0),
             jnp.concatenate([prompt_grad_values, grad_values[PROMPT:]], axis=0),
         ],

time: 4170 us -> 1900 us (0.46)
  matrix products: 2050 us -> 148 us
  other arithmetic: 714 us -> 122 us
  Pallas kernels: 0 us -> 300 us
  local copies, waits for them, and re-layouts: 316 us -> 207 us
  waiting for transfers between devices: 645 us -> 709 us
    dot_general x45 -> x1, matrix products: 1900 us -> 0.29 us  [table_grad(): return jnp.dot(dd[:, 0, :], hot, precision=lax.Precision.HIGHEST)]
    reduce_sum x12 -> x3, other arithmetic: 336 us -> 5.26 us  [the longest x1 4.89 us: bias_rows(): rows = jnp.sum(hot[None] * table, axis=-1)]
    pallas_call x0 -> x2, Pallas kernels: none -> 300 us  [the longest x1 181 us: attention_backward(): pl.pallas_call(functools.partial(bwd_kernel, scale), grid_spec=pltpu.Pref...]
    and x15 -> x0, other arithmetic: 247 us -> none  [block_scores(): (distance >= 0) & ((key_sequence[None, :] < 0) | (key_sequence[None, :] =...]
    reduce_scatter x2, waiting for transfers between devices: 39.1 us -> 83.9 us  [the longest x1 46.8 us: per_device(): lax.psum_scatter(grad_keys[:PROMPT], 'dp', scatter_dimension=0, tiled=True)]
  transfers between devices with their start and end apart: 13 -> 13, of which waited for: 10 -> 11; matrix products, arithmetic and copies ran while one was open for 37% -> 9% of each run, Pallas kernels for 0% -> 6%
where the time goes in v1:
time: 1900 us
  waiting for transfers between devices  709 us (37%)
  blocking collectives  376 us (20%)
  Pallas kernels  300 us (16%)
  local copies, waits for them, and re-layouts  207 us (11%)
  matrix products  148 us (8%)
  other arithmetic  122 us (6%)
    all_gather x1, blocking collectives, dense_gather(): lax.all_gather(w_router, ('dp', 'expert'), axis=0, tiled=True)  183 us
    pallas_call x1, Pallas kernels, attention_backward(): pl.pallas_call(functools.partial(bwd_kernel, scale), grid_spec=pltpu.Pref...  181 us
    all_to_all x1, blocking collectives, per_device(): lax.all_to_all(outgoing_grads, 'expert', split_axis=0, concat_axis=0, til...  145 us
    all_to_all x1, waiting for transfers between devices, per_device(): lax.all_to_all(outgoing, 'expert', split_axis=0, concat_axis=0, tiled=True)  138 us
    reduce_scatter x1, waiting for transfers between devices, per_device(): lax.psum_scatter(grad_qkv, ('dp', 'expert'), scatter_dimension=0, tiled=T...  125 us
    pallas_call x1, Pallas kernels, attention_forward(): pl.pallas_call(functools.partial(fwd_kernel, scale2), grid_spec=pltpu.Pre...  120 us
    all_to_all x1, waiting for transfers between devices, per_device(): lax.all_to_all(back_rows, 'expert', split_axis=0, concat_axis=0, tiled=True)  96.7 us
    all_gather x1, waiting for transfers between devices, dense_gather(): lax.all_gather(w_qkv, ('dp', 'expert'), axis=0, tiled=True)  63.2 us
  transfers between devices with their start and end apart: 13, of which 11 were waited for; matrix products, arithmetic and copies ran while one was open for 9% of the time, Pallas kernels for 6%

profile of v1, /device:TPU:0, one launch (start us, length us, event | category | flops | bytes accessed | tf_op | source)
XLA Modules:
  0.0 1895.2 jit_solution(12184252879964265981)
XLA Ops:
  10.8 63.2 %all-gather.7.cloned.1.call-done = bf16[768,2304]{1,0:T(8,128)(2,1)} async-done(((bf16[24,2304]{1,0:T(8,128)(2,1)}), bf16[768,2304]{1,0:T(8,128)(2,1)}) %all-gather.7.cloned.1.call-update) | async-done | bytes 3538960 | tf_op jit(solution)/shard_map/all_gather | solution.py:33
  74.0 6.4 convolution_convert_fusion
  87.2 7.7 all-reduce
  98.6 9.2 reduce-window.6
  109.2 4.9 multiply_reduce_fusion
  115.5 2.7 slice.58.q_ref
  118.1 8.2 all-gather.11.cloned.1.call-done
  126.3 4.3 pad_maximum_fusion.1.v_ref
  130.6 41.5 %all-gather.9.cloned.1.call-done = bf16[2048,768]{1,0:T(8,128)(2,1)} async-done(((bf16[512,768]{1,0:T(8,128)(2,1)}), bf16[2048,768]{1,0:T(8,128)(2,1)}) %all-gather.9.cloned.1.call-update) | async-done | bytes 3145744 | tf_op jit(solution)/shard_map/all_gather | solution.py:49
  172.1 4.0 pad_maximum_fusion.k_ref
  177.0 119.7 %attention_forward.1 = (f32[1024,768]{1,0:T(8,128)}, f32[1024,128]{1,0:T(8,128)}) custom-call(s32[6]{0:T(128)} %pad_add_fusion.info, bf16[1024,768]{1,0:T(8,128)(2,1)} %slice.58.q_ref, bf16[2560,768]{1,0:T(8,128)(2,1)} %pad_maximum_fusion.k_ref, bf16[2560,768]{1,0:T(8,128)(2,1)} %pad_maximum_fusion.1.v_ref, f32[12,8,2816]{2,1,0:T(8,128)} %broadcast_select_fusion.r_ref, ...), custom_call_target="tpu_custom_call" | custom-call | tf_op jit(solution)/shard_map/attention_forward/pallas_call | solution.py:156
  296.7 3.9 multiply_reduce_fusion.5
  303.5 3.3 broadcast_in_dim.185
  306.8 7.8 reshape.734
  314.5 14.0 scatter_custom_fusion
  328.5 6.3 all-to-all-start
  335.9 138.0 %all-to-all-done = bf16[8,512,768]{2,1,0:T(8,128)(2,1)} async-done(((bf16[8,512,768]{2,1,0:T(8,128)(2,1)}), bf16[8,512,768]{2,1,0:T(8,128)(2,1)}, u32[]{:S(2)}, u32[]{:S(2)}) %all-to-all-start) | async-done | bytes 6291488 | tf_op jit(solution)/shard_map/all_to_all | solution.py:443
  473.9 20.0 %scatter_custom_fusion.1 = bf16[2048,768]{1,0:T(8,128)(2,1)S(1)} fusion(s32[4096]{0:T(1024)S(1)} %bitcast.129, bf16[4096,768]{1,0:T(8,128)(2,1)} %bitcast.16, bf16[]{:T(256)} %constant.82.clone.1), kind=kCustom, calls=%fused_computation.75 | custom fusion | bytes 3146240 | tf_op jit(solution)/shard_map/scatter | solution.py:447
  494.0 22.9 %multiply_convert_fusion = (bf16[2048,3072]{1,0:T(8,128)(2,1)}, f32[2048,3072]{1,0:T(8,128)}) fusion(bf16[2048,768]{1,0:T(8,128)(2,1)S(1)} %scatter_custom_fusion.1, bf16[1,768,3072]{2,1,0:T(8,128)(2,1)} %param.27), kind=kOutput, calls=%fused_computation.18 | convolution fusion | flops 9720299520 | bytes 45613056 | tf_op jit(solution)/shard_map/ecd,edf->ecf/dot_general | solution.py:450
  516.9 14.2 fusion.24
  531.1 17.7 gather_fusion
  548.8 7.9 select_select_fusion.1
  556.7 4.9 all-to-all-start.1
  564.7 6.7 mul.326
  571.5 8.6 mul.327
  580.1 183.1 %all-gather.1 = bf16[32,24,8]{1,2,0:T(8,128)(2,1)S(1)} all-gather(bf16[1,24,8]{1,2,0:T(8,128)(2,1)S(1)} %bitcast.137), channel_id=1, replica_groups=mesh['dp'=4,'expert'=8] {'dp','expert'}, dimensions={0}, use_global_device_ids=true | all-gather | bytes 12672 | tf_op jit(solution)/shard_map/all_gather | solution.py:35
  763.8 12.1 gather_fusion.1
  775.9 5.3 multiply_reduce_fusion.1
  782.4 14.9 scatter_custom_fusion.2
  797.3 144.7 %all_to_all.20 = bf16[8,512,768]{2,1,0:T(8,128)(2,1)} all-to-all(bf16[8,512,768]{2,1,0:T(8,128)(2,1)} %bitcast.110), channel_id=1, replica_groups=mesh['dp'=4,'expert'=8] {'expert'}, dimensions={0} | all-to-all | bytes 12582912 | tf_op jit(solution)/shard_map/all_to_all | solution.py:477
  942.0 20.0 %scatter_custom_fusion.3 = bf16[2048,768]{1,0:T(8,128)(2,1)S(1)} fusion(s32[4096]{0:T(1024)S(1)} %bitcast.130, bf16[4096,768]{1,0:T(8,128)(2,1)} %bitcast.111, bf16[]{:T(256)} %constant.82.clone.1), kind=kCustom, calls=%fused_computation.73 | custom fusion | bytes 3146240 | tf_op jit(solution)/shard_map/scatter | solution.py:483
  963.7 27.1 %fusion.6 = bf16[2048,3072]{1,0:T(8,128)(2,1)} fusion(f32[2048,3072]{1,0:T(8,128)} %get-tuple-element.107, bf16[2048,768]{1,0:T(8,128)(2,1)S(1)} %scatter_custom_fusion.3, bf16[1,3072,768]{2,1,0:T(8,128)(2,1)} %param.28), kind=kOutput, calls=%fused_computation.17 | convolution fusion | flops 9789505536 | bytes 45613056 | tf_op jit(solution)/shard_map/ecd,efd->ecf/dot_general | solution.py:490
  990.8 14.3 fusion.21
  1005.2 17.8 gather_fusion.2
  1022.9 8.0 select_select_fusion
  1030.9 4.7 all-to-all-start.3
  1036.1 8.1 reshape.692
  1044.3 31.3 %multiply_reduce_fusion.2 = f32[1024,768]{1,0:T(8,128)S(1)} fusion(f32[1024,2,768]{2,1,0:T(2,128)} %reshape.692, f32[1024,2]{1,0:T(8,128)} %copy-done.15), kind=kLoop, calls=%fused_computation.24 | loop fusion | flops 2359296 | bytes 9445376 | tf_op jit(solution)/shard_map/reduce_sum | solution.py:466
  1077.9 96.7 %all-to-all-done.3 = bf16[8,512,768]{2,1,0:T(8,128)(2,1)} async-done(((bf16[8,512,768]{2,1,0:T(8,128)(2,1)}), bf16[8,512,768]{2,1,0:T(8,128)(2,1)}, u32[]{:S(2)}, u32[]{:S(2)}) %all-to-all-start.3) | async-done | bytes 6291488 | tf_op jit(solution)/shard_map/all_to_all | solution.py:511
  1174.6 12.1 gather_fusion.3
  1186.7 3.9 convert_select_fusion
  1190.5 8.3 reshape.697
  1198.9 11.9 reduce_sum.273
  1210.8 3.7 copy.133
  1214.5 3.1 multiply_reduce_fusion.3
  1219.9 2.6 convolution_convert_fusion.3.do_ref
  1222.5 180.8 %attention_backward.1 = (bf16[1024,768]{1,0:T(8,128)(2,1)}, bf16[2560,768]{1,0:T(8,128)(2,1)}, bf16[2560,768]{1,0:T(8,128)(2,1)}, f32[12,1,2816]{2,1,0:T(1,128)}) custom-call(s32[6]{0:T(128)} %pad_add_fusion.info, bf16[1024,768]{1,0:T(8,128)(2,1)} %slice.58.q_ref, bf16[1024,768]{1,0:T(8,128)(2,1)} %convolution_convert_fusion.3.do_ref, ...), custom_call_target="tpu_custom_call" | custom-call | tf_op jit(solution)/shard_map/attention_backward/pallas_call | solution.py:306
  1403.3 3.8 slice.48
  1407.2 3.7 slice.46
  1412.8 14.5 fusion.18
  1429.1 14.8 fusion.17
  1445.8 4.8 fusion.43
  1453.6 37.1 %reduce-scatter.10.cloned.1.call-done = bf16[512,768]{1,0:T(8,128)(2,1)} async-done(((bf16[2048,768]{1,0:T(8,128)(2,1)}), bf16[512,768]{1,0:T(8,128)(2,1)}) %reduce-scatter.10.cloned.1.call-update) | async-done | bytes 786448 | tf_op jit(solution)/shard_map/reduce_scatter | solution.py:543
  1490.6 46.8 %reduce-scatter.8.cloned.1.call-done = bf16[512,768]{1,0:T(8,128)(2,1)} async-done(((bf16[2048,768]{1,0:T(8,128)(2,1)}), bf16[512,768]{1,0:T(8,128)(2,1)}) %reduce-scatter.8.cloned.1.call-update) | async-done | bytes 786448 | tf_op jit(solution)/shard_map/reduce_scatter | solution.py:540
  1537.5 8.7 fusion.48
  1548.5 49.0 %reduce-scatter.18.cloned.1.call-done = bf16[1,768,768]{2,1,0:T(8,128)(2,1)} async-done(((bf16[1,3072,768]{2,1,0:T(8,128)(2,1)}), bf16[1,768,768]{2,1,0:T(8,128)(2,1)}) %reduce-scatter.18.cloned.1.call-update) | async-done | bytes 1179664 | tf_op jit(solution)/shard_map/reduce_scatter | solution.py:569
  1597.6 2.8 convert_element_type.375
  1600.4 57.3 %reduce-scatter.16.cloned.1.call-done = bf16[1,192,3072]{2,1,0:T(8,128)(2,1)} async-done(((bf16[1,768,3072]{2,1,0:T(8,128)(2,1)}), bf16[1,192,3072]{2,1,0:T(8,128)(2,1)}) %reduce-scatter.16.cloned.1.call-update) | async-done | bytes 1179664 | tf_op jit(solution)/shard_map/reduce_scatter | solution.py:566
  1657.7 2.9 convert_element_type.372
  1662.7 9.6 fusion.28
  1674.8 3.6 copy.138
  1678.3 40.5 %all-reduce.2 = (f32[768]{0:T(1024)}, f32[31,12]{0,1:T(8,128)}, f32[768]{0:T(1024)}, f32[768,8]{0,1:T(8,128)S(1)}) all-reduce(f32[768]{0:T(1024)S(1)} %get-tuple-element.76, f32[31,12]{0,1:T(8,128)S(1)} %fusion.52, f32[768]{0:T(1024)S(1)} %get-tuple-element.74, ...), channel_id=1, replica_groups=mesh['dp'=4,'expert'=8] {'dp','expert'}, use_global_device_ids=true, to_apply=%region_36.39 | all-reduce | flops 8052 | bytes 64416 | tf_op jit(solution)/shard_map/psum | solution.py:573
  1719.4 43.5 %reduce-scatter.14.cloned.1.call-done = f32[24,768]{1,0:T(8,128)} async-done(((f32[768,768]{1,0:T(8,128)}), f32[24,768]{1,0:T(8,128)}) %reduce-scatter.14.cloned.1.call-update) | async-done | bytes 73744 | tf_op jit(solution)/shard_map/reduce_scatter | solution.py:562
  1762.9 125.3 %reduce-scatter.12.cloned.1.call-done = f32[24,2304]{1,0:T(8,128)} async-done(((f32[768,2304]{1,0:T(8,128)}), f32[24,2304]{1,0:T(8,128)}) %reduce-scatter.12.cloned.1.call-update) | async-done | bytes 221200 | tf_op jit(solution)/shard_map/reduce_scatter | solution.py:561
  (212 shorter events, 48.2 us)
Async XLA Ops:
  7.2 66.8 %copy-start.38 = (f32[768]{0:T(1024)S(1)}, f32[768]{0:T(1024)}, u32[]{:S(2)}) copy-start(f32[768]{0:T(1024)} %param.21) | copy-start | bytes 9220
  7.2 66.8 %all-gather.7.cloned.1.call-start = ((), (), s32[]{:S(2)}) async-start(), calls=%async_computation.10 | async-start | bytes 3649536 | tf_op jit(solution)/shard_map/all_gather | solution.py:33
  7.9 118.4 %all-gather.11.cloned.1.call-start = ((), (), s32[]{:S(2)}) async-start(), calls=%async_computation.12 | async-start | bytes 3932160 | tf_op jit(solution)/shard_map/all_gather | solution.py:50
  9.7 287.0 %copy-start.8 = (bf16[1024,768]{0,1:T(8,128)(2,1)}, bf16[1024,768]{0,1:T(8,128)(2,1)S(1)}, u32[]{:S(2)}) copy-start(bf16[1024,768]{0,1:T(8,128)(2,1)S(1)} %copy.114) | copy-start | bytes 4718596
  10.1 0.7 copy-start.27
  10.8 69.6 %copy-start.34 = (f32[1024]{0:T(1024)}, f32[1024]{0:T(1024)S(1)}, u32[]{:S(2)}) copy-start(f32[1024]{0:T(1024)S(1)} %fusion.101) | copy-start | bytes 12292
  80.4 2.8 copy-start.14
  80.4 4.2 copy-start.33
  80.4 4.6 copy-start.24
  80.4 4.6 copy-start.37
  80.5 5.2 copy-start.42
  83.3 88.8 %all-gather.9.cloned.1.call-start = ((), (), s32[]{:S(2)}) async-start(), calls=%async_computation.11 | async-start | bytes 3932160 | tf_op jit(solution)/shard_map/all_gather | solution.py:49
  84.0 212.7 %all-gather.13.cloned.1.call-start = ((), (), s32[]{:S(2)}) async-start(), calls=%async_computation.13 | async-start | bytes 1216512 | tf_op jit(solution)/shard_map/all_gather | solution.py:34
  84.6 13.5 copy-start.36
  296.7 5.7 copy-start.31
  300.6 1.8 copy-start
  300.6 1.8 copy-start.29
  300.7 2.8 copy-start.25
  302.7 4.0 copy-start.5
  328.5 145.4 %all-to-all-start = ((bf16[8,512,768]{2,1,0:T(8,128)(2,1)}), bf16[8,512,768]{2,1,0:T(8,128)(2,1)}, u32[]{:S(2)}, u32[]{:S(2)}) async-start(bf16[8,512,768]{2,1,0:T(8,128)(2,1)} %bitcast.107), calls=%async_computation | async-start | bytes 12582912 | tf_op jit(solution)/shard_map/all_to_all | solution.py:443
  494.0 22.9 %copy-start.16 = (bf16[2048,768]{1,0:T(8,128)(2,1)}, bf16[2048,768]{1,0:T(8,128)(2,1)S(1)}, u32[]{:S(2)}) copy-start(bf16[2048,768]{1,0:T(8,128)(2,1)S(1)} %scatter_custom_fusion.1) | copy-start | bytes 9437188
  556.7 4.9 copy-start.20
  556.7 207.1 %all-to-all-start.1 = ((bf16[8,512,768]{2,1,0:T(8,128)(2,1)}), bf16[8,512,768]{2,1,0:T(8,128)(2,1)}, u32[]{:S(2)}, u32[]{:S(2)}) async-start(bf16[8,512,768]{2,1,0:T(8,128)(2,1)} %bitcast.108), calls=%async_computation.1 | async-start | bytes 12582912 | tf_op jit(solution)/shard_map/all_to_all | solution.py:460
  562.4 2.3 copy-start.10
  571.5 8.6 copy-start.40
  571.5 191.9 %copy-start.6 = (bf16[1024,768]{0,1:T(8,128)(2,1)S(1)}, bf16[1024,768]{0,1:T(8,128)(2,1)}, u32[]{:S(2)}) copy-start(bf16[1024,768]{0,1:T(8,128)(2,1)} %copy-done.5) | copy-start | bytes 4718596
  782.1 15.2 copy-start.15
  962.0 1.7 copy-start.18
  1030.9 143.7 %all-to-all-start.3 = ((bf16[8,512,768]{2,1,0:T(8,128)(2,1)}), bf16[8,512,768]{2,1,0:T(8,128)(2,1)}, u32[]{:S(2)}, u32[]{:S(2)}) async-start(bf16[8,512,768]{2,1,0:T(8,128)(2,1)} %bitcast.109), calls=%async_computation.3 | async-start | bytes 12582912 | tf_op jit(solution)/shard_map/all_to_all | solution.py:511
  1035.7 455.0 %reduce-scatter.10.cloned.1.call-start = ((), (), s32[]{:S(2)}) async-start(), calls=%async_computation.15 | async-start | bytes 3932160 | tf_op jit(solution)/shard_map/reduce_scatter | solution.py:543
  1210.8 3.7 copy-start.1
  1210.8 3.7 copy-start.26
  1210.8 3.7 copy-start.32
  1214.4 3.1 copy-start.30
  1214.4 3.2 copy-start.11
  1214.5 3.3 copy-start.12
  1217.8 2.2 copy-start.21
  1219.9 2.6 copy-start.3
  1407.1 130.4 %reduce-scatter.8.cloned.1.call-start = ((), (), s32[]{:S(2)}) async-start(), calls=%async_computation.14 | async-start | bytes 3932160 | tf_op jit(solution)/shard_map/reduce_scatter | solution.py:540
  1410.9 1.9 copy-start.19
  1410.9 186.7 %reduce-scatter.18.cloned.1.call-start = ((), (), s32[]{:S(2)}) async-start(), calls=%async_computation.19 | async-start | bytes 5898240 | tf_op jit(solution)/shard_map/reduce_scatter | solution.py:569
  1427.2 1.9 copy-start.17
  1427.2 230.4 %reduce-scatter.16.cloned.1.call-start = ((), (), s32[]{:S(2)}) async-start(), calls=%async_computation.18 | async-start | bytes 5898240 | tf_op jit(solution)/shard_map/reduce_scatter | solution.py:566
  1443.9 1.9 copy-start.2
  1443.9 319.0 %reduce-scatter.14.cloned.1.call-start = ((), (), s32[]{:S(2)}) async-start(), calls=%async_computation.17 | async-start | bytes 2433024 | tf_op jit(solution)/shard_map/reduce_scatter | solution.py:562
  1450.6 86.9 %copy-start.9 = (bf16[1024,768]{0,1:T(8,128)(2,1)S(1)}, bf16[1024,768]{0,1:T(8,128)(2,1)}, u32[]{:S(2)}) copy-start(bf16[1024,768]{0,1:T(8,128)(2,1)} %copy-done.8) | copy-start | bytes 4718596
  1450.6 86.9 %copy-start.35 = (f32[1024]{0:T(1024)S(1)}, f32[1024]{0:T(1024)}, u32[]{:S(2)}) copy-start(f32[1024]{0:T(1024)} %copy-done.34) | copy-start | bytes 12292
  1450.6 86.9 %copy-start.39 = (f32[768]{0:T(1024)S(1)}, f32[768]{0:T(1024)}, u32[]{:S(2)}) copy-start(f32[768]{0:T(1024)} %param.21) | copy-start | bytes 9220
  1450.6 437.6 %reduce-scatter.12.cloned.1.call-start = ((), (), s32[]{:S(2)}) async-start(), calls=%async_computation.16 | async-start | bytes 7299072 | tf_op jit(solution)/shard_map/reduce_scatter | solution.py:561
  1451.9 94.2 %copy-start.22 = (bf16[512,768]{1,0:T(8,128)(2,1)}, bf16[512,768]{1,0:T(8,128)(2,1)S(1)}, u32[]{:S(2)}) copy-start(bf16[512,768]{1,0:T(8,128)(2,1)S(1)} %slice.47) | copy-start | bytes 2359300
  1453.5 92.6 %copy-start.23 = (bf16[512,768]{1,0:T(8,128)(2,1)}, bf16[512,768]{1,0:T(8,128)(2,1)S(1)}, u32[]{:S(2)}) copy-start(bf16[512,768]{1,0:T(8,128)(2,1)S(1)} %slice.49) | copy-start | bytes 2359300
  1546.2 1.9 copy-start.7
  1548.5 112.1 %copy-start.13 = (bf16[1024,768]{0,1:T(8,128)(2,1)S(1)}, bf16[1024,768]{0,1:T(8,128)(2,1)}, u32[]{:S(2)}) copy-start(bf16[1024,768]{0,1:T(8,128)(2,1)} %get-tuple-element.100) | copy-start | bytes 4718596
  1600.4 61.9 %copy-start.41 = (f32[12,1,2816]{2,1,0:T(1,128)S(1)}, f32[12,1,2816]{2,1,0:T(1,128)}, u32[]{:S(2)}) copy-start(f32[12,1,2816]{2,1,0:T(1,128)} %get-tuple-element.23) | copy-start | bytes 405508
  1662.6 9.6 copy-start.28
  1662.6 9.6 copy-start.4
Sparse Core Ops, SparseCore 0:
  11.0 62.9 all-gather.6
  83.4 42.8 all-gather.10
  128.2 43.9 all-gather.8
  175.0 54.2 all-gather.12
  1407.2 83.3 reduce-scatter.9
  1493.5 43.9 reduce-scatter.7
  1540.4 57.0 reduce-scatter.17
  1600.5 57.0 reduce-scatter.15
  1663.5 99.3 reduce-scatter.13
  1770.0 118.1 reduce-scatter.11

commit v2 on v1

--- a/solution.py
+++ b/solution.py
@@ -26,22 +26,6 @@
 
 def normed(values, gain):
     return values * lax.rsqrt(jnp.mean(values * values, axis=-1, keepdims=True) + EPSILON) * gain
-
-
-def dense_gather(w_qkv, w_out, w_router):
-    return (
-        lax.all_gather(w_qkv, ("dp", "expert"), axis=0, tiled=True),
-        lax.all_gather(w_out, ("dp", "expert"), axis=0, tiled=True),
-        lax.all_gather(w_router, ("dp", "expert"), axis=0, tiled=True),
-    )
-
-
-def dense_regather(w_qkv, w_out, w_router):
-    return (
-        lax.all_gather(w_qkv, ("dp", "expert"), axis=0, tiled=True),
-        lax.all_gather(w_out, ("dp", "expert"), axis=0, tiled=True),
-        lax.all_gather(w_router, ("dp", "expert"), axis=0, tiled=True),
-    )
 
 
 def prompt_gather(own_keys, own_values):
@@ -337,6 +321,411 @@
     return jnp.broadcast_to(starts[:, None], (ids.shape[0], 128))
 
 
+TN = (((0,), (0,)), ((), ()))
+MOE_ROWS = 256
+FF_TILE = 768
+
+
+def expert_slots(ids, levels, expert, capacity):
+    hits = ids == expert
+    hit = jnp.any(hits, axis=2)
+    level = jnp.sum(jnp.where(hits, levels, 0), axis=2)
+    hot = hit[:, :, None] & (level[:, :, None] == jnp.arange(PRIO)[None, None, :])
+    tokens = ids.shape[1]
+    earlier = (jnp.arange(tokens)[:, None] > jnp.arange(tokens)[None, :]).astype(BF16)
+    rank = jnp.einsum("ut,dtl->dul", earlier, hot.astype(BF16), preferred_element_type=F32).astype(jnp.int32)
+    counts = jnp.sum(hot.astype(jnp.int32), axis=1)
+    totals = jnp.sum(counts, axis=0)
+    lower = jnp.cumsum(totals) - totals
+    base = lower[None, :] + jnp.cumsum(counts, axis=0) - counts
+    slot = jnp.sum(jnp.where(hot, base[:, None, :] + rank, 0), axis=2)
+    kept = hit & (slot < capacity)
+    rank = jnp.einsum("ut,dt->du", earlier, kept.astype(BF16), preferred_element_type=F32).astype(jnp.int32)
+    place = jnp.where(kept, rank, -1)
+    sizes = jnp.sum(kept.astype(jnp.int32), axis=1)
+    padded = (sizes + 15) // 16 * 16
+    ends = jnp.cumsum(padded)
+    other = jnp.sum(jnp.where(hits, 0, ids), axis=2)
+    return place, jnp.concatenate([ends - padded, sizes, ends[-1:]]).astype(jnp.int32), other
+
+
+def pack_kernel(sources, info, place_ref, *refs):
+    ins, outs = refs[:len(refs) // 2], refs[len(refs) // 2:]
+    d = pl.program_id(0)
+
+    @pl.when(d == 0)
+    def _():
+        for out in outs:
+            out[...] = jnp.zeros_like(out)
+
+    tokens = place_ref.shape[2]
+    row = lax.broadcasted_iota(jnp.int32, (MOE_ROWS, tokens), 0)
+
+    def chunk(j, _):
+        pick = jnp.where(place_ref[0] == row + MOE_ROWS * j, 1.0, 0.0).astype(BF16)
+        at = pl.ds(pl.multiple_of(info[d] + MOE_ROWS * j, 16), MOE_ROWS)
+        for x, out in zip(ins, outs):
+            out[at, :] = dot(pick, x[...]).astype(BF16)
+        return 0
+    lax.fori_loop(0, (info[sources + d] + MOE_ROWS - 1) // MOE_ROWS, chunk, 0)
+
+
+def pack(info, place, arrays, room):
+    sources, tokens = place.shape
+    return pl.pallas_call(
+        functools.partial(pack_kernel, sources),
+        grid_spec=pltpu.PrefetchScalarGridSpec(
+            num_scalar_prefetch=1, grid=(sources,),
+            in_specs=[pl.BlockSpec((1, 1, tokens), lambda d, *_: (d, 0, 0))]
+            + [pl.BlockSpec((tokens, x.shape[1]), lambda d, *_: (d, 0)) for x in arrays],
+            out_specs=[pl.BlockSpec((room, x.shape[1]), lambda d, *_: (0, 0)) for x in arrays]),
+        out_shape=[jax.ShapeDtypeStruct((room, x.shape[1]), BF16) for x in arrays],
+        compiler_params=pltpu.CompilerParams(vmem_limit_bytes=40 << 20),
+        name="pack_tokens",
+    )(info, place[:, None, :], *arrays)
+
+
+def unpack_kernel(sources, info, place_ref, *refs):
+    ins, outs = refs[:len(refs) // 2], refs[len(refs) // 2:]
+    d = pl.program_id(0)
+    tokens = place_ref.shape[0]
+    lane = lax.broadcasted_iota(jnp.int32, (tokens, 128), 1)
+    for x, out in zip(ins, outs):
+        def chunk(j, total):
+            put = jnp.concatenate(
+                [jnp.where(place_ref[...] == lane + (MOE_ROWS * j + 128 * b), 1.0, 0.0).astype(BF16)
+                 for b in range(MOE_ROWS // 128)], axis=1)
+            at = pl.ds(pl.multiple_of(info[d] + MOE_ROWS * j, 16), MOE_ROWS)
+            return total + dot(put, x[at, :])
+        total = lax.fori_loop(0, (info[sources + d] + MOE_ROWS - 1) // MOE_ROWS, chunk,
+                              jnp.zeros((tokens, x.shape[1]), F32))
+        out[...] = total.astype(out.dtype)
+
+
+def unpack(info, place, arrays, dtypes):
+    sources, tokens = place.shape
+    spread = jnp.broadcast_to(place.reshape(-1, 1), (sources * tokens, 128))
+    return pl.pallas_call(
+        functools.partial(unpack_kernel, sources),
+        grid_spec=pltpu.PrefetchScalarGridSpec(
+            num_scalar_prefetch=1, grid=(sources,),
+            in_specs=[pl.BlockSpec((tokens, 128), lambda d, *_: (d, 0))]
+            + [pl.BlockSpec(x.shape, lambda d, *_: (0, 0)) for x in arrays],
+            out_specs=[pl.BlockSpec((tokens, x.shape[1]), lambda d, *_: (d, 0)) for x in arrays]),
+        out_shape=[jax.ShapeDtypeStruct((sources * tokens, x.shape[1]), t) for x, t in zip(arrays, dtypes)],
+        compiler_params=pltpu.CompilerParams(vmem_limit_bytes=40 << 20),
+        name="unpack_tokens",
+    )(info, spread, *arrays)
+
+
+def gelu_and_slope(v):
+    c = math.sqrt(2.0 / math.pi)
+    t = jnp.tanh(c * (v + 0.044715 * (v * v * v)))
+    half = 0.5 * (1.0 + t)
+    return v * half, half + 0.5 * v * (1.0 - t * t) * (c * (1.0 + 3 * 0.044715 * (v * v)))
+
+
+def expert_kernel(sources, info, expert, x_ref, o_ref, c_ref, r_ref, wi_ref, wd_ref,
+                  gi_ref, eo_ref, gg_ref, dwi_ref, dwd_ref, geo, gate, eo, gi, dwi, dwd):
+    f = pl.program_id(0)
+    last = pl.num_programs(0) - 1
+    tiles = (info[2 * sources] + MOE_ROWS - 1) // MOE_ROWS
+    lane = lax.broadcasted_iota(jnp.int32, (MOE_ROWS, 128), 1)
+
+    def rows_of(i):
+        return pl.ds(pl.multiple_of(i * MOE_ROWS, MOE_ROWS), MOE_ROWS)
+
+    @pl.when(f == 0)
+    def _():
+        gi_ref[...] = jnp.zeros_like(gi_ref)
+        eo_ref[...] = jnp.zeros_like(eo_ref)
+        gg_ref[...] = jnp.zeros_like(gg_ref)
+
+        def start(i, _):
+            at = rows_of(i)
+            logits = dot(x_ref[at, :], r_ref[...])
+            mine = jnp.sum(jnp.where(lane == expert[0], logits, 0.0), axis=1, keepdims=True)
+            other = jnp.sum(jnp.where(o_ref[at, :] > 0, logits, 0.0), axis=1, keepdims=True)
+            top = jnp.maximum(mine, other)
+            a, b = jnp.exp(mine - top), jnp.exp(other - top)
+            g = a / (a + b)
+            gate[at, :] = jnp.broadcast_to(g, (MOE_ROWS, 128))
+            geo[at, :] = (c_ref[at, :].astype(F32) * g).astype(BF16)
+            eo[at, :] = jnp.zeros((MOE_ROWS, eo.shape[1]), F32)
+            gi[at, :] = jnp.zeros((MOE_ROWS, gi.shape[1]), F32)
+            return 0
+        lax.fori_loop(0, tiles, start, 0)
+
+    dwi[...] = jnp.zeros_like(dwi)
+    dwd[...] = jnp.zeros_like(dwd)
+
+    def tile(i, _):
+        at = rows_of(i)
+        x, g = x_ref[at, :], geo[at, :]
+        act, slope = gelu_and_slope(dot(x, wi_ref[...]))
+        act = act.astype(BF16)
+        eo[at, :] += dot(act, wd_ref[...])
+        gh = (dot(g, wd_ref[...], NT) * slope).astype(BF16)
+        gi[at, :] += dot(gh, wi_ref[...], NT)
+        dwd[...] += dot(act, g, TN)
+        dwi[...] += dot(x, gh, TN)
+        return 0
+    lax.fori_loop(0, tiles, tile, 0)
+    dwi_ref[...] = dwi[...].astype(BF16)
+    dwd_ref[...] = dwd[...].astype(BF16)
+
+    @pl.when(f == last)
+    def _():
+        def finish(i, _):
+            at = rows_of(i)
+            out = eo[at, :].astype(BF16).astype(F32)
+            gg = jnp.sum(out * c_ref[at, :].astype(F32), axis=1, keepdims=True)
+            parts = split3(gg)
+            spread = jnp.zeros((MOE_ROWS, 128), BF16)
+            for n in range(3):
+                spread = jnp.where(lane == n, jnp.broadcast_to(parts[n], (MOE_ROWS, 128)), spread)
+            gg_ref[at, :] = spread
+            eo_ref[at, :] = (out * gate[at, :1]).astype(BF16)
+            gi_ref[at, :] = gi[at, :].astype(BF16)
+            return 0
+        lax.fori_loop(0, tiles, finish, 0)
+
+
+def expert_layer(info, expert, x, other, cot, router, w_in, w_down, sources):
+    room, width = x.shape
+    hidden = w_in.shape[1]
+    whole = lambda a: pl.BlockSpec(a.shape, lambda f, *_: (0, 0))
+    fixed = lambda cols: pl.BlockSpec((room, cols), lambda f, *_: (0, 0))
+    return pl.pallas_call(
+        functools.partial(expert_kernel, sources),
+        grid_spec=pltpu.PrefetchScalarGridSpec(
+            num_scalar_prefetch=2, grid=(hidden // FF_TILE,),
+            in_specs=[whole(x), whole(other), whole(cot), whole(router),
+                      pl.BlockSpec((width, FF_TILE), lambda f, *_: (0, f)),
+                      pl.BlockSpec((FF_TILE, width), lambda f, *_: (f, 0))],
+            out_specs=[fixed(width), fixed(width), fixed(128),
+                       pl.BlockSpec((width, FF_TILE), lambda f, *_: (0, f)),
+                       pl.BlockSpec((FF_TILE, width), lambda f, *_: (f, 0))],
+            scratch_shapes=[pltpu.VMEM((room, width), BF16), pltpu.VMEM((room, 128), F32),
+                            pltpu.VMEM((room, width), F32), pltpu.VMEM((room, width), F32),
+                            pltpu.VMEM((width, FF_TILE), F32), pltpu.VMEM((FF_TILE, width), F32)]),
+        out_shape=[jax.ShapeDtypeStruct((room, width), BF16), jax.ShapeDtypeStruct((room, width), BF16),
+                   jax.ShapeDtypeStruct((room, 128), BF16),
+                   jax.ShapeDtypeStruct(w_in.shape, BF16), jax.ShapeDtypeStruct(w_down.shape, BF16)],
+        compiler_params=pltpu.CompilerParams(vmem_limit_bytes=63 << 20),
+        name="expert_layer",
+    )(info, expert, x, other, cot, router, w_in, w_down)
+
+
+def exchange_pairs(normed_ffn, middle, cotangent, expert_ids, priority, router, w_in, w_down):
+    rows, width = normed_ffn.shape
+    logits = jnp.dot(normed_ffn, router, preferred_element_type=jnp.float32)
+    experts_total = router.shape[1]
+    picks = expert_ids[:, :, None] == jnp.arange(experts_total)[None, None, :]
+    chosen = jnp.sum(jnp.where(picks, logits[:, None, :], 0.0), axis=2)
+    gates = jax.nn.softmax(chosen, axis=-1)
+    top = expert_ids.shape[1]
+    levels = PRIO
+    local_experts = w_in.shape[0]
+    capacity = rows * top // local_experts
+    send = max(2, 2 * rows * top // experts_total)
+    flat_expert = expert_ids.reshape(-1)
+    code = priority.reshape(-1) * experts_total + flat_expert
+    onehot = (code[:, None] == jnp.arange(levels * experts_total)[None, :]).astype(jnp.int32)
+    rank = jnp.sum((jnp.cumsum(onehot, axis=0) - onehot) * onehot, axis=1)
+    counts = jnp.sum(onehot, axis=0)
+    every = lax.all_gather(counts[None, :], "expert", axis=0, tiled=True).reshape(
+        -1, levels, experts_total
+    )
+    expert_index = lax.axis_index("expert")
+    totals = jnp.sum(every, axis=0)
+    lower = jnp.cumsum(totals, axis=0) - totals
+    earlier_sources = jnp.cumsum(every, axis=0) - every
+    mine_prefix = lax.dynamic_index_in_dim(earlier_sources, expert_index, 0, keepdims=False)
+    base = (lower + mine_prefix).reshape(-1)
+    slot = rank + jnp.sum(onehot * base[None, :], axis=1)
+    kept = slot < capacity
+    own_counts = counts.reshape(levels, experts_total)
+    own_lower = (jnp.cumsum(own_counts, axis=0) - own_counts).reshape(-1)
+    place = rank + jnp.sum(onehot * own_lower[None, :], axis=1)
+    target = flat_expert * send + place
+    first_mine = expert_index * local_experts
+    counts_mine = lax.dynamic_slice_in_dim(every, first_mine, local_experts, 2)
+    base_mine = lax.dynamic_slice_in_dim(
+        lower[None] + earlier_sources, first_mine, local_experts, 2
+    )
+    band_end = jnp.cumsum(counts_mine, axis=1)
+    band_start = band_end - counts_mine
+    place_index = jnp.arange(send, dtype=jnp.int32)
+    level = jnp.sum(
+        (place_index[None, None, None, :] >= band_end[:, :, :, None]).astype(jnp.int32), axis=1
+    )
+    level_hot = level[:, None, :, :] == jnp.arange(levels)[None, :, None, None]
+    start_of = jnp.sum(jnp.where(level_hot, band_start[:, :, :, None], 0), axis=1)
+    base_of = jnp.sum(jnp.where(level_hot, base_mine[:, :, :, None], 0), axis=1)
+    arrived_slot = base_of + place_index[None, None, :] - start_of
+    usable = (level < levels) & (arrived_slot < capacity)
+    landing = jnp.where(
+        usable,
+        jnp.arange(local_experts)[None, :, None] * capacity + arrived_slot,
+        local_experts * capacity,
+    ).reshape(-1)
+    live = landing < local_experts * capacity
+    safe = jnp.minimum(landing, local_experts * capacity - 1)
+    pair_inputs = jnp.repeat(normed_ffn, top, axis=0)
+    outgoing = (
+        jnp.zeros((experts_total * send, width), jnp.bfloat16)
+        .at[target]
+        .set(pair_inputs)
+        .reshape(experts_total, send, width)
+    )
+    arrived = lax.all_to_all(outgoing, "expert", split_axis=0, concat_axis=0, tiled=True)
+    expert_inputs = (
+        jnp.zeros((local_experts * capacity, width), jnp.bfloat16)
+        .at[landing]
+        .set(arrived.reshape(-1, width), mode="drop")
+        .reshape(local_experts, capacity, width)
+    )
+    hidden = jnp.einsum("ecd,edf->ecf", expert_inputs, w_in, preferred_element_type=jnp.float32)
+    activated = jax.nn.gelu(hidden).astype(jnp.bfloat16)
+    expert_out = jnp.einsum(
+        "ecf,efd->ecd", activated, w_down, preferred_element_type=jnp.float32
+    ).astype(jnp.bfloat16)
+    returning = jnp.where(
+        live[:, None],
+        jnp.take(expert_out.reshape(-1, width), safe, axis=0),
+        jnp.zeros((), jnp.bfloat16),
+    ).reshape(experts_total, send, width)
+    returned = lax.all_to_all(returning, "expert", split_axis=0, concat_axis=0, tiled=True)
+    pair_out = jnp.where(
+        kept[:, None],
+        jnp.take(returned.reshape(-1, width), target, axis=0).astype(jnp.float32),
+        0.0,
+    ).reshape(rows, top, width)
+    mixed = jnp.sum(gates[:, :, None] * pair_out, axis=1)
+    grad_out = cotangent.astype(jnp.float32)
+    grad_gates = jnp.sum(grad_out[:, None, :] * pair_out, axis=2)
+    pair_grads = (gates[:, :, None] * grad_out[:, None, :]).astype(jnp.bfloat16).reshape(-1, width)
+    outgoing_grads = (
+        jnp.zeros((experts_total * send, width), jnp.bfloat16)
+        .at[target]
+        .set(pair_grads)
+        .reshape(experts_total, send, width)
+    )
+    arrived_grads = lax.all_to_all(
+        outgoing_grads, "expert", split_axis=0, concat_axis=0, tiled=True
+    )
+    grad_expert_out = (
+        jnp.zeros((local_experts * capacity, width), jnp.bfloat16)
+        .at[landing]
+        .set(arrived_grads.reshape(-1, width), mode="drop")
+        .reshape(local_experts, capacity, width)
+    )
+    hidden_again = jnp.einsum(
+        "ecd,edf->ecf", expert_inputs, w_in, preferred_element_type=jnp.float32
+    )
+    activated_again, gelu_back = jax.vjp(jax.nn.gelu, hidden_again)
+    grad_activated = jnp.einsum(
+        "ecd,efd->ecf", grad_expert_out, w_down, preferred_element_type=jnp.float32
+    )
+    grad_hidden = gelu_back(grad_activated)[0].astype(jnp.bfloat16)
+    grad_w_down = jnp.einsum(
+        "ecf,ecd->efd",
+        activated_again.astype(jnp.bfloat16),
+        grad_expert_out,
+        preferred_element_type=jnp.float32,
+    )
+    grad_w_in = jnp.einsum(
+        "ecd,ecf->edf", expert_inputs, grad_hidden, preferred_element_type=jnp.float32
+    )
+    grad_inputs = jnp.einsum(
+        "ecf,edf->ecd", grad_hidden, w_in, preferred_element_type=jnp.float32
+    ).astype(jnp.bfloat16)
+    back_rows = jnp.where(
+        live[:, None],
+        jnp.take(grad_inputs.reshape(-1, width), safe, axis=0),
+        jnp.zeros((), jnp.bfloat16),
+    ).reshape(experts_total, send, width)
+    came_back = lax.all_to_all(back_rows, "expert", split_axis=0, concat_axis=0, tiled=True)
+    pair_back = jnp.where(
+        kept[:, None],
+        jnp.take(came_back.reshape(-1, width), target, axis=0).astype(jnp.float32),
+        0.0,
+    )
+    grad_normed_ffn = jnp.sum(pair_back.reshape(rows, top, width), axis=1)
+    grad_chosen = gates * (grad_gates - jnp.sum(gates * grad_gates, axis=-1, keepdims=True))
+    grad_logits = jnp.sum(jnp.where(picks, grad_chosen[:, :, None], 0.0), axis=1).astype(
+        jnp.bfloat16
+    )
+    grad_normed_ffn = grad_normed_ffn + jnp.dot(
+        grad_logits, router.T, preferred_element_type=jnp.float32
+    )
+    expert_parts = (
+        lax.psum_scatter(
+            grad_w_in.astype(jnp.bfloat16), "dp", scatter_dimension=1, tiled=True
+        ).astype(jnp.float32),
+        lax.psum_scatter(
+            grad_w_down.astype(jnp.bfloat16), "dp", scatter_dimension=1, tiled=True
+        ).astype(jnp.float32),
+    )
+    return mixed, grad_logits, grad_normed_ffn, expert_parts
+
+
+def gather_codes(expert_ids, priority):
+    return lax.all_gather(expert_ids * PRIO + priority, "expert", axis=0)
+
+
+def plan_tokens(codes, rows, top):
+    expert = lax.axis_index("expert").astype(jnp.int32)
+    place, info, other = expert_slots(codes // PRIO, codes % PRIO, expert, rows * top)
+    other_hot = (other.reshape(-1, 1) == jnp.arange(128)[None, :]).astype(jnp.bfloat16)
+    return place, info, other_hot
+
+
+def exchange_tokens(normed_ffn, all_cotangents, plan, expert_ids, router, w_in, w_down):
+    rows, width = normed_ffn.shape
+    experts_total = router.shape[1]
+    top = expert_ids.shape[1]
+    expert = lax.axis_index("expert").astype(jnp.int32)
+    place, info, other_hot = plan
+    sources = place.shape[0]
+    room = (rows * top + 16 * sources + 2 * MOE_ROWS - 1) // MOE_ROWS * MOE_ROWS
+    sent, all_cotangents = lax.optimization_barrier((normed_ffn, all_cotangents))
+    all_tokens = lax.all_gather(sent, "expert", axis=0, tiled=True)
+    packed_cot, packed_other = pack(info, place, [all_cotangents, other_hot], room)
+    (packed,) = pack(info, place, [all_tokens], room)
+    wide_router = jnp.pad(router, ((0, 0), (0, 128 - experts_total)))
+    grad_rows, mixed_rows, grad_gate, grad_w_in, grad_w_down = expert_layer(
+        info, expert[None], packed, packed_other, packed_cot, wide_router, w_in[0], w_down[0], sources
+    )
+    grad_all, gate_all = unpack(info, place, [grad_rows, grad_gate], [jnp.bfloat16, jnp.float32])
+    gate_all = jnp.sum(gate_all[:, :3], axis=1).reshape(sources, rows)
+    gate_own = lax.all_to_all(gate_all, "expert", split_axis=0, concat_axis=0, tiled=True)
+    grad_own = lax.psum_scatter(grad_all, "expert", scatter_dimension=0, tiled=True)
+    (mixed_all,) = unpack(info, place, [mixed_rows], [jnp.bfloat16])
+    mixed_all, grad_own = lax.optimization_barrier((mixed_all, grad_own))
+    mixed = lax.psum_scatter(mixed_all, "expert", scatter_dimension=0, tiled=True)
+    grad_w_in, grad_w_down, mixed = lax.optimization_barrier((grad_w_in, grad_w_down, mixed))
+    expert_parts = (
+        lax.psum_scatter(grad_w_in[None], "dp", scatter_dimension=1, tiled=True).astype(jnp.float32),
+        lax.psum_scatter(grad_w_down[None], "dp", scatter_dimension=1, tiled=True).astype(jnp.float32),
+    )
+    mixed = mixed.astype(jnp.float32)
+    logits = jnp.dot(normed_ffn, router, preferred_element_type=jnp.float32)
+    picks = expert_ids[:, :, None] == jnp.arange(experts_total)[None, None, :]
+    chosen = jnp.sum(jnp.where(picks, logits[:, None, :], 0.0), axis=2)
+    gates = jax.nn.softmax(chosen, axis=-1)
+    grad_gates = jnp.sum(jnp.where(picks, gate_own.T[:, None, :], 0.0), axis=2)
+    grad_chosen = gates * (grad_gates - jnp.sum(gates * grad_gates, axis=-1, keepdims=True))
+    grad_logits = jnp.sum(jnp.where(picks, grad_chosen[:, :, None], 0.0), axis=1).astype(
+        jnp.bfloat16
+    )
+    grad_normed_ffn = grad_own.astype(jnp.float32) + jnp.dot(
+        grad_logits, router.T, preferred_element_type=jnp.float32
+    )
+    return mixed, grad_logits, grad_normed_ffn, expert_parts
+
+
 def per_device(
     tokens_in,
     cont_ids,
@@ -357,12 +746,17 @@
     dp_count = lax.axis_size("dp")
     dp_index = lax.axis_index("dp")
     prompt_rows = PROMPT // dp_count
-    cont_rows = rows - prompt_rows
+    few_experts = lax.axis_size("expert") <= 16 and w_in.shape[0] == 1
     local_ids = cont_ids[0]
     info = info_of(local_ids, dp_index)
     row_start = row_start_of(local_ids)
     rows_bias = bias_rows(rel_table)
-    whole_qkv, whole_out, whole_router = dense_gather(w_qkv, w_out, w_router)
+    if few_experts:
+        codes = gather_codes(expert_ids, priority)
+    whole_qkv = lax.all_gather(w_qkv, ("dp", "expert"), axis=0, tiled=True)
+    if few_experts:
+        plan = plan_tokens(codes, rows, expert_ids.shape[1])
+        whole_qkv, rows_bias, plan = lax.optimization_barrier((whole_qkv, rows_bias, plan))
     inputs = tokens_in.astype(jnp.float32)
     normed_attn = normed(inputs, gain_attn).astype(jnp.bfloat16)
     projected = jnp.dot(normed_attn, whole_qkv, preferred_element_type=jnp.float32).astype(
@@ -372,6 +766,16 @@
     own_keys = projected[:, width : 2 * width]
     own_values = projected[:, 2 * width :]
     prompt_keys, prompt_values = prompt_gather(own_keys[:prompt_rows], own_values[:prompt_rows])
+    experts_total = w_router.shape[1]
+    late = jnp.concatenate([w_out, jnp.pad(w_router, ((0, 0), (0, 128 - experts_total)))], axis=1)
+    late, late_cotangent, prompt_keys, prompt_values = lax.optimization_barrier(
+        (late, cotangent, prompt_keys, prompt_values)
+    )
+    late = lax.all_gather(late, ("dp", "expert"), axis=0, tiled=True)
+    whole_out, whole_router = late[:, :width], late[:, width : width + experts_total]
+    if few_experts:
+        late_cotangent, _ = lax.optimization_barrier((late_cotangent, late))
+        all_cotangents = lax.all_gather(late_cotangent, "expert", axis=0, tiled=True)
     all_keys = jnp.concatenate([prompt_keys, own_keys[prompt_rows:]], axis=0)
     all_values = jnp.concatenate([prompt_values, own_values[prompt_rows:]], axis=0)
     exact, log_total = attention_forward(
@@ -380,149 +784,16 @@
     attended = exact.astype(jnp.bfloat16)
     middle = inputs + jnp.dot(attended, whole_out, preferred_element_type=jnp.float32)
     normed_ffn = normed(middle, gain_ffn).astype(jnp.bfloat16)
-    logits = jnp.dot(normed_ffn, whole_router, preferred_element_type=jnp.float32)
-    experts_total = whole_router.shape[1]
-    top = expert_ids.shape[1]
-    picks = expert_ids[:, :, None] == jnp.arange(experts_total)[None, None, :]
-    chosen = jnp.sum(jnp.where(picks, logits[:, None, :], 0.0), axis=2)
-    gates = jax.nn.softmax(chosen, axis=-1)
-    levels = PRIO
-    local_experts = w_in.shape[0]
-    capacity = rows * top // local_experts
-    send = max(2, 2 * rows * top // experts_total)
-    flat_expert = expert_ids.reshape(-1)
-    code = priority.reshape(-1) * experts_total + flat_expert
-    onehot = (code[:, None] == jnp.arange(levels * experts_total)[None, :]).astype(jnp.int32)
-    rank = jnp.sum((jnp.cumsum(onehot, axis=0) - onehot) * onehot, axis=1)
-    counts = jnp.sum(onehot, axis=0)
-    every = lax.all_gather(counts[None, :], "expert", axis=0, tiled=True).reshape(
-        -1, levels, experts_total
-    )
-    expert_index = lax.axis_index("expert")
-    totals = jnp.sum(every, axis=0)
-    lower = jnp.cumsum(totals, axis=0) - totals
-    earlier_sources = jnp.cumsum(every, axis=0) - every
-    mine_prefix = lax.dynamic_index_in_dim(earlier_sources, expert_index, 0, keepdims=False)
-    base = (lower + mine_prefix).reshape(-1)
-    slot = rank + jnp.sum(onehot * base[None, :], axis=1)
-    kept = slot < capacity
-    own_counts = counts.reshape(levels, experts_total)
-    own_lower = (jnp.cumsum(own_counts, axis=0) - own_counts).reshape(-1)
-    place = rank + jnp.sum(onehot * own_lower[None, :], axis=1)
-    target = flat_expert * send + place
-    first_mine = expert_index * local_experts
-    counts_mine = lax.dynamic_slice_in_dim(every, first_mine, local_experts, 2)
-    base_mine = lax.dynamic_slice_in_dim(
-        lower[None] + earlier_sources, first_mine, local_experts, 2
-    )
-    band_end = jnp.cumsum(counts_mine, axis=1)
-    band_start = band_end - counts_mine
-    place_index = jnp.arange(send, dtype=jnp.int32)
-    level = jnp.sum(
-        (place_index[None, None, None, :] >= band_end[:, :, :, None]).astype(jnp.int32), axis=1
-    )
-    level_hot = level[:, None, :, :] == jnp.arange(levels)[None, :, None, None]
-    start_of = jnp.sum(jnp.where(level_hot, band_start[:, :, :, None], 0), axis=1)
-    base_of = jnp.sum(jnp.where(level_hot, base_mine[:, :, :, None], 0), axis=1)
-    arrived_slot = base_of + place_index[None, None, :] - start_of
-    usable = (level < levels) & (arrived_slot < capacity)
-    landing = jnp.where(
-        usable,
-        jnp.arange(local_experts)[None, :, None] * capacity + arrived_slot,
-        local_experts * capacity,
-    ).reshape(-1)
-    live = landing < local_experts * capacity
-    safe = jnp.minimum(landing, local_experts * capacity - 1)
-    pair_inputs = jnp.repeat(normed_ffn, top, axis=0)
-    outgoing = (
-        jnp.zeros((experts_total * send, width), jnp.bfloat16)
-        .at[target]
-        .set(pair_inputs)
-        .reshape(experts_total, send, width)
-    )
-    arrived = lax.all_to_all(outgoing, "expert", split_axis=0, concat_axis=0, tiled=True)
-    expert_inputs = (
-        jnp.zeros((local_experts * capacity, width), jnp.bfloat16)
-        .at[landing]
-        .set(arrived.reshape(-1, width), mode="drop")
-        .reshape(local_experts, capacity, width)
-    )
-    hidden = jnp.einsum("ecd,edf->ecf", expert_inputs, w_in, preferred_element_type=jnp.float32)
-    activated = jax.nn.gelu(hidden).astype(jnp.bfloat16)
-    expert_out = jnp.einsum(
-        "ecf,efd->ecd", activated, w_down, preferred_element_type=jnp.float32
-    ).astype(jnp.bfloat16)
-    returning = jnp.where(
-        live[:, None],
-        jnp.take(expert_out.reshape(-1, width), safe, axis=0),
-        jnp.zeros((), jnp.bfloat16),
-    ).reshape(experts_total, send, width)
-    returned = lax.all_to_all(returning, "expert", split_axis=0, concat_axis=0, tiled=True)
-    pair_out = jnp.where(
-        kept[:, None],
-        jnp.take(returned.reshape(-1, width), target, axis=0).astype(jnp.float32),
-        0.0,
-    ).reshape(rows, top, width)
-    mixed = jnp.sum(gates[:, :, None] * pair_out, axis=1)
+    if few_experts:
+        mixed, grad_logits, grad_normed_ffn, expert_parts = exchange_tokens(
+            normed_ffn, all_cotangents, plan, expert_ids, whole_router, w_in, w_down
+        )
+    else:
+        mixed, grad_logits, grad_normed_ffn, expert_parts = exchange_pairs(
+            normed_ffn, middle, cotangent, expert_ids, priority, whole_router, w_in, w_down
+        )
     output = (middle + mixed).astype(jnp.bfloat16)
     grad_out = cotangent.astype(jnp.float32)
-    grad_gates = jnp.sum(grad_out[:, None, :] * pair_out, axis=2)
-    pair_grads = (gates[:, :, None] * grad_out[:, None, :]).astype(jnp.bfloat16).reshape(-1, width)
-    outgoing_grads = (
-        jnp.zeros((experts_total * send, width), jnp.bfloat16)
-        .at[target]
-        .set(pair_grads)
-        .reshape(experts_total, send, width)
-    )
-    arrived_grads = lax.all_to_all(
-        outgoing_grads, "expert", split_axis=0, concat_axis=0, tiled=True
-    )
-    grad_expert_out = (
-        jnp.zeros((local_experts * capacity, width), jnp.bfloat16)
-        .at[landing]
-        .set(arrived_grads.reshape(-1, width), mode="drop")
-        .reshape(local_experts, capacity, width)
-    )
-    hidden_again = jnp.einsum(
-        "ecd,edf->ecf", expert_inputs, w_in, preferred_element_type=jnp.float32
-    )
-    activated_again, gelu_back = jax.vjp(jax.nn.gelu, hidden_again)
-    grad_activated = jnp.einsum(
-        "ecd,efd->ecf", grad_expert_out, w_down, preferred_element_type=jnp.float32
-    )
-    grad_hidden = gelu_back(grad_activated)[0].astype(jnp.bfloat16)
-    grad_w_down = jnp.einsum(
-        "ecf,ecd->efd",
-        activated_again.astype(jnp.bfloat16),
-        grad_expert_out,
-        preferred_element_type=jnp.float32,
-    )
-    grad_w_in = jnp.einsum(
-        "ecd,ecf->edf", expert_inputs, grad_hidden, preferred_element_type=jnp.float32
-    )
-    grad_inputs = jnp.einsum(
-        "ecf,edf->ecd", grad_hidden, w_in, preferred_element_type=jnp.float32
-    ).astype(jnp.bfloat16)
-    back_rows = jnp.where(
-        live[:, None],
-        jnp.take(grad_inputs.reshape(-1, width), safe, axis=0),
-        jnp.zeros((), jnp.bfloat16),
-    ).reshape(experts_total, send, width)
-    came_back = lax.all_to_all(back_rows, "expert", split_axis=0, concat_axis=0, tiled=True)
-    pair_back = jnp.where(
-        kept[:, None],
-        jnp.take(came_back.reshape(-1, width), target, axis=0).astype(jnp.float32),
-        0.0,
-    )
-    grad_normed_ffn = jnp.sum(pair_back.reshape(rows, top, width), axis=1)
-    grad_chosen = gates * (grad_gates - jnp.sum(gates * grad_gates, axis=-1, keepdims=True))
-    grad_logits = jnp.sum(jnp.where(picks, grad_chosen[:, :, None], 0.0), axis=1).astype(
-        jnp.bfloat16
-    )
-    back_qkv, back_out, back_router = dense_regather(w_qkv, w_out, w_router)
-    grad_normed_ffn = grad_normed_ffn + jnp.dot(
-        grad_logits, back_router.T, preferred_element_type=jnp.float32
-    )
     grad_router = jnp.dot(normed_ffn.T, grad_logits, preferred_element_type=jnp.float32)
     _, ffn_norm_back = jax.vjp(normed, middle, gain_ffn)
     grad_middle_part, grad_gain_ffn = ffn_norm_back(grad_normed_ffn)
@@ -530,56 +801,44 @@
     grad_branch = grad_middle.astype(jnp.bfloat16)
     grad_out_weight = jnp.dot(attended.T, grad_branch, preferred_element_type=jnp.float32)
     grad_attended = jnp.dot(
-        grad_branch, back_out.T, preferred_element_type=jnp.float32
+        grad_branch, whole_out.T, preferred_element_type=jnp.float32
     ).astype(jnp.bfloat16)
     grad_query, grad_keys, grad_values, grad_lines = attention_backward(
         info, query, grad_attended, exact, log_total, all_keys, all_values, rows_bias, row_start, heads
     )
     grad_table = table_grad(grad_lines, rel_table.shape[0])
-    prompt_grad_keys, prompt_grad_values = (
-        lax.psum_scatter(
-            grad_keys[:PROMPT], "dp", scatter_dimension=0, tiled=True
-        ),
-        lax.psum_scatter(
-            grad_values[:PROMPT], "dp", scatter_dimension=0, tiled=True
-        ),
+    prompt_grads = lax.psum_scatter(
+        jnp.concatenate([grad_keys[:PROMPT], grad_values[:PROMPT]], axis=1),
+        "dp", scatter_dimension=0, tiled=True,
     )
     grad_projected = jnp.concatenate(
         [
             grad_query,
-            jnp.concatenate([prompt_grad_keys, grad_keys[PROMPT:]], axis=0),
-            jnp.concatenate([prompt_grad_values, grad_values[PROMPT:]], axis=0),
+            jnp.concatenate(
+                [prompt_grads, jnp.concatenate([grad_keys[PROMPT:], grad_values[PROMPT:]], axis=1)], axis=0
+            ),
         ],
         axis=1,
-    ).astype(jnp.bfloat16)
-    grad_normed_attn = jnp.dot(grad_projected, back_qkv.T, preferred_element_type=jnp.float32)
+    )
+    grad_normed_attn = jnp.dot(grad_projected, whole_qkv.T, preferred_element_type=jnp.float32)
     grad_qkv = jnp.dot(normed_attn.T, grad_projected, preferred_element_type=jnp.float32)
     _, attn_norm_back = jax.vjp(normed, inputs, gain_attn)
     grad_inputs_part, grad_gain_attn = attn_norm_back(grad_normed_attn)
     grad_tokens = grad_middle + grad_inputs_part
-    dense_parts = (
-        lax.psum_scatter(grad_qkv, ("dp", "expert"), scatter_dimension=0, tiled=True),
-        lax.psum_scatter(grad_out_weight, ("dp", "expert"), scatter_dimension=0, tiled=True),
-        lax.psum_scatter(grad_router, ("dp", "expert"), scatter_dimension=0, tiled=True),
-    )
-    expert_parts = (
-        lax.psum_scatter(
-            grad_w_in.astype(jnp.bfloat16), "dp", scatter_dimension=1, tiled=True
-        ).astype(jnp.float32),
-        lax.psum_scatter(
-            grad_w_down.astype(jnp.bfloat16), "dp", scatter_dimension=1, tiled=True
-        ).astype(jnp.float32),
-    )
+    dense = lax.psum_scatter(
+        jnp.concatenate([grad_qkv, grad_out_weight], axis=1), ("dp", "expert"), scatter_dimension=0, tiled=True
+    )
+    own_router = lax.psum_scatter(grad_router, ("dp", "expert"), scatter_dimension=0, tiled=True)
     small_parts = lax.psum((grad_gain_attn, grad_gain_ffn, grad_table.T), ("dp", "expert"))
     return (
         output,
         grad_tokens,
         small_parts[0],
-        dense_parts[0],
+        dense[:, : 3 * width],
         small_parts[2],
-        dense_parts[1],
+        dense[:, 3 * width :],
         small_parts[1],
-        dense_parts[2],
+        own_router,
         expert_parts[0],
         expert_parts[1],
     )

time: 1900 us -> 1520 us (0.80)
  blocking collectives: 376 us -> 56.1 us
  local copies, waits for them, and re-layouts: 207 us -> 36.8 us
  Pallas kernels: 300 us -> 470 us
  waiting for transfers between devices: 709 us -> 816 us
  matrix products: 148 us -> 53.3 us
  other arithmetic: 122 us -> 52 us
    all_to_all x3 -> x1, waiting for transfers between devices: 235 us -> 3.83 us  [exchange_tokens(): lax.all_to_all(gate_all, 'expert', split_axis=0, concat_axis=0, tiled=True)]
    pallas_call x0 -> x5, Pallas kernels: none -> 170 us  [the longest x1 99.3 us: expert_layer(): pl.pallas_call(functools.partial(expert_kernel, sources), grid_spec=pltpu...]
    all_gather x2 -> x4, waiting for transfers between devices: 63.2 us -> 232 us  [the longest x1 137 us: exchange_tokens(): all_tokens = lax.all_gather(sent, 'expert', axis=0, tiled=True)]
    all_gather x1, blocking collectives: 183 us -> 15.6 us  [gather_codes(): return lax.all_gather(expert_ids * PRIO + priority, 'expert', axis=0)]
    all_to_all x1 -> x0, blocking collectives: 145 us -> none  [per_device(): lax.all_to_all(outgoing_grads, 'expert', split_axis=0, concat_axis=0, til...]
    reduce_scatter x6, waiting for transfers between devices: 359 us -> 489 us  [the longest x1 112 us: exchange_tokens(): lax.psum_scatter(mixed_all, 'expert', scatter_dimension=0, tiled=True)]
    dot_general x10 -> x6, matrix products: 123 us -> 27.7 us  [the longest x1 17.7 us: per_device(): jnp.dot(grad_projected, whole_qkv.T, preferred_element_type=jnp.float32)]
    gather x4 -> x0, local copies, waits for them, and re-layouts: 59.6 us -> none  [the longest x1 17.8 us: per_device(): jnp.take(grad_inputs.reshape(-1, width), safe, axis=0)]
  transfers between devices with their start and end apart: 13 -> 13, of which waited for: 11 -> 12; matrix products, arithmetic and copies ran while one was open for 9% -> 6% of each run, Pallas kernels for 6% -> 10%
where the time goes in v2:
time: 1520 us
  waiting for transfers between devices  816 us (54%)
  Pallas kernels  470 us (31%)
  blocking collectives  56.1 us (4%)
  matrix products  53.3 us (4%)
  other arithmetic  52 us (3%)
  local copies, waits for them, and re-layouts  36.8 us (2%)
  starting transfers between devices  16.4 us (1%)
    pallas_call x1, Pallas kernels, attention_backward(): pl.pallas_call(functools.partial(bwd_kernel, scale), grid_spec=pltpu.Pref...  181 us
    all_gather x1, waiting for transfers between devices, exchange_tokens(): all_tokens = lax.all_gather(sent, 'expert', axis=0, tiled=True)  137 us
    pallas_call x1, Pallas kernels, attention_forward(): pl.pallas_call(functools.partial(fwd_kernel, scale2), grid_spec=pltpu.Pre...  120 us
    reduce_scatter x1, waiting for transfers between devices, exchange_tokens(): lax.psum_scatter(mixed_all, 'expert', scatter_dimension=0, tiled=True)  112 us
    reduce_scatter x1, waiting for transfers between devices, exchange_tokens(): lax.psum_scatter(grad_all, 'expert', scatter_dimension=0, tiled=True)  104 us
    reduce_scatter x1, waiting for transfers between devices, per_device(): lax.psum_scatter(jnp.concatenate([grad_keys[:PROMPT], grad_values[:PROMPT...  101 us
    pallas_call x1, Pallas kernels, expert_layer(): pl.pallas_call(functools.partial(expert_kernel, sources), grid_spec=pltpu...  99.3 us
    reduce_scatter x1, waiting for transfers between devices, per_device(): lax.psum_scatter(jnp.concatenate([grad_qkv, grad_out_weight], axis=1), ('...  74.3 us
  transfers between devices with their start and end apart: 13, of which 12 were waited for; matrix products, arithmetic and copies ran while one was open for 6% of the time, Pallas kernels for 10%

profile of v2, /device:TPU:0, one launch (start us, length us, event | category | flops | bytes accessed | tf_op | source)
XLA Modules:
  0.0 1515.4 jit_solution(1855501274607245327)
XLA Ops:
  8.7 15.6 %all-gather = s32[8192,2]{0,1:T(2,128)S(1)} all-gather(s32[1024,2]{0,1:T(2,128)S(1)} %multiply_add_fusion), channel_id=2, replica_groups=mesh['dp'=4,'expert'=8] {'expert'}, dimensions={0}, use_global_device_ids=true | all-gather | bytes 73728 | tf_op jit(solution)/shard_map/all_gather | solution.py:675
  28.6 3.1 multiply_reduce_fusion
  31.8 1.1 broadcast_select_fusion.r_ref
  32.9 3.7 fusion.2.refs_1_
  36.6 37.5 %all-gather.8.cloned.1.call-done = bf16[768,2304]{1,0:T(8,128)(2,1)} async-done(((bf16[24,2304]{1,0:T(8,128)(2,1)}), bf16[768,2304]{1,0:T(8,128)(2,1)}) %all-gather.8.cloned.1.call-update) | async-done | bytes 3538960 | tf_op jit(solution)/shard_map/all_gather | solution.py:756
  74.1 6.4 convolution_convert_fusion
  80.5 2.1 copy-done.17
  82.6 1.4 fusion.108
  85.6 41.4 %all-gather.10.cloned.1.call-done = bf16[2048,768]{1,0:T(8,128)(2,1)} async-done(((bf16[512,768]{1,0:T(8,128)(2,1)}), bf16[2048,768]{1,0:T(8,128)(2,1)}) %all-gather.10.cloned.1.call-update) | async-done | bytes 3145744 | tf_op jit(solution)/shard_map/all_gather | solution.py:33
  127.0 46.4 %all-gather.12.cloned.1.call-done = bf16[2048,768]{1,0:T(8,128)(2,1)} async-done(((bf16[512,768]{1,0:T(8,128)(2,1)}), bf16[2048,768]{1,0:T(8,128)(2,1)}) %all-gather.12.cloned.1.call-update) | async-done | bytes 3145744 | tf_op jit(solution)/shard_map/all_gather | solution.py:34
  173.5 57.9 %all-gather.14.cloned.1.call-done = bf16[768,896]{1,0:T(8,128)(2,1)} async-done(((bf16[24,896]{1,0:T(8,128)(2,1)}), bf16[768,896]{1,0:T(8,128)(2,1)}) %all-gather.14.cloned.1.call-update) | async-done | bytes 1376272 | tf_op jit(solution)/shard_map/all_gather | solution.py:774
  231.5 12.0 all-gather.18.cloned.1.call-start
  244.5 2.7 slice.70.q_ref
  247.2 5.2 pad_maximum_fusion.2
  252.4 0.8 broadcast_in_dim.70.st_ref
  253.2 120.0 %attention_forward.1 = (f32[1024,768]{1,0:T(8,128)}, f32[1024,128]{1,0:T(8,128)}) custom-call(s32[6]{0:T(128)} %pad_add_fusion.info, bf16[1024,768]{1,0:T(8,128)(2,1)} %slice.70.q_ref, bf16[2560,768]{1,0:T(8,128)(2,1)} %get-tuple-element.103.k_ref, bf16[2560,768]{1,0:T(8,128)(2,1)} %get-tuple-element.104.v_ref, f32[12,8,2816]{2,1,0:T(8,128)} %broadcast_select_fusion.r_ref, ...), custom_call_target="tpu_custom_call" | custom-call | tf_op jit(solution)/shard_map/attention_forward/pallas_call | solution.py:140
  373.3 3.9 multiply_reduce_fusion.3
  377.2 1.6 copy-done.11
  378.8 1.5 multiply_convert_fusion
  381.9 12.5 pack_tokens.3
  394.4 1.9 copy-done.5
  396.2 0.8 copy-done.7
  397.1 136.7 %all-gather.18.cloned.1.call-done.refs_0_ = bf16[8192,768]{1,0:T(8,128)(2,1)} async-done(((bf16[1024,768]{1,0:T(8,128)(2,1)}), bf16[8192,768]{1,0:T(8,128)(2,1)}) %all-gather.18.cloned.1.call-update) | async-done | bytes 12582928 | tf_op jit(solution)/shard_map/all_gather | solution.py:694
  533.7 11.2 pack_tokens.2.x_ref
  545.0 2.0 copy-done.2
  546.9 99.3 %expert_layer.1 = (bf16[2560,768]{1,0:T(8,128)(2,1)}, bf16[2560,768]{1,0:T(8,128)(2,1)}, bf16[2560,128]{1,0:T(8,128)(2,1)}, bf16[768,3072]{1,0:T(8,128)(2,1)}, bf16[3072,768]{1,0:T(8,128)(2,1)}) custom-call(s32[17]{0:T(128)} %copy-done.9, s32[1]{0:T(128)} %bitcast.10.expert, bf16[2560,768]{1,0:T(8,128)(2,1)} %copy-done.2, bf16[2560,128]{1,0:T(8,128)(2,1)} %copy-done.7, ...), custom_call_target="tpu_custom_call" | custom-call | tf_op jit(solution)/shard_map/expert_layer/pallas_call | solution.py:499
  646.3 1.2 broadcast_in_dim.78.place_ref
  647.5 0.8 copy-done.6
  648.4 1.6 copy-done.8
  649.9 25.9 %unpack_tokens.3 = (bf16[8192,768]{1,0:T(8,128)(2,1)}, f32[8192,128]{1,0:T(8,128)S(1)}) custom-call(s32[17]{0:T(128)S(1)} %copy-done.10, s32[8192,128]{1,0:T(8,128)S(1)} %broadcast_in_dim.78.place_ref, bf16[2560,768]{1,0:T(8,128)(2,1)S(1)} %copy-done.6, bf16[2560,128]{1,0:T(8,128)(2,1)S(1)} %copy-done.8), custom_call_target="tpu_custom_call" | custom-call | tf_op jit(solution)/shard_map/unpack_tokens/pallas_call | solution.py:408
  675.8 2.1 copy-done.3
  678.0 2.2 copy-done.1
  680.2 2.1 copy-done.4
  682.3 20.9 %unpack_tokens.2 = bf16[8192,768]{1,0:T(8,128)(2,1)} custom-call(s32[17]{0:T(128)S(1)} %copy-done.10, s32[8192,128]{1,0:T(8,128)S(1)} %copy-done.1, bf16[2560,768]{1,0:T(8,128)(2,1)S(1)} %copy-done.4), custom_call_target="tpu_custom_call" | custom-call | tf_op jit(solution)/shard_map/unpack_tokens/pallas_call | solution.py:408
  703.1 104.3 %reduce-scatter.8.cloned.1.call-done = bf16[1024,768]{1,0:T(8,128)(2,1)} async-done(((bf16[8192,768]{1,0:T(8,128)(2,1)}), bf16[1024,768]{1,0:T(8,128)(2,1)}) %reduce-scatter.8.cloned.1.call-update) | async-done | bytes 1572880 | tf_op jit(solution)/shard_map/reduce_scatter | solution.py:704
  807.4 4.1 slice_reduce_fusion
  811.5 3.4 all-to-all-start
  815.2 2.0 fusion.105
  817.2 3.8 all-to-all-done
  821.2 4.4 multiply_reduce_fusion.1
  825.6 112.2 %reduce-scatter.10.cloned.1.call-done = bf16[1024,768]{1,0:T(8,128)(2,1)} async-done(((bf16[8192,768]{1,0:T(8,128)(2,1)}), bf16[1024,768]{1,0:T(8,128)(2,1)}) %reduce-scatter.10.cloned.1.call-update) | async-done | bytes 1572880 | tf_op jit(solution)/shard_map/reduce_scatter | solution.py:707
  937.8 4.4 fusion.9
  942.2 2.6 convolution_convert_fusion.1.do_ref
  944.8 180.6 %attention_backward.1 = (bf16[1024,768]{1,0:T(8,128)(2,1)}, bf16[2560,768]{1,0:T(8,128)(2,1)}, bf16[2560,768]{1,0:T(8,128)(2,1)}, f32[12,1,2816]{2,1,0:T(1,128)}) custom-call(s32[6]{0:T(128)} %pad_add_fusion.info, bf16[1024,768]{1,0:T(8,128)(2,1)} %slice.70.q_ref, bf16[1024,768]{1,0:T(8,128)(2,1)} %convolution_convert_fusion.1.do_ref, ...), custom_call_target="tpu_custom_call" | custom-call | tf_op jit(solution)/shard_map/attention_backward/pallas_call | solution.py:290
  1125.5 2.2 slice.65
  1127.7 0.8 copy-done.18
  1128.7 3.2 pad_maximum_fusion.1
  1133.7 1.2 slice.67
  1134.9 1.5 slice.66
  1136.4 6.0 fusion.35
  1142.4 101.3 %reduce-scatter.12.cloned.1.call-done = bf16[512,1536]{1,0:T(8,128)(2,1)} async-done(((bf16[2048,1536]{1,0:T(8,128)(2,1)}), bf16[512,1536]{1,0:T(8,128)(2,1)}) %reduce-scatter.12.cloned.1.call-update) | async-done | bytes 1572880 | tf_op jit(solution)/shard_map/reduce_scatter | solution.py:810
  1243.7 8.7 fusion.33
  1252.5 9.3 pad_maximum_fusion
  1261.9 1.3 copy-done.13
  1263.8 39.8 %reduce-scatter.16.cloned.1.call-done = bf16[1,192,3072]{2,1,0:T(8,128)(2,1)} async-done(((bf16[1,768,3072]{2,1,0:T(8,128)(2,1)}), bf16[1,192,3072]{2,1,0:T(8,128)(2,1)}) %reduce-scatter.16.cloned.1.call-update) | async-done | bytes 1179664 | tf_op jit(solution)/shard_map/reduce_scatter | solution.py:710
  1303.7 2.9 convert_element_type.339
  1306.6 57.2 %reduce-scatter.18.cloned.1.call-done = bf16[1,768,768]{2,1,0:T(8,128)(2,1)} async-done(((bf16[1,3072,768]{2,1,0:T(8,128)(2,1)}), bf16[1,768,768]{2,1,0:T(8,128)(2,1)}) %reduce-scatter.18.cloned.1.call-update) | async-done | bytes 1179664 | tf_op jit(solution)/shard_map/reduce_scatter | solution.py:711
  1363.8 3.0 convert_element_type.340
  1366.8 17.7 %fusion.8 = (f32[768]{0:T(1024)S(1)}, f32[1024]{0:T(1024)S(1)}, f32[1024,768]{1,0:T(8,128)}) fusion(bf16[1024,768]{1,0:T(8,128)(2,1)S(1)} %copy-done.15, f32[1024]{0:T(1024)S(1)} %copy-done.34, f32[768]{0:T(1024)S(1)} %copy-done.37, bf16[768,2304]{1,0:T(8,128)(2,1)S(1)} %copy-done.39, bf16[512,768]{1,0:T(8,128)(2,1)S(1)} %copy-done.23, ...), kind=kOutput, calls=%fused_computation.24 | convolution fusion | flops 3648256256 | bytes 12990464 | tf_op jit(solution)/shard_map/dot_general | solution.py:823
  1384.5 40.4 %all-reduce.3 = (f32[768]{0:T(1024)}, f32[31,12]{0,1:T(8,128)}, f32[768]{0:T(1024)}, f32[768,8]{0,1:T(8,128)S(1)}) all-reduce(f32[768]{0:T(1024)S(1)} %get-tuple-element.76, f32[31,12]{0,1:T(8,128)S(1)} %fusion.43, f32[768]{0:T(1024)S(1)} %get-tuple-element.74, ...), channel_id=1, replica_groups=mesh['dp'=4,'expert'=8] {'dp','expert'}, use_global_device_ids=true, to_apply=%region_28.29 | all-reduce | flops 8052 | bytes 64416 | tf_op jit(solution)/shard_map/psum | solution.py:832
  1425.6 5.3 fusion.10
  1430.9 74.3 %reduce-scatter.14.cloned.1.call-done = f32[24,3072]{1,0:T(8,128)} async-done(((f32[768,3072]{1,0:T(8,128)}), f32[24,3072]{1,0:T(8,128)}) %reduce-scatter.14.cloned.1.call-update) | async-done | bytes 294928 | tf_op jit(solution)/shard_map/reduce_scatter | solution.py:828
  1505.2 1.6 slice.77
  1506.9 1.5 slice.78
  (143 shorter events, 13.7 us)
Async XLA Ops:
  7.2 20.2 %copy-start.14 = (bf16[1024,768]{1,0:T(8,128)(2,1)S(1)}, bf16[1024,768]{1,0:T(8,128)(2,1)}, u32[]{:S(2)}) copy-start(bf16[1024,768]{1,0:T(8,128)(2,1)} %param.13) | copy-start | bytes 4718596
  7.2 20.5 %copy-start.35 = (f32[31,12]{0,1:T(8,128)S(1)}, f32[31,12]{0,1:T(8,128)}, u32[]{:S(2)}) copy-start(f32[31,12]{0,1:T(8,128)} %param.19) | copy-start | bytes 4468
  7.2 66.9 %all-gather.8.cloned.1.call-start = ((), (), s32[]{:S(2)}) async-start(), calls=%async_computation.7 | async-start | bytes 3649536 | tf_op jit(solution)/shard_map/all_gather | solution.py:756
  7.9 119.1 %all-gather.10.cloned.1.call-start = ((), (), s32[]{:S(2)}) async-start(), calls=%async_computation.8 | async-start | bytes 3932160 | tf_op jit(solution)/shard_map/all_gather | solution.py:33
  27.3 506.4 %copy-start.9 = (s32[17]{0:T(128)}, s32[17]{0:T(128)S(1)}, u32[]{:S(2)}) copy-start(s32[17]{0:T(128)S(1)} %pad_add_fusion.1.info) | copy-start | bytes 208
  27.7 46.4 %copy-start.33 = (f32[1024]{0:T(1024)}, f32[1024]{0:T(1024)S(1)}, u32[]{:S(2)}) copy-start(f32[1024]{0:T(1024)S(1)} %fusion.99) | copy-start | bytes 12292
  28.2 352.1 %copy-start.26 = (s32[8,1024]{1,0:T(8,128)}, s32[8,1024]{1,0:T(8,128)S(1)}, u32[]{:S(2)}) copy-start(s32[8,1024]{1,0:T(8,128)S(1)} %fusion.30) | copy-start | bytes 98308
  31.7 42.4 %copy-start.36 = (f32[768]{0:T(1024)S(1)}, f32[768]{0:T(1024)}, u32[]{:S(2)}) copy-start(f32[768]{0:T(1024)} %param.17) | copy-start | bytes 9220
  80.5 2.1 copy-start.17
  82.6 2.3 copy-start.38
  82.6 2.4 copy-start.31
  84.1 159.4 %copy-start.32 = (s32[1,512]{1,0:T(1,128)S(1)}, s32[1,512]{1,0:T(1,128)}, u32[]{:S(2)}) copy-start(s32[1,512]{1,0:T(1,128)} %param.14) | copy-start | bytes 6148
  84.1 89.4 %all-gather.12.cloned.1.call-start = ((), (), s32[]{:S(2)}) async-start(), calls=%async_computation.9 | async-start | bytes 3932160 | tf_op jit(solution)/shard_map/all_gather | solution.py:34
  84.8 146.6 %all-gather.14.cloned.1.call-start = ((), (), s32[]{:S(2)}) async-start(), calls=%async_computation.10 | async-start | bytes 1419264 | tf_op jit(solution)/shard_map/all_gather | solution.py:774
  173.5 206.8 %all-gather.16.cloned.1.call-start = ((), (), s32[]{:S(2)}) async-start(), calls=%async_computation.11 | async-start | bytes 14155776 | tf_op jit(solution)/shard_map/all_gather | solution.py:778
  231.5 302.3 %all-gather.18.cloned.1.call-start = ((), (), s32[]{:S(2)}) async-start(), calls=%async_computation.12 | async-start | bytes 14155776 | tf_op jit(solution)/shard_map/all_gather | solution.py:694
  243.5 3.7 copy-start.19
  253.2 120.0 %copy-start.20 = (bf16[768,896]{1,0:T(8,128)(2,1)S(1)}, bf16[768,896]{1,0:T(8,128)(2,1)}, u32[]{:S(2)}) copy-start(bf16[768,896]{1,0:T(8,128)(2,1)} %all-gather.14.cloned.1.call-done) | copy-start | bytes 4128772
  373.2 5.5 copy-start.28
  377.1 1.6 copy-start.11
  377.2 3.1 copy-start.29
  380.3 427.1 %reduce-scatter.8.cloned.1.call-start = ((), (), s32[]{:S(2)}) async-start(), calls=%async_computation.13 | async-start | bytes 14155776 | tf_op jit(solution)/shard_map/reduce_scatter | solution.py:704
  394.4 1.9 copy-start.5
  396.2 0.8 copy-start.7
  545.0 2.0 copy-start.2
  646.3 2.1 copy-start.6
  646.3 2.1 copy-start.10
  647.5 28.3 %copy-start = (s32[8192,128]{1,0:T(8,128)}, s32[8192,128]{1,0:T(8,128)S(1)}, u32[]{:S(2)}) copy-start(s32[8192,128]{1,0:T(8,128)S(1)} %broadcast_in_dim.78.place_ref) | copy-start | bytes 12582916
  648.4 1.6 copy-start.8
  675.8 2.1 copy-start.3
  677.9 259.9 %reduce-scatter.10.cloned.1.call-start = ((), (), s32[]{:S(2)}) async-start(), calls=%async_computation.14 | async-start | bytes 14155776 | tf_op jit(solution)/shard_map/reduce_scatter | solution.py:707
  678.0 2.2 copy-start.1
  680.2 2.1 copy-start.4
  807.4 13.6 copy-start.27
  807.4 13.8 copy-start.12
  811.5 9.4 all-to-all-start
  814.9 428.8 %reduce-scatter.12.cloned.1.call-start = ((), (), s32[]{:S(2)}) async-start(), calls=%async_computation.15 | async-start | bytes 7864320 | tf_op jit(solution)/shard_map/reduce_scatter | solution.py:810
  821.2 4.4 copy-start.30
  937.8 4.4 copy-start.21
  942.2 2.6 copy-start.16
  1125.5 3.1 copy-start.18
  1131.9 171.8 %reduce-scatter.16.cloned.1.call-start = ((), (), s32[]{:S(2)}) async-start(), calls=%async_computation.17 | async-start | bytes 5898240 | tf_op jit(solution)/shard_map/reduce_scatter | solution.py:710
  1132.5 231.3 %reduce-scatter.18.cloned.1.call-start = ((), (), s32[]{:S(2)}) async-start(), calls=%async_computation.18 | async-start | bytes 5898240 | tf_op jit(solution)/shard_map/reduce_scatter | solution.py:711
  1133.2 372.0 %reduce-scatter.14.cloned.1.call-start = ((), (), s32[]{:S(2)}) async-start(), calls=%async_computation.16 | async-start | bytes 9732096 | tf_op jit(solution)/shard_map/reduce_scatter | solution.py:828
  1134.9 108.8 %copy-start.22 = (bf16[512,768]{1,0:T(8,128)(2,1)}, bf16[512,768]{1,0:T(8,128)(2,1)S(1)}, u32[]{:S(2)}) copy-start(bf16[512,768]{1,0:T(8,128)(2,1)S(1)} %slice.67) | copy-start | bytes 2359300
  1136.4 107.4 %copy-start.24 = (bf16[512,768]{1,0:T(8,128)(2,1)}, bf16[512,768]{1,0:T(8,128)(2,1)S(1)}, u32[]{:S(2)}) copy-start(bf16[512,768]{1,0:T(8,128)(2,1)S(1)} %slice.66) | copy-start | bytes 2359300
  1136.4 107.4 %copy-start.15 = (bf16[1024,768]{1,0:T(8,128)(2,1)S(1)}, bf16[1024,768]{1,0:T(8,128)(2,1)}, u32[]{:S(2)}) copy-start(bf16[1024,768]{1,0:T(8,128)(2,1)} %param.13) | copy-start | bytes 4718596
  1136.4 107.3 %copy-start.34 = (f32[1024]{0:T(1024)S(1)}, f32[1024]{0:T(1024)}, u32[]{:S(2)}) copy-start(f32[1024]{0:T(1024)} %copy-done.33) | copy-start | bytes 12292
  1136.4 107.3 %copy-start.37 = (f32[768]{0:T(1024)S(1)}, f32[768]{0:T(1024)}, u32[]{:S(2)}) copy-start(f32[768]{0:T(1024)} %param.17) | copy-start | bytes 9220
  1261.8 1.4 copy-start.13
  1261.8 1.7 copy-start.40
  1263.8 103.0 %copy-start.23 = (bf16[512,768]{1,0:T(8,128)(2,1)S(1)}, bf16[512,768]{1,0:T(8,128)(2,1)}, u32[]{:S(2)}) copy-start(bf16[512,768]{1,0:T(8,128)(2,1)} %copy-done.22) | copy-start | bytes 2359300
  1263.8 103.0 %copy-start.25 = (bf16[512,768]{1,0:T(8,128)(2,1)S(1)}, bf16[512,768]{1,0:T(8,128)(2,1)}, u32[]{:S(2)}) copy-start(bf16[512,768]{1,0:T(8,128)(2,1)} %copy-done.24) | copy-start | bytes 2359300
  1363.8 3.0 copy-start.39
Sparse Core Ops, SparseCore 0:
  11.1 62.9 all-gather.7
  84.2 42.7 all-gather.9
  129.5 43.9 all-gather.11
  176.7 54.6 all-gather.13
  232.9 115.6 all-gather.15
  380.4 153.2 all-gather.17
  678.0 129.3 reduce-scatter.7
  809.7 128.0 reduce-scatter.9
  1132.0 111.6 reduce-scatter.11
  1246.6 57.0 reduce-scatter.15
  1306.7 57.0 reduce-scatter.17
  1369.6 135.6 reduce-scatter.13

commit v3 on v2

--- a/solution.py
+++ b/solution.py
@@ -28,11 +28,18 @@
     return values * lax.rsqrt(jnp.mean(values * values, axis=-1, keepdims=True) + EPSILON) * gain
 
 
-def prompt_gather(own_keys, own_values):
-    return (
-        lax.all_gather(own_keys, "dp", axis=0, tiled=True),
-        lax.all_gather(own_values, "dp", axis=0, tiled=True),
-    )
+def pairs_together(w_qkv):
+    width = w_qkv.shape[1] // 3
+    rows = w_qkv.shape[0]
+    keys_values = w_qkv[:, width:].reshape(rows, 2, width // 128, 128).swapaxes(1, 2)
+    return jnp.concatenate([w_qkv[:, :width], keys_values.reshape(rows, 2 * width)], axis=1)
+
+
+def pairs_apart(grad):
+    width = grad.shape[1] // 3
+    rows = grad.shape[0]
+    keys_values = grad[:, width:].reshape(rows, width // 128, 2, 128).swapaxes(1, 2)
+    return jnp.concatenate([grad[:, :width], keys_values.reshape(rows, 2 * width)], axis=1)
 
 
 LOG2E = math.log2(math.e)
@@ -40,6 +47,7 @@
 QT = 256
 KT = 512
 RUN = 256
+PARTS = 2
 ROWS = 32
 NT = (((1,), (1,)), ((), ()))
 NN = (((1,), (0,)), ((), ()))
@@ -131,25 +139,30 @@
         tile(KT + QT * j, PROMPT // KT + 1,
              lambda t: b_scr[pl.ds(QT * j, QT), pl.ds(pl.multiple_of(t * KT, KT), KT)], lambda t: t)
 
-def attention_forward(info, q, k, v, rows_bias, row_start, heads):
-    n, width = q.shape
-    keys = k.shape[0]
-    pair = lambda r: pl.BlockSpec((r, 128), lambda h, *_: (0, h // 2))
-    whole = pl.BlockSpec((n, 128), lambda h, *_: (0, 0))
-    scale2 = (width // heads) ** -0.5 * LOG2E
+def attention_forward(info, projected, keys_values, rows_bias, row_start, part):
+    n = projected.shape[0]
+    keys, columns = keys_values.shape
+    heads = columns // 128
+    head_size = 64
+    scale2 = head_size ** -0.5 * LOG2E
+    first = part * heads // 2
     return pl.pallas_call(
         functools.partial(fwd_kernel, scale2),
         grid_spec=pltpu.PrefetchScalarGridSpec(
             num_scalar_prefetch=1, grid=(heads,),
-            in_specs=[pair(n), pair(keys), pair(keys),
-                      pl.BlockSpec((1, 8, rows_bias.shape[2]), lambda h, *_: (h, 0, 0)),
+            in_specs=[pl.BlockSpec((n, 128), lambda h, *_: (0, first + h // 2)),
+                      pl.BlockSpec((keys, 128), lambda h, *_: (0, h // 2 * 2)),
+                      pl.BlockSpec((keys, 128), lambda h, *_: (0, h // 2 * 2 + 1)),
+                      pl.BlockSpec((1, 8, rows_bias.shape[2]), lambda h, *_: (2 * first + h, 0, 0)),
                       pl.BlockSpec((KT, 128), lambda h, *_: (0, 0))],
-            out_specs=[pair(n), whole],
+            out_specs=[pl.BlockSpec((n, 128), lambda h, *_: (0, h // 2)),
+                       pl.BlockSpec((n, 128), lambda h, *_: (0, 0))],
             scratch_shapes=[pltpu.VMEM((128, rows_bias.shape[2]), F32), pltpu.VMEM((KT, PROMPT + KT), F32)]),
-        out_shape=[jax.ShapeDtypeStruct((n, width), F32), jax.ShapeDtypeStruct((n, 128), F32)],
+        out_shape=[jax.ShapeDtypeStruct((n, heads * 64), F32), jax.ShapeDtypeStruct((n, 128), F32)],
         compiler_params=pltpu.CompilerParams(vmem_limit_bytes=60 << 20),
+        cost_estimate=pl.CostEstimate(flops=heads * n * keys * 128 * 4, bytes_accessed=n * keys * 4, transcendentals=heads * n * keys),
         name="attention_forward",
-    )(info, q, k, v, rows_bias, row_start)
+    )(info, projected, keys_values, keys_values, rows_bias, row_start)
 
 def split3(x):
     hi = x.astype(BF16)
@@ -158,7 +171,7 @@
     return hi, mid, (rest - mid.astype(F32)).astype(BF16)
 
 def bwd_kernel(scale, info, q_ref, do_ref, o_ref, lse_ref, k_ref, v_ref, r_ref, st_ref,
-               dq_ref, dk_ref, dv_ref, dd_ref,
+               dq_ref, dkv_ref, dd_ref,
                t_scr, b_scr, e_scr, db_scr, qa, da, ka, va, qt, dot_t, dkt, dvt):
     h = pl.program_id(0)
     dp = info[5]
@@ -275,36 +288,41 @@
 
     @pl.when(half == 1)
     def _():
-        dk_ref[...] = (dkt[...] * scale).T.astype(BF16)
-        dv_ref[...] = dvt[...].T.astype(BF16)
-
-def attention_backward(info, q, do, o32, lse, k, v, rows_bias, row_start, heads):
-    n, width = q.shape
-    keys = k.shape[0]
+        dkv_ref[:, :128] = (dkt[...] * scale).T.astype(BF16)
+        dkv_ref[:, 128:] = dvt[...].T.astype(BF16)
+
+def attention_backward(info, projected, do, o32, lse, keys_values, rows_bias, row_start, part):
+    n = projected.shape[0]
+    keys, columns = keys_values.shape
+    heads = columns // 128
     wide = rows_bias.shape[2]
-    pair = lambda r: pl.BlockSpec((r, 128), lambda h, *_: (0, h // 2))
-    whole = pl.BlockSpec((n, 128), lambda h, *_: (0, 0))
-    line = pl.BlockSpec((1, 1, wide), lambda h, *_: (h, 0, 0))
-    scale = (width // heads) ** -0.5
+    first = part * heads // 2
+    own = pl.BlockSpec((n, 128), lambda h, *_: (0, h // 2))
+    shifted = pl.BlockSpec((n, 128), lambda h, *_: (0, first + h // 2))
     cols = PROMPT + KT
     return pl.pallas_call(
-        functools.partial(bwd_kernel, scale),
+        functools.partial(bwd_kernel, 64 ** -0.5),
         grid_spec=pltpu.PrefetchScalarGridSpec(
             num_scalar_prefetch=1, grid=(heads,),
-            in_specs=[pair(n), pair(n), pair(n), whole, pair(keys), pair(keys),
-                      pl.BlockSpec((1, 8, wide), lambda h, *_: (h, 0, 0)), pl.BlockSpec((KT, 128), lambda h, *_: (0, 0))],
-            out_specs=[pair(n), pair(keys), pair(keys), line],
+            in_specs=[shifted, shifted, own, pl.BlockSpec((n, 128), lambda h, *_: (0, 0)),
+                      pl.BlockSpec((keys, 128), lambda h, *_: (0, h // 2 * 2)),
+                      pl.BlockSpec((keys, 128), lambda h, *_: (0, h // 2 * 2 + 1)),
+                      pl.BlockSpec((1, 8, wide), lambda h, *_: (2 * first + h, 0, 0)),
+                      pl.BlockSpec((KT, 128), lambda h, *_: (0, 0))],
+            out_specs=[own, pl.BlockSpec((keys, 256), lambda h, *_: (0, h // 2)),
+                       pl.BlockSpec((1, 1, wide), lambda h, *_: (h, 0, 0))],
             scratch_shapes=[pltpu.VMEM((128, wide), F32), pltpu.VMEM((KT, cols), F32),
                             pltpu.VMEM((128, wide), F32), pltpu.VMEM((KT, cols), F32),
                             pltpu.VMEM((n, 128), BF16), pltpu.VMEM((n, 128), BF16),
                             pltpu.VMEM((keys, 128), BF16), pltpu.VMEM((keys, 128), BF16),
                             pltpu.VMEM((128, n), BF16), pltpu.VMEM((128, n), BF16),
                             pltpu.VMEM((128, keys), F32), pltpu.VMEM((128, keys), F32)]),
-        out_shape=[jax.ShapeDtypeStruct((n, width), BF16), jax.ShapeDtypeStruct((keys, width), BF16),
-                   jax.ShapeDtypeStruct((keys, width), BF16), jax.ShapeDtypeStruct((heads, 1, wide), F32)],
+        out_shape=[jax.ShapeDtypeStruct((n, heads * 64), BF16), jax.ShapeDtypeStruct((keys, columns), BF16),
+                   jax.ShapeDtypeStruct((heads, 1, wide), F32)],
         compiler_params=pltpu.CompilerParams(vmem_limit_bytes=60 << 20),
+        cost_estimate=pl.CostEstimate(flops=heads * n * keys * 128 * 10, bytes_accessed=n * keys * 4, transcendentals=heads * n * keys),
         name="attention_backward",
-    )(info, q, do, o32, lse, k, v, rows_bias, row_start)
+    )(info, projected, do, o32, lse, keys_values, keys_values, rows_bias, row_start)
 
 def info_of(ids, dp):
     starts = jnp.sum((ids[None, :] < jnp.arange(5)[:, None]).astype(jnp.int32), axis=1)
@@ -416,6 +434,38 @@
         compiler_params=pltpu.CompilerParams(vmem_limit_bytes=40 << 20),
         name="unpack_tokens",
     )(info, spread, *arrays)
+
+
+def collect_kernel(place_ref, x_ref, out_ref):
+    tokens = place_ref.shape[0]
+    lane = lax.broadcasted_iota(jnp.int32, (tokens, 128), 1)
+    put = jnp.concatenate(
+        [jnp.where(place_ref[...] == lane + 128 * b, 1.0, 0.0).astype(BF16) for b in range(x_ref.shape[0] // 128)],
+        axis=1)
+    total = dot(put, x_ref[...])
+
+    @pl.when(pl.program_id(0) == 0)
+    def _():
+        out_ref[...] = total
+
+    @pl.when(pl.program_id(0) > 0)
+    def _():
+        out_ref[...] += total
+
+
+def collect(place, returned, send):
+    experts, tokens = place.shape
+    width = returned.shape[1]
+    spread = jnp.broadcast_to(place.reshape(-1, 1), (experts * tokens, 128))
+    return pl.pallas_call(
+        collect_kernel,
+        grid=(experts,),
+        in_specs=[pl.BlockSpec((tokens, 128), lambda e: (e, 0)), pl.BlockSpec((send, width), lambda e: (e, 0))],
+        out_specs=pl.BlockSpec((tokens, width), lambda e: (0, 0)),
+        out_shape=jax.ShapeDtypeStruct((tokens, width), F32),
+        compiler_params=pltpu.CompilerParams(vmem_limit_bytes=40 << 20),
+        name="collect_rows",
+    )(spread, returned)
 
 
 def gelu_and_slope(v):
@@ -661,12 +711,8 @@
         grad_logits, router.T, preferred_element_type=jnp.float32
     )
     expert_parts = (
-        lax.psum_scatter(
-            grad_w_in.astype(jnp.bfloat16), "dp", scatter_dimension=1, tiled=True
-        ).astype(jnp.float32),
-        lax.psum_scatter(
-            grad_w_down.astype(jnp.bfloat16), "dp", scatter_dimension=1, tiled=True
-        ).astype(jnp.float32),
+        lax.psum_scatter(grad_w_in.astype(jnp.bfloat16), "dp", scatter_dimension=1, tiled=True),
+        lax.psum_scatter(grad_w_down.astype(jnp.bfloat16), "dp", scatter_dimension=1, tiled=True),
     )
     return mixed, grad_logits, grad_normed_ffn, expert_parts
 
@@ -679,7 +725,8 @@
     expert = lax.axis_index("expert").astype(jnp.int32)
     place, info, other = expert_slots(codes // PRIO, codes % PRIO, expert, rows * top)
     other_hot = (other.reshape(-1, 1) == jnp.arange(128)[None, :]).astype(jnp.bfloat16)
-    return place, info, other_hot
+    own_place = lax.all_to_all(place, "expert", split_axis=0, concat_axis=0, tiled=True)
+    return place, info, other_hot, own_place
 
 
 def exchange_tokens(normed_ffn, all_cotangents, plan, expert_ids, router, w_in, w_down):
@@ -687,7 +734,7 @@
     experts_total = router.shape[1]
     top = expert_ids.shape[1]
     expert = lax.axis_index("expert").astype(jnp.int32)
-    place, info, other_hot = plan
+    place, info, other_hot, own_place = plan
     sources = place.shape[0]
     room = (rows * top + 16 * sources + 2 * MOE_ROWS - 1) // MOE_ROWS * MOE_ROWS
     sent, all_cotangents = lax.optimization_barrier((normed_ffn, all_cotangents))
@@ -702,15 +749,16 @@
     gate_all = jnp.sum(gate_all[:, :3], axis=1).reshape(sources, rows)
     gate_own = lax.all_to_all(gate_all, "expert", split_axis=0, concat_axis=0, tiled=True)
     grad_own = lax.psum_scatter(grad_all, "expert", scatter_dimension=0, tiled=True)
-    (mixed_all,) = unpack(info, place, [mixed_rows], [jnp.bfloat16])
-    mixed_all, grad_own = lax.optimization_barrier((mixed_all, grad_own))
-    mixed = lax.psum_scatter(mixed_all, "expert", scatter_dimension=0, tiled=True)
-    grad_w_in, grad_w_down, mixed = lax.optimization_barrier((grad_w_in, grad_w_down, mixed))
+    send = 2 * rows * top // experts_total
+    windows = jnp.concatenate([lax.dynamic_slice_in_dim(mixed_rows, info[d], send, 0) for d in range(sources)], axis=0)
+    windows, grad_w_in, grad_w_down, grad_own = lax.optimization_barrier(
+        (windows, grad_w_in, grad_w_down, grad_own)
+    )
+    mixed = (lax.all_to_all(windows, "expert", split_axis=0, concat_axis=0, tiled=True), own_place)
     expert_parts = (
-        lax.psum_scatter(grad_w_in[None], "dp", scatter_dimension=1, tiled=True).astype(jnp.float32),
-        lax.psum_scatter(grad_w_down[None], "dp", scatter_dimension=1, tiled=True).astype(jnp.float32),
-    )
-    mixed = mixed.astype(jnp.float32)
+        lax.psum_scatter(grad_w_in[None], "dp", scatter_dimension=1, tiled=True),
+        lax.psum_scatter(grad_w_down[None], "dp", scatter_dimension=1, tiled=True),
+    )
     logits = jnp.dot(normed_ffn, router, preferred_element_type=jnp.float32)
     picks = expert_ids[:, :, None] == jnp.arange(experts_total)[None, None, :]
     chosen = jnp.sum(jnp.where(picks, logits[:, None, :], 0.0), axis=2)
@@ -753,35 +801,38 @@
     rows_bias = bias_rows(rel_table)
     if few_experts:
         codes = gather_codes(expert_ids, priority)
-    whole_qkv = lax.all_gather(w_qkv, ("dp", "expert"), axis=0, tiled=True)
+    experts_total = w_router.shape[1]
+    dense = jnp.concatenate(
+        [pairs_together(w_qkv), w_out, jnp.pad(w_router, ((0, 0), (0, 128 - experts_total)))], axis=1
+    )
+    dense = lax.all_gather(dense, ("dp", "expert"), axis=0, tiled=True)
     if few_experts:
         plan = plan_tokens(codes, rows, expert_ids.shape[1])
-        whole_qkv, rows_bias, plan = lax.optimization_barrier((whole_qkv, rows_bias, plan))
+        dense, rows_bias, plan = lax.optimization_barrier((dense, rows_bias, plan))
+    whole_qkv, whole_out = dense[:, : 3 * width], dense[:, 3 * width : 4 * width]
+    whole_router = dense[:, 4 * width : 4 * width + experts_total]
     inputs = tokens_in.astype(jnp.float32)
     normed_attn = normed(inputs, gain_attn).astype(jnp.bfloat16)
     projected = jnp.dot(normed_attn, whole_qkv, preferred_element_type=jnp.float32).astype(
         jnp.bfloat16
     )
-    query = projected[:, :width]
-    own_keys = projected[:, width : 2 * width]
-    own_values = projected[:, 2 * width :]
-    prompt_keys, prompt_values = prompt_gather(own_keys[:prompt_rows], own_values[:prompt_rows])
-    experts_total = w_router.shape[1]
-    late = jnp.concatenate([w_out, jnp.pad(w_router, ((0, 0), (0, 128 - experts_total)))], axis=1)
-    late, late_cotangent, prompt_keys, prompt_values = lax.optimization_barrier(
-        (late, cotangent, prompt_keys, prompt_values)
-    )
-    late = lax.all_gather(late, ("dp", "expert"), axis=0, tiled=True)
-    whole_out, whole_router = late[:, :width], late[:, width : width + experts_total]
+    parts = PARTS
+    columns = 2 * width // parts
+    kept = [projected[:, width + columns * g : width + columns * (g + 1)] for g in range(parts)]
+    gathered = [lax.all_gather(kv[:prompt_rows], "dp", axis=0, tiled=True) for kv in kept]
     if few_experts:
-        late_cotangent, _ = lax.optimization_barrier((late_cotangent, late))
+        late_cotangent, gathered[0] = lax.optimization_barrier((cotangent, gathered[0]))
         all_cotangents = lax.all_gather(late_cotangent, "expert", axis=0, tiled=True)
-    all_keys = jnp.concatenate([prompt_keys, own_keys[prompt_rows:]], axis=0)
-    all_values = jnp.concatenate([prompt_values, own_values[prompt_rows:]], axis=0)
-    exact, log_total = attention_forward(
-        info, query, all_keys, all_values, rows_bias, row_start, heads
-    )
-    attended = exact.astype(jnp.bfloat16)
+    keys_values = []
+    exact, log_total = [], []
+    for g in range(parts):
+        if g:
+            gathered[g], exact[-1] = lax.optimization_barrier((gathered[g], exact[-1]))
+        keys_values.append(jnp.concatenate([gathered[g], kept[g][prompt_rows:]], axis=0))
+        out, total = attention_forward(info, projected, keys_values[g], rows_bias, row_start, g)
+        exact.append(out)
+        log_total.append(total)
+    attended = jnp.concatenate(exact, axis=1).astype(jnp.bfloat16)
     middle = inputs + jnp.dot(attended, whole_out, preferred_element_type=jnp.float32)
     normed_ffn = normed(middle, gain_ffn).astype(jnp.bfloat16)
     if few_experts:
@@ -792,7 +843,6 @@
         mixed, grad_logits, grad_normed_ffn, expert_parts = exchange_pairs(
             normed_ffn, middle, cotangent, expert_ids, priority, whole_router, w_in, w_down
         )
-    output = (middle + mixed).astype(jnp.bfloat16)
     grad_out = cotangent.astype(jnp.float32)
     grad_router = jnp.dot(normed_ffn.T, grad_logits, preferred_element_type=jnp.float32)
     _, ffn_norm_back = jax.vjp(normed, middle, gain_ffn)
@@ -803,29 +853,34 @@
     grad_attended = jnp.dot(
         grad_branch, whole_out.T, preferred_element_type=jnp.float32
     ).astype(jnp.bfloat16)
-    grad_query, grad_keys, grad_values, grad_lines = attention_backward(
-        info, query, grad_attended, exact, log_total, all_keys, all_values, rows_bias, row_start, heads
-    )
-    grad_table = table_grad(grad_lines, rel_table.shape[0])
-    prompt_grads = lax.psum_scatter(
-        jnp.concatenate([grad_keys[:PROMPT], grad_values[:PROMPT]], axis=1),
-        "dp", scatter_dimension=0, tiled=True,
-    )
+    grad_queries, grad_prompts, grad_conts, grad_lines = [], [], [], []
+    for g in range(parts):
+        if g:
+            grad_attended, expert_parts, grad_queries[-1] = lax.optimization_barrier(
+                (grad_attended, expert_parts, grad_queries[-1])
+            )
+        grad_query, grad_kv, lines = attention_backward(
+            info, projected, grad_attended, exact[g], log_total[g], keys_values[g], rows_bias, row_start, g
+        )
+        grad_queries.append(grad_query)
+        grad_prompts.append(lax.psum_scatter(grad_kv[:PROMPT], "dp", scatter_dimension=0, tiled=True))
+        grad_conts.append(grad_kv[PROMPT:])
+        grad_lines.append(lines)
+    mixed, middle, grad_queries[-1] = lax.optimization_barrier((mixed, middle, grad_queries[-1]))
+    if few_experts:
+        returned, own_place = mixed
+        mixed = collect(own_place, returned, returned.shape[0] // own_place.shape[0])
+    output = (middle + mixed).astype(jnp.bfloat16)
+    grad_table = table_grad(jnp.concatenate(grad_lines, axis=0), rel_table.shape[0])
     grad_projected = jnp.concatenate(
-        [
-            grad_query,
-            jnp.concatenate(
-                [prompt_grads, jnp.concatenate([grad_keys[PROMPT:], grad_values[PROMPT:]], axis=1)], axis=0
-            ),
-        ],
-        axis=1,
+        grad_queries + [jnp.concatenate([a, b], axis=0) for a, b in zip(grad_prompts, grad_conts)], axis=1
     )
     grad_normed_attn = jnp.dot(grad_projected, whole_qkv.T, preferred_element_type=jnp.float32)
     grad_qkv = jnp.dot(normed_attn.T, grad_projected, preferred_element_type=jnp.float32)
     _, attn_norm_back = jax.vjp(normed, inputs, gain_attn)
     grad_inputs_part, grad_gain_attn = attn_norm_back(grad_normed_attn)
     grad_tokens = grad_middle + grad_inputs_part
-    dense = lax.psum_scatter(
+    dense_grad = lax.psum_scatter(
         jnp.concatenate([grad_qkv, grad_out_weight], axis=1), ("dp", "expert"), scatter_dimension=0, tiled=True
     )
     own_router = lax.psum_scatter(grad_router, ("dp", "expert"), scatter_dimension=0, tiled=True)
@@ -834,13 +889,13 @@
         output,
         grad_tokens,
         small_parts[0],
-        dense[:, : 3 * width],
+        pairs_apart(dense_grad[:, : 3 * width]),
         small_parts[2],
-        dense[:, 3 * width :],
+        dense_grad[:, 3 * width :],
         small_parts[1],
         own_router,
-        expert_parts[0],
-        expert_parts[1],
+        expert_parts[0].astype(jnp.float32),
+        expert_parts[1].astype(jnp.float32),
     )
 
 

time: 1520 us -> 1180 us (0.78)
  waiting for transfers between devices: 816 us -> 499 us
  Pallas kernels: 470 us -> 426 us
  local copies, waits for them, and re-layouts: 36.8 us -> 52.7 us
  between operations: 14.9 us -> 30.3 us
    reduce_scatter x2, waiting for transfers between devices: 214 us -> 43.6 us  [per_device(): lax.psum_scatter(grad_kv[:PROMPT], 'dp', scatter_dimension=0, tiled=True)]
    all_gather x4 -> x3, waiting for transfers between devices: 183 us -> 75.3 us  [the longest x2 42.2 us: per_device(): lax.all_gather(kv[:prompt_rows], 'dp', axis=0, tiled=True)]
    reduce_scatter x1, waiting for transfers between devices: 57.2 us -> 0.02 us  [exchange_tokens(): lax.psum_scatter(grad_w_down[None], 'dp', scatter_dimension=1, tiled=True)]
    reduce_scatter x1, waiting for transfers between devices: 104 us -> 147 us  [exchange_tokens(): lax.psum_scatter(grad_all, 'expert', scatter_dimension=0, tiled=True)]
    reduce_scatter x1, waiting for transfers between devices: 39.8 us -> 0.02 us  [exchange_tokens(): lax.psum_scatter(grad_w_in[None], 'dp', scatter_dimension=1, tiled=True)]
    pallas_call x1, Pallas kernels: 99.3 us -> 60.4 us  [expert_layer(): pl.pallas_call(functools.partial(expert_kernel, sources), grid_spec=pltpu...]
    all_to_all x0 -> x2, waiting for transfers between devices: none -> 31.2 us  [the longest x1 31.2 us: exchange_tokens(): lax.all_to_all(windows, 'expert', split_axis=0, concat_axis=0, tiled=True)]
    pallas_call x2 -> x1, Pallas kernels: 46.7 us -> 20.6 us  [unpack(): pl.pallas_call(functools.partial(unpack_kernel, sources), grid_spec=pltpu...]
  transfers between devices with their start and end apart: 13 -> 14, of which waited for: 12 -> 9; matrix products, arithmetic and copies ran while one was open for 6% -> 8% of each run, Pallas kernels for 10% -> 29%
where the time goes in v3:
time: 1180 us; the launch traced here: 1170 us
  waiting for transfers between devices  499 us (42%)
  Pallas kernels  426 us (36%)
  blocking collectives  57 us (5%)
  local copies, waits for them, and re-layouts  52.7 us (4%)
  other arithmetic  52.3 us (4%)
  matrix products  41 us (3%)
  between operations  30.3 us (3%)
  starting transfers between devices  14.2 us (1%)
    pallas_call x2, Pallas kernels, attention_backward(): pl.pallas_call(functools.partial(bwd_kernel, 64 ** (-0.5)), grid_spec=plt...  188 us
    reduce_scatter x1, waiting for transfers between devices, exchange_tokens(): lax.psum_scatter(grad_all, 'expert', scatter_dimension=0, tiled=True)  147 us
    pallas_call x2, Pallas kernels, attention_forward(): pl.pallas_call(functools.partial(fwd_kernel, scale2), grid_spec=pltpu.Pre...  125 us
    all_gather x1, waiting for transfers between devices, exchange_tokens(): all_tokens = lax.all_gather(sent, 'expert', axis=0, tiled=True)  118 us
    pallas_call x1, Pallas kernels, expert_layer(): pl.pallas_call(functools.partial(expert_kernel, sources), grid_spec=pltpu...  60.4 us
    reduce_scatter x1, waiting for transfers between devices, per_device(): lax.psum_scatter(jnp.concatenate([grad_qkv, grad_out_weight], axis=1), ('...  60 us
    reduce_scatter x2, waiting for transfers between devices, per_device(): lax.psum_scatter(grad_kv[:PROMPT], 'dp', scatter_dimension=0, tiled=True)  43.6 us
    all_gather x2, waiting for transfers between devices, per_device(): lax.all_gather(kv[:prompt_rows], 'dp', axis=0, tiled=True)  42.2 us
  transfers between devices with their start and end apart: 14, of which 9 were waited for; matrix products, arithmetic and copies ran while one was open for 8% of the time, Pallas kernels for 29%

profile of v3, /device:TPU:0, one launch (start us, length us, event | category | flops | bytes accessed | tf_op | source)
XLA Modules:
  0.0 1172.8 jit_solution(1876156400638942690)
XLA Ops:
  10.0 1.4 fusion.50
  12.2 15.6 %all-gather = s32[8192,2]{0,1:T(2,128)S(1)} all-gather(s32[1024,2]{0,1:T(2,128)S(1)} %multiply_add_fusion), channel_id=2, replica_groups=mesh['dp'=4,'expert'=8] {'expert'}, dimensions={0}, use_global_device_ids=true | all-gather | bytes 73728 | tf_op jit(solution)/shard_map/all_gather | solution.py:721
  30.4 4.7 all-to-all-start
  36.9 3.1 multiply_reduce_fusion
  41.2 3.7 fusion.2.refs_1_
  45.6 33.1 %all-gather.7.cloned.1.call-done = bf16[768,3200]{1,0:T(8,128)(2,1)} async-done(((bf16[24,3200]{1,0:T(8,128)(2,1)}), bf16[768,3200]{1,0:T(8,128)(2,1)}) %all-gather.7.cloned.1.call-update) | async-done | bytes 4915216 | tf_op jit(solution)/shard_map/all_gather | solution.py:808
  78.7 6.4 convolution_convert_fusion.q_ref
  85.2 2.2 copy-done.17
  87.3 1.4 fusion.108
  89.6 42.2 %all-gather.11.cloned.1.call-done = bf16[2048,768]{1,0:T(8,128)(2,1)} async-done(((bf16[512,768]{1,0:T(8,128)(2,1)}), bf16[2048,768]{1,0:T(8,128)(2,1)}) %all-gather.11.cloned.1.call-update) | async-done | bytes 3145744 | tf_op jit(solution)/shard_map/all_gather | solution.py:822
  133.0 4.3 pad_maximum_fusion.1.k_ref.v_ref
  138.1 62.5 %attention_forward.2 = (f32[1024,384]{1,0:T(8,128)}, f32[1024,128]{1,0:T(8,128)}) custom-call(s32[6]{0:T(128)} %pad_add_fusion.1.info, bf16[1024,2304]{1,0:T(8,128)(2,1)} %copy-done.17, bf16[2560,768]{1,0:T(8,128)(2,1)} %pad_maximum_fusion.1.k_ref.v_ref, bf16[2560,768]{1,0:T(8,128)(2,1)} %pad_maximum_fusion.1.k_ref.v_ref, ...), custom_call_target="tpu_custom_call" | custom-call | flops 8053063680 | bytes 10485760 | tf_op jit(solution)/shard_map/attention_forward/pallas_call | solution.py:149
  200.5 4.0 pad_maximum_fusion.2.k_ref.v_ref
  204.5 62.5 %attention_forward.3 = (f32[1024,384]{1,0:T(8,128)}, f32[1024,128]{1,0:T(8,128)}) custom-call(s32[6]{0:T(128)} %pad_add_fusion.1.info, bf16[1024,2304]{1,0:T(8,128)(2,1)} %copy-done.17, bf16[2560,768]{1,0:T(8,128)(2,1)} %pad_maximum_fusion.2.k_ref.v_ref, bf16[2560,768]{1,0:T(8,128)(2,1)} %pad_maximum_fusion.2.k_ref.v_ref, ...), custom_call_target="tpu_custom_call" | custom-call | flops 8053063680 | bytes 10485760 | tf_op jit(solution)/shard_map/attention_forward/pallas_call | solution.py:149
  267.0 1.6 convert.7
  268.7 1.8 convert.6
  270.5 3.1 multiply_reduce_fusion.3
  273.6 1.6 copy-done.8
  275.3 1.5 multiply_convert_fusion
  276.7 19.7 %all-gather.13.cloned.1.call-done.refs_0_ = bf16[8192,768]{1,0:T(8,128)(2,1)} async-done(((bf16[1024,768]{1,0:T(8,128)(2,1)}), bf16[8192,768]{1,0:T(8,128)(2,1)}) %all-gather.13.cloned.1.call-update) | async-done | bytes 12582928 | tf_op jit(solution)/shard_map/all_gather | solution.py:825
  297.7 10.5 pack_tokens.3
  308.3 1.9 copy-done.2
  311.1 117.7 %all-gather.15.cloned.1.call-done.refs_0_ = bf16[8192,768]{1,0:T(8,128)(2,1)} async-done(((bf16[1024,768]{1,0:T(8,128)(2,1)}), bf16[8192,768]{1,0:T(8,128)(2,1)}) %all-gather.15.cloned.1.call-update) | async-done | bytes 12582928 | tf_op jit(solution)/shard_map/all_gather | solution.py:741
  428.7 9.8 pack_tokens.2.x_ref
  438.5 1.9 copy-done
  440.4 60.4 %expert_layer.1 = (bf16[2560,768]{1,0:T(8,128)(2,1)}, bf16[2560,768]{1,0:T(8,128)(2,1)}, bf16[2560,128]{1,0:T(8,128)(2,1)}, bf16[768,3072]{1,0:T(8,128)(2,1)}, bf16[3072,768]{1,0:T(8,128)(2,1)}) custom-call(s32[17]{0:T(128)} %copy-done.6, s32[1]{0:T(128)} %bitcast.10.expert, bf16[2560,768]{1,0:T(8,128)(2,1)} %copy-done, bf16[2560,128]{1,0:T(8,128)(2,1)} %copy-done.4, ...), custom_call_target="tpu_custom_call" | custom-call | tf_op jit(solution)/shard_map/expert_layer/pallas_call | solution.py:549
  500.8 1.2 broadcast_in_dim.82.place_ref
  504.0 20.6 %unpack_tokens.1 = (bf16[8192,768]{1,0:T(8,128)(2,1)}, f32[8192,128]{1,0:T(8,128)S(1)}) custom-call(s32[17]{0:T(128)S(1)} %copy-done.7, s32[8192,128]{1,0:T(8,128)S(1)} %broadcast_in_dim.82.place_ref, bf16[2560,768]{1,0:T(8,128)(2,1)S(1)} %copy-done.3, bf16[2560,128]{1,0:T(8,128)(2,1)S(1)} %copy-done.5), custom_call_target="tpu_custom_call" | custom-call | tf_op jit(solution)/shard_map/unpack_tokens/pallas_call | solution.py:426
  524.6 2.0 copy-done.1
  542.7 2.4 dynamic-slice_dynamic-update-slice_fusion.7
  545.1 2.2 dynamic-slice_dynamic-update-slice_fusion.6
  547.3 2.2 dynamic-slice_dynamic-update-slice_fusion.5
  550.6 1.1 dynamic-slice_dynamic-update-slice_fusion.3
  551.7 1.1 dynamic-slice_dynamic-update-slice_fusion.2
  555.0 146.6 %reduce-scatter.8.cloned.1.call-done = bf16[1024,768]{1,0:T(8,128)(2,1)} async-done(((bf16[8192,768]{1,0:T(8,128)(2,1)}), bf16[1024,768]{1,0:T(8,128)(2,1)}) %reduce-scatter.8.cloned.1.call-update) | async-done | bytes 1572880 | tf_op jit(solution)/shard_map/reduce_scatter | solution.py:751
  702.4 4.1 slice_reduce_fusion
  706.5 3.3 all-to-all-start.2
  710.1 1.9 fusion.105
  712.0 3.5 all-to-all-done.2
  715.8 3.1 multiply_reduce_fusion.1
  720.2 2.6 convolution_convert_fusion.1.do_ref
  722.8 94.1 %attention_backward.2 = (bf16[1024,384]{1,0:T(8,128)(2,1)}, bf16[2560,768]{1,0:T(8,128)(2,1)}, f32[6,1,2816]{2,1,0:T(1,128)}) custom-call(s32[6]{0:T(128)} %pad_add_fusion.1.info, bf16[1024,2304]{1,0:T(8,128)(2,1)} %copy-done.17, bf16[1024,768]{1,0:T(8,128)(2,1)} %convolution_convert_fusion.1.do_ref, f32[1024,384]{1,0:T(8,128)} %get-tuple-element.59.o_ref, ...), custom_call_target="tpu_custom_call" | custom-call | flops 20132659200 | bytes 10485760 | tf_op jit(solution)/shard_map/attention_backward/pallas_call | solution.py:303
  817.0 3.7 slice.110
  820.7 4.8 all-to-all-start.1
  825.6 94.2 %attention_backward.3 = (bf16[1024,384]{1,0:T(8,128)(2,1)}, bf16[2560,768]{1,0:T(8,128)(2,1)}, f32[6,1,2816]{2,1,0:T(1,128)}) custom-call(s32[6]{0:T(128)} %pad_add_fusion.1.info, bf16[1024,2304]{1,0:T(8,128)(2,1)} %copy-done.17, bf16[1024,768]{1,0:T(8,128)(2,1)} %convolution_convert_fusion.1.do_ref, f32[1024,384]{1,0:T(8,128)} %get-tuple-element.61.o_ref, ...), custom_call_target="tpu_custom_call" | custom-call | flops 20132659200 | bytes 10485760 | tf_op jit(solution)/shard_map/attention_backward/pallas_call | solution.py:303
  919.8 3.8 slice.112
  923.8 2.1 slice.111
  925.9 5.2 fusion.36
  931.1 2.1 slice.113
  933.2 31.2 %all-to-all-done.1 = bf16[8,512,768]{2,1,0:T(8,128)(2,1)} async-done(((bf16[8,512,768]{2,1,0:T(8,128)(2,1)}), bf16[8,512,768]{2,1,0:T(8,128)(2,1)}, u32[]{:S(2)}, u32[]{:S(2)}) %all-to-all-start.1) | async-done | bytes 6291488 | tf_op jit(solution)/shard_map/all_to_all | solution.py:757
  964.4 43.6 %reduce-scatter.16.cloned.1.call-done = bf16[512,768]{1,0:T(8,128)(2,1)} async-done(((bf16[2048,768]{1,0:T(8,128)(2,1)}), bf16[512,768]{1,0:T(8,128)(2,1)}) %reduce-scatter.16.cloned.1.call-update) | async-done | bytes 786448 | tf_op jit(solution)/shard_map/reduce_scatter | solution.py:866
  1008.0 9.7 fusion.39
  1017.7 8.8 pad_maximum_fusion
  1026.6 1.8 fusion.111
  1028.4 3.0 convert_element_type.332
  1031.4 1.6 convert_element_type.333
  1033.4 1.2 broadcast_in_dim.143.place_ref
  1034.7 11.6 collect_rows.1
  1046.3 1.4 add_convert_fusion
  1049.9 5.7 fusion.8
  1055.6 41.4 %all-reduce.3 = (f32[768]{0:T(1024)}, f32[31,12]{0,1:T(8,128)}, f32[768]{0:T(1024)}, f32[768,8]{0,1:T(8,128)S(1)}) all-reduce(f32[768]{0:T(1024)S(1)} %get-tuple-element.98, f32[31,12]{0,1:T(8,128)S(1)} %fusion.43, f32[768]{0:T(1024)S(1)} %get-tuple-element.96, ...), channel_id=1, replica_groups=mesh['dp'=4,'expert'=8] {'dp','expert'}, use_global_device_ids=true, to_apply=%region_30.31 | all-reduce | flops 8052 | bytes 64416 | tf_op jit(solution)/shard_map/psum | solution.py:887
  1097.7 4.9 fusion.10
  1102.6 60.0 %reduce-scatter.18.cloned.1.call-done = f32[24,3072]{1,0:T(8,128)} async-done(((f32[768,3072]{1,0:T(8,128)}), f32[24,3072]{1,0:T(8,128)}) %reduce-scatter.18.cloned.1.call-update) | async-done | bytes 294928 | tf_op jit(solution)/shard_map/reduce_scatter | solution.py:883
  1163.7 1.6 fusion.109
  (172 shorter events, 28.4 us)
Async XLA Ops:
  7.2 28.7 %copy-start.14 = (bf16[1024,768]{1,0:T(8,128)(2,1)S(1)}, bf16[1024,768]{1,0:T(8,128)(2,1)}, u32[]{:S(2)}) copy-start(bf16[1024,768]{1,0:T(8,128)(2,1)} %param.13) | copy-start | bytes 4718596
  7.2 29.1 %copy-start.30 = (f32[31,12]{0,1:T(8,128)S(1)}, f32[31,12]{0,1:T(8,128)}, u32[]{:S(2)}) copy-start(f32[31,12]{0,1:T(8,128)} %param.19) | copy-start | bytes 4468
  7.2 71.5 %all-gather.7.cloned.1.call-start = ((), (), s32[]{:S(2)}) async-start(), calls=%async_computation.9 | async-start | bytes 5068800 | tf_op jit(solution)/shard_map/all_gather | solution.py:808
  30.4 15.2 %all-to-all-start = ((s32[8,1,1024]{2,1,0:T(1,128)}), s32[8,1,1024]{2,1,0:T(1,128)S(1)}, u32[]{:S(2)}, u32[]{:S(2)}) async-start(s32[8,1,1024]{2,1,0:T(1,128)} %copy.57), calls=%async_computation | async-start | bytes 65536 | tf_op jit(solution)/shard_map/all_to_all | solution.py:728
  35.0 96.7 %all-gather.11.cloned.1.call-start = ((), (), s32[]{:S(2)}) async-start(), calls=%async_computation.11 | async-start | bytes 3932160 | tf_op jit(solution)/shard_map/all_gather | solution.py:822
  36.3 0.6 copy-start.27
  40.0 38.7 %copy-start.31 = (f32[768]{0:T(1024)S(1)}, f32[768]{0:T(1024)}, u32[]{:S(2)}) copy-start(f32[768]{0:T(1024)} %param.17) | copy-start | bytes 9220
  45.6 383.2 %copy-start.6 = (s32[17]{0:T(128)}, s32[17]{0:T(128)S(1)}, u32[]{:S(2)}) copy-start(s32[17]{0:T(128)S(1)} %pad_add_fusion.info) | copy-start | bytes 208
  85.2 2.2 copy-start.17
  88.8 43.3 %copy-start.29 = (s32[1,512]{1,0:T(1,128)S(1)}, s32[1,512]{1,0:T(1,128)}, u32[]{:S(2)}) copy-start(s32[1,512]{1,0:T(1,128)} %param.14) | copy-start | bytes 6148
  88.8 111.7 %all-gather.9.cloned.1.call-start = ((), (), s32[]{:S(2)}) async-start(), calls=%async_computation.10 | async-start | bytes 3932160 | tf_op jit(solution)/shard_map/all_gather | solution.py:822
  89.5 206.9 %all-gather.13.cloned.1.call-start = ((), (), s32[]{:S(2)}) async-start(), calls=%async_computation.12 | async-start | bytes 14155776 | tf_op jit(solution)/shard_map/all_gather | solution.py:825
  131.8 297.0 %all-gather.15.cloned.1.call-start = ((), (), s32[]{:S(2)}) async-start(), calls=%async_computation.13 | async-start | bytes 14155776 | tf_op jit(solution)/shard_map/all_gather | solution.py:741
  267.0 3.4 copy-start.15
  268.6 4.9 copy-start.21
  270.5 3.1 copy-start.22
  270.5 4.8 copy-start.26
  273.6 1.7 copy-start.8
  275.3 21.7 %slice-start.4 = ((bf16[768,3200]{1,0:T(8,128)(2,1)}), bf16[768,8]{1,0:T(8,128)(2,1)S(1)}, s32[]{:S(2)}) async-start(bf16[768,3200]{1,0:T(8,128)(2,1)} %all-gather.7.cloned.1.call-done), calls=%async_computation.24 | async-start | bytes 393216 | tf_op jit(solution)/shard_map/slice | solution.py:813
  296.5 405.1 %reduce-scatter.8.cloned.1.call-start = ((), (), s32[]{:S(2)}) async-start(), calls=%async_computation.14 | async-start | bytes 14155776 | tf_op jit(solution)/shard_map/reduce_scatter | solution.py:751
  308.2 1.9 copy-start.2
  310.1 0.9 copy-start.4
  438.5 1.9 copy-start
  500.8 2.1 copy-start.3
  500.8 2.1 copy-start.7
  502.9 1.1 copy-start.5
  524.6 2.0 copy-start.1
  526.6 298.9 %reduce-scatter.10.cloned.1.call-start = ((), (), s32[]{:S(2)}) async-start(), calls=%async_computation.15 | async-start | bytes 5898240 | tf_op jit(solution)/shard_map/reduce_scatter | solution.py:759
  542.7 6.8 copy-start.12
  701.6 124.0 %reduce-scatter.12.cloned.1.call-start = ((), (), s32[]{:S(2)}) async-start(), calls=%async_computation.16 | async-start | bytes 5898240 | tf_op jit(solution)/shard_map/reduce_scatter | solution.py:760
  702.4 13.2 %copy-start.23 = (s32[1024,2]{0,1:T(2,128)S(1)}, s32[1024,2]{0,1:T(2,128)}, u32[]{:S(2)}) copy-start(s32[1024,2]{0,1:T(2,128)} %param.15) | copy-start | bytes 24580
  702.4 13.4 %copy-start.9 = (f32[1024,768]{1,0:T(8,128)S(1)}, f32[1024,768]{1,0:T(8,128)}, u32[]{:S(2)}) copy-start(f32[1024,768]{1,0:T(8,128)} %copy-done.8) | copy-start | bytes 9437188
  706.5 9.0 all-to-all-start.2
  709.8 254.6 %reduce-scatter.14.cloned.1.call-start = ((), (), s32[]{:S(2)}) async-start(), calls=%async_computation.17 | async-start | bytes 3932160 | tf_op jit(solution)/shard_map/reduce_scatter | solution.py:866
  715.7 3.2 copy-start.13
  715.7 4.0 slice-start
  718.9 1.3 slice-start.1
  720.2 2.7 copy-start.10
  820.7 143.7 %all-to-all-start.1 = ((bf16[8,512,768]{2,1,0:T(8,128)(2,1)}), bf16[8,512,768]{2,1,0:T(8,128)(2,1)}, u32[]{:S(2)}, u32[]{:S(2)}) async-start(bf16[8,512,768]{2,1,0:T(8,128)(2,1)} %bitcast.23), calls=%async_computation.2 | async-start | bytes 12582912 | tf_op jit(solution)/shard_map/all_to_all | solution.py:757
  825.5 182.5 %reduce-scatter.16.cloned.1.call-start = ((), (), s32[]{:S(2)}) async-start(), calls=%async_computation.18 | async-start | bytes 3932160 | tf_op jit(solution)/shard_map/reduce_scatter | solution.py:866
  923.6 239.0 %reduce-scatter.18.cloned.1.call-start = ((), (), s32[]{:S(2)}) async-start(), calls=%async_computation.19 | async-start | bytes 9732096 | tf_op jit(solution)/shard_map/reduce_scatter | solution.py:883
  1026.5 4.8 copy-start.18
  1028.4 4.6 copy-start.24
  1028.4 4.6 copy-start.25
  1031.4 16.4 %slice-start.2 = ((s8[4915200]{0:T(1024)(128)(4,1)}), s8[4194304]{0:T(1024)(128)(4,1)S(1)}, s32[]{:S(2)}) async-start(s8[4915200]{0:T(1024)(128)(4,1)} %bitcast.130), calls=%async_computation.22 | async-start | bytes 8388608
  1034.7 13.1 %slice-start.3 = ((s8[4915200]{0:T(1024)(128)(4,1)}), s8[720896]{0:T(1024)(128)(4,1)S(1)}, s32[]{:S(2)}) async-start(s8[4915200]{0:T(1024)(128)(4,1)} %bitcast.130), calls=%async_computation.23 | async-start | bytes 1441792
  1046.3 1.8 copy-start.16
  1046.3 2.3 copy-start.19
  1046.3 2.5 copy-start.20
  1046.3 2.8 copy-start.32
  1046.3 3.0 copy-start.33
  1046.3 3.3 copy-start.34
  1046.3 3.6 copy-start.35
  1049.9 47.8 %copy-start.28 = (f32[1024]{0:T(1024)S(1)}, f32[1024]{0:T(1024)}, u32[]{:S(2)}) copy-start(f32[1024]{0:T(1024)} %copy-done.27) | copy-start | bytes 12292
  1049.9 47.8 %copy-start.11 = (f32[1024,768]{1,0:T(8,128)S(1)}, f32[1024,768]{1,0:T(8,128)}, u32[]{:S(2)}) copy-start(f32[1024,768]{1,0:T(8,128)} %copy-done.10) | copy-start | bytes 9437188
Sparse Core Ops, SparseCore 0:
  11.6 67.1 all-gather.6
  88.9 42.7 all-gather.10
  134.2 43.9 all-gather.8
  179.7 116.7 all-gather.12
  298.5 130.1 all-gather.14
  526.8 174.7 reduce-scatter.7
  704.6 55.4 reduce-scatter.9
  763.0 57.0 reduce-scatter.11
  823.2 59.4 reduce-scatter.13
  923.7 84.3 reduce-scatter.15
  1026.7 135.8 reduce-scatter.17

commit v4 on v3

--- a/solution.py
+++ b/solution.py
@@ -64,7 +64,8 @@
     rows = jnp.sum(hot[None] * table, axis=-1)
     return jnp.where(distance[None] >= 0, rows, MASKED)
 
-def build_bias(info, base, row_start, t_scr, b_scr):
+def bias_kernel(info, base_ref, row_start, t_ref, b_ref):
+    base, t_scr, b_scr = base_ref[0], t_ref.at[0], b_ref.at[0]
     width = base.shape[-1]
     for a in range(16):
         t_scr[8 * a:8 * a + 8, :] = pltpu.roll(base, 8 * a, 1) if a else base
@@ -98,14 +99,31 @@
             b_scr[rows, PROMPT + 128 * b:PROMPT + 128 * b + 128] = jnp.where(
                 lane + 128 * b >= own, t_scr[:, first:first + 128], MASKED)
 
+def bias_tables(info, rows_bias, row_start, first, heads):
+    wide = rows_bias.shape[2]
+    block = lambda rows, cols: pl.BlockSpec((1, rows, cols), lambda h, *_: (h, 0, 0))
+    return pl.pallas_call(
+        bias_kernel,
+        grid_spec=pltpu.PrefetchScalarGridSpec(
+            num_scalar_prefetch=1, grid=(heads,),
+            in_specs=[pl.BlockSpec((1, 8, wide), lambda h, *_: (first + h, 0, 0)),
+                      pl.BlockSpec((KT, 128), lambda h, *_: (0, 0))],
+            out_specs=[block(128, wide), block(KT, PROMPT + KT)]),
+        out_shape=[jax.ShapeDtypeStruct((heads, 128, wide), F32),
+                   jax.ShapeDtypeStruct((heads, KT, PROMPT + KT), F32)],
+        compiler_params=pltpu.CompilerParams(vmem_limit_bytes=32 << 20),
+        cost_estimate=pl.CostEstimate(flops=0, bytes_accessed=heads * KT * (PROMPT + KT) * 8, transcendentals=0),
+        name="bias_tables",
+    )(info, rows_bias, row_start)
+
 def own_lanes(h, rows):
     lane = lax.broadcasted_iota(jnp.int32, (rows, 128), 1)
     return lane // 64 == h % 2
 
-def fwd_kernel(scale2, info, q_ref, k_ref, v_ref, r_ref, st_ref, o_ref, lse_ref, t_scr, b_scr):
+def fwd_kernel(scale2, info, q_ref, k_ref, v_ref, t_ref, b_ref, o_ref, lse_ref):
     h = pl.program_id(0)
     dp = info[5]
-    build_bias(info, r_ref[0], st_ref, t_scr, b_scr)
+    t_scr, b_scr = t_ref.at[0], b_ref.at[0]
     own = own_lanes(h, QT)
     head_lane = lax.broadcasted_iota(jnp.int32, (QT, 128), 1) == h
 
@@ -118,7 +136,7 @@
             s = dot(q, k_ref[cols, :], NT) * scale2 + bias_of(t)
             new = jnp.maximum(m, jnp.max(s, axis=1, keepdims=True))
             keep = jnp.exp2(m - new)
-            p = jnp.exp2(s - new[:, :1])
+            p = jnp.exp2(s - jnp.concatenate([new] * (KT // 128), axis=1))
             part = p[:, :128]
             for c in range(1, KT // 128):
                 part = part + p[:, 128 * c:128 * (c + 1)]
@@ -139,7 +157,7 @@
         tile(KT + QT * j, PROMPT // KT + 1,
              lambda t: b_scr[pl.ds(QT * j, QT), pl.ds(pl.multiple_of(t * KT, KT), KT)], lambda t: t)
 
-def attention_forward(info, projected, keys_values, rows_bias, row_start, part):
+def attention_forward(info, projected, keys_values, tables, part):
     n = projected.shape[0]
     keys, columns = keys_values.shape
     heads = columns // 128
@@ -153,16 +171,14 @@
             in_specs=[pl.BlockSpec((n, 128), lambda h, *_: (0, first + h // 2)),
                       pl.BlockSpec((keys, 128), lambda h, *_: (0, h // 2 * 2)),
                       pl.BlockSpec((keys, 128), lambda h, *_: (0, h // 2 * 2 + 1)),
-                      pl.BlockSpec((1, 8, rows_bias.shape[2]), lambda h, *_: (2 * first + h, 0, 0)),
-                      pl.BlockSpec((KT, 128), lambda h, *_: (0, 0))],
+                      *[pl.BlockSpec((1,) + t.shape[1:], lambda h, *_: (h, 0, 0)) for t in tables]],
             out_specs=[pl.BlockSpec((n, 128), lambda h, *_: (0, h // 2)),
-                       pl.BlockSpec((n, 128), lambda h, *_: (0, 0))],
-            scratch_shapes=[pltpu.VMEM((128, rows_bias.shape[2]), F32), pltpu.VMEM((KT, PROMPT + KT), F32)]),
+                       pl.BlockSpec((n, 128), lambda h, *_: (0, 0))]),
         out_shape=[jax.ShapeDtypeStruct((n, heads * 64), F32), jax.ShapeDtypeStruct((n, 128), F32)],
         compiler_params=pltpu.CompilerParams(vmem_limit_bytes=60 << 20),
         cost_estimate=pl.CostEstimate(flops=heads * n * keys * 128 * 4, bytes_accessed=n * keys * 4, transcendentals=heads * n * keys),
         name="attention_forward",
-    )(info, projected, keys_values, keys_values, rows_bias, row_start)
+    )(info, projected, keys_values, keys_values, *tables)
 
 def split3(x):
     hi = x.astype(BF16)
@@ -170,14 +186,14 @@
     mid = rest.astype(BF16)
     return hi, mid, (rest - mid.astype(F32)).astype(BF16)
 
-def bwd_kernel(scale, info, q_ref, do_ref, o_ref, lse_ref, k_ref, v_ref, r_ref, st_ref,
+def bwd_kernel(scale, info, q_ref, do_ref, o_ref, lse_ref, k_ref, v_ref, t_ref, b_ref,
                dq_ref, dkv_ref, dd_ref,
-               t_scr, b_scr, e_scr, db_scr, qa, da, ka, va, qt, dot_t, dkt, dvt):
+               e_scr, db_scr, qa, da, ka, va, qt, dot_t, dkt, dvt):
     h = pl.program_id(0)
     dp = info[5]
     n, keys = q_ref.shape[0], k_ref.shape[0]
     half = h % 2
-    build_bias(info, r_ref[0], st_ref, t_scr, b_scr)
+    t_scr, b_scr = t_ref.at[0], b_ref.at[0]
     base = pl.multiple_of(64 * half, 64)
     other = 64 - 64 * half
 
@@ -277,7 +293,7 @@
     for i in range(KT // 128):
         first = PROMPT + RUN - 128 * i
         e_scr[:, first:first + KT] += db_scr[128 * i:128 * i + 128, PROMPT:]
-    width = r_ref.shape[2]
+    width = t_ref.shape[2]
     acc = e_scr[0:8, :]
     for a in range(1, 16):
         acc = acc + pltpu.roll(e_scr[8 * a:8 * a + 8, :], width - 8 * a, 1)
@@ -291,11 +307,11 @@
         dkv_ref[:, :128] = (dkt[...] * scale).T.astype(BF16)
         dkv_ref[:, 128:] = dvt[...].T.astype(BF16)
 
-def attention_backward(info, projected, do, o32, lse, keys_values, rows_bias, row_start, part):
+def attention_backward(info, projected, do, o32, lse, keys_values, tables, part):
     n = projected.shape[0]
     keys, columns = keys_values.shape
     heads = columns // 128
-    wide = rows_bias.shape[2]
+    wide = tables[0].shape[2]
     first = part * heads // 2
     own = pl.BlockSpec((n, 128), lambda h, *_: (0, h // 2))
     shifted = pl.BlockSpec((n, 128), lambda h, *_: (0, first + h // 2))
@@ -307,12 +323,10 @@
             in_specs=[shifted, shifted, own, pl.BlockSpec((n, 128), lambda h, *_: (0, 0)),
                       pl.BlockSpec((keys, 128), lambda h, *_: (0, h // 2 * 2)),
                       pl.BlockSpec((keys, 128), lambda h, *_: (0, h // 2 * 2 + 1)),
-                      pl.BlockSpec((1, 8, wide), lambda h, *_: (2 * first + h, 0, 0)),
-                      pl.BlockSpec((KT, 128), lambda h, *_: (0, 0))],
+                      *[pl.BlockSpec((1,) + t.shape[1:], lambda h, *_: (h, 0, 0)) for t in tables]],
             out_specs=[own, pl.BlockSpec((keys, 256), lambda h, *_: (0, h // 2)),
                        pl.BlockSpec((1, 1, wide), lambda h, *_: (h, 0, 0))],
             scratch_shapes=[pltpu.VMEM((128, wide), F32), pltpu.VMEM((KT, cols), F32),
-                            pltpu.VMEM((128, wide), F32), pltpu.VMEM((KT, cols), F32),
                             pltpu.VMEM((n, 128), BF16), pltpu.VMEM((n, 128), BF16),
                             pltpu.VMEM((keys, 128), BF16), pltpu.VMEM((keys, 128), BF16),
                             pltpu.VMEM((128, n), BF16), pltpu.VMEM((128, n), BF16),
@@ -322,7 +336,7 @@
         compiler_params=pltpu.CompilerParams(vmem_limit_bytes=60 << 20),
         cost_estimate=pl.CostEstimate(flops=heads * n * keys * 128 * 10, bytes_accessed=n * keys * 4, transcendentals=heads * n * keys),
         name="attention_backward",
-    )(info, projected, do, o32, lse, keys_values, keys_values, rows_bias, row_start)
+    )(info, projected, do, o32, lse, keys_values, keys_values, *tables)
 
 def info_of(ids, dp):
     starts = jnp.sum((ids[None, :] < jnp.arange(5)[:, None]).astype(jnp.int32), axis=1)
@@ -806,9 +820,12 @@
         [pairs_together(w_qkv), w_out, jnp.pad(w_router, ((0, 0), (0, 128 - experts_total)))], axis=1
     )
     dense = lax.all_gather(dense, ("dp", "expert"), axis=0, tiled=True)
+    part_heads = heads // PARTS
+    tables = [bias_tables(info, rows_bias, row_start, g * part_heads, part_heads) for g in range(PARTS)]
+    dense, tables[0] = lax.optimization_barrier((dense, tables[0]))
     if few_experts:
         plan = plan_tokens(codes, rows, expert_ids.shape[1])
-        dense, rows_bias, plan = lax.optimization_barrier((dense, rows_bias, plan))
+        dense, plan = lax.optimization_barrier((dense, plan))
     whole_qkv, whole_out = dense[:, : 3 * width], dense[:, 3 * width : 4 * width]
     whole_router = dense[:, 4 * width : 4 * width + experts_total]
     inputs = tokens_in.astype(jnp.float32)
@@ -823,13 +840,14 @@
     if few_experts:
         late_cotangent, gathered[0] = lax.optimization_barrier((cotangent, gathered[0]))
         all_cotangents = lax.all_gather(late_cotangent, "expert", axis=0, tiled=True)
+    gathered[0], tables = lax.optimization_barrier((gathered[0], tables))
     keys_values = []
     exact, log_total = [], []
     for g in range(parts):
         if g:
             gathered[g], exact[-1] = lax.optimization_barrier((gathered[g], exact[-1]))
         keys_values.append(jnp.concatenate([gathered[g], kept[g][prompt_rows:]], axis=0))
-        out, total = attention_forward(info, projected, keys_values[g], rows_bias, row_start, g)
+        out, total = attention_forward(info, projected, keys_values[g], tables[g], g)
         exact.append(out)
         log_total.append(total)
     attended = jnp.concatenate(exact, axis=1).astype(jnp.bfloat16)
@@ -860,7 +878,7 @@
                 (grad_attended, expert_parts, grad_queries[-1])
             )
         grad_query, grad_kv, lines = attention_backward(
-            info, projected, grad_attended, exact[g], log_total[g], keys_values[g], rows_bias, row_start, g
+            info, projected, grad_attended, exact[g], log_total[g], keys_values[g], tables[g], g
         )
         grad_queries.append(grad_query)
         grad_prompts.append(lax.psum_scatter(grad_kv[:PROMPT], "dp", scatter_dimension=0, tiled=True))

time: 1180 us -> 1130 us (0.958)
  waiting for transfers between devices: 499 us -> 419 us
  Pallas kernels: 426 us -> 451 us
    reduce_scatter x1, waiting for transfers between devices: 147 us -> 97.5 us  [exchange_tokens(): lax.psum_scatter(grad_all, 'expert', scatter_dimension=0, tiled=True)]
    pallas_call x0 -> x2, Pallas kernels: none -> 46.6 us  [bias_tables(): pl.pallas_call(bias_kernel, grid_spec=pltpu.PrefetchScalarGridSpec(num_sc...]
    pallas_call x1, Pallas kernels: 60.4 us -> 99.3 us  [expert_layer(): pl.pallas_call(functools.partial(expert_kernel, sources), grid_spec=pltpu...]
    pallas_call x2, Pallas kernels: 188 us -> 151 us  [attention_backward(): pl.pallas_call(functools.partial(bwd_kernel, 64 ** (-0.5)), grid_spec=plt...]
    pallas_call x2, Pallas kernels: 125 us -> 88.6 us  [attention_forward(): pl.pallas_call(functools.partial(fwd_kernel, scale2), grid_spec=pltpu.Pre...]
    all_gather x1, waiting for transfers between devices: 33.1 us -> 6.52 us  [per_device(): dense = lax.all_gather(dense, ('dp', 'expert'), axis=0, tiled=True)]
    reduce_scatter x2, waiting for transfers between devices: 43.6 us -> 24.2 us  [per_device(): lax.psum_scatter(grad_kv[:PROMPT], 'dp', scatter_dimension=0, tiled=True)]
    all_gather x1, waiting for transfers between devices: 118 us -> 103 us  [exchange_tokens(): all_tokens = lax.all_gather(sent, 'expert', axis=0, tiled=True)]
  transfers between devices with their start and end apart: 14 -> 14, of which waited for: 9 -> 10; matrix products, arithmetic and copies ran while one was open for 8% -> 8% of each run, Pallas kernels for 29% -> 28%
where the time goes in v4:
time: 1130 us; the launch traced here: 1120 us
  Pallas kernels  451 us (40%)
  waiting for transfers between devices  419 us (37%)
  local copies, waits for them, and re-layouts  58.5 us (5%)
  blocking collectives  57 us (5%)
  other arithmetic  51.4 us (5%)
  matrix products  40.9 us (4%)
  between operations  30.7 us (3%)
  starting transfers between devices  14.2 us (1%)
    pallas_call x2, Pallas kernels, attention_backward(): pl.pallas_call(functools.partial(bwd_kernel, 64 ** (-0.5)), grid_spec=plt...  151 us
    all_gather x1, waiting for transfers between devices, exchange_tokens(): all_tokens = lax.all_gather(sent, 'expert', axis=0, tiled=True)  103 us
    pallas_call x1, Pallas kernels, expert_layer(): pl.pallas_call(functools.partial(expert_kernel, sources), grid_spec=pltpu...  99.3 us
    reduce_scatter x1, waiting for transfers between devices, exchange_tokens(): lax.psum_scatter(grad_all, 'expert', scatter_dimension=0, tiled=True)  97.5 us
    pallas_call x2, Pallas kernels, attention_forward(): pl.pallas_call(functools.partial(fwd_kernel, scale2), grid_spec=pltpu.Pre...  88.6 us
    reduce_scatter x1, waiting for transfers between devices, per_device(): lax.psum_scatter(jnp.concatenate([grad_qkv, grad_out_weight], axis=1), ('...  60 us
    pallas_call x2, Pallas kernels, bias_tables(): pl.pallas_call(bias_kernel, grid_spec=pltpu.PrefetchScalarGridSpec(num_sc...  46.6 us
    all_gather x2, waiting for transfers between devices, per_device(): lax.all_gather(kv[:prompt_rows], 'dp', axis=0, tiled=True)  41.9 us
  transfers between devices with their start and end apart: 14, of which 10 were waited for; matrix products, arithmetic and copies ran while one was open for 8% of the time, Pallas kernels for 28%

profile of v4, /device:TPU:0, one launch (start us, length us, event | category | flops | bytes accessed | tf_op | source)
XLA Modules:
  0.0 1122.8 jit_solution(7744510552526089217)
XLA Ops:
  9.9 1.4 fusion.50
  12.1 15.6 %all-gather = s32[8192,2]{0,1:T(2,128)S(1)} all-gather(s32[1024,2]{0,1:T(2,128)S(1)} %multiply_add_fusion), channel_id=2, replica_groups=mesh['dp'=4,'expert'=8] {'expert'}, dimensions={0}, use_global_device_ids=true | all-gather | bytes 73728 | tf_op jit(solution)/shard_map/all_gather | solution.py:735
  30.3 4.7 all-to-all-start
  36.6 3.1 multiply_reduce_fusion
  40.0 23.3 %bias_tables.2 = (f32[6,128,2816]{2,1,0:T(8,128)S(1)}, f32[6,512,2560]{2,1,0:T(8,128)}) custom-call(s32[6]{0:T(128)S(1)} %pad_add_fusion.info, f32[12,8,2816]{2,1,0:T(8,128)S(1)} %broadcast_select_fusion.base_ref, s32[512,128]{1,0:T(8,128)S(1)} %broadcast_in_dim.76.row_start), custom_call_target="tpu_custom_call" | custom-call | bytes 62914560 | tf_op jit(solution)/shard_map/bias_tables/pallas_call | solution.py:105
  63.3 3.3 copy-done.1
  67.0 3.7 fusion.2.refs_1_
  72.1 6.5 all-gather.7.cloned.1.call-done
  78.6 6.4 convolution_convert_fusion.q_ref
  85.1 1.8 fusion.108
  89.2 41.9 %all-gather.11.cloned.1.call-done = bf16[2048,768]{1,0:T(8,128)(2,1)} async-done(((bf16[512,768]{1,0:T(8,128)(2,1)}), bf16[2048,768]{1,0:T(8,128)(2,1)}) %all-gather.11.cloned.1.call-update) | async-done | bytes 3145744 | tf_op jit(solution)/shard_map/all_gather | solution.py:839
  131.3 23.4 %bias_tables.3 = (f32[6,128,2816]{2,1,0:T(8,128)S(1)}, f32[6,512,2560]{2,1,0:T(8,128)}) custom-call(s32[6]{0:T(128)S(1)} %pad_add_fusion.info, f32[12,8,2816]{2,1,0:T(8,128)S(1)} %broadcast_select_fusion.base_ref, s32[512,128]{1,0:T(8,128)S(1)} %broadcast_in_dim.76.row_start), custom_call_target="tpu_custom_call" | custom-call | bytes 62914560 | tf_op jit(solution)/shard_map/bias_tables/pallas_call | solution.py:105
  154.6 3.3 copy-done.2
  157.9 4.7 pad_maximum_fusion.1.k_ref.v_ref
  162.6 44.3 %attention_forward.2 = (f32[1024,384]{1,0:T(8,128)}, f32[1024,128]{1,0:T(8,128)}) custom-call(s32[6]{0:T(128)} %copy-done.10, bf16[1024,2304]{1,0:T(8,128)(2,1)} %copy-done.13, bf16[2560,768]{1,0:T(8,128)(2,1)} %pad_maximum_fusion.1.k_ref.v_ref, bf16[2560,768]{1,0:T(8,128)(2,1)} %pad_maximum_fusion.1.k_ref.v_ref, f32[6,128,2816]{2,1,0:T(8,128)} %copy-done.1, ...), custom_call_target="tpu_custom_call" | custom-call | flops 8053063680 | bytes 10485760 | tf_op jit(solution)/shard_map/attention_forward/pallas_call | solution.py:167
  206.9 4.1 pad_maximum_fusion.2.k_ref.v_ref
  211.0 44.3 %attention_forward.3 = (f32[1024,384]{1,0:T(8,128)}, f32[1024,128]{1,0:T(8,128)}) custom-call(s32[6]{0:T(128)} %copy-done.10, bf16[1024,2304]{1,0:T(8,128)(2,1)} %copy-done.13, bf16[2560,768]{1,0:T(8,128)(2,1)} %pad_maximum_fusion.2.k_ref.v_ref, bf16[2560,768]{1,0:T(8,128)(2,1)} %pad_maximum_fusion.2.k_ref.v_ref, f32[6,128,2816]{2,1,0:T(8,128)} %copy-done.2, ...), custom_call_target="tpu_custom_call" | custom-call | flops 8053063680 | bytes 10485760 | tf_op jit(solution)/shard_map/attention_forward/pallas_call | solution.py:167
  255.4 1.6 convert.7
  257.0 1.8 convert.6
  258.8 3.1 multiply_reduce_fusion.3
  262.0 1.6 copy-done.11
  263.6 1.5 multiply_convert_fusion
  265.1 30.8 %all-gather.13.cloned.1.call-done.refs_0_ = bf16[8192,768]{1,0:T(8,128)(2,1)} async-done(((bf16[1024,768]{1,0:T(8,128)(2,1)}), bf16[8192,768]{1,0:T(8,128)(2,1)}) %all-gather.13.cloned.1.call-update) | async-done | bytes 12582928 | tf_op jit(solution)/shard_map/all_gather | solution.py:842
  297.1 13.5 %pack_tokens.3 = (bf16[2560,768]{1,0:T(8,128)(2,1)S(1)}, bf16[2560,128]{1,0:T(8,128)(2,1)S(1)}) custom-call(s32[17]{0:T(128)S(1)} %pad_add_fusion.1.info, s32[8,1,1024]{2,1,0:T(1,128)S(1)} %broadcast_in_dim.80.place_ref, bf16[8192,768]{1,0:T(8,128)(2,1)} %all-gather.13.cloned.1.call-done.refs_0_, bf16[8192,128]{1,0:T(8,128)(2,1)S(1)} %fusion.2.refs_1_), custom_call_target="tpu_custom_call" | custom-call | tf_op jit(solution)/shard_map/pack_tokens/pallas_call | solution.py:407
  310.6 1.9 copy-done.4
  313.3 102.7 %all-gather.15.cloned.1.call-done.refs_0_ = bf16[8192,768]{1,0:T(8,128)(2,1)} async-done(((bf16[1024,768]{1,0:T(8,128)(2,1)}), bf16[8192,768]{1,0:T(8,128)(2,1)}) %all-gather.15.cloned.1.call-update) | async-done | bytes 12582928 | tf_op jit(solution)/shard_map/all_gather | solution.py:755
  416.1 11.9 %pack_tokens.2.x_ref = bf16[2560,768]{1,0:T(8,128)(2,1)S(1)} custom-call(s32[17]{0:T(128)S(1)} %pad_add_fusion.1.info, s32[8,1,1024]{2,1,0:T(1,128)S(1)} %broadcast_in_dim.80.place_ref, bf16[8192,768]{1,0:T(8,128)(2,1)} %all-gather.15.cloned.1.call-done.refs_0_), custom_call_target="tpu_custom_call" | custom-call | tf_op jit(solution)/shard_map/pack_tokens/pallas_call | solution.py:407
  428.0 1.8 copy-done
  429.8 99.3 %expert_layer.1 = (bf16[2560,768]{1,0:T(8,128)(2,1)}, bf16[2560,768]{1,0:T(8,128)(2,1)}, bf16[2560,128]{1,0:T(8,128)(2,1)}, bf16[768,3072]{1,0:T(8,128)(2,1)}, bf16[3072,768]{1,0:T(8,128)(2,1)}) custom-call(s32[17]{0:T(128)} %copy-done.8, s32[1]{0:T(128)} %bitcast.12.expert, bf16[2560,768]{1,0:T(8,128)(2,1)} %copy-done, bf16[2560,128]{1,0:T(8,128)(2,1)} %copy-done.6, ...), custom_call_target="tpu_custom_call" | custom-call | tf_op jit(solution)/shard_map/expert_layer/pallas_call | solution.py:563
  532.4 28.5 %unpack_tokens.1 = (bf16[8192,768]{1,0:T(8,128)(2,1)}, f32[8192,128]{1,0:T(8,128)S(1)}) custom-call(s32[17]{0:T(128)S(1)} %copy-done.9, s32[8192,128]{1,0:T(8,128)S(1)} %broadcast_in_dim.82.place_ref, bf16[2560,768]{1,0:T(8,128)(2,1)S(1)} %copy-done.5, bf16[2560,128]{1,0:T(8,128)(2,1)S(1)} %copy-done.7), custom_call_target="tpu_custom_call" | custom-call | tf_op jit(solution)/shard_map/unpack_tokens/pallas_call | solution.py:440
  560.9 2.0 copy-done.3
  579.4 2.4 dynamic-slice_dynamic-update-slice_fusion.7
  581.8 2.2 dynamic-slice_dynamic-update-slice_fusion.6
  584.0 2.2 dynamic-slice_dynamic-update-slice_fusion.5
  591.7 97.5 %reduce-scatter.8.cloned.1.call-done = bf16[1024,768]{1,0:T(8,128)(2,1)} async-done(((bf16[8192,768]{1,0:T(8,128)(2,1)}), bf16[1024,768]{1,0:T(8,128)(2,1)}) %reduce-scatter.8.cloned.1.call-update) | async-done | bytes 1572880 | tf_op jit(solution)/shard_map/reduce_scatter | solution.py:765
  690.0 4.1 slice_reduce_fusion
  694.1 3.3 all-to-all-start.2
  697.7 1.9 fusion.105
  699.6 3.5 all-to-all-done.2
  703.4 3.1 multiply_reduce_fusion.1
  707.8 2.6 convolution_convert_fusion.1.do_ref
  710.4 75.8 %attention_backward.2 = (bf16[1024,384]{1,0:T(8,128)(2,1)}, bf16[2560,768]{1,0:T(8,128)(2,1)}, f32[6,1,2816]{2,1,0:T(1,128)}) custom-call(s32[6]{0:T(128)} %copy-done.10, bf16[1024,2304]{1,0:T(8,128)(2,1)} %copy-done.13, bf16[1024,768]{1,0:T(8,128)(2,1)} %convolution_convert_fusion.1.do_ref, f32[1024,384]{1,0:T(8,128)} %get-tuple-element.79.o_ref, ...), custom_call_target="tpu_custom_call" | custom-call | flops 20132659200 | bytes 10485760 | tf_op jit(solution)/shard_map/attention_backward/pallas_call | solution.py:319
  786.2 3.8 slice.110
  790.0 4.8 all-to-all-start.1
  794.9 12.9 %reduce-scatter.12.cloned.1.call-done = bf16[1,768,768]{2,1,0:T(8,128)(2,1)} async-done(((bf16[1,3072,768]{2,1,0:T(8,128)(2,1)}), bf16[1,768,768]{2,1,0:T(8,128)(2,1)}) %reduce-scatter.12.cloned.1.call-update) | async-done | bytes 1179664 | tf_op jit(solution)/shard_map/reduce_scatter | solution.py:774
  807.8 75.6 %attention_backward.3 = (bf16[1024,384]{1,0:T(8,128)(2,1)}, bf16[2560,768]{1,0:T(8,128)(2,1)}, f32[6,1,2816]{2,1,0:T(1,128)}) custom-call(s32[6]{0:T(128)} %copy-done.10, bf16[1024,2304]{1,0:T(8,128)(2,1)} %copy-done.13, bf16[1024,768]{1,0:T(8,128)(2,1)} %convolution_convert_fusion.1.do_ref, f32[1024,384]{1,0:T(8,128)} %get-tuple-element.83.o_ref, ...), custom_call_target="tpu_custom_call" | custom-call | flops 20132659200 | bytes 10485760 | tf_op jit(solution)/shard_map/attention_backward/pallas_call | solution.py:319
  883.4 3.7 slice.112
  887.4 2.1 slice.111
  889.5 5.2 fusion.36
  894.8 2.1 slice.113
  896.9 36.9 %all-to-all-done.1 = bf16[8,512,768]{2,1,0:T(8,128)(2,1)} async-done(((bf16[8,512,768]{2,1,0:T(8,128)(2,1)}), bf16[8,512,768]{2,1,0:T(8,128)(2,1)}, u32[]{:S(2)}, u32[]{:S(2)}) %all-to-all-start.1) | async-done | bytes 6291488 | tf_op jit(solution)/shard_map/all_to_all | solution.py:771
  933.8 24.2 %reduce-scatter.16.cloned.1.call-done = bf16[512,768]{1,0:T(8,128)(2,1)} async-done(((bf16[2048,768]{1,0:T(8,128)(2,1)}), bf16[512,768]{1,0:T(8,128)(2,1)}) %reduce-scatter.16.cloned.1.call-update) | async-done | bytes 786448 | tf_op jit(solution)/shard_map/reduce_scatter | solution.py:884
  958.0 9.6 fusion.39
  967.6 8.8 pad_maximum_fusion
  976.5 1.8 fusion.111
  978.3 3.0 convert_element_type.332
  981.3 1.6 convert_element_type.333
  984.6 11.6 %collect_rows.1 = f32[1024,768]{1,0:T(8,128)S(1)} custom-call(s32[8192,128]{1,0:T(8,128)S(1)} %broadcast_in_dim.143.place_ref, bf16[4096,768]{1,0:T(8,128)(2,1)} %bitcast.24.x_ref), custom_call_target="tpu_custom_call" | custom-call | tf_op jit(solution)/shard_map/collect_rows/pallas_call | solution.py:474
  996.2 1.4 add_convert_fusion
  999.8 5.7 fusion.8
  1005.5 41.4 %all-reduce.3 = (f32[768]{0:T(1024)}, f32[31,12]{0,1:T(8,128)}, f32[768]{0:T(1024)}, f32[768,8]{0,1:T(8,128)S(1)}) all-reduce(f32[768]{0:T(1024)S(1)} %get-tuple-element.120, f32[31,12]{0,1:T(8,128)S(1)} %fusion.43, f32[768]{0:T(1024)S(1)} %get-tuple-element.118, ...), channel_id=1, replica_groups=mesh['dp'=4,'expert'=8] {'dp','expert'}, use_global_device_ids=true, to_apply=%region_30.31 | all-reduce | flops 8052 | bytes 64416 | tf_op jit(solution)/shard_map/psum | solution.py:905
  1047.6 4.9 fusion.10
  1052.5 60.0 %reduce-scatter.18.cloned.1.call-done = f32[24,3072]{1,0:T(8,128)} async-done(((f32[768,3072]{1,0:T(8,128)}), f32[24,3072]{1,0:T(8,128)}) %reduce-scatter.18.cloned.1.call-update) | async-done | bytes 294928 | tf_op jit(solution)/shard_map/reduce_scatter | solution.py:901
  1113.6 1.6 fusion.109
  (184 shorter events, 32.6 us)
Async XLA Ops:
  7.2 28.6 %copy-start.34 = (s32[1,512]{1,0:T(1,128)S(1)}, s32[1,512]{1,0:T(1,128)}, u32[]{:S(2)}) copy-start(s32[1,512]{1,0:T(1,128)} %param.14) | copy-start | bytes 6148
  7.2 29.1 %copy-start.35 = (f32[31,12]{0,1:T(8,128)S(1)}, f32[31,12]{0,1:T(8,128)}, u32[]{:S(2)}) copy-start(f32[31,12]{0,1:T(8,128)} %param.19) | copy-start | bytes 4468
  7.2 71.4 %all-gather.7.cloned.1.call-start = ((), (), s32[]{:S(2)}) async-start(), calls=%async_computation.9 | async-start | bytes 5068800 | tf_op jit(solution)/shard_map/all_gather | solution.py:822
  30.3 41.2 %all-to-all-start = ((s32[8,1,1024]{2,1,0:T(1,128)}), s32[8,1,1024]{2,1,0:T(1,128)S(1)}, u32[]{:S(2)}, u32[]{:S(2)}) async-start(s32[8,1,1024]{2,1,0:T(1,128)} %copy.57), calls=%async_computation | async-start | bytes 65536 | tf_op jit(solution)/shard_map/all_to_all | solution.py:742
  34.9 96.2 %all-gather.11.cloned.1.call-start = ((), (), s32[]{:S(2)}) async-start(), calls=%async_computation.11 | async-start | bytes 3932160 | tf_op jit(solution)/shard_map/all_gather | solution.py:839
  36.0 95.3 %copy-start.10 = (s32[6]{0:T(128)}, s32[6]{0:T(128)S(1)}, u32[]{:S(2)}) copy-start(s32[6]{0:T(128)S(1)} %pad_add_fusion.info) | copy-start | bytes 76
  36.6 30.0 %copy-start.18 = (bf16[1024,768]{1,0:T(8,128)(2,1)S(1)}, bf16[1024,768]{1,0:T(8,128)(2,1)}, u32[]{:S(2)}) copy-start(bf16[1024,768]{1,0:T(8,128)(2,1)} %param.13) | copy-start | bytes 4718596
  39.9 38.7 %copy-start.36 = (f32[768]{0:T(1024)S(1)}, f32[768]{0:T(1024)}, u32[]{:S(2)}) copy-start(f32[768]{0:T(1024)} %param.17) | copy-start | bytes 9220
  63.3 3.3 copy-start.1
  67.0 3.8 copy-start.32
  71.5 344.6 %copy-start.8 = (s32[17]{0:T(128)}, s32[17]{0:T(128)S(1)}, u32[]{:S(2)}) copy-start(s32[17]{0:T(128)S(1)} %pad_add_fusion.1.info) | copy-start | bytes 208
  85.0 3.2 copy-start.13
  88.2 118.7 %all-gather.9.cloned.1.call-start = ((), (), s32[]{:S(2)}) async-start(), calls=%async_computation.10 | async-start | bytes 3932160 | tf_op jit(solution)/shard_map/all_gather | solution.py:839
  89.0 206.9 %all-gather.13.cloned.1.call-start = ((), (), s32[]{:S(2)}) async-start(), calls=%async_computation.12 | async-start | bytes 14155776 | tf_op jit(solution)/shard_map/all_gather | solution.py:842
  131.2 284.9 %all-gather.15.cloned.1.call-start = ((), (), s32[]{:S(2)}) async-start(), calls=%async_computation.13 | async-start | bytes 14155776 | tf_op jit(solution)/shard_map/all_gather | solution.py:755
  154.6 3.3 copy-start.2
  162.6 44.3 %copy-start.21 = (bf16[512,768]{1,0:T(8,128)(2,1)S(1)}, bf16[512,768]{1,0:T(8,128)(2,1)}, u32[]{:S(2)}) copy-start(bf16[512,768]{1,0:T(8,128)(2,1)} %get-tuple-element.138) | copy-start | bytes 2359300
  255.4 3.4 copy-start.19
  257.0 4.9 copy-start.25
  258.8 3.1 copy-start.26
  258.8 4.8 copy-start.31
  261.9 1.7 copy-start.11
  263.6 32.8 %slice-start.4 = ((bf16[768,3200]{1,0:T(8,128)(2,1)}), bf16[768,8]{1,0:T(8,128)(2,1)S(1)}, s32[]{:S(2)}) async-start(bf16[768,3200]{1,0:T(8,128)(2,1)} %all-gather.7.cloned.1.call-done), calls=%async_computation.24 | async-start | bytes 393216 | tf_op jit(solution)/shard_map/slice | solution.py:830
  295.9 393.3 %reduce-scatter.8.cloned.1.call-start = ((), (), s32[]{:S(2)}) async-start(), calls=%async_computation.14 | async-start | bytes 14155776 | tf_op jit(solution)/shard_map/reduce_scatter | solution.py:765
  310.6 1.9 copy-start.4
  312.5 0.8 copy-start.6
  428.0 1.9 copy-start
  529.2 2.1 copy-start.5
  529.2 2.1 copy-start.9
  531.3 1.1 copy-start.7
  560.9 2.0 copy-start.3
  562.9 232.0 %reduce-scatter.10.cloned.1.call-start = ((), (), s32[]{:S(2)}) async-start(), calls=%async_computation.15 | async-start | bytes 5898240 | tf_op jit(solution)/shard_map/reduce_scatter | solution.py:773
  579.4 6.9 copy-start.16
  689.2 118.6 %reduce-scatter.12.cloned.1.call-start = ((), (), s32[]{:S(2)}) async-start(), calls=%async_computation.16 | async-start | bytes 5898240 | tf_op jit(solution)/shard_map/reduce_scatter | solution.py:774
  690.0 13.2 %copy-start.28 = (s32[1024,2]{0,1:T(2,128)S(1)}, s32[1024,2]{0,1:T(2,128)}, u32[]{:S(2)}) copy-start(s32[1024,2]{0,1:T(2,128)} %param.15) | copy-start | bytes 24580
  690.0 13.4 %copy-start.12 = (f32[1024,768]{1,0:T(8,128)S(1)}, f32[1024,768]{1,0:T(8,128)}, u32[]{:S(2)}) copy-start(f32[1024,768]{1,0:T(8,128)} %copy-done.11) | copy-start | bytes 9437188
  694.1 9.0 all-to-all-start.2
  697.5 236.3 %reduce-scatter.14.cloned.1.call-start = ((), (), s32[]{:S(2)}) async-start(), calls=%async_computation.17 | async-start | bytes 3932160 | tf_op jit(solution)/shard_map/reduce_scatter | solution.py:884
  703.3 3.2 copy-start.17
  703.4 4.0 slice-start
  706.5 1.3 slice-start.1
  707.8 2.6 copy-start.14
  790.0 143.7 %all-to-all-start.1 = ((bf16[8,512,768]{2,1,0:T(8,128)(2,1)}), bf16[8,512,768]{2,1,0:T(8,128)(2,1)}, u32[]{:S(2)}, u32[]{:S(2)}) async-start(bf16[8,512,768]{2,1,0:T(8,128)(2,1)} %bitcast.23), calls=%async_computation.2 | async-start | bytes 12582912 | tf_op jit(solution)/shard_map/all_to_all | solution.py:771
  794.8 163.2 %reduce-scatter.16.cloned.1.call-start = ((), (), s32[]{:S(2)}) async-start(), calls=%async_computation.18 | async-start | bytes 3932160 | tf_op jit(solution)/shard_map/reduce_scatter | solution.py:884
  887.2 225.3 %reduce-scatter.18.cloned.1.call-start = ((), (), s32[]{:S(2)}) async-start(), calls=%async_computation.19 | async-start | bytes 9732096 | tf_op jit(solution)/shard_map/reduce_scatter | solution.py:901
  976.4 4.8 copy-start.22
  978.3 4.6 copy-start.29
  978.3 4.6 copy-start.30
  978.3 5.0 copy-start.27
  981.3 16.4 %slice-start.2 = ((s8[4915200]{0:T(1024)(128)(4,1)}), s8[4194304]{0:T(1024)(128)(4,1)S(1)}, s32[]{:S(2)}) async-start(s8[4915200]{0:T(1024)(128)(4,1)} %bitcast.130), calls=%async_computation.22 | async-start | bytes 8388608
  984.6 13.1 %slice-start.3 = ((s8[4915200]{0:T(1024)(128)(4,1)}), s8[720896]{0:T(1024)(128)(4,1)S(1)}, s32[]{:S(2)}) async-start(s8[4915200]{0:T(1024)(128)(4,1)} %bitcast.130), calls=%async_computation.23 | async-start | bytes 1441792
  996.2 1.8 copy-start.20
  996.2 2.3 copy-start.23
  996.2 2.5 copy-start.24
  996.2 2.8 copy-start.37
  996.2 3.0 copy-start.38
  996.2 3.3 copy-start.39
  996.2 3.6 copy-start.40
  999.8 47.8 %copy-start.33 = (f32[1024]{0:T(1024)S(1)}, f32[1024]{0:T(1024)}, u32[]{:S(2)}) copy-start(f32[1024]{0:T(1024)} %copy-done.32) | copy-start | bytes 12292
  999.8 47.8 %copy-start.15 = (f32[1024,768]{1,0:T(8,128)S(1)}, f32[1024,768]{1,0:T(8,128)}, u32[]{:S(2)}) copy-start(f32[1024,768]{1,0:T(8,128)} %copy-done.14) | copy-start | bytes 9437188
Sparse Core Ops, SparseCore 0:
  11.5 67.1 all-gather.6
  88.4 42.7 all-gather.10
  133.6 43.9 all-gather.8
  179.1 116.7 all-gather.12
  297.9 118.1 all-gather.14
  563.0 126.1 reduce-scatter.7
  692.2 55.4 reduce-scatter.9
  750.7 57.0 reduce-scatter.11
  810.8 43.9 reduce-scatter.13
  887.3 70.6 reduce-scatter.15
  976.5 135.8 reduce-scatter.17

commit v5 on v4

--- a/solution.py
+++ b/solution.py
@@ -417,28 +417,22 @@
     )(info, place[:, None, :], *arrays)
 
 
-def unpack_kernel(sources, info, place_ref, *refs):
+def unpack_kernel(send, info, place_ref, *refs):
     ins, outs = refs[:len(refs) // 2], refs[len(refs) // 2:]
-    d = pl.program_id(0)
     tokens = place_ref.shape[0]
     lane = lax.broadcasted_iota(jnp.int32, (tokens, 128), 1)
+    put = jnp.concatenate(
+        [jnp.where(place_ref[...] == lane + 128 * b, 1.0, 0.0).astype(BF16) for b in range(send // 128)], axis=1)
+    at = pl.ds(pl.multiple_of(info[pl.program_id(0)], 16), send)
     for x, out in zip(ins, outs):
-        def chunk(j, total):
-            put = jnp.concatenate(
-                [jnp.where(place_ref[...] == lane + (MOE_ROWS * j + 128 * b), 1.0, 0.0).astype(BF16)
-                 for b in range(MOE_ROWS // 128)], axis=1)
-            at = pl.ds(pl.multiple_of(info[d] + MOE_ROWS * j, 16), MOE_ROWS)
-            return total + dot(put, x[at, :])
-        total = lax.fori_loop(0, (info[sources + d] + MOE_ROWS - 1) // MOE_ROWS, chunk,
-                              jnp.zeros((tokens, x.shape[1]), F32))
-        out[...] = total.astype(out.dtype)
-
-
-def unpack(info, place, arrays, dtypes):
+        out[...] = dot(put, x[at, :]).astype(out.dtype)
+
+
+def unpack(info, place, arrays, dtypes, send):
     sources, tokens = place.shape
     spread = jnp.broadcast_to(place.reshape(-1, 1), (sources * tokens, 128))
     return pl.pallas_call(
-        functools.partial(unpack_kernel, sources),
+        functools.partial(unpack_kernel, send),
         grid_spec=pltpu.PrefetchScalarGridSpec(
             num_scalar_prefetch=1, grid=(sources,),
             in_specs=[pl.BlockSpec((tokens, 128), lambda d, *_: (d, 0))]
@@ -579,6 +573,137 @@
         compiler_params=pltpu.CompilerParams(vmem_limit_bytes=63 << 20),
         name="expert_layer",
     )(info, expert, x, other, cot, router, w_in, w_down)
+
+
+MESH_ID = pl.DeviceIdType.MESH
+
+
+def dense_kernel(q_ref, w_ref, s_ref, out_ref, small_ref, give, h, r0, ra1, rb1, ra2, rb2, rz, s_acc, s_got, s_all,
+                 send, recv, s_send, s_recv):
+    i, j = lax.axis_index("dp"), lax.axis_index("expert")
+    y, x, z, c = i // 2, i % 2, j // 2, j % 2
+    other_core = (i, z * 2 + 1 - c)
+    other_x = (y * 2 + 1 - x, j)
+    other_y = ((1 - y) * 2 + x, j)
+    peers = [(i, (z + d) % 4 * 2 + c) for d in (1, 2, 3)]
+    barrier = pltpu.get_barrier_semaphore()
+    for device in [other_core, other_x, other_y] + peers:
+        pl.semaphore_signal(barrier, inc=1, device_id=device, device_id_type=MESH_ID)
+    pl.semaphore_wait(barrier, 6)
+
+    def copy(n, src, dst, device):
+        return pltpu.make_async_remote_copy(src_ref=src, dst_ref=dst, send_sem=send.at[n], recv_sem=recv.at[n],
+                                            device_id=device, device_id_type=MESH_ID)
+
+    def small_copy(n, src, dst, device):
+        return pltpu.make_async_remote_copy(src_ref=src, dst_ref=dst, send_sem=s_send.at[n], recv_sem=s_recv.at[n],
+                                            device_id=device, device_id_type=MESH_ID)
+
+    def block(b, core):
+        rows = jnp.concatenate([q_ref[b, core], w_ref[b, core]], axis=1)
+        half = rows.shape[1] // 2
+        return jnp.concatenate([rows[:, :half], rows[:, half:]], axis=0)
+
+    small = small_copy(0, s_ref, s_got.at[0], other_core)
+    small.start()
+    copies = []
+    for g in range(4):
+        def convert(b, _):
+            give[b] = block(b, 1 - c).astype(BF16)
+            return 0
+        lax.fori_loop(4 * g, 4 * g + 4, convert, 0)
+        copies.append(copy(g, give.at[pl.ds(4 * g, 4)], r0.at[pl.ds(4 * g, 4)], other_core))
+        copies[-1].start()
+    small.wait()
+    s_acc[0] = s_ref[...] + s_got[0]
+    small = small_copy(1, s_acc.at[0], s_got.at[1], other_x)
+    small.start()
+    for g in range(4):
+        copies[g].wait()
+        def add(b, _):
+            h[b // 8, b // 4 % 2, b % 4] = (block(b, c) + r0[b].astype(F32)).astype(BF16)
+            return 0
+        lax.fori_loop(4 * g, 4 * g + 4, add, 0)
+
+    half = h.shape[4] // 2
+    left, right = pl.ds(0, half), pl.ds(half, half)
+    ca = copy(4, h.at[:, 1 - x, :, :, left], ra1, other_x)
+    cb = copy(5, h.at[1 - y, :, :, :, right], rb1, other_y)
+    ca.start()
+    cb.start()
+    small.wait()
+    s_acc[1] = s_acc[0] + s_got[1]
+    small = small_copy(2, s_acc.at[1], s_got.at[2], other_y)
+    small.start()
+    ca.wait()
+
+    def add_x(b, _):
+        u, v = b // 4, b % 4
+        h[u, x, v, :, left] = (h[u, x, v, :, left].astype(F32) + ra1[u, v].astype(F32)).astype(BF16)
+        return 0
+    lax.fori_loop(0, 8, add_x, 0)
+    ca = copy(6, h.at[1 - y, x, :, :, left], ra2, other_y)
+    ca.start()
+    cb.wait()
+
+    def add_y(b, _):
+        u, v = b // 4, b % 4
+        h[y, u, v, :, right] = (h[y, u, v, :, right].astype(F32) + rb1[u, v].astype(F32)).astype(BF16)
+        return 0
+    lax.fori_loop(0, 8, add_y, 0)
+    cb = copy(7, h.at[y, 1 - x, :, :, right], rb2, other_x)
+    cb.start()
+    small.wait()
+    s_acc[2] = s_acc[1] + s_got[2]
+    smalls = [small_copy(3 + n, s_acc.at[2], s_all.at[z], device) for n, device in enumerate(peers)]
+    for one in smalls:
+        one.start()
+    ca.wait()
+    cb.wait()
+
+    def add_both(v, _):
+        h[y, x, v, :, left] = (h[y, x, v, :, left].astype(F32) + ra2[v].astype(F32)).astype(BF16)
+        h[y, x, v, :, right] = (h[y, x, v, :, right].astype(F32) + rb2[v].astype(F32)).astype(BF16)
+        return 0
+    lax.fori_loop(0, 4, add_both, 0)
+    copies = [copy(8 + n, h.at[y, x, (z + 1 + n) % 4], rz.at[n], device) for n, device in enumerate(peers)]
+    for one in copies:
+        one.start()
+    total = h[y, x, z].astype(F32)
+    for one in smalls:
+        one.wait()
+    s_all[z] = s_acc[2]
+    small_ref[...] = (s_all[0] + s_all[1]) + (s_all[2] + s_all[3])
+    for n, one in enumerate(copies):
+        one.wait()
+        total = total + rz[n].astype(F32)
+    rows = total.shape[0] // 2
+    out_ref[:, :2 * half] = total[:rows]
+    out_ref[:, 2 * half:] = total[rows:]
+
+
+def dense_sum(grad_qkv, grad_out, small):
+    rows, wide = grad_qkv.shape
+    narrow = grad_out.shape[1]
+    own = rows // 32
+    width = wide + narrow
+    half = width // 2
+    pair = own * 2
+    vmem = pl.BlockSpec(memory_space=pltpu.VMEM)
+    return pl.pallas_call(
+        dense_kernel,
+        in_specs=[vmem] * 3, out_specs=[vmem] * 2,
+        out_shape=[jax.ShapeDtypeStruct((own, width), F32), jax.ShapeDtypeStruct(small.shape, F32)],
+        scratch_shapes=[
+            pltpu.VMEM((16, pair, half), BF16), pltpu.VMEM((2, 2, 4, pair, half), BF16), pltpu.VMEM((16, pair, half), BF16),
+            pltpu.VMEM((2, 4, pair, half // 2), BF16), pltpu.VMEM((2, 4, pair, half // 2), BF16),
+            pltpu.VMEM((4, pair, half // 2), BF16), pltpu.VMEM((4, pair, half // 2), BF16), pltpu.VMEM((3, pair, half), BF16),
+            pltpu.VMEM((3,) + small.shape, F32), pltpu.VMEM((3,) + small.shape, F32), pltpu.VMEM((4,) + small.shape, F32),
+            pltpu.SemaphoreType.DMA((11,)), pltpu.SemaphoreType.DMA((11,)),
+            pltpu.SemaphoreType.DMA((6,)), pltpu.SemaphoreType.DMA((6,))],
+        compiler_params=pltpu.CompilerParams(collective_id=0, has_side_effects=True, vmem_limit_bytes=48 << 20),
+        name="dense_sum",
+    )(grad_qkv.reshape(16, 2, own, wide), grad_out.reshape(16, 2, own, narrow), small)
 
 
 def exchange_pairs(normed_ffn, middle, cotangent, expert_ids, priority, router, w_in, w_down):
@@ -750,7 +875,8 @@
     expert = lax.axis_index("expert").astype(jnp.int32)
     place, info, other_hot, own_place = plan
     sources = place.shape[0]
-    room = (rows * top + 16 * sources + 2 * MOE_ROWS - 1) // MOE_ROWS * MOE_ROWS
+    send = 2 * rows * top // experts_total
+    room = (rows * top + 16 * sources + send + MOE_ROWS - 1) // MOE_ROWS * MOE_ROWS
     sent, all_cotangents = lax.optimization_barrier((normed_ffn, all_cotangents))
     all_tokens = lax.all_gather(sent, "expert", axis=0, tiled=True)
     packed_cot, packed_other = pack(info, place, [all_cotangents, other_hot], room)
@@ -759,11 +885,10 @@
     grad_rows, mixed_rows, grad_gate, grad_w_in, grad_w_down = expert_layer(
         info, expert[None], packed, packed_other, packed_cot, wide_router, w_in[0], w_down[0], sources
     )
-    grad_all, gate_all = unpack(info, place, [grad_rows, grad_gate], [jnp.bfloat16, jnp.float32])
+    grad_all, gate_all = unpack(info, place, [grad_rows, grad_gate], [jnp.bfloat16, jnp.float32], send)
     gate_all = jnp.sum(gate_all[:, :3], axis=1).reshape(sources, rows)
     gate_own = lax.all_to_all(gate_all, "expert", split_axis=0, concat_axis=0, tiled=True)
     grad_own = lax.psum_scatter(grad_all, "expert", scatter_dimension=0, tiled=True)
-    send = 2 * rows * top // experts_total
     windows = jnp.concatenate([lax.dynamic_slice_in_dim(mixed_rows, info[d], send, 0) for d in range(sources)], axis=0)
     windows, grad_w_in, grad_w_down, grad_own = lax.optimization_barrier(
         (windows, grad_w_in, grad_w_down, grad_own)
@@ -838,7 +963,7 @@
     kept = [projected[:, width + columns * g : width + columns * (g + 1)] for g in range(parts)]
     gathered = [lax.all_gather(kv[:prompt_rows], "dp", axis=0, tiled=True) for kv in kept]
     if few_experts:
-        late_cotangent, gathered[0] = lax.optimization_barrier((cotangent, gathered[0]))
+        late_cotangent, gathered[0], tables = lax.optimization_barrier((cotangent, gathered[0], tables))
         all_cotangents = lax.all_gather(late_cotangent, "expert", axis=0, tiled=True)
     gathered[0], tables = lax.optimization_barrier((gathered[0], tables))
     keys_values = []
@@ -898,11 +1023,28 @@
     _, attn_norm_back = jax.vjp(normed, inputs, gain_attn)
     grad_inputs_part, grad_gain_attn = attn_norm_back(grad_normed_attn)
     grad_tokens = grad_middle + grad_inputs_part
-    dense_grad = lax.psum_scatter(
-        jnp.concatenate([grad_qkv, grad_out_weight], axis=1), ("dp", "expert"), scatter_dimension=0, tiled=True
-    )
-    own_router = lax.psum_scatter(grad_router, ("dp", "expert"), scatter_dimension=0, tiled=True)
-    small_parts = lax.psum((grad_gain_attn, grad_gain_ffn, grad_table.T), ("dp", "expert"))
+    if (dp_count, lax.axis_size("expert")) == (4, 8):
+        pieces = [grad_gain_attn, grad_gain_ffn, grad_table.reshape(-1), grad_router.reshape(-1)]
+        sizes = [piece.shape[0] for piece in pieces]
+        small = jnp.concatenate(pieces)
+        small = jnp.pad(small, (0, -small.shape[0] % 1024)).reshape(-1, 128)
+        dense_grad, small = dense_sum(grad_qkv, grad_out_weight, small)
+        ends = [sum(sizes[: n + 1]) for n in range(4)]
+        flat = small.reshape(-1)
+        grad_gain_attn, grad_gain_ffn = flat[: ends[0]], flat[ends[0] : ends[1]]
+        grad_table = flat[ends[1] : ends[2]].reshape(grad_table.shape)
+        own_rows = w_router.shape[0]
+        mine = (dp_index * lax.axis_size("expert") + lax.axis_index("expert")) * own_rows
+        own_router = lax.dynamic_slice_in_dim(
+            flat[ends[2] : ends[3]].reshape(grad_router.shape), mine, own_rows, 0
+        )
+        small_parts = (grad_gain_attn, grad_gain_ffn, grad_table.T)
+    else:
+        dense_grad = lax.psum_scatter(
+            jnp.concatenate([grad_qkv, grad_out_weight], axis=1), ("dp", "expert"), scatter_dimension=0, tiled=True
+        )
+        own_router = lax.psum_scatter(grad_router, ("dp", "expert"), scatter_dimension=0, tiled=True)
+        small_parts = lax.psum((grad_gain_attn, grad_gain_ffn, grad_table.T), ("dp", "expert"))
     return (
         output,
         grad_tokens,

time: 1130 us -> 1050 us (0.929)
  waiting for transfers between devices: 419 us -> 334 us
  blocking collectives: 57 us -> 15.6 us
  Pallas kernels: 451 us -> 484 us
    reduce_scatter x1 -> x0, waiting for transfers between devices: 60 us -> none  [per_device(): lax.psum_scatter(jnp.concatenate([grad_qkv, grad_out_weight], axis=1), ('...]
    psum x1 -> x0, blocking collectives: 41.4 us -> none  [per_device(): lax.psum((grad_gain_attn, grad_gain_ffn, grad_table.T), ('dp', 'expert'))]
    pallas_call x1 -> x2, Pallas kernels: 28.5 us -> 66.7 us  [the longest x1 54.8 us: dense_sum(): pl.pallas_call(dense_kernel, in_specs=[vmem] * 3, out_specs=[vmem] * 2, o...]
    all_gather x1, waiting for transfers between devices: 30.8 us -> 57 us  [per_device(): lax.all_gather(late_cotangent, 'expert', axis=0, tiled=True)]
    all_gather x2, waiting for transfers between devices: 41.9 us -> 16.9 us  [per_device(): lax.all_gather(kv[:prompt_rows], 'dp', axis=0, tiled=True)]
    reduce_scatter x1, waiting for transfers between devices: 0.02 us -> 14.5 us  [exchange_tokens(): lax.psum_scatter(grad_w_in[None], 'dp', scatter_dimension=1, tiled=True)]
    reduce_scatter x2, waiting for transfers between devices: 24.2 us -> 10.9 us  [per_device(): lax.psum_scatter(grad_kv[:PROMPT], 'dp', scatter_dimension=0, tiled=True)]
    reduce_scatter x1, waiting for transfers between devices: 12.9 us -> 0.02 us  [exchange_tokens(): lax.psum_scatter(grad_w_down[None], 'dp', scatter_dimension=1, tiled=True)]
  transfers between devices with their start and end apart: 14 -> 13, of which waited for: 10 -> 9; matrix products, arithmetic and copies ran while one was open for 8% -> 9% of each run, Pallas kernels for 28% -> 29%
where the time goes in v5:
time: 1050 us; the launch traced here: 1040 us
  Pallas kernels  484 us (46%)
  waiting for transfers between devices  334 us (32%)
  local copies, waits for them, and re-layouts  66.4 us (6%)
  matrix products  48 us (5%)
  other arithmetic  43.3 us (4%)
  between operations  30.9 us (3%)
  blocking collectives  15.6 us (1%)
  starting transfers between devices  14.1 us (1%)
    pallas_call x2, Pallas kernels, attention_backward(): pl.pallas_call(functools.partial(bwd_kernel, 64 ** (-0.5)), grid_spec=plt...  148 us
    pallas_call x1, Pallas kernels, expert_layer(): pl.pallas_call(functools.partial(expert_kernel, sources), grid_spec=pltpu...  99.9 us
    all_gather x1, waiting for transfers between devices, exchange_tokens(): all_tokens = lax.all_gather(sent, 'expert', axis=0, tiled=True)  99.2 us
    reduce_scatter x1, waiting for transfers between devices, exchange_tokens(): lax.psum_scatter(grad_all, 'expert', scatter_dimension=0, tiled=True)  92.8 us
    pallas_call x2, Pallas kernels, attention_forward(): pl.pallas_call(functools.partial(fwd_kernel, scale2), grid_spec=pltpu.Pre...  89.4 us
    all_gather x1, waiting for transfers between devices, per_device(): lax.all_gather(late_cotangent, 'expert', axis=0, tiled=True)  57 us
    pallas_call x1, Pallas kernels, dense_sum(): pl.pallas_call(dense_kernel, in_specs=[vmem] * 3, out_specs=[vmem] * 2, o...  54.8 us
    pallas_call x2, Pallas kernels, bias_tables(): pl.pallas_call(bias_kernel, grid_spec=pltpu.PrefetchScalarGridSpec(num_sc...  43.2 us
  transfers between devices with their start and end apart: 13, of which 9 were waited for; matrix products, arithmetic and copies ran while one was open for 9% of the time, Pallas kernels for 29%

profile of v5, /device:TPU:0, one launch (start us, length us, event | category | flops | bytes accessed | tf_op | source)
XLA Modules:
  0.0 1036.8 jit_solution(13683384657860002507)
XLA Ops:
  12.1 15.6 %all-gather = s32[8192,2]{0,1:T(2,128)S(1)} all-gather(s32[1024,2]{0,1:T(2,128)S(1)} %multiply_add_fusion), channel_id=2, replica_groups=mesh['dp'=4,'expert'=8] {'expert'}, dimensions={0}, use_global_device_ids=true | all-gather | bytes 73728 | tf_op jit(solution)/shard_map/all_gather | solution.py:860
  30.3 4.6 all-to-all-start
  36.6 3.1 multiply_reduce_fusion
  40.0 21.5 %bias_tables.2 = (f32[6,128,2816]{2,1,0:T(8,128)S(1)}, f32[6,512,2560]{2,1,0:T(8,128)}) custom-call(s32[6]{0:T(128)S(1)} %pad_add_fusion.info, f32[12,8,2816]{2,1,0:T(8,128)S(1)} %broadcast_select_fusion.base_ref, s32[512,128]{1,0:T(8,128)S(1)} %broadcast_in_dim.76.row_start), custom_call_target="tpu_custom_call" | custom-call | bytes 62914560 | tf_op jit(solution)/shard_map/bias_tables/pallas_call | solution.py:105
  61.6 3.3 copy-done.1
  65.3 3.7 fusion.2.refs_1_
  70.4 8.3 all-gather.7.cloned.1.call-done
  78.6 6.4 convolution_convert_fusion.q_ref
  85.1 2.2 copy-done.14
  87.3 1.7 fusion.108
  90.0 21.6 %bias_tables.3 = (f32[6,128,2816]{2,1,0:T(8,128)S(1)}, f32[6,512,2560]{2,1,0:T(8,128)}) custom-call(s32[6]{0:T(128)S(1)} %pad_add_fusion.info, f32[12,8,2816]{2,1,0:T(8,128)S(1)} %broadcast_select_fusion.base_ref, s32[512,128]{1,0:T(8,128)S(1)} %broadcast_in_dim.76.row_start), custom_call_target="tpu_custom_call" | custom-call | bytes 62914560 | tf_op jit(solution)/shard_map/bias_tables/pallas_call | solution.py:105
  111.6 3.4 copy-done.2
  115.0 16.9 %all-gather.11.cloned.1.call-done = bf16[2048,768]{1,0:T(8,128)(2,1)} async-done(((bf16[512,768]{1,0:T(8,128)(2,1)}), bf16[2048,768]{1,0:T(8,128)(2,1)}) %all-gather.11.cloned.1.call-update) | async-done | bytes 3145744 | tf_op jit(solution)/shard_map/all_gather | solution.py:964
  132.0 4.3 pad_maximum_fusion.k_ref.v_ref
  136.3 44.3 %attention_forward.2 = (f32[1024,384]{1,0:T(8,128)}, f32[1024,128]{1,0:T(8,128)}) custom-call(s32[6]{0:T(128)} %copy-done.10, bf16[1024,2304]{1,0:T(8,128)(2,1)} %copy-done.14, bf16[2560,768]{1,0:T(8,128)(2,1)} %pad_maximum_fusion.k_ref.v_ref, bf16[2560,768]{1,0:T(8,128)(2,1)} %pad_maximum_fusion.k_ref.v_ref, f32[6,128,2816]{2,1,0:T(8,128)} %copy-done.1, ...), custom_call_target="tpu_custom_call" | custom-call | flops 8053063680 | bytes 10485760 | tf_op jit(solution)/shard_map/attention_forward/pallas_call | solution.py:167
  180.6 4.1 pad_maximum_fusion.1.k_ref.v_ref
  184.7 45.2 %attention_forward.3 = (f32[1024,384]{1,0:T(8,128)}, f32[1024,128]{1,0:T(8,128)}) custom-call(s32[6]{0:T(128)} %copy-done.10, bf16[1024,2304]{1,0:T(8,128)(2,1)} %copy-done.14, bf16[2560,768]{1,0:T(8,128)(2,1)} %pad_maximum_fusion.1.k_ref.v_ref, bf16[2560,768]{1,0:T(8,128)(2,1)} %pad_maximum_fusion.1.k_ref.v_ref, f32[6,128,2816]{2,1,0:T(8,128)} %copy-done.2, ...), custom_call_target="tpu_custom_call" | custom-call | flops 8053063680 | bytes 10485760 | tf_op jit(solution)/shard_map/attention_forward/pallas_call | solution.py:167
  229.9 1.7 convert.7
  231.6 1.8 convert.6
  233.4 3.1 multiply_reduce_fusion.3
  236.6 1.6 copy-done.11
  239.7 57.0 %all-gather.13.cloned.1.call-done.refs_0_ = bf16[8192,768]{1,0:T(8,128)(2,1)} async-done(((bf16[1024,768]{1,0:T(8,128)(2,1)}), bf16[8192,768]{1,0:T(8,128)(2,1)}) %all-gather.13.cloned.1.call-update) | async-done | bytes 12582928 | tf_op jit(solution)/shard_map/all_gather | solution.py:967
  297.9 13.7 %pack_tokens.3 = (bf16[2816,768]{1,0:T(8,128)(2,1)S(1)}, bf16[2816,128]{1,0:T(8,128)(2,1)S(1)}) custom-call(s32[17]{0:T(128)S(1)} %pad_add_fusion.1.info, s32[8,1,1024]{2,1,0:T(1,128)S(1)} %broadcast_in_dim.80.place_ref, bf16[8192,768]{1,0:T(8,128)(2,1)} %all-gather.13.cloned.1.call-done.refs_0_, bf16[8192,128]{1,0:T(8,128)(2,1)S(1)} %fusion.2.refs_1_), custom_call_target="tpu_custom_call" | custom-call | tf_op jit(solution)/shard_map/pack_tokens/pallas_call | solution.py:407
  311.7 2.0 copy-done.3
  314.5 99.2 %all-gather.15.cloned.1.call-done.refs_0_ = bf16[8192,768]{1,0:T(8,128)(2,1)} async-done(((bf16[1024,768]{1,0:T(8,128)(2,1)}), bf16[8192,768]{1,0:T(8,128)(2,1)}) %all-gather.15.cloned.1.call-update) | async-done | bytes 12582928 | tf_op jit(solution)/shard_map/all_gather | solution.py:881
  413.7 11.8 %pack_tokens.2.x_ref = bf16[2816,768]{1,0:T(8,128)(2,1)S(1)} custom-call(s32[17]{0:T(128)S(1)} %pad_add_fusion.1.info, s32[8,1,1024]{2,1,0:T(1,128)S(1)} %broadcast_in_dim.80.place_ref, bf16[8192,768]{1,0:T(8,128)(2,1)} %all-gather.15.cloned.1.call-done.refs_0_), custom_call_target="tpu_custom_call" | custom-call | tf_op jit(solution)/shard_map/pack_tokens/pallas_call | solution.py:407
  425.6 2.0 copy-done
  427.6 99.9 %expert_layer.1 = (bf16[2816,768]{1,0:T(8,128)(2,1)}, bf16[2816,768]{1,0:T(8,128)(2,1)}, bf16[2816,128]{1,0:T(8,128)(2,1)}, bf16[768,3072]{1,0:T(8,128)(2,1)}, bf16[3072,768]{1,0:T(8,128)(2,1)}) custom-call(s32[17]{0:T(128)} %copy-done.8, s32[1]{0:T(128)} %bitcast.12.expert, bf16[2816,768]{1,0:T(8,128)(2,1)} %copy-done, bf16[2816,128]{1,0:T(8,128)(2,1)} %copy-done.6, ...), custom_call_target="tpu_custom_call" | custom-call | tf_op jit(solution)/shard_map/expert_layer/pallas_call | solution.py:557
  528.8 2.2 copy-done.4
  531.0 11.9 %unpack_tokens.1 = (bf16[8192,768]{1,0:T(8,128)(2,1)}, f32[8192,128]{1,0:T(8,128)S(1)}) custom-call(s32[17]{0:T(128)S(1)} %copy-done.9, s32[8192,128]{1,0:T(8,128)S(1)} %broadcast_in_dim.82.place_ref, bf16[2816,768]{1,0:T(8,128)(2,1)S(1)} %copy-done.4, bf16[2816,128]{1,0:T(8,128)(2,1)S(1)} %copy-done.7), custom_call_target="tpu_custom_call" | custom-call | tf_op jit(solution)/shard_map/unpack_tokens/pallas_call | solution.py:434
  542.9 2.0 copy-done.5
  561.3 2.3 dynamic-slice_dynamic-update-slice_fusion.7
  563.5 2.2 dynamic-slice_dynamic-update-slice_fusion.6
  565.8 2.3 dynamic-slice_dynamic-update-slice_fusion.5
  568.0 2.2 dynamic-slice_dynamic-update-slice_fusion.4
  570.2 2.3 dynamic-slice_dynamic-update-slice_fusion.3
  572.5 2.3 dynamic-slice_dynamic-update-slice_fusion.2
  574.8 2.3 dynamic-slice_dynamic-update-slice_fusion.1
  577.0 2.2 dynamic-slice_dynamic-update-slice_fusion
  579.2 92.8 %reduce-scatter.6.cloned.1.call-done = bf16[1024,768]{1,0:T(8,128)(2,1)} async-done(((bf16[8192,768]{1,0:T(8,128)(2,1)}), bf16[1024,768]{1,0:T(8,128)(2,1)}) %reduce-scatter.6.cloned.1.call-update) | async-done | bytes 1572880 | tf_op jit(solution)/shard_map/reduce_scatter | solution.py:891
  672.8 4.1 slice_reduce_fusion
  676.9 3.3 all-to-all-start.2
  680.5 1.9 fusion.105
  682.4 3.5 all-to-all-done.2
  686.2 3.1 multiply_reduce_fusion.1
  690.6 2.6 convolution_convert_fusion.1.do_ref
  693.2 73.9 %attention_backward.2 = (bf16[1024,384]{1,0:T(8,128)(2,1)}, bf16[2560,768]{1,0:T(8,128)(2,1)}, f32[6,1,2816]{2,1,0:T(1,128)}) custom-call(s32[6]{0:T(128)} %copy-done.10, bf16[1024,2304]{1,0:T(8,128)(2,1)} %copy-done.14, bf16[1024,768]{1,0:T(8,128)(2,1)} %convolution_convert_fusion.1.do_ref, f32[1024,384]{1,0:T(8,128)} %get-tuple-element.89.o_ref, ...), custom_call_target="tpu_custom_call" | custom-call | flops 20132659200 | bytes 10485760 | tf_op jit(solution)/shard_map/attention_backward/pallas_call | solution.py:319
  767.2 3.8 slice.128
  771.0 4.7 all-to-all-start.1
  776.1 14.5 %reduce-scatter.8.cloned.1.call-done = bf16[1,192,3072]{2,1,0:T(8,128)(2,1)} async-done(((bf16[1,768,3072]{2,1,0:T(8,128)(2,1)}), bf16[1,192,3072]{2,1,0:T(8,128)(2,1)}) %reduce-scatter.8.cloned.1.call-update) | async-done | bytes 1179664 | tf_op jit(solution)/shard_map/reduce_scatter | solution.py:898
  790.6 73.7 %attention_backward.3 = (bf16[1024,384]{1,0:T(8,128)(2,1)}, bf16[2560,768]{1,0:T(8,128)(2,1)}, f32[6,1,2816]{2,1,0:T(1,128)}) custom-call(s32[6]{0:T(128)} %copy-done.10, bf16[1024,2304]{1,0:T(8,128)(2,1)} %copy-done.14, bf16[1024,768]{1,0:T(8,128)(2,1)} %convolution_convert_fusion.1.do_ref, f32[1024,384]{1,0:T(8,128)} %get-tuple-element.93.o_ref, ...), custom_call_target="tpu_custom_call" | custom-call | flops 20132659200 | bytes 10485760 | tf_op jit(solution)/shard_map/attention_backward/pallas_call | solution.py:319
  864.3 3.7 slice.130
  870.8 2.1 slice.129
  872.9 3.6 fusion.36
  876.5 2.2 slice.131
  880.5 2.9 convert_element_type.334
  883.5 1.6 convert_element_type.335
  885.1 29.7 %all-to-all-done.1 = bf16[8,512,768]{2,1,0:T(8,128)(2,1)} async-done(((bf16[8,512,768]{2,1,0:T(8,128)(2,1)}), bf16[8,512,768]{2,1,0:T(8,128)(2,1)}, u32[]{:S(2)}, u32[]{:S(2)}) %all-to-all-start.1) | async-done | bytes 6291488 | tf_op jit(solution)/shard_map/all_to_all | solution.py:896
  916.7 11.7 %collect_rows.1 = f32[1024,768]{1,0:T(8,128)S(1)} custom-call(s32[8192,128]{1,0:T(8,128)S(1)} %broadcast_in_dim.143.place_ref, bf16[4096,768]{1,0:T(8,128)(2,1)} %bitcast.24.x_ref), custom_call_target="tpu_custom_call" | custom-call | tf_op jit(solution)/shard_map/collect_rows/pallas_call | solution.py:468
  929.8 10.9 %reduce-scatter.14.cloned.1.call-done = bf16[512,768]{1,0:T(8,128)(2,1)} async-done(((bf16[2048,768]{1,0:T(8,128)(2,1)}), bf16[512,768]{1,0:T(8,128)(2,1)}) %reduce-scatter.14.cloned.1.call-update) | async-done | bytes 786448 | tf_op jit(solution)/shard_map/reduce_scatter | solution.py:1009
  940.8 15.2 %fusion.8 = (f32[768]{0:T(1024)S(1)}, f32[1024]{0:T(1024)S(1)}, f32[1024,768]{1,0:T(8,128)}) fusion(bf16[1024,768]{1,0:T(8,128)(2,1)} %param.13, f32[1024]{0:T(1024)S(1)} %fusion.99, f32[768]{0:T(1024)S(1)} %copy-done.37, bf16[768,3200]{1,0:T(8,128)(2,1)} %all-gather.7.cloned.1.call-done, bf16[512,768]{1,0:T(8,128)(2,1)} %slice.131, ...), kind=kOutput, calls=%fused_computation.22 | convolution fusion | flops 3657693440 | bytes 12990464 | tf_op jit(solution)/shard_map/dot_general | solution.py:1021
  956.0 9.5 fusion.39
  965.5 54.8 %dense_sum.1 = (f32[24,3072]{1,0:T(8,128)S(1)}, f32[64,128]{1,0:T(8,128)S(1)}) custom-call(f32[16,2,24,2304]{3,2,1,0:T(8,128)} %bitcast.135, f32[16,2,24,768]{3,2,1,0:T(8,128)S(1)} %bitcast.132, f32[64,128]{1,0:T(8,128)S(1)} %pad_bitcast_fusion.s_ref), custom_call_target="tpu_custom_call" | custom-call | tf_op jit(solution)/shard_map/dense_sum/pallas_call | solution.py:693
  1024.2 5.3 fusion.10
  (179 shorter events, 32.3 us)
Async XLA Ops:
  7.2 28.6 %copy-start.34 = (s32[1,512]{1,0:T(1,128)S(1)}, s32[1,512]{1,0:T(1,128)}, u32[]{:S(2)}) copy-start(s32[1,512]{1,0:T(1,128)} %param.14) | copy-start | bytes 6148
  7.2 29.1 %copy-start.36 = (f32[31,12]{0,1:T(8,128)S(1)}, f32[31,12]{0,1:T(8,128)}, u32[]{:S(2)}) copy-start(f32[31,12]{0,1:T(8,128)} %param.19) | copy-start | bytes 4468
  7.2 71.4 %all-gather.7.cloned.1.call-start = ((), (), s32[]{:S(2)}) async-start(), calls=%async_computation.8 | async-start | bytes 5068800 | tf_op jit(solution)/shard_map/all_gather | solution.py:947
  30.3 39.4 %all-to-all-start = ((s32[8,1,1024]{2,1,0:T(1,128)}), s32[8,1,1024]{2,1,0:T(1,128)S(1)}, u32[]{:S(2)}, u32[]{:S(2)}) async-start(s32[8,1,1024]{2,1,0:T(1,128)} %copy.59), calls=%async_computation | async-start | bytes 65536 | tf_op jit(solution)/shard_map/all_to_all | solution.py:867
  34.9 97.0 %all-gather.11.cloned.1.call-start = ((), (), s32[]{:S(2)}) async-start(), calls=%async_computation.10 | async-start | bytes 3932160 | tf_op jit(solution)/shard_map/all_gather | solution.py:964
  36.0 54.0 %copy-start.10 = (s32[6]{0:T(128)}, s32[6]{0:T(128)S(1)}, u32[]{:S(2)}) copy-start(s32[6]{0:T(128)S(1)} %pad_add_fusion.info) | copy-start | bytes 76
  36.6 28.3 %copy-start.18 = (bf16[1024,768]{1,0:T(8,128)(2,1)S(1)}, bf16[1024,768]{1,0:T(8,128)(2,1)}, u32[]{:S(2)}) copy-start(bf16[1024,768]{1,0:T(8,128)(2,1)} %param.13) | copy-start | bytes 4718596
  39.9 38.7 %copy-start.37 = (f32[768]{0:T(1024)S(1)}, f32[768]{0:T(1024)}, u32[]{:S(2)}) copy-start(f32[768]{0:T(1024)} %param.17) | copy-start | bytes 9220
  61.6 3.3 copy-start.1
  65.2 3.8 copy-start.32
  69.7 344.0 %copy-start.8 = (s32[17]{0:T(128)}, s32[17]{0:T(128)S(1)}, u32[]{:S(2)}) copy-start(s32[17]{0:T(128)S(1)} %pad_add_fusion.1.info) | copy-start | bytes 208
  85.0 2.2 copy-start.14
  89.0 91.6 %all-gather.9.cloned.1.call-start = ((), (), s32[]{:S(2)}) async-start(), calls=%async_computation.9 | async-start | bytes 3932160 | tf_op jit(solution)/shard_map/all_gather | solution.py:964
  89.7 207.0 %all-gather.13.cloned.1.call-start = ((), (), s32[]{:S(2)}) async-start(), calls=%async_computation.11 | async-start | bytes 14155776 | tf_op jit(solution)/shard_map/all_gather | solution.py:967
  111.6 3.4 copy-start.2
  132.0 281.8 %all-gather.15.cloned.1.call-start = ((), (), s32[]{:S(2)}) async-start(), calls=%async_computation.12 | async-start | bytes 14155776 | tf_op jit(solution)/shard_map/all_gather | solution.py:881
  136.3 44.3 %copy-start.21 = (bf16[512,768]{1,0:T(8,128)(2,1)S(1)}, bf16[512,768]{1,0:T(8,128)(2,1)}, u32[]{:S(2)}) copy-start(bf16[512,768]{1,0:T(8,128)(2,1)} %get-tuple-element.186) | copy-start | bytes 2359300
  229.9 3.5 copy-start.19
  231.6 4.9 copy-start.24
  233.4 3.1 copy-start.26
  233.4 4.8 copy-start.31
  236.5 1.7 copy-start.11
  238.2 59.0 %slice-start.2 = ((bf16[768,3200]{1,0:T(8,128)(2,1)}), bf16[768,8]{1,0:T(8,128)(2,1)S(1)}, s32[]{:S(2)}) async-start(bf16[768,3200]{1,0:T(8,128)(2,1)} %all-gather.7.cloned.1.call-done), calls=%async_computation.20 | async-start | bytes 393216 | tf_op jit(solution)/shard_map/slice | solution.py:955
  296.7 375.3 %reduce-scatter.6.cloned.1.call-start = ((), (), s32[]{:S(2)}) async-start(), calls=%async_computation.13 | async-start | bytes 14155776 | tf_op jit(solution)/shard_map/reduce_scatter | solution.py:891
  311.7 2.0 copy-start.3
  313.7 0.8 copy-start.6
  425.6 2.0 copy-start
  527.5 1.3 copy-start.7
  527.5 1.3 copy-start.9
  528.8 2.2 copy-start.4
  542.9 2.0 copy-start.5
  544.9 231.1 %reduce-scatter.10.cloned.1.call-start = ((), (), s32[]{:S(2)}) async-start(), calls=%async_computation.15 | async-start | bytes 5898240 | tf_op jit(solution)/shard_map/reduce_scatter | solution.py:899
  672.0 118.6 %reduce-scatter.8.cloned.1.call-start = ((), (), s32[]{:S(2)}) async-start(), calls=%async_computation.14 | async-start | bytes 5898240 | tf_op jit(solution)/shard_map/reduce_scatter | solution.py:898
  672.8 13.2 %copy-start.28 = (s32[1024,2]{0,1:T(2,128)S(1)}, s32[1024,2]{0,1:T(2,128)}, u32[]{:S(2)}) copy-start(s32[1024,2]{0,1:T(2,128)} %param.15) | copy-start | bytes 24580
  672.8 13.4 %copy-start.12 = (f32[1024,768]{1,0:T(8,128)S(1)}, f32[1024,768]{1,0:T(8,128)}, u32[]{:S(2)}) copy-start(f32[1024,768]{1,0:T(8,128)} %copy-done.11) | copy-start | bytes 9437188
  676.9 9.0 all-to-all-start.2
  680.3 249.6 %reduce-scatter.12.cloned.1.call-start = ((), (), s32[]{:S(2)}) async-start(), calls=%async_computation.16 | async-start | bytes 3932160 | tf_op jit(solution)/shard_map/reduce_scatter | solution.py:1009
  686.1 3.2 copy-start.17
  686.2 4.0 slice-start
  689.3 1.3 slice-start.1
  690.6 2.6 copy-start.16
  771.0 143.7 %all-to-all-start.1 = ((bf16[8,512,768]{2,1,0:T(8,128)(2,1)}), bf16[8,512,768]{2,1,0:T(8,128)(2,1)}, u32[]{:S(2)}, u32[]{:S(2)}) async-start(bf16[8,512,768]{2,1,0:T(8,128)(2,1)} %bitcast.23), calls=%async_computation.2 | async-start | bytes 12582912 | tf_op jit(solution)/shard_map/all_to_all | solution.py:896
  775.8 165.0 %reduce-scatter.14.cloned.1.call-start = ((), (), s32[]{:S(2)}) async-start(), calls=%async_computation.17 | async-start | bytes 3932160 | tf_op jit(solution)/shard_map/reduce_scatter | solution.py:1009
  868.0 1.4 copy-start.15
  868.0 4.9 copy-start.25
  872.9 5.8 copy-start.29
  872.9 5.8 copy-start.30
  872.9 5.9 copy-start.35
  876.5 7.0 copy-start.22
  916.7 11.7 %copy-start.13 = (f32[1024,768]{1,0:T(8,128)S(1)}, f32[1024,768]{1,0:T(8,128)}, u32[]{:S(2)}) copy-start(f32[1024,768]{1,0:T(8,128)} %copy-done.11) | copy-start | bytes 9437188
  928.4 12.4 %copy-start.23 = (bf16[512,768]{1,0:T(8,128)(2,1)S(1)}, bf16[512,768]{1,0:T(8,128)(2,1)}, u32[]{:S(2)}) copy-start(bf16[512,768]{1,0:T(8,128)(2,1)} %slice.129) | copy-start | bytes 2359300
  929.8 26.1 %copy-start.27 = (f32[6144]{0:T(1024)S(1)}, f32[6144]{0:T(1024)}, u32[]{:S(2)}) copy-start(f32[6144]{0:T(1024)} %reshape.450) | copy-start | bytes 73732
  965.5 58.0 %copy-start.33 = (f32[1024]{0:T(1024)S(1)}, f32[1024]{0:T(1024)}, u32[]{:S(2)}) copy-start(f32[1024]{0:T(1024)} %copy-done.32) | copy-start | bytes 12292
  1020.4 3.8 copy-start.20
Sparse Core Ops, SparseCore 0:
  11.5 67.1 all-gather.6
  89.1 42.7 all-gather.10
  134.3 43.9 all-gather.8
  179.9 116.7 all-gather.12
  298.7 114.9 all-gather.14
  545.0 126.8 reduce-scatter.5
  675.0 55.4 reduce-scatter.9
  733.5 57.0 reduce-scatter.7
  793.6 43.9 reduce-scatter.11
  868.2 72.5 reduce-scatter.13

commit v6 on v5

--- a/solution.py
+++ b/solution.py
@@ -47,6 +47,7 @@
 QT = 256
 KT = 512
 RUN = 256
+EARLY = pl.CostEstimate(flops=1 << 20, bytes_accessed=1 << 20, transcendentals=0)
 PARTS = 2
 ROWS = 32
 NT = (((1,), (1,)), ((), ()))
@@ -112,7 +113,7 @@
         out_shape=[jax.ShapeDtypeStruct((heads, 128, wide), F32),
                    jax.ShapeDtypeStruct((heads, KT, PROMPT + KT), F32)],
         compiler_params=pltpu.CompilerParams(vmem_limit_bytes=32 << 20),
-        cost_estimate=pl.CostEstimate(flops=0, bytes_accessed=heads * KT * (PROMPT + KT) * 8, transcendentals=0),
+        cost_estimate=EARLY,
         name="bias_tables",
     )(info, rows_bias, row_start)
 
@@ -120,10 +121,10 @@
     lane = lax.broadcasted_iota(jnp.int32, (rows, 128), 1)
     return lane // 64 == h % 2
 
-def fwd_kernel(scale2, info, q_ref, k_ref, v_ref, t_ref, b_ref, o_ref, lse_ref):
+def fwd_kernel(scale2, cont, info, q_ref, k_ref, v_ref, table_ref, o_ref, lse_ref):
     h = pl.program_id(0)
     dp = info[5]
-    t_scr, b_scr = t_ref.at[0], b_ref.at[0]
+    table = table_ref.at[0]
     own = own_lanes(h, QT)
     head_lane = lax.broadcasted_iota(jnp.int32, (QT, 128), 1) == h
 
@@ -147,38 +148,38 @@
         o_ref[rows, :] = jnp.where(own, acc / l, o_ref[rows, :])
         lse_ref[rows, :] = jnp.where(head_lane, m + jnp.log2(l), lse_ref[rows, :])
 
-    for j in range(2):
+    for j in range(KT // QT):
+        if cont:
+            tile(QT * j, PROMPT // KT + 1,
+                 lambda t: table[pl.ds(QT * j, QT), pl.ds(pl.multiple_of(t * KT, KT), KT)], lambda t: t)
+            continue
         shift = PROMPT - KT * dp - QT * j + RUN
         def bias(t, shift=shift):
             first = (dp - t) * KT + shift
-            return jnp.concatenate([t_scr[:, pl.ds(pl.multiple_of(first - 128 * x, 128), KT)] for x in range(QT // 128)], axis=0)
+            return jnp.concatenate([table[:, pl.ds(pl.multiple_of(first - 128 * x, 128), KT)] for x in range(QT // 128)], axis=0)
         tile(QT * j, dp + 1, bias, lambda t: dp - t)
-    for j in range(2):
-        tile(KT + QT * j, PROMPT // KT + 1,
-             lambda t: b_scr[pl.ds(QT * j, QT), pl.ds(pl.multiple_of(t * KT, KT), KT)], lambda t: t)
-
-def attention_forward(info, projected, keys_values, tables, part):
-    n = projected.shape[0]
+
+def attention_forward(info, projected, keys_values, tables, part, cont):
     keys, columns = keys_values.shape
     heads = columns // 128
-    head_size = 64
-    scale2 = head_size ** -0.5 * LOG2E
+    scale2 = 64 ** -0.5 * LOG2E
     first = part * heads // 2
+    table = tables[int(cont)]
     return pl.pallas_call(
-        functools.partial(fwd_kernel, scale2),
+        functools.partial(fwd_kernel, scale2, cont),
         grid_spec=pltpu.PrefetchScalarGridSpec(
             num_scalar_prefetch=1, grid=(heads,),
-            in_specs=[pl.BlockSpec((n, 128), lambda h, *_: (0, first + h // 2)),
+            in_specs=[pl.BlockSpec((KT, 128), lambda h, *_: (int(cont), first + h // 2)),
                       pl.BlockSpec((keys, 128), lambda h, *_: (0, h // 2 * 2)),
                       pl.BlockSpec((keys, 128), lambda h, *_: (0, h // 2 * 2 + 1)),
-                      *[pl.BlockSpec((1,) + t.shape[1:], lambda h, *_: (h, 0, 0)) for t in tables]],
-            out_specs=[pl.BlockSpec((n, 128), lambda h, *_: (0, h // 2)),
-                       pl.BlockSpec((n, 128), lambda h, *_: (0, 0))]),
-        out_shape=[jax.ShapeDtypeStruct((n, heads * 64), F32), jax.ShapeDtypeStruct((n, 128), F32)],
+                      pl.BlockSpec((1,) + table.shape[1:], lambda h, *_: (h, 0, 0))],
+            out_specs=[pl.BlockSpec((KT, 128), lambda h, *_: (0, h // 2)),
+                       pl.BlockSpec((KT, 128), lambda h, *_: (0, 0))]),
+        out_shape=[jax.ShapeDtypeStruct((KT, heads * 64), F32), jax.ShapeDtypeStruct((KT, 128), F32)],
         compiler_params=pltpu.CompilerParams(vmem_limit_bytes=60 << 20),
-        cost_estimate=pl.CostEstimate(flops=heads * n * keys * 128 * 4, bytes_accessed=n * keys * 4, transcendentals=heads * n * keys),
+        cost_estimate=EARLY,
         name="attention_forward",
-    )(info, projected, keys_values, keys_values, *tables)
+    )(info, projected, keys_values, keys_values, table)
 
 def split3(x):
     hi = x.astype(BF16)
@@ -334,7 +335,7 @@
         out_shape=[jax.ShapeDtypeStruct((n, heads * 64), BF16), jax.ShapeDtypeStruct((keys, columns), BF16),
                    jax.ShapeDtypeStruct((heads, 1, wide), F32)],
         compiler_params=pltpu.CompilerParams(vmem_limit_bytes=60 << 20),
-        cost_estimate=pl.CostEstimate(flops=heads * n * keys * 128 * 10, bytes_accessed=n * keys * 4, transcendentals=heads * n * keys),
+        cost_estimate=EARLY,
         name="attention_backward",
     )(info, projected, do, o32, lse, keys_values, keys_values, *tables)
 
@@ -374,11 +375,22 @@
     kept = hit & (slot < capacity)
     rank = jnp.einsum("ut,dt->du", earlier, kept.astype(BF16), preferred_element_type=F32).astype(jnp.int32)
     place = jnp.where(kept, rank, -1)
+    other = jnp.sum(jnp.where(hits, 0, ids), axis=2)
+    return place, other
+
+
+def half_plan(place, other, half):
+    tokens = place.shape[1] // 2
+    before = jnp.sum((place[:, : half * tokens] >= 0).astype(jnp.int32), axis=1)
+    part = place[:, half * tokens : (half + 1) * tokens]
+    kept = part >= 0
     sizes = jnp.sum(kept.astype(jnp.int32), axis=1)
+    part = jnp.where(kept, part - before[:, None], -1)
     padded = (sizes + 15) // 16 * 16
     ends = jnp.cumsum(padded)
-    other = jnp.sum(jnp.where(hits, 0, ids), axis=2)
-    return place, jnp.concatenate([ends - padded, sizes, ends[-1:]]).astype(jnp.int32), other
+    info = jnp.concatenate([ends - padded, sizes, ends[-1:]]).astype(jnp.int32)
+    hot = other[:, half * tokens : (half + 1) * tokens].reshape(-1, 1) == jnp.arange(128)[None, :]
+    return info, part, hot.astype(jnp.bfloat16)
 
 
 def pack_kernel(sources, info, place_ref, *refs):
@@ -402,17 +414,18 @@
     lax.fori_loop(0, (info[sources + d] + MOE_ROWS - 1) // MOE_ROWS, chunk, 0)
 
 
-def pack(info, place, arrays, room):
+def pack(info, place, arrays, room, halves=1, half=0):
     sources, tokens = place.shape
     return pl.pallas_call(
         functools.partial(pack_kernel, sources),
         grid_spec=pltpu.PrefetchScalarGridSpec(
             num_scalar_prefetch=1, grid=(sources,),
             in_specs=[pl.BlockSpec((1, 1, tokens), lambda d, *_: (d, 0, 0))]
-            + [pl.BlockSpec((tokens, x.shape[1]), lambda d, *_: (d, 0)) for x in arrays],
+            + [pl.BlockSpec((tokens, x.shape[1]), lambda d, *_: (halves * d + half, 0)) for x in arrays],
             out_specs=[pl.BlockSpec((room, x.shape[1]), lambda d, *_: (0, 0)) for x in arrays]),
         out_shape=[jax.ShapeDtypeStruct((room, x.shape[1]), BF16) for x in arrays],
         compiler_params=pltpu.CompilerParams(vmem_limit_bytes=40 << 20),
+        cost_estimate=EARLY,
         name="pack_tokens",
     )(info, place[:, None, :], *arrays)
 
@@ -440,6 +453,7 @@
             out_specs=[pl.BlockSpec((tokens, x.shape[1]), lambda d, *_: (d, 0)) for x in arrays]),
         out_shape=[jax.ShapeDtypeStruct((sources * tokens, x.shape[1]), t) for x, t in zip(arrays, dtypes)],
         compiler_params=pltpu.CompilerParams(vmem_limit_bytes=40 << 20),
+        cost_estimate=EARLY,
         name="unpack_tokens",
     )(info, spread, *arrays)
 
@@ -472,6 +486,7 @@
         out_specs=pl.BlockSpec((tokens, width), lambda e: (0, 0)),
         out_shape=jax.ShapeDtypeStruct((tokens, width), F32),
         compiler_params=pltpu.CompilerParams(vmem_limit_bytes=40 << 20),
+        cost_estimate=EARLY,
         name="collect_rows",
     )(spread, returned)
 
@@ -571,6 +586,7 @@
                    jax.ShapeDtypeStruct((room, 128), BF16),
                    jax.ShapeDtypeStruct(w_in.shape, BF16), jax.ShapeDtypeStruct(w_down.shape, BF16)],
         compiler_params=pltpu.CompilerParams(vmem_limit_bytes=63 << 20),
+        cost_estimate=EARLY,
         name="expert_layer",
     )(info, expert, x, other, cot, router, w_in, w_down)
 
@@ -862,34 +878,57 @@
 
 def plan_tokens(codes, rows, top):
     expert = lax.axis_index("expert").astype(jnp.int32)
-    place, info, other = expert_slots(codes // PRIO, codes % PRIO, expert, rows * top)
-    other_hot = (other.reshape(-1, 1) == jnp.arange(128)[None, :]).astype(jnp.bfloat16)
+    place, other = expert_slots(codes // PRIO, codes % PRIO, expert, rows * top)
     own_place = lax.all_to_all(place, "expert", split_axis=0, concat_axis=0, tiled=True)
-    return place, info, other_hot, own_place
-
-
-def exchange_tokens(normed_ffn, all_cotangents, plan, expert_ids, router, w_in, w_down):
-    rows, width = normed_ffn.shape
+    return own_place, half_plan(place, other, 0), half_plan(place, other, 1)
+
+
+def expert_half(all_tokens, all_cotangents, number, half, router, w_in, w_down, send):
+    info, place, other_hot = half
+    sources, tokens = place.shape
+    room = (4 * tokens + 16 * sources + send + MOE_ROWS - 1) // MOE_ROWS * MOE_ROWS
+    expert = lax.axis_index("expert").astype(jnp.int32)
+    (packed_cot,) = pack(info, place, [all_cotangents], room, 2, number)
+    packed, packed_other = pack(info, place, [all_tokens, other_hot], room)
+    grad_rows, mixed_rows, grad_gate, grad_w_in, grad_w_down = expert_layer(
+        info, expert[None], packed, packed_other, packed_cot, router, w_in[0], w_down[0], sources
+    )
+    grad_all, gate_all = unpack(info, place, [grad_rows, grad_gate], [jnp.bfloat16, jnp.float32], send)
+    gate_all = jnp.sum(gate_all[:, :3], axis=1).reshape(sources, tokens)
+    return grad_all, gate_all, mixed_rows, grad_w_in, grad_w_down
+
+
+def exchange_tokens(normed_halves, all_cotangents, plan, expert_ids, router, w_in, w_down):
+    rows = expert_ids.shape[0]
     experts_total = router.shape[1]
     top = expert_ids.shape[1]
-    expert = lax.axis_index("expert").astype(jnp.int32)
-    place, info, other_hot, own_place = plan
-    sources = place.shape[0]
+    own_place, *halves = plan
     send = 2 * rows * top // experts_total
-    room = (rows * top + 16 * sources + send + MOE_ROWS - 1) // MOE_ROWS * MOE_ROWS
-    sent, all_cotangents = lax.optimization_barrier((normed_ffn, all_cotangents))
-    all_tokens = lax.all_gather(sent, "expert", axis=0, tiled=True)
-    packed_cot, packed_other = pack(info, place, [all_cotangents, other_hot], room)
-    (packed,) = pack(info, place, [all_tokens], room)
     wide_router = jnp.pad(router, ((0, 0), (0, 128 - experts_total)))
-    grad_rows, mixed_rows, grad_gate, grad_w_in, grad_w_down = expert_layer(
-        info, expert[None], packed, packed_other, packed_cot, wide_router, w_in[0], w_down[0], sources
-    )
-    grad_all, gate_all = unpack(info, place, [grad_rows, grad_gate], [jnp.bfloat16, jnp.float32], send)
-    gate_all = jnp.sum(gate_all[:, :3], axis=1).reshape(sources, rows)
+    tokens = [lax.all_gather(x, "expert", axis=0, tiled=True) for x in normed_halves]
+    first = expert_half(tokens[0], all_cotangents, 0, halves[0], wide_router, w_in, w_down, send)
+    grad_own = [lax.psum_scatter(first[0], "expert", scatter_dimension=0, tiled=True)]
+    tokens[1], all_cotangents, _ = lax.optimization_barrier((tokens[1], all_cotangents, first))
+    second = expert_half(tokens[1], all_cotangents, 1, halves[1], wide_router, w_in, w_down, send)
+    grad_later, grad_own[0] = lax.optimization_barrier((second[0], grad_own[0]))
+    grad_own.append(lax.psum_scatter(grad_later, "expert", scatter_dimension=0, tiled=True))
+    gate_all = jnp.concatenate([first[1], second[1]], axis=1)
     gate_own = lax.all_to_all(gate_all, "expert", split_axis=0, concat_axis=0, tiled=True)
-    grad_own = lax.psum_scatter(grad_all, "expert", scatter_dimension=0, tiled=True)
-    windows = jnp.concatenate([lax.dynamic_slice_in_dim(mixed_rows, info[d], send, 0) for d in range(sources)], axis=0)
+    info, later = halves[0][0], halves[1][0]
+    sources = halves[0][1].shape[0]
+    shifted = jnp.pad(second[2], ((send, 0), (0, 0)))
+    row = jnp.arange(send)[:, None]
+    windows = jnp.concatenate([
+        jnp.where(
+            row < info[sources + d],
+            lax.dynamic_slice_in_dim(first[2], info[d], send, 0),
+            lax.dynamic_slice_in_dim(shifted, later[d] + send - info[sources + d], send, 0),
+        )
+        for d in range(sources)
+    ], axis=0)
+    grad_w_in, grad_w_down = first[3] + second[3], first[4] + second[4]
+    grad_own = jnp.concatenate(grad_own, axis=0)
+    normed_ffn = jnp.concatenate(normed_halves, axis=0)
     windows, grad_w_in, grad_w_down, grad_own = lax.optimization_barrier(
         (windows, grad_w_in, grad_w_down, grad_own)
     )
@@ -933,7 +972,7 @@
     dp_count = lax.axis_size("dp")
     dp_index = lax.axis_index("dp")
     prompt_rows = PROMPT // dp_count
-    few_experts = lax.axis_size("expert") <= 16 and w_in.shape[0] == 1
+    few_experts = lax.axis_size("expert") <= 16 and w_in.shape[0] == 1 and prompt_rows == KT
     local_ids = cont_ids[0]
     info = info_of(local_ids, dp_index)
     row_start = row_start_of(local_ids)
@@ -961,26 +1000,53 @@
     parts = PARTS
     columns = 2 * width // parts
     kept = [projected[:, width + columns * g : width + columns * (g + 1)] for g in range(parts)]
-    gathered = [lax.all_gather(kv[:prompt_rows], "dp", axis=0, tiled=True) for kv in kept]
+    gathered = [lax.all_gather(kept[0][:prompt_rows], "dp", axis=0, tiled=True)]
+    for kv in kept[1:]:
+        copies = jnp.broadcast_to(kv[None, :prompt_rows], (dp_count, prompt_rows, columns))
+        gathered.append(
+            lax.all_to_all(copies, "dp", split_axis=0, concat_axis=0, tiled=True).reshape(PROMPT, columns)
+        )
     if few_experts:
         late_cotangent, gathered[0], tables = lax.optimization_barrier((cotangent, gathered[0], tables))
         all_cotangents = lax.all_gather(late_cotangent, "expert", axis=0, tiled=True)
     gathered[0], tables = lax.optimization_barrier((gathered[0], tables))
+    results = {}
     keys_values = []
-    exact, log_total = [], []
-    for g in range(parts):
-        if g:
-            gathered[g], exact[-1] = lax.optimization_barrier((gathered[g], exact[-1]))
-        keys_values.append(jnp.concatenate([gathered[g], kept[g][prompt_rows:]], axis=0))
-        out, total = attention_forward(info, projected, keys_values[g], tables[g], g)
-        exact.append(out)
-        log_total.append(total)
-    attended = jnp.concatenate(exact, axis=1).astype(jnp.bfloat16)
-    middle = inputs + jnp.dot(attended, whole_out, preferred_element_type=jnp.float32)
-    normed_ffn = normed(middle, gain_ffn).astype(jnp.bfloat16)
+    middles, normed_halves, attended_halves = [], [], []
+    order = [(g, c) for g in range(parts) for c in (0, 1)]
+
+    def after_attention(c):
+        attended = jnp.concatenate([results[g, c][0] for g in range(parts)], axis=1).astype(jnp.bfloat16)
+        middle = inputs[c * KT : (c + 1) * KT] + jnp.dot(attended, whole_out, preferred_element_type=jnp.float32)
+        attended_halves.append(attended)
+        middles.append(middle)
+        normed_halves.append(normed(middle, gain_ffn).astype(jnp.bfloat16))
+
+    last = None
+    for g, c in order:
+        if last is not None:
+            gathered[g], results[last] = lax.optimization_barrier((gathered[g], results[last]))
+        if c == 0:
+            source = gathered[g]
+        else:
+            source = jnp.concatenate([gathered[g], kept[g][prompt_rows:]], axis=0)
+            keys_values.append(source)
+        results[g, c] = attention_forward(info, projected, source, tables[g], g, bool(c))
+        last = (g, c)
+        if (g, c) == (parts - 1, 0):
+            after_attention(0)
+            if few_experts:
+                normed_halves[0], all_cotangents = lax.optimization_barrier((normed_halves[0], all_cotangents))
+            gathered[g], normed_halves[0] = lax.optimization_barrier((gathered[g], normed_halves[0]))
+    after_attention(1)
+    exact = [jnp.concatenate([results[g, 0][0], results[g, 1][0]], axis=0) for g in range(parts)]
+    log_total = [jnp.concatenate([results[g, 0][1], results[g, 1][1]], axis=0) for g in range(parts)]
+    attended = jnp.concatenate(attended_halves, axis=0)
+    middle = jnp.concatenate(middles, axis=0)
+    normed_ffn = jnp.concatenate(normed_halves, axis=0)
     if few_experts:
         mixed, grad_logits, grad_normed_ffn, expert_parts = exchange_tokens(
-            normed_ffn, all_cotangents, plan, expert_ids, whole_router, w_in, w_down
+            normed_halves, all_cotangents, plan, expert_ids, whole_router, w_in, w_down
         )
     else:
         mixed, grad_logits, grad_normed_ffn, expert_parts = exchange_pairs(

time: 1050 us -> 942 us (0.90)
  waiting for transfers between devices: 334 us -> 158 us
  other arithmetic: 43.3 us -> 83.2 us
  Pallas kernels: 484 us -> 502 us
    all_gather x3, waiting for transfers between devices: 116 us -> 24 us  [the longest x1 16.2 us: per_device(): gathered = [lax.all_gather(kept[0][:prompt_rows], 'dp', axis=0, tiled=True)]]
    reduce_scatter x1 -> x2, waiting for transfers between devices: 92.8 us -> 30.9 us  [the longest x1 30.9 us: exchange_tokens(): lax.psum_scatter(grad_later, 'expert', scatter_dimension=0, tiled=True)]
    all_gather x1, waiting for transfers between devices: 57 us -> 36.8 us  [per_device(): lax.all_gather(late_cotangent, 'expert', axis=0, tiled=True)]
    add x0 -> x2, other arithmetic: none -> 15 us  [exchange_tokens(): grad_w_in, grad_w_down = (first[3] + second[3], first[4] + second[4])]
    reduce_scatter x1, waiting for transfers between devices: 14.5 us -> 0.01 us  [exchange_tokens(): lax.psum_scatter(grad_w_in[None], 'dp', scatter_dimension=1, tiled=True)]
    pallas_call x2 -> x4, Pallas kernels: 89.4 us -> 97.1 us  [attention_forward(): pl.pallas_call(functools.partial(fwd_kernel, scale2, cont), grid_spec=plt...]
    unnamed x94 -> x160, local copies, waits for them, and re-layouts: 39.5 us -> 34.3 us
    pallas_call x1 -> x2, Pallas kernels: 99.9 us -> 103 us  [expert_layer(): pl.pallas_call(functools.partial(expert_kernel, sources), grid_spec=pltpu...]
  transfers between devices with their start and end apart: 13 -> 15, of which waited for: 9 -> 9; matrix products, arithmetic and copies ran while one was open for 9% -> 12% of each run, Pallas kernels for 29% -> 48%
where the time goes in v6:
time: 942 us; the launch traced here: 932 us
  Pallas kernels  502 us (53%)
  waiting for transfers between devices  158 us (17%)
  other arithmetic  83.2 us (9%)
  local copies, waits for them, and re-layouts  62.6 us (7%)
  matrix products  51.5 us (5%)
  between operations  39.8 us (4%)
  starting transfers between devices  19.5 us (2%)
  blocking collectives  15.6 us (2%)
    pallas_call x2, Pallas kernels, attention_backward(): pl.pallas_call(functools.partial(bwd_kernel, 64 ** (-0.5)), grid_spec=plt...  151 us
    pallas_call x2, Pallas kernels, expert_layer(): pl.pallas_call(functools.partial(expert_kernel, sources), grid_spec=pltpu...  103 us
    pallas_call x4, Pallas kernels, attention_forward(): pl.pallas_call(functools.partial(fwd_kernel, scale2, cont), grid_spec=plt...  97.1 us
    pallas_call x1, Pallas kernels, dense_sum(): pl.pallas_call(dense_kernel, in_specs=[vmem] * 3, out_specs=[vmem] * 2, o...  51.9 us
    pallas_call x2, Pallas kernels, bias_tables(): pl.pallas_call(bias_kernel, grid_spec=pltpu.PrefetchScalarGridSpec(num_sc...  46.7 us
    all_to_all x1, waiting for transfers between devices, exchange_tokens(): lax.all_to_all(windows, 'expert', split_axis=0, concat_axis=0, tiled=True)  40.1 us
    all_gather x1, waiting for transfers between devices, per_device(): lax.all_gather(late_cotangent, 'expert', axis=0, tiled=True)  36.8 us
    unnamed x160, local copies, waits for them, and re-layouts  34.3 us
  transfers between devices with their start and end apart: 15, of which 9 were waited for; matrix products, arithmetic and copies ran while one was open for 12% of the time, Pallas kernels for 48%

profile of v6, /device:TPU:0, one launch (start us, length us, event | category | flops | bytes accessed | tf_op | source)
XLA Modules:
  0.0 932.3 jit_solution(2075123617151493126)
XLA Ops:
  12.1 15.6 %all-gather = s32[8192,2]{0,1:T(2,128)S(1)} all-gather(s32[1024,2]{0,1:T(2,128)S(1)} %multiply_add_fusion), channel_id=2, replica_groups=mesh['dp'=4,'expert'=8] {'expert'}, dimensions={0}, use_global_device_ids=true | all-gather | bytes 73728 | tf_op jit(solution)/shard_map/all_gather | solution.py:876
  30.2 4.6 all-to-all-start
  37.6 3.1 multiply_reduce_fusion
  41.0 23.4 %bias_tables.2 = (f32[6,128,2816]{2,1,0:T(8,128)S(1)}, f32[6,512,2560]{2,1,0:T(8,128)}) custom-call(s32[6]{0:T(128)S(1)} %pad_add_fusion.info, f32[12,8,2816]{2,1,0:T(8,128)S(1)} %broadcast_select_fusion.base_ref, s32[512,128]{1,0:T(8,128)S(1)} %broadcast_in_dim.199.row_start), custom_call_target="tpu_custom_call" | custom-call | flops 1048576 | bytes 1048576 | tf_op jit(solution)/shard_map/bias_tables/pallas_call | solution.py:106
  64.5 3.3 copy-done
  68.2 2.4 fusion.10
  72.6 6.0 all-gather.7.cloned.1.call-done
  78.6 6.4 convolution_convert_fusion.q_ref
  88.3 23.2 %bias_tables.3 = (f32[6,128,2816]{2,1,0:T(8,128)S(1)}, f32[6,512,2560]{2,1,0:T(8,128)}) custom-call(s32[6]{0:T(128)S(1)} %pad_add_fusion.info, f32[12,8,2816]{2,1,0:T(8,128)S(1)} %broadcast_select_fusion.base_ref, s32[512,128]{1,0:T(8,128)S(1)} %broadcast_in_dim.199.row_start), custom_call_target="tpu_custom_call" | custom-call | flops 1048576 | bytes 1048576 | tf_op jit(solution)/shard_map/bias_tables/pallas_call | solution.py:106
  111.5 3.3 copy-done.1
  114.8 16.2 %all-gather.9.cloned.1.call-done.k_ref.v_ref = bf16[2048,768]{1,0:T(8,128)(2,1)} async-done(((bf16[512,768]{1,0:T(8,128)(2,1)}), bf16[2048,768]{1,0:T(8,128)(2,1)}) %all-gather.9.cloned.1.call-update) | async-done | bytes 3145744 | tf_op jit(solution)/shard_map/all_gather | solution.py:1003
  131.0 1.9 broadcast_in_dim.206
  132.9 4.7 all-to-all-start.1
  137.6 3.3 convert_element_type.324
  140.9 12.8 %attention_forward.4 = (f32[512,384]{1,0:T(8,128)}, f32[512,128]{1,0:T(8,128)}) custom-call(s32[6]{0:T(128)} %copy-done.19, bf16[1024,2304]{1,0:T(8,128)(2,1)} %copy-done.20, bf16[2048,768]{1,0:T(8,128)(2,1)} %all-gather.9.cloned.1.call-done.k_ref.v_ref, bf16[2048,768]{1,0:T(8,128)(2,1)} %all-gather.9.cloned.1.call-done.k_ref.v_ref, f32[6,128,2816]{2,1,0:T(8,128)} %copy-done), custom_call_target="tpu_custom_call" | custom-call | flops 1048576 | bytes 1048576 | tf_op jit(solution)/shard_map/attention_forward/pallas_call | solution.py:168
  153.7 4.0 pad_maximum_fusion.k_ref.v_ref
  157.7 35.8 %attention_forward.5 = (f32[512,384]{1,0:T(8,128)}, f32[512,128]{1,0:T(8,128)}) custom-call(s32[6]{0:T(128)} %copy-done.19, bf16[1024,2304]{1,0:T(8,128)(2,1)} %copy-done.20, bf16[2560,768]{1,0:T(8,128)(2,1)} %pad_maximum_fusion.k_ref.v_ref, bf16[2560,768]{1,0:T(8,128)(2,1)} %pad_maximum_fusion.k_ref.v_ref, f32[6,512,2560]{2,1,0:T(8,128)} %get-tuple-element.119.table_ref.b_ref), custom_call_target="tpu_custom_call" | custom-call | flops 1048576 | bytes 1048576 | tf_op jit(solution)/shard_map/attention_forward/pallas_call | solution.py:168
  193.5 12.5 %attention_forward.6 = (f32[512,384]{1,0:T(8,128)}, f32[512,128]{1,0:T(8,128)}) custom-call(s32[6]{0:T(128)} %copy-done.19, bf16[1024,2304]{1,0:T(8,128)(2,1)} %copy-done.20, bf16[2048,768]{1,0:T(8,128)(2,1)} %bitcast.18.k_ref.v_ref, bf16[2048,768]{1,0:T(8,128)(2,1)} %bitcast.18.k_ref.v_ref, f32[6,128,2816]{2,1,0:T(8,128)} %copy-done.1), custom_call_target="tpu_custom_call" | custom-call | flops 1048576 | bytes 1048576 | tf_op jit(solution)/shard_map/attention_forward/pallas_call | solution.py:168
  207.3 3.0 multiply_reduce_fusion.8
  212.6 36.8 %all-gather.11.cloned.1.call-done.refs_0_ = bf16[8192,768]{1,0:T(8,128)(2,1)} async-done(((bf16[1024,768]{1,0:T(8,128)(2,1)}), bf16[8192,768]{1,0:T(8,128)(2,1)}) %all-gather.11.cloned.1.call-update) | async-done | bytes 12582928 | tf_op jit(solution)/shard_map/all_gather | solution.py:1011
  249.5 4.2 pad_maximum_fusion.1.k_ref.v_ref
  253.7 36.0 %attention_forward.7 = (f32[512,384]{1,0:T(8,128)}, f32[512,128]{1,0:T(8,128)}) custom-call(s32[6]{0:T(128)} %copy-done.19, bf16[1024,2304]{1,0:T(8,128)(2,1)} %copy-done.20, bf16[2560,768]{1,0:T(8,128)(2,1)} %pad_maximum_fusion.1.k_ref.v_ref, bf16[2560,768]{1,0:T(8,128)(2,1)} %pad_maximum_fusion.1.k_ref.v_ref, ...), custom_call_target="tpu_custom_call" | custom-call | flops 1048576 | bytes 1048576 | tf_op jit(solution)/shard_map/attention_forward/pallas_call | solution.py:168
  290.9 2.8 multiply_reduce_fusion.7
  297.1 7.5 pack_tokens.5.c_ref
  304.6 2.0 copy-done.2
  306.6 7.8 all-gather.13.cloned.1.call-done.refs_0_
  314.5 2.8 copy-done.5
  317.3 4.7 pack_tokens.4
  322.0 2.1 copy-done.7
  324.9 51.5 %expert_layer.2 = (bf16[2816,768]{1,0:T(8,128)(2,1)}, bf16[2816,768]{1,0:T(8,128)(2,1)}, bf16[2816,128]{1,0:T(8,128)(2,1)}, bf16[768,3072]{1,0:T(8,128)(2,1)}, bf16[3072,768]{1,0:T(8,128)(2,1)}) custom-call(s32[17]{0:T(128)} %copy-done.15, s32[1]{0:T(128)} %bitcast.16.expert, bf16[2816,768]{1,0:T(8,128)(2,1)} %copy-done.7, bf16[2816,128]{1,0:T(8,128)(2,1)} %copy-done.12, ...), custom_call_target="tpu_custom_call" | custom-call | flops 1048576 | bytes 1048576 | tf_op jit(solution)/shard_map/expert_layer/pallas_call | solution.py:572
  377.0 2.2 copy-done.9
  380.3 7.8 unpack_tokens.2
  389.2 7.8 pack_tokens.7.c_ref
  397.0 2.0 copy-done.3
  399.0 4.7 pack_tokens.6
  403.7 2.0 copy-done.6
  406.5 51.5 %expert_layer.3 = (bf16[2816,768]{1,0:T(8,128)(2,1)}, bf16[2816,768]{1,0:T(8,128)(2,1)}, bf16[2816,128]{1,0:T(8,128)(2,1)}, bf16[768,3072]{1,0:T(8,128)(2,1)}, bf16[3072,768]{1,0:T(8,128)(2,1)}) custom-call(s32[17]{0:T(128)} %copy-done.17, s32[1]{0:T(128)} %bitcast.16.expert, bf16[2816,768]{1,0:T(8,128)(2,1)} %copy-done.6, bf16[2816,128]{1,0:T(8,128)(2,1)} %copy-done.11, ...), custom_call_target="tpu_custom_call" | custom-call | flops 1048576 | bytes 1048576 | tf_op jit(solution)/shard_map/expert_layer/pallas_call | solution.py:572
  458.6 2.3 copy-done.8
  462.0 7.8 unpack_tokens.3
  501.1 7.6 add.562
  508.7 7.4 add.561
  527.2 30.9 %reduce-scatter.9.cloned.1.call-done = bf16[512,768]{1,0:T(8,128)(2,1)} async-done(((bf16[4096,768]{1,0:T(8,128)(2,1)}), bf16[512,768]{1,0:T(8,128)(2,1)}) %reduce-scatter.9.cloned.1.call-update) | async-done | bytes 786448 | tf_op jit(solution)/shard_map/reduce_scatter | solution.py:914
  558.1 2.4 pad_maximum_fusion.3
  562.4 2.9 pad_maximum_fusion.5.o_ref
  568.5 3.3 all-to-all-start.3
  572.1 5.4 all-to-all-done.3
  577.7 4.2 multiply_reduce_fusion.1
  582.0 2.5 fusion.4
  586.2 2.6 convolution_convert_fusion.1.do_ref
  588.8 75.6 %attention_backward.2 = (bf16[1024,384]{1,0:T(8,128)(2,1)}, bf16[2560,768]{1,0:T(8,128)(2,1)}, f32[6,1,2816]{2,1,0:T(1,128)}) custom-call(s32[6]{0:T(128)} %copy-done.19, bf16[1024,2304]{1,0:T(8,128)(2,1)} %copy-done.20, bf16[1024,768]{1,0:T(8,128)(2,1)} %convolution_convert_fusion.1.do_ref, f32[1024,384]{1,0:T(8,128)} %pad_maximum_fusion.5.o_ref, ...), custom_call_target="tpu_custom_call" | custom-call | flops 1048576 | bytes 1048576 | tf_op jit(solution)/shard_map/attention_backward/pallas_call | solution.py:320
  664.4 3.7 slice.237
  668.2 4.9 all-to-all-start.2
  676.7 75.7 %attention_backward.3 = (bf16[1024,384]{1,0:T(8,128)(2,1)}, bf16[2560,768]{1,0:T(8,128)(2,1)}, f32[6,1,2816]{2,1,0:T(1,128)}) custom-call(s32[6]{0:T(128)} %copy-done.19, bf16[1024,2304]{1,0:T(8,128)(2,1)} %copy-done.20, bf16[1024,768]{1,0:T(8,128)(2,1)} %convolution_convert_fusion.1.do_ref, f32[1024,384]{1,0:T(8,128)} %pad_maximum_fusion.6.o_ref, ...), custom_call_target="tpu_custom_call" | custom-call | flops 1048576 | bytes 1048576 | tf_op jit(solution)/shard_map/attention_backward/pallas_call | solution.py:320
  752.4 3.8 slice.239
  758.7 2.2 slice.238
  760.9 3.9 fusion.12
  764.8 2.1 slice.240
  772.0 40.1 %all-to-all-done.2 = bf16[8,512,768]{2,1,0:T(8,128)(2,1)} async-done(((bf16[8,512,768]{2,1,0:T(8,128)(2,1)}), bf16[8,512,768]{2,1,0:T(8,128)(2,1)}, u32[]{:S(2)}, u32[]{:S(2)}) %all-to-all-start.2) | async-done | bytes 6291488 | tf_op jit(solution)/shard_map/all_to_all | solution.py:935
  813.4 11.7 %collect_rows.1 = f32[1024,768]{1,0:T(8,128)S(1)} custom-call(s32[8192,128]{1,0:T(8,128)S(1)} %broadcast_in_dim.227.place_ref, bf16[4096,768]{1,0:T(8,128)(2,1)} %bitcast.45.x_ref), custom_call_target="tpu_custom_call" | custom-call | flops 1048576 | bytes 1048576 | tf_op jit(solution)/shard_map/collect_rows/pallas_call | solution.py:482
  826.6 13.1 %reduce-scatter.17.cloned.1.call-done = bf16[512,768]{1,0:T(8,128)(2,1)} async-done(((bf16[2048,768]{1,0:T(8,128)(2,1)}), bf16[512,768]{1,0:T(8,128)(2,1)}) %reduce-scatter.17.cloned.1.call-update) | async-done | bytes 786448 | tf_op jit(solution)/shard_map/reduce_scatter | solution.py:1075
  839.6 15.2 %multiply_reduce_fusion.2 = (f32[768]{0:T(1024)S(1)}, f32[1024]{0:T(1024)S(1)}, f32[1024,768]{1,0:T(8,128)}) fusion(bf16[1024,768]{1,0:T(8,128)(2,1)} %param.13, f32[1024]{0:T(1024)S(1)} %copy-done.64, f32[768]{0:T(1024)S(1)} %copy-done.67, bf16[768,3200]{1,0:T(8,128)(2,1)} %all-gather.7.cloned.1.call-done, bf16[512,768]{1,0:T(8,128)(2,1)} %slice.240, ...), kind=kOutput, calls=%fused_computation.23 | convolution fusion | flops 3657693440 | bytes 12990464 | tf_op jit(solution)/shard_map/dot_general | solution.py:1087
  854.9 9.4 %fusion.66 = f32[768,2304]{1,0:T(8,128)} fusion(bf16[1024,768]{1,0:T(8,128)(2,1)} %param.13, f32[768]{0:T(1024)S(1)} %copy-done.67, f32[1024]{0:T(1024)S(1)} %copy-done.64, bf16[512,768]{1,0:T(8,128)(2,1)} %slice.240, bf16[512,768]{1,0:T(8,128)(2,1)} %reduce-scatter.17.cloned.1.call-done, bf16[512,768]{1,0:T(8,128)(2,1)S(1)} %copy-done.44, ...), kind=kOutput, calls=%fused_computation.102 | convolution fusion | flops 3655335936 | bytes 13376512 | tf_op jit(solution)/shard_map/dot_general | solution.py:1088
  864.3 51.9 %dense_sum.1 = (f32[24,3072]{1,0:T(8,128)S(1)}, f32[64,128]{1,0:T(8,128)S(1)}) custom-call(f32[16,2,24,2304]{3,2,1,0:T(8,128)} %bitcast.174, f32[16,2,24,768]{3,2,1,0:T(8,128)S(1)} %bitcast.161, f32[64,128]{1,0:T(8,128)S(1)} %pad_bitcast_fusion.s_ref), custom_call_target="tpu_custom_call" | custom-call | tf_op jit(solution)/shard_map/dense_sum/pallas_call | solution.py:709
  920.1 5.3 fusion.5
  (303 shorter events, 73.2 us)
Async XLA Ops:
  7.2 29.6 %copy-start.62 = (s32[1,512]{1,0:T(1,128)S(1)}, s32[1,512]{1,0:T(1,128)}, u32[]{:S(2)}) copy-start(s32[1,512]{1,0:T(1,128)} %param.14) | copy-start | bytes 6148
  7.2 30.0 %copy-start.65 = (f32[31,12]{0,1:T(8,128)S(1)}, f32[31,12]{0,1:T(8,128)}, u32[]{:S(2)}) copy-start(f32[31,12]{0,1:T(8,128)} %param.19) | copy-start | bytes 4468
  7.2 71.4 %all-gather.7.cloned.1.call-start = ((), (), s32[]{:S(2)}) async-start(), calls=%async_computation.10 | async-start | bytes 5068800 | tf_op jit(solution)/shard_map/all_gather | solution.py:986
  30.2 41.9 %all-to-all-start = ((s32[8,1,1024]{2,1,0:T(1,128)}), s32[8,1,1024]{2,1,0:T(1,128)S(1)}, u32[]{:S(2)}, u32[]{:S(2)}) async-start(s32[8,1,1024]{2,1,0:T(1,128)} %copy.62), calls=%async_computation | async-start | bytes 65536 | tf_op jit(solution)/shard_map/all_to_all | solution.py:882
  34.8 96.2 %all-gather.9.cloned.1.call-start = ((), (), s32[]{:S(2)}) async-start(), calls=%async_computation.11 | async-start | bytes 3932160 | tf_op jit(solution)/shard_map/all_gather | solution.py:1003
  37.0 51.3 %copy-start.19 = (s32[6]{0:T(128)}, s32[6]{0:T(128)S(1)}, u32[]{:S(2)}) copy-start(s32[6]{0:T(128)S(1)} %pad_add_fusion.info) | copy-start | bytes 76
  37.6 30.2 %copy-start.27 = (bf16[1024,768]{1,0:T(8,128)(2,1)S(1)}, bf16[1024,768]{1,0:T(8,128)(2,1)}, u32[]{:S(2)}) copy-start(bf16[1024,768]{1,0:T(8,128)(2,1)} %param.13) | copy-start | bytes 4718596
  40.9 37.7 %copy-start.66 = (f32[768]{0:T(1024)S(1)}, f32[768]{0:T(1024)}, u32[]{:S(2)}) copy-start(f32[768]{0:T(1024)} %param.17) | copy-start | bytes 9220
  68.2 16.9 %copy-start.60 = (f32[1024]{0:T(1024)}, f32[1024]{0:T(1024)S(1)}, u32[]{:S(2)}) copy-start(f32[1024]{0:T(1024)S(1)} %multiply_reduce_fusion.6) | copy-start | bytes 12292
  68.2 16.8 %copy-start.63 = (f32[1024]{0:T(1024)}, f32[1024]{0:T(1024)S(1)}, u32[]{:S(2)}) copy-start(f32[1024]{0:T(1024)S(1)} %fusion.127) | copy-start | bytes 12292
  72.0 242.5 %copy-start.15 = (s32[17]{0:T(128)}, s32[17]{0:T(128)S(1)}, u32[]{:S(2)}) copy-start(s32[17]{0:T(128)S(1)} %get-tuple-element.102.info) | copy-start | bytes 208
  72.0 325.0 %copy-start.17 = (s32[17]{0:T(128)}, s32[17]{0:T(128)S(1)}, u32[]{:S(2)}) copy-start(s32[17]{0:T(128)S(1)} %get-tuple-element.134.info) | copy-start | bytes 208
  88.0 161.4 %all-gather.11.cloned.1.call-start = ((), (), s32[]{:S(2)}) async-start(), calls=%async_computation.12 | async-start | bytes 14155776 | tf_op jit(solution)/shard_map/all_gather | solution.py:1011
  132.9 60.6 %all-to-all-start.1 = ((bf16[4,512,768]{2,1,0:T(8,128)(2,1)}), bf16[4,512,768]{2,1,0:T(8,128)(2,1)}, u32[]{:S(2)}, u32[]{:S(2)}) async-start(bf16[4,512,768]{2,1,0:T(8,128)(2,1)} %broadcast_in_dim.206), calls=%async_computation.1 | async-start | bytes 6291456 | tf_op jit(solution)/shard_map/all_to_all | solution.py:1007
  137.6 176.9 %all-gather.13.cloned.1.call-start = ((), (), s32[]{:S(2)}) async-start(), calls=%async_computation.13 | async-start | bytes 7077888 | tf_op jit(solution)/shard_map/all_gather | solution.py:908
  140.9 12.8 %copy-start.41 = (bf16[512,768]{1,0:T(8,128)(2,1)S(1)}, bf16[512,768]{1,0:T(8,128)(2,1)}, u32[]{:S(2)}) copy-start(bf16[512,768]{1,0:T(8,128)(2,1)} %get-tuple-element.245) | copy-start | bytes 2359300
  193.5 13.7 %copy-start.38 = (f32[512,384]{1,0:T(8,128)S(1)}, f32[512,384]{1,0:T(8,128)}, u32[]{:S(2)}) copy-start(f32[512,384]{1,0:T(8,128)} %get-tuple-element.123) | copy-start | bytes 2359300
  207.3 4.2 copy-start.59
  207.3 42.1 %copy-start.39 = (f32[512,384]{1,0:T(8,128)S(1)}, f32[512,384]{1,0:T(8,128)}, u32[]{:S(2)}) copy-start(f32[512,384]{1,0:T(8,128)} %get-tuple-element.136) | copy-start | bytes 2359300
  210.4 39.2 %copy-start.40 = (bf16[512,768]{1,0:T(8,128)(2,1)S(1)}, bf16[512,768]{1,0:T(8,128)(2,1)}, u32[]{:S(2)}) copy-start(bf16[512,768]{1,0:T(8,128)(2,1)} %get-tuple-element.244) | copy-start | bytes 2359300
  249.4 139.7 %all-gather.15.cloned.1.call-start = ((), (), s32[]{:S(2)}) async-start(), calls=%async_computation.14 | async-start | bytes 7077888 | tf_op jit(solution)/shard_map/all_gather | solution.py:908
  249.5 41.4 %copy-start.48 = (bf16[512,384]{1,0:T(8,128)(2,1)}, bf16[512,384]{1,0:T(8,128)(2,1)S(1)}, u32[]{:S(2)}) copy-start(bf16[512,384]{1,0:T(8,128)(2,1)S(1)} %convert.14) | copy-start | bytes 1179652
  290.9 5.1 copy-start.49
  296.1 173.7 %reduce-scatter.7.cloned.1.call-start = ((), (), s32[]{:S(2)}) async-start(), calls=%async_computation.15 | async-start | bytes 7077888 | tf_op jit(solution)/shard_map/reduce_scatter | solution.py:910
  324.9 52.1 %copy-start.16 = (s32[17]{0:T(128)S(1)}, s32[17]{0:T(128)}, u32[]{:S(2)}) copy-start(s32[17]{0:T(128)} %copy-done.15) | copy-start | bytes 208
  388.2 169.9 %reduce-scatter.9.cloned.1.call-start = ((), (), s32[]{:S(2)}) async-start(), calls=%async_computation.16 | async-start | bytes 7077888 | tf_op jit(solution)/shard_map/reduce_scatter | solution.py:914
  389.2 9.8 %copy-start.4 = (bf16[4096,768]{1,0:T(8,128)(2,1)S(1)}, bf16[4096,768]{1,0:T(8,128)(2,1)}, u32[]{:S(2)}) copy-start(bf16[4096,768]{1,0:T(8,128)(2,1)} %all-gather.15.cloned.1.call-done.refs_0_) | copy-start | bytes 18874372
  389.2 9.8 %copy-start.10 = (bf16[4096,128]{1,0:T(8,128)(2,1)S(1)}, bf16[4096,128]{1,0:T(8,128)(2,1)}, u32[]{:S(2)}) copy-start(bf16[4096,128]{1,0:T(8,128)(2,1)} %get-tuple-element.149.refs_1_) | copy-start | bytes 3145732
  406.5 52.1 %copy-start.18 = (s32[17]{0:T(128)S(1)}, s32[17]{0:T(128)}, u32[]{:S(2)}) copy-start(s32[17]{0:T(128)} %copy-done.17) | copy-start | bytes 208
  469.8 205.7 %reduce-scatter.11.cloned.1.call-start = ((), (), s32[]{:S(2)}) async-start(), calls=%async_computation.17 | async-start | bytes 5898240 | tf_op jit(solution)/shard_map/reduce_scatter | solution.py:937
  501.0 7.6 copy-start.32
  501.1 15.0 %slice-start = ((s8[4325376]{0:T(1024)(128)(4,1)}), s8[4194304]{0:T(1024)(128)(4,1)S(1)}, s32[]{:S(2)}) async-start(s8[4325376]{0:T(1024)(128)(4,1)} %bitcast.164), calls=%async_computation.21 | async-start | bytes 8388608
  501.1 15.0 %slice-start.2 = ((s8[4325376]{0:T(1024)(128)(4,1)}), s8[4194304]{0:T(1024)(128)(4,1)S(1)}, s32[]{:S(2)}) async-start(s8[4325376]{0:T(1024)(128)(4,1)} %bitcast.172), calls=%async_computation.23 | async-start | bytes 8388608
  508.7 7.4 slice-start.1
  508.7 7.4 slice-start.3
  525.8 32.3 %copy-start.45 = (bf16[512,768]{1,0:T(8,128)(2,1)S(1)}, bf16[512,768]{1,0:T(8,128)(2,1)}, u32[]{:S(2)}) copy-start(bf16[512,768]{1,0:T(8,128)(2,1)} %reduce-scatter.7.cloned.1.call-done) | copy-start | bytes 2359300
  560.5 116.2 %reduce-scatter.13.cloned.1.call-start = ((), (), s32[]{:S(2)}) async-start(), calls=%async_computation.18 | async-start | bytes 5898240 | tf_op jit(solution)/shard_map/reduce_scatter | solution.py:938
  561.6 3.8 copy-start.25
  565.6 11.9 %copy-start.56 = (s32[1024,2]{0,1:T(2,128)S(1)}, s32[1024,2]{0,1:T(2,128)}, u32[]{:S(2)}) copy-start(s32[1024,2]{0,1:T(2,128)} %param.15) | copy-start | bytes 24580
  568.5 9.0 all-to-all-start.3
  571.8 254.7 %reduce-scatter.15.cloned.1.call-start = ((), (), s32[]{:S(2)}) async-start(), calls=%async_computation.19 | async-start | bytes 3932160 | tf_op jit(solution)/shard_map/reduce_scatter | solution.py:1075
  577.7 4.2 copy-start.23
  577.7 4.2 copy-start.26
  577.7 4.2 copy-start.31
  577.7 8.5 slice-start.4
  582.0 4.3 slice-start.5
  668.2 5.2 copy-start.50
  668.2 5.2 copy-start.51
  668.2 6.0 copy-start.36
  668.2 6.0 copy-start.37
  668.2 143.9 %all-to-all-start.2 = ((bf16[8,512,768]{2,1,0:T(8,128)(2,1)}), bf16[8,512,768]{2,1,0:T(8,128)(2,1)}, u32[]{:S(2)}, u32[]{:S(2)}) async-start(bf16[8,512,768]{2,1,0:T(8,128)(2,1)} %bitcast.44), calls=%async_computation.4 | async-start | bytes 12582912 | tf_op jit(solution)/shard_map/all_to_all | solution.py:935
  673.1 166.5 %reduce-scatter.17.cloned.1.call-start = ((), (), s32[]{:S(2)}) async-start(), calls=%async_computation.20 | async-start | bytes 3932160 | tf_op jit(solution)/shard_map/reduce_scatter | solution.py:1075
  760.8 6.0 copy-start.57
  760.8 6.0 copy-start.58
  760.9 6.2 copy-start.68
  760.9 7.9 copy-start.42
  770.4 41.7 %copy-start.54 = (s32[8,1,1024]{2,0,1:T(8,128)S(1)}, s32[8,1,1024]{2,0,1:T(8,128)}, u32[]{:S(2)}) copy-start(s32[8,1,1024]{2,0,1:T(8,128)} %copy.113) | copy-start | bytes 98308
  813.4 11.7 %copy-start.30 = (f32[1024,768]{1,0:T(8,128)S(1)}, f32[1024,768]{1,0:T(8,128)}, u32[]{:S(2)}) copy-start(f32[1024,768]{1,0:T(8,128)} %get-tuple-element.175) | copy-start | bytes 9437188
  825.1 14.5 %copy-start.44 = (bf16[512,768]{1,0:T(8,128)(2,1)S(1)}, bf16[512,768]{1,0:T(8,128)(2,1)}, u32[]{:S(2)}) copy-start(bf16[512,768]{1,0:T(8,128)(2,1)} %slice.238) | copy-start | bytes 2359300
  825.1 14.5 %copy-start.64 = (f32[1024]{0:T(1024)S(1)}, f32[1024]{0:T(1024)}, u32[]{:S(2)}) copy-start(f32[1024]{0:T(1024)} %copy-done.63) | copy-start | bytes 12292
  825.1 14.5 %copy-start.67 = (f32[768]{0:T(1024)S(1)}, f32[768]{0:T(1024)}, u32[]{:S(2)}) copy-start(f32[768]{0:T(1024)} %param.17) | copy-start | bytes 9220
  826.6 28.2 %copy-start.55 = (f32[6144]{0:T(1024)S(1)}, f32[6144]{0:T(1024)}, u32[]{:S(2)}) copy-start(f32[6144]{0:T(1024)} %reshape.601) | copy-start | bytes 73732
  864.3 55.0 %copy-start.61 = (f32[1024]{0:T(1024)S(1)}, f32[1024]{0:T(1024)}, u32[]{:S(2)}) copy-start(f32[1024]{0:T(1024)} %copy-done.60) | copy-start | bytes 12292
  916.2 3.8 copy-start.28
  (27 other events, 56.6 us)
Sparse Core Ops, SparseCore 0:
  11.5 67.1 all-gather.6
  88.1 42.7 all-gather.8
  132.6 116.7 all-gather.10
  251.5 62.9 all-gather.12
  316.0 63.3 all-gather.14
  388.3 78.3 reduce-scatter.6
  469.9 88.1 reduce-scatter.8
  561.1 55.4 reduce-scatter.10
  619.6 57.0 reduce-scatter.12
  679.5 50.5 reduce-scatter.14
  756.3 83.2 reduce-scatter.16

commit v7 on v6

--- a/solution.py
+++ b/solution.py
@@ -187,14 +187,16 @@
     mid = rest.astype(BF16)
     return hi, mid, (rest - mid.astype(F32)).astype(BF16)
 
-def bwd_kernel(scale, info, q_ref, do_ref, o_ref, lse_ref, k_ref, v_ref, t_ref, b_ref,
-               dq_ref, dkv_ref, dd_ref,
-               e_scr, db_scr, qa, da, ka, va, qt, dot_t, dkt, dvt):
+def bwd_kernel(scale, cont, info, q_ref, do_ref, o_ref, lse_ref, k_ref, v_ref, table_ref, *refs):
+    if cont:
+        prev_ref, dq_ref, dkv_ref, dd_ref, e_scr, qa, da, ka, va, qt, dot_t, dkt, dvt, db_scr = refs
+    else:
+        dq_ref, dkv_ref, dd_ref, e_scr, qa, da, ka, va, qt, dot_t, dkt, dvt = refs
+    table = table_ref.at[0]
     h = pl.program_id(0)
     dp = info[5]
     n, keys = q_ref.shape[0], k_ref.shape[0]
     half = h % 2
-    t_scr, b_scr = t_ref.at[0], b_ref.at[0]
     base = pl.multiple_of(64 * half, 64)
     other = 64 - 64 * half
 
@@ -254,47 +256,49 @@
         dq = lax.fori_loop(0, key_tiles, step, jnp.zeros((QT, 128), F32))
         dq_ref[rows, :] = jnp.where(own_n, dq * scale, dq_ref[rows, :].astype(F32)).astype(BF16)
 
-    for j in range(2):
+    for j in range(KT // QT):
+        if cont:
+            def where(t):
+                return (pl.ds(QT * j, QT), pl.ds(pl.multiple_of(t * KT, KT), KT))
+            def put(t, ds):
+                db_scr[where(t)] = ds
+            tile(QT * j, PROMPT // KT + 1, lambda t: table[where(t)], put)
+            continue
         shift = PROMPT - KT * dp - QT * j + RUN
         def part(t, x, shift=shift):
             return (slice(None), pl.ds(pl.multiple_of(t * KT + shift - 128 * x, 128), KT))
         def bias(t):
-            return jnp.concatenate([t_scr[part(t, x)] for x in range(QT // 128)], axis=0)
+            return jnp.concatenate([table[part(t, x)] for x in range(QT // 128)], axis=0)
         def add(t, ds):
             for x in range(QT // 128):
                 e_scr[part(t, x)] += ds[128 * x:128 * x + 128, :]
         tile(QT * j, dp + 1, bias, add)
-    for j in range(2):
-        def where(t):
-            return (pl.ds(QT * j, QT), pl.ds(pl.multiple_of(t * KT, KT), KT))
-        def put(t, ds):
-            db_scr[where(t)] = ds
-        tile(KT + QT * j, PROMPT // KT + 1, lambda t: b_scr[where(t)], put)
-
-    lane = lax.broadcasted_iota(jnp.int32, (ROWS, 128), 1)
-    sub = lax.broadcasted_iota(jnp.int32, (ROWS, 128), 0)
-    for s in range(4):
-        start, end = info[s], info[s + 1]
-        turn = start % 128
-        def fold(g, _):
-            at = pl.ds(pl.multiple_of(ROWS * g, ROWS), ROWS)
-            first = start - turn + RUN - 128 * (g // (128 // ROWS))
-            to = pl.ds(pl.multiple_of(ROWS * (g % (128 // ROWS)), ROWS), ROWS)
-            mine = (sub + ROWS * g >= start) & (sub + ROWS * g < end)
-            before = jnp.zeros((ROWS, 128), F32)
-            for b in range(PROMPT // 128 + 1):
-                if b < PROMPT // 128:
-                    turned = pltpu.roll(jnp.where(mine, db_scr[at, 128 * b:128 * b + 128], 0.0), turn, 1)
-                else:
-                    turned = jnp.zeros((ROWS, 128), F32)
-                e_scr[to, pl.ds(pl.multiple_of(first + 128 * b, 128), 128)] += jnp.where(lane >= turn, turned, before)
-                before = turned
-            return 0
-        lax.fori_loop(start // ROWS, (end + ROWS - 1) // ROWS, fold, 0)
-    for i in range(KT // 128):
-        first = PROMPT + RUN - 128 * i
-        e_scr[:, first:first + KT] += db_scr[128 * i:128 * i + 128, PROMPT:]
-    width = t_ref.shape[2]
+
+    if cont:
+        lane = lax.broadcasted_iota(jnp.int32, (ROWS, 128), 1)
+        sub = lax.broadcasted_iota(jnp.int32, (ROWS, 128), 0)
+        for s in range(4):
+            start, end = info[s], info[s + 1]
+            turn = start % 128
+            def fold(g, _):
+                at = pl.ds(pl.multiple_of(ROWS * g, ROWS), ROWS)
+                first = start - turn + RUN - 128 * (g // (128 // ROWS))
+                to = pl.ds(pl.multiple_of(ROWS * (g % (128 // ROWS)), ROWS), ROWS)
+                mine = (sub + ROWS * g >= start) & (sub + ROWS * g < end)
+                before = jnp.zeros((ROWS, 128), F32)
+                for b in range(PROMPT // 128 + 1):
+                    if b < PROMPT // 128:
+                        turned = pltpu.roll(jnp.where(mine, db_scr[at, 128 * b:128 * b + 128], 0.0), turn, 1)
+                    else:
+                        turned = jnp.zeros((ROWS, 128), F32)
+                    e_scr[to, pl.ds(pl.multiple_of(first + 128 * b, 128), 128)] += jnp.where(lane >= turn, turned, before)
+                    before = turned
+                return 0
+            lax.fori_loop(start // ROWS, (end + ROWS - 1) // ROWS, fold, 0)
+        for i in range(KT // 128):
+            first = PROMPT + RUN - 128 * i
+            e_scr[:, first:first + KT] += db_scr[128 * i:128 * i + 128, PROMPT:]
+    width = e_scr.shape[1]
     acc = e_scr[0:8, :]
     for a in range(1, 16):
         acc = acc + pltpu.roll(e_scr[8 * a:8 * a + 8, :], width - 8 * a, 1)
@@ -305,39 +309,46 @@
 
     @pl.when(half == 1)
     def _():
-        dkv_ref[:, :128] = (dkt[...] * scale).T.astype(BF16)
-        dkv_ref[:, 128:] = dvt[...].T.astype(BF16)
-
-def attention_backward(info, projected, do, o32, lse, keys_values, tables, part):
-    n = projected.shape[0]
+        for at, total in ((0, dkt[...] * scale), (128, dvt[...])):
+            total = total.T
+            if cont:
+                dkv_ref[:PROMPT, at:at + 128] = (total[:PROMPT] + prev_ref[:, at:at + 128].astype(F32)).astype(BF16)
+                dkv_ref[PROMPT:, at:at + 128] = total[PROMPT:].astype(BF16)
+            else:
+                dkv_ref[:, at:at + 128] = total.astype(BF16)
+
+def attention_backward(info, projected, do, o32, lse, keys_values, tables, part, cont, prev):
     keys, columns = keys_values.shape
     heads = columns // 128
     wide = tables[0].shape[2]
     first = part * heads // 2
-    own = pl.BlockSpec((n, 128), lambda h, *_: (0, h // 2))
-    shifted = pl.BlockSpec((n, 128), lambda h, *_: (0, first + h // 2))
-    cols = PROMPT + KT
+    own = pl.BlockSpec((KT, 128), lambda h, *_: (0, h // 2))
+    table = tables[int(cont)]
+    before = [pl.BlockSpec((PROMPT, 256), lambda h, *_: (0, h // 2))] if cont else []
+    scores = [pltpu.VMEM((KT, PROMPT + KT), F32)] if cont else []
     return pl.pallas_call(
-        functools.partial(bwd_kernel, 64 ** -0.5),
+        functools.partial(bwd_kernel, 64 ** -0.5, cont),
         grid_spec=pltpu.PrefetchScalarGridSpec(
             num_scalar_prefetch=1, grid=(heads,),
-            in_specs=[shifted, shifted, own, pl.BlockSpec((n, 128), lambda h, *_: (0, 0)),
+            in_specs=[pl.BlockSpec((KT, 128), lambda h, *_: (int(cont), first + h // 2)),
+                      pl.BlockSpec((KT, 128), lambda h, *_: (0, first + h // 2)),
+                      own, pl.BlockSpec((KT, 128), lambda h, *_: (0, 0)),
                       pl.BlockSpec((keys, 128), lambda h, *_: (0, h // 2 * 2)),
                       pl.BlockSpec((keys, 128), lambda h, *_: (0, h // 2 * 2 + 1)),
-                      *[pl.BlockSpec((1,) + t.shape[1:], lambda h, *_: (h, 0, 0)) for t in tables]],
+                      pl.BlockSpec((1,) + table.shape[1:], lambda h, *_: (h, 0, 0))] + before,
             out_specs=[own, pl.BlockSpec((keys, 256), lambda h, *_: (0, h // 2)),
                        pl.BlockSpec((1, 1, wide), lambda h, *_: (h, 0, 0))],
-            scratch_shapes=[pltpu.VMEM((128, wide), F32), pltpu.VMEM((KT, cols), F32),
-                            pltpu.VMEM((n, 128), BF16), pltpu.VMEM((n, 128), BF16),
+            scratch_shapes=[pltpu.VMEM((128, wide), F32),
+                            pltpu.VMEM((KT, 128), BF16), pltpu.VMEM((KT, 128), BF16),
                             pltpu.VMEM((keys, 128), BF16), pltpu.VMEM((keys, 128), BF16),
-                            pltpu.VMEM((128, n), BF16), pltpu.VMEM((128, n), BF16),
-                            pltpu.VMEM((128, keys), F32), pltpu.VMEM((128, keys), F32)]),
-        out_shape=[jax.ShapeDtypeStruct((n, heads * 64), BF16), jax.ShapeDtypeStruct((keys, columns), BF16),
+                            pltpu.VMEM((128, KT), BF16), pltpu.VMEM((128, KT), BF16),
+                            pltpu.VMEM((128, keys), F32), pltpu.VMEM((128, keys), F32)] + scores),
+        out_shape=[jax.ShapeDtypeStruct((KT, heads * 64), BF16), jax.ShapeDtypeStruct((keys, columns), BF16),
                    jax.ShapeDtypeStruct((heads, 1, wide), F32)],
         compiler_params=pltpu.CompilerParams(vmem_limit_bytes=60 << 20),
         cost_estimate=EARLY,
         name="attention_backward",
-    )(info, projected, do, o32, lse, keys_values, keys_values, *tables)
+    )(info, projected, do, o32, lse, keys_values, keys_values, table, *([prev] if cont else []))
 
 def info_of(ids, dp):
     starts = jnp.sum((ids[None, :] < jnp.arange(5)[:, None]).astype(jnp.int32), axis=1)
@@ -458,13 +469,45 @@
     )(info, spread, *arrays)
 
 
-def collect_kernel(place_ref, x_ref, out_ref):
+def window_kernel(sources, info, later, x_ref, y_ref, *out_refs):
+    d = pl.program_id(0)
+    send = out_refs[0].shape[0]
+    count = info[sources + d]
+    row = lax.broadcasted_iota(jnp.int32, (send, send), 0)
+    column = lax.broadcasted_iota(jnp.int32, (send, send), 1)
+    pick = jnp.where(column == row - count, 1.0, 0.0).astype(BF16)
+    moved = dot(pick, y_ref[pl.ds(pl.multiple_of(later[d], 16), send), :]).astype(BF16)
+    rows = x_ref[pl.ds(pl.multiple_of(info[d], 16), send), :]
+    first = lax.broadcasted_iota(jnp.int32, rows.shape, 0) < count
+    both = jnp.where(first, rows, moved)
+    at = 0
+    for out_ref in out_refs:
+        out_ref[...] = both[:, at:at + out_ref.shape[1]]
+        at += out_ref.shape[1]
+
+
+def windows_of(info, later, x, y, sources, send, columns):
+    whole = pl.BlockSpec(x.shape, lambda d, *_: (0, 0))
+    return pl.pallas_call(
+        functools.partial(window_kernel, sources),
+        grid_spec=pltpu.PrefetchScalarGridSpec(
+            num_scalar_prefetch=2, grid=(sources,), in_specs=[whole, whole],
+            out_specs=[pl.BlockSpec((send, n), lambda d, *_: (d, 0)) for n in columns]),
+        out_shape=[jax.ShapeDtypeStruct((sources * send, n), BF16) for n in columns],
+        compiler_params=pltpu.CompilerParams(vmem_limit_bytes=40 << 20),
+        cost_estimate=EARLY,
+        name="window_rows",
+    )(info, later, x, y)
+
+
+def collect_kernel(place_ref, *refs):
+    x_refs, out_ref = refs[:-1], refs[-1]
     tokens = place_ref.shape[0]
     lane = lax.broadcasted_iota(jnp.int32, (tokens, 128), 1)
     put = jnp.concatenate(
-        [jnp.where(place_ref[...] == lane + 128 * b, 1.0, 0.0).astype(BF16) for b in range(x_ref.shape[0] // 128)],
+        [jnp.where(place_ref[...] == lane + 128 * b, 1.0, 0.0).astype(BF16) for b in range(x_refs[0].shape[0] // 128)],
         axis=1)
-    total = dot(put, x_ref[...])
+    total = jnp.concatenate([dot(put, x_ref[...]) for x_ref in x_refs], axis=1)
 
     @pl.when(pl.program_id(0) == 0)
     def _():
@@ -477,18 +520,18 @@
 
 def collect(place, returned, send):
     experts, tokens = place.shape
-    width = returned.shape[1]
+    width = sum(x.shape[1] for x in returned)
     spread = jnp.broadcast_to(place.reshape(-1, 1), (experts * tokens, 128))
     return pl.pallas_call(
         collect_kernel,
         grid=(experts,),
-        in_specs=[pl.BlockSpec((tokens, 128), lambda e: (e, 0)), pl.BlockSpec((send, width), lambda e: (e, 0))],
+        in_specs=[pl.BlockSpec((tokens, 128), lambda e: (e, 0)), *[pl.BlockSpec((send, x.shape[1]), lambda e: (e, 0)) for x in returned]],
         out_specs=pl.BlockSpec((tokens, width), lambda e: (0, 0)),
         out_shape=jax.ShapeDtypeStruct((tokens, width), F32),
         compiler_params=pltpu.CompilerParams(vmem_limit_bytes=40 << 20),
         cost_estimate=EARLY,
         name="collect_rows",
-    )(spread, returned)
+    )(spread, *returned)
 
 
 def gelu_and_slope(v):
@@ -498,8 +541,10 @@
     return v * half, half + 0.5 * v * (1.0 - t * t) * (c * (1.0 + 3 * 0.044715 * (v * v)))
 
 
-def expert_kernel(sources, info, expert, x_ref, o_ref, c_ref, r_ref, wi_ref, wd_ref,
-                  gi_ref, eo_ref, gg_ref, dwi_ref, dwd_ref, geo, gate, eo, gi, dwi, dwd):
+def expert_kernel(sources, more, info, expert, x_ref, o_ref, c_ref, r_ref, wi_ref, wd_ref, *refs):
+    if more:
+        dwi_before, dwd_before, *refs = refs
+    gi_ref, eo_ref, gg_ref, dwi_ref, dwd_ref, geo, gate, eo, gi, dwi, dwd = refs
     f = pl.program_id(0)
     last = pl.num_programs(0) - 1
     tiles = (info[2 * sources] + MOE_ROWS - 1) // MOE_ROWS
@@ -529,8 +574,8 @@
             return 0
         lax.fori_loop(0, tiles, start, 0)
 
-    dwi[...] = jnp.zeros_like(dwi)
-    dwd[...] = jnp.zeros_like(dwd)
+    dwi[...] = dwi_before[...].astype(F32) if more else jnp.zeros_like(dwi)
+    dwd[...] = dwd_before[...].astype(F32) if more else jnp.zeros_like(dwd)
 
     def tile(i, _):
         at = rows_of(i)
@@ -564,18 +609,18 @@
         lax.fori_loop(0, tiles, finish, 0)
 
 
-def expert_layer(info, expert, x, other, cot, router, w_in, w_down, sources):
+def expert_layer(info, expert, x, other, cot, router, w_in, w_down, sources, before):
     room, width = x.shape
     hidden = w_in.shape[1]
     whole = lambda a: pl.BlockSpec(a.shape, lambda f, *_: (0, 0))
     fixed = lambda cols: pl.BlockSpec((room, cols), lambda f, *_: (0, 0))
     return pl.pallas_call(
-        functools.partial(expert_kernel, sources),
+        functools.partial(expert_kernel, sources, bool(before)),
         grid_spec=pltpu.PrefetchScalarGridSpec(
             num_scalar_prefetch=2, grid=(hidden // FF_TILE,),
             in_specs=[whole(x), whole(other), whole(cot), whole(router),
-                      pl.BlockSpec((width, FF_TILE), lambda f, *_: (0, f)),
-                      pl.BlockSpec((FF_TILE, width), lambda f, *_: (f, 0))],
+                      *([pl.BlockSpec((width, FF_TILE), lambda f, *_: (0, f)),
+                         pl.BlockSpec((FF_TILE, width), lambda f, *_: (f, 0))] * (2 if before else 1))],
             out_specs=[fixed(width), fixed(width), fixed(128),
                        pl.BlockSpec((width, FF_TILE), lambda f, *_: (0, f)),
                        pl.BlockSpec((FF_TILE, width), lambda f, *_: (f, 0))],
@@ -588,7 +633,7 @@
         compiler_params=pltpu.CompilerParams(vmem_limit_bytes=63 << 20),
         cost_estimate=EARLY,
         name="expert_layer",
-    )(info, expert, x, other, cot, router, w_in, w_down)
+    )(info, expert, x, other, cot, router, w_in, w_down, *before)
 
 
 MESH_ID = pl.DeviceIdType.MESH
@@ -883,7 +928,7 @@
     return own_place, half_plan(place, other, 0), half_plan(place, other, 1)
 
 
-def expert_half(all_tokens, all_cotangents, number, half, router, w_in, w_down, send):
+def expert_half(all_tokens, all_cotangents, number, half, router, w_in, w_down, send, before):
     info, place, other_hot = half
     sources, tokens = place.shape
     room = (4 * tokens + 16 * sources + send + MOE_ROWS - 1) // MOE_ROWS * MOE_ROWS
@@ -891,7 +936,7 @@
     (packed_cot,) = pack(info, place, [all_cotangents], room, 2, number)
     packed, packed_other = pack(info, place, [all_tokens, other_hot], room)
     grad_rows, mixed_rows, grad_gate, grad_w_in, grad_w_down = expert_layer(
-        info, expert[None], packed, packed_other, packed_cot, router, w_in[0], w_down[0], sources
+        info, expert[None], packed, packed_other, packed_cot, router, w_in[0], w_down[0], sources, before
     )
     grad_all, gate_all = unpack(info, place, [grad_rows, grad_gate], [jnp.bfloat16, jnp.float32], send)
     gate_all = jnp.sum(gate_all[:, :3], axis=1).reshape(sources, tokens)
@@ -906,50 +951,25 @@
     send = 2 * rows * top // experts_total
     wide_router = jnp.pad(router, ((0, 0), (0, 128 - experts_total)))
     tokens = [lax.all_gather(x, "expert", axis=0, tiled=True) for x in normed_halves]
-    first = expert_half(tokens[0], all_cotangents, 0, halves[0], wide_router, w_in, w_down, send)
+    first = expert_half(tokens[0], all_cotangents, 0, halves[0], wide_router, w_in, w_down, send, ())
     grad_own = [lax.psum_scatter(first[0], "expert", scatter_dimension=0, tiled=True)]
     tokens[1], all_cotangents, _ = lax.optimization_barrier((tokens[1], all_cotangents, first))
-    second = expert_half(tokens[1], all_cotangents, 1, halves[1], wide_router, w_in, w_down, send)
+    second = expert_half(tokens[1], all_cotangents, 1, halves[1], wide_router, w_in, w_down, send, first[3:])
     grad_later, grad_own[0] = lax.optimization_barrier((second[0], grad_own[0]))
     grad_own.append(lax.psum_scatter(grad_later, "expert", scatter_dimension=0, tiled=True))
-    gate_all = jnp.concatenate([first[1], second[1]], axis=1)
-    gate_own = lax.all_to_all(gate_all, "expert", split_axis=0, concat_axis=0, tiled=True)
-    info, later = halves[0][0], halves[1][0]
-    sources = halves[0][1].shape[0]
-    shifted = jnp.pad(second[2], ((send, 0), (0, 0)))
-    row = jnp.arange(send)[:, None]
-    windows = jnp.concatenate([
-        jnp.where(
-            row < info[sources + d],
-            lax.dynamic_slice_in_dim(first[2], info[d], send, 0),
-            lax.dynamic_slice_in_dim(shifted, later[d] + send - info[sources + d], send, 0),
-        )
-        for d in range(sources)
-    ], axis=0)
-    grad_w_in, grad_w_down = first[3] + second[3], first[4] + second[4]
-    grad_own = jnp.concatenate(grad_own, axis=0)
-    normed_ffn = jnp.concatenate(normed_halves, axis=0)
-    windows, grad_w_in, grad_w_down, grad_own = lax.optimization_barrier(
-        (windows, grad_w_in, grad_w_down, grad_own)
-    )
-    mixed = (lax.all_to_all(windows, "expert", split_axis=0, concat_axis=0, tiled=True), own_place)
-    expert_parts = (
-        lax.psum_scatter(grad_w_in[None], "dp", scatter_dimension=1, tiled=True),
-        lax.psum_scatter(grad_w_down[None], "dp", scatter_dimension=1, tiled=True),
-    )
+    gate_own = [lax.all_to_all(x[1], "expert", split_axis=0, concat_axis=0, tiled=True) for x in (first, second)]
+    windows = windows_of(halves[0][0], halves[1][0], first[2], second[2], own_place.shape[0], send, (256, first[2].shape[1] - 256))
+    return grad_own, gate_own, windows, second[3], second[4]
+
+
+def router_back(normed_ffn, expert_ids, router, gate_own):
     logits = jnp.dot(normed_ffn, router, preferred_element_type=jnp.float32)
-    picks = expert_ids[:, :, None] == jnp.arange(experts_total)[None, None, :]
+    picks = expert_ids[:, :, None] == jnp.arange(router.shape[1])[None, None, :]
     chosen = jnp.sum(jnp.where(picks, logits[:, None, :], 0.0), axis=2)
     gates = jax.nn.softmax(chosen, axis=-1)
     grad_gates = jnp.sum(jnp.where(picks, gate_own.T[:, None, :], 0.0), axis=2)
     grad_chosen = gates * (grad_gates - jnp.sum(gates * grad_gates, axis=-1, keepdims=True))
-    grad_logits = jnp.sum(jnp.where(picks, grad_chosen[:, :, None], 0.0), axis=1).astype(
-        jnp.bfloat16
-    )
-    grad_normed_ffn = grad_own.astype(jnp.float32) + jnp.dot(
-        grad_logits, router.T, preferred_element_type=jnp.float32
-    )
-    return mixed, grad_logits, grad_normed_ffn, expert_parts
+    return jnp.sum(jnp.where(picks, grad_chosen[:, :, None], 0.0), axis=1).astype(jnp.bfloat16)
 
 
 def per_device(
@@ -1039,50 +1059,82 @@
                 normed_halves[0], all_cotangents = lax.optimization_barrier((normed_halves[0], all_cotangents))
             gathered[g], normed_halves[0] = lax.optimization_barrier((gathered[g], normed_halves[0]))
     after_attention(1)
-    exact = [jnp.concatenate([results[g, 0][0], results[g, 1][0]], axis=0) for g in range(parts)]
-    log_total = [jnp.concatenate([results[g, 0][1], results[g, 1][1]], axis=0) for g in range(parts)]
     attended = jnp.concatenate(attended_halves, axis=0)
     middle = jnp.concatenate(middles, axis=0)
     normed_ffn = jnp.concatenate(normed_halves, axis=0)
+    cut = [slice(0, KT), slice(KT, rows)]
     if few_experts:
-        mixed, grad_logits, grad_normed_ffn, expert_parts = exchange_tokens(
+        grad_own, gate_own, windows, *grad_w = exchange_tokens(
             normed_halves, all_cotangents, plan, expert_ids, whole_router, w_in, w_down
         )
     else:
         mixed, grad_logits, grad_normed_ffn, expert_parts = exchange_pairs(
             normed_ffn, middle, cotangent, expert_ids, priority, whole_router, w_in, w_down
         )
+        grad_logits = [grad_logits[at] for at in cut]
+        grad_normed_halves = [grad_normed_ffn[at] for at in cut]
+    if few_experts:
+        grad_logits, grad_normed_halves = [None, None], [None, None]
     grad_out = cotangent.astype(jnp.float32)
-    grad_router = jnp.dot(normed_ffn.T, grad_logits, preferred_element_type=jnp.float32)
-    _, ffn_norm_back = jax.vjp(normed, middle, gain_ffn)
-    grad_middle_part, grad_gain_ffn = ffn_norm_back(grad_normed_ffn)
-    grad_middle = grad_out + grad_middle_part
-    grad_branch = grad_middle.astype(jnp.bfloat16)
+    grad_middles, grad_branches, grad_gain_ffn = [], [], 0.0
+    grad_queries, grad_kv, grad_lines = {}, [None] * parts, 0.0
+    grad_prompts, grad_conts = [], []
+    for c in (0, 1):
+        if few_experts:
+            if c:
+                grad_own[1], gate_own[1], grad_kv = lax.optimization_barrier((grad_own[1], gate_own[1], grad_kv))
+                grad_own[1], windows, grad_w = lax.optimization_barrier((grad_own[1], windows, grad_w))
+                mixed = [lax.all_to_all(x, "expert", split_axis=0, concat_axis=0, tiled=True) for x in windows]
+                expert_in = lax.psum_scatter(grad_w[0][None], "dp", scatter_dimension=1, tiled=True)
+            grad_logits[c] = router_back(normed_halves[c], expert_ids[cut[c]], whole_router, gate_own[c])
+            grad_normed_halves[c] = grad_own[c].astype(jnp.float32) + jnp.dot(
+                grad_logits[c], whole_router.T, preferred_element_type=jnp.float32
+            )
+        _, ffn_norm_back = jax.vjp(normed, middles[c], gain_ffn)
+        grad_middle_part, grad_gain = ffn_norm_back(grad_normed_halves[c])
+        grad_gain_ffn = grad_gain_ffn + grad_gain
+        grad_middles.append(grad_out[cut[c]] + grad_middle_part)
+        grad_branches.append(grad_middles[c].astype(jnp.bfloat16))
+        grad_attended = jnp.dot(
+            grad_branches[c], whole_out.T, preferred_element_type=jnp.float32
+        ).astype(jnp.bfloat16)
+        lines = []
+        for g in range(parts):
+            if c and g and few_experts:
+                grad_attended, expert_in, grad_queries[g - 1, c] = lax.optimization_barrier(
+                    (grad_attended, expert_in, grad_queries[g - 1, c])
+                )
+            out, total = results[g, c]
+            grad_queries[g, c], grad_kv[g], line = attention_backward(
+                info, projected, grad_attended, out, total, keys_values[g] if c else gathered[g], tables[g], g, bool(c),
+                grad_kv[g],
+            )
+            lines.append(line)
+            if c:
+                if g:
+                    grad_kv[g], grad_prompts[-1] = lax.optimization_barrier((grad_kv[g], grad_prompts[-1]))
+                    if few_experts:
+                        grad_kv[g], mixed[0] = lax.optimization_barrier((grad_kv[g], mixed[0]))
+                grad_prompts.append(lax.psum_scatter(grad_kv[g][:PROMPT], "dp", scatter_dimension=0, tiled=True))
+                grad_conts.append(grad_kv[g][PROMPT:])
+        grad_lines = grad_lines + jnp.concatenate(lines, axis=0)
+    if few_experts:
+        grad_prompts[-1], grad_down = lax.optimization_barrier((grad_prompts[-1], grad_w[1]))
+        expert_parts = (expert_in, lax.psum_scatter(grad_down[None], "dp", scatter_dimension=1, tiled=True))
+    grad_middle = jnp.concatenate(grad_middles, axis=0)
+    grad_branch = jnp.concatenate(grad_branches, axis=0)
+    grad_router = jnp.dot(
+        normed_ffn.T, jnp.concatenate(grad_logits, axis=0), preferred_element_type=jnp.float32
+    )
     grad_out_weight = jnp.dot(attended.T, grad_branch, preferred_element_type=jnp.float32)
-    grad_attended = jnp.dot(
-        grad_branch, whole_out.T, preferred_element_type=jnp.float32
-    ).astype(jnp.bfloat16)
-    grad_queries, grad_prompts, grad_conts, grad_lines = [], [], [], []
-    for g in range(parts):
-        if g:
-            grad_attended, expert_parts, grad_queries[-1] = lax.optimization_barrier(
-                (grad_attended, expert_parts, grad_queries[-1])
-            )
-        grad_query, grad_kv, lines = attention_backward(
-            info, projected, grad_attended, exact[g], log_total[g], keys_values[g], tables[g], g
-        )
-        grad_queries.append(grad_query)
-        grad_prompts.append(lax.psum_scatter(grad_kv[:PROMPT], "dp", scatter_dimension=0, tiled=True))
-        grad_conts.append(grad_kv[PROMPT:])
-        grad_lines.append(lines)
-    mixed, middle, grad_queries[-1] = lax.optimization_barrier((mixed, middle, grad_queries[-1]))
+    mixed, middle, grad_prompts[-1] = lax.optimization_barrier((mixed, middle, grad_prompts[-1]))
     if few_experts:
-        returned, own_place = mixed
-        mixed = collect(own_place, returned, returned.shape[0] // own_place.shape[0])
+        mixed = collect(plan[0], mixed, mixed[0].shape[0] // plan[0].shape[0])
     output = (middle + mixed).astype(jnp.bfloat16)
-    grad_table = table_grad(jnp.concatenate(grad_lines, axis=0), rel_table.shape[0])
+    grad_table = table_grad(grad_lines, rel_table.shape[0])
     grad_projected = jnp.concatenate(
-        grad_queries + [jnp.concatenate([a, b], axis=0) for a, b in zip(grad_prompts, grad_conts)], axis=1
+        [jnp.concatenate([grad_queries[g, 0], grad_queries[g, 1]], axis=0) for g in range(parts)]
+        + [jnp.concatenate([a, b], axis=0) for a, b in zip(grad_prompts, grad_conts)], axis=1
     )
     grad_normed_attn = jnp.dot(grad_projected, whole_qkv.T, preferred_element_type=jnp.float32)
     grad_qkv = jnp.dot(normed_attn.T, grad_projected, preferred_element_type=jnp.float32)

time: 942 us -> 985 us (1.046)
  Pallas kernels: 502 us -> 556 us
  other arithmetic: 83.2 us -> 50.6 us
  starting transfers between devices: 19.5 us -> 46.4 us
  between operations: 39.8 us -> 15.4 us
    reduce_scatter x4, waiting for transfers between devices: 14.3 us -> 82 us  [the longest x2 71.3 us: per_device(): lax.psum_scatter(grad_kv[g][:PROMPT], 'dp', scatter_dimension=0, tiled=True)]
    all_to_all x2 -> x4, waiting for transfers between devices: 45.6 us -> 12.7 us  [the longest x2 7.18 us: per_device(): lax.all_to_all(x, 'expert', split_axis=0, concat_axis=0, tiled=True)]
    pallas_call x4 -> x7, Pallas kernels: 254 us -> 287 us  [the longest x4 175 us: attention_backward(): pl.pallas_call(functools.partial(bwd_kernel, 64 ** (-0.5), cont), grid_sp...]
    reduce_scatter x1, waiting for transfers between devices: 30.9 us -> 0.02 us  [exchange_tokens(): lax.psum_scatter(grad_later, 'expert', scatter_dimension=0, tiled=True)]
    all_to_all x2 -> x4, starting transfers between devices: 8.24 us -> 35.3 us  [the longest x2 27.1 us: exchange_tokens(): lax.all_to_all(x[1], 'expert', split_axis=0, concat_axis=0, tiled=True)]
    pallas_call x1, Pallas kernels: 51.9 us -> 75 us  [dense_sum(): pl.pallas_call(dense_kernel, in_specs=[vmem] * 3, out_specs=[vmem] * 2, o...]
    add x3 -> x1, other arithmetic: 17.5 us -> 0.01 us  [per_device(): grad_gain_ffn = grad_gain_ffn + grad_gain]
    unnamed x160 -> x157, local copies, waits for them, and re-layouts: 34.3 us -> 43.9 us
  transfers between devices with their start and end apart: 15 -> 17, of which waited for: 9 -> 9; matrix products, arithmetic and copies ran while one was open for 12% -> 12% of each run, Pallas kernels for 48% -> 57%
where the time goes in v7:
time: 985 us; the launch traced here: 974 us
  Pallas kernels  556 us (56%)
  waiting for transfers between devices  162 us (16%)
  local copies, waits for them, and re-layouts  68.9 us (7%)
  matrix products  59.6 us (6%)
  other arithmetic  50.6 us (5%)
  starting transfers between devices  46.4 us (5%)
  blocking collectives  15.6 us (2%)
  between operations  15.4 us (2%)
    pallas_call x4, Pallas kernels, attention_backward(): pl.pallas_call(functools.partial(bwd_kernel, 64 ** (-0.5), cont), grid_sp...  175 us
    pallas_call x2, Pallas kernels, expert_layer(): pl.pallas_call(functools.partial(expert_kernel, sources, bool(before)), g...  104 us
    pallas_call x4, Pallas kernels, attention_forward(): pl.pallas_call(functools.partial(fwd_kernel, scale2, cont), grid_spec=plt...  97.3 us
    pallas_call x1, Pallas kernels, dense_sum(): pl.pallas_call(dense_kernel, in_specs=[vmem] * 3, out_specs=[vmem] * 2, o...  75 us
    reduce_scatter x2, waiting for transfers between devices, per_device(): lax.psum_scatter(grad_kv[g][:PROMPT], 'dp', scatter_dimension=0, tiled=True)  71.3 us
    pallas_call x2, Pallas kernels, bias_tables(): pl.pallas_call(bias_kernel, grid_spec=pltpu.PrefetchScalarGridSpec(num_sc...  44.9 us
    unnamed x157, local copies, waits for them, and re-layouts  43.9 us
    all_gather x1, waiting for transfers between devices, per_device(): lax.all_gather(late_cotangent, 'expert', axis=0, tiled=True)  36.8 us
  transfers between devices with their start and end apart: 17, of which 9 were waited for; matrix products, arithmetic and copies ran while one was open for 12% of the time, Pallas kernels for 57%

profile of v7, /device:TPU:0, one launch (start us, length us, event | category | flops | bytes accessed | tf_op | source)
XLA Modules:
  0.0 973.9 jit_solution(17863287035743593763)
XLA Ops:
  12.1 15.6 %all-gather = s32[8192,2]{0,1:T(2,128)S(1)} all-gather(s32[1024,2]{0,1:T(2,128)S(1)} %multiply_add_fusion), channel_id=2, replica_groups=mesh['dp'=4,'expert'=8] {'expert'}, dimensions={0}, use_global_device_ids=true | all-gather | bytes 73728 | tf_op jit(solution)/shard_map/all_gather | solution.py:921
  30.2 4.6 all-to-all-start
  37.6 3.1 multiply_reduce_fusion
  41.0 22.4 %bias_tables.2 = (f32[6,128,2816]{2,1,0:T(8,128)S(1)}, f32[6,512,2560]{2,1,0:T(8,128)}) custom-call(s32[6]{0:T(128)S(1)} %pad_add_fusion.info, f32[12,8,2816]{2,1,0:T(8,128)S(1)} %broadcast_select_fusion.base_ref, s32[512,128]{1,0:T(8,128)S(1)} %broadcast_in_dim.109.row_start), custom_call_target="tpu_custom_call" | custom-call | flops 1048576 | bytes 1048576 | tf_op jit(solution)/shard_map/bias_tables/pallas_call | solution.py:106
  63.4 3.4 copy-done
  67.3 2.4 fusion.9
  71.7 6.9 all-gather.7.cloned.1.call-done
  78.6 6.4 convolution_convert_fusion.q_ref
  88.3 22.5 %bias_tables.3 = (f32[6,128,2816]{2,1,0:T(8,128)S(1)}, f32[6,512,2560]{2,1,0:T(8,128)}) custom-call(s32[6]{0:T(128)S(1)} %pad_add_fusion.info, f32[12,8,2816]{2,1,0:T(8,128)S(1)} %broadcast_select_fusion.base_ref, s32[512,128]{1,0:T(8,128)S(1)} %broadcast_in_dim.109.row_start), custom_call_target="tpu_custom_call" | custom-call | flops 1048576 | bytes 1048576 | tf_op jit(solution)/shard_map/bias_tables/pallas_call | solution.py:106
  110.8 3.4 copy-done.1
  114.2 16.8 %all-gather.9.cloned.1.call-done.k_ref.v_ref = bf16[2048,768]{1,0:T(8,128)(2,1)} async-done(((bf16[512,768]{1,0:T(8,128)(2,1)}), bf16[2048,768]{1,0:T(8,128)(2,1)}) %all-gather.9.cloned.1.call-update) | async-done | bytes 3145744 | tf_op jit(solution)/shard_map/all_gather | solution.py:1023
  132.9 4.7 all-to-all-start.1
  137.6 3.3 convert_element_type.310
  140.9 12.8 %attention_forward.4 = (f32[512,384]{1,0:T(8,128)}, f32[512,128]{1,0:T(8,128)}) custom-call(s32[6]{0:T(128)} %copy-done.21, bf16[1024,2304]{1,0:T(8,128)(2,1)} %copy-done.26, bf16[2048,768]{1,0:T(8,128)(2,1)} %all-gather.9.cloned.1.call-done.k_ref.v_ref, bf16[2048,768]{1,0:T(8,128)(2,1)} %all-gather.9.cloned.1.call-done.k_ref.v_ref, f32[6,128,2816]{2,1,0:T(8,128)} %copy-done), custom_call_target="tpu_custom_call" | custom-call | flops 1048576 | bytes 1048576 | tf_op jit(solution)/shard_map/attention_forward/pallas_call | solution.py:168
  153.7 4.1 pad_maximum_fusion.k_ref.v_ref
  157.7 35.8 %attention_forward.5 = (f32[512,384]{1,0:T(8,128)}, f32[512,128]{1,0:T(8,128)}) custom-call(s32[6]{0:T(128)} %copy-done.21, bf16[1024,2304]{1,0:T(8,128)(2,1)} %copy-done.26, bf16[2560,768]{1,0:T(8,128)(2,1)} %pad_maximum_fusion.k_ref.v_ref, bf16[2560,768]{1,0:T(8,128)(2,1)} %pad_maximum_fusion.k_ref.v_ref, f32[6,512,2560]{2,1,0:T(8,128)} %get-tuple-element.137.table_ref), custom_call_target="tpu_custom_call" | custom-call | flops 1048576 | bytes 1048576 | tf_op jit(solution)/shard_map/attention_forward/pallas_call | solution.py:168
  193.5 12.5 %attention_forward.6 = (f32[512,384]{1,0:T(8,128)}, f32[512,128]{1,0:T(8,128)}) custom-call(s32[6]{0:T(128)} %copy-done.21, bf16[1024,2304]{1,0:T(8,128)(2,1)} %copy-done.26, bf16[2048,768]{1,0:T(8,128)(2,1)} %bitcast.16.k_ref.v_ref, bf16[2048,768]{1,0:T(8,128)(2,1)} %bitcast.16.k_ref.v_ref, f32[6,128,2816]{2,1,0:T(8,128)} %copy-done.1), custom_call_target="tpu_custom_call" | custom-call | flops 1048576 | bytes 1048576 | tf_op jit(solution)/shard_map/attention_forward/pallas_call | solution.py:168
  207.4 3.0 multiply_reduce_fusion.9
  212.6 36.8 %all-gather.11.cloned.1.call-done.refs_0_ = bf16[8192,768]{1,0:T(8,128)(2,1)} async-done(((bf16[1024,768]{1,0:T(8,128)(2,1)}), bf16[8192,768]{1,0:T(8,128)(2,1)}) %all-gather.11.cloned.1.call-update) | async-done | bytes 12582928 | tf_op jit(solution)/shard_map/all_gather | solution.py:1031
  249.6 4.3 pad_maximum_fusion.1.k_ref.v_ref
  253.8 36.2 %attention_forward.7 = (f32[512,384]{1,0:T(8,128)}, f32[512,128]{1,0:T(8,128)}) custom-call(s32[6]{0:T(128)} %copy-done.21, bf16[1024,2304]{1,0:T(8,128)(2,1)} %copy-done.26, bf16[2560,768]{1,0:T(8,128)(2,1)} %pad_maximum_fusion.1.k_ref.v_ref, bf16[2560,768]{1,0:T(8,128)(2,1)} %pad_maximum_fusion.1.k_ref.v_ref, f32[6,512,2560]{2,1,0:T(8,128)} %get-tuple-element.150.table_ref), custom_call_target="tpu_custom_call" | custom-call | flops 1048576 | bytes 1048576 | tf_op jit(solution)/shard_map/attention_forward/pallas_call | solution.py:168
  292.0 2.7 multiply_reduce_fusion.8
  298.1 7.5 pack_tokens.5.c_ref
  307.7 6.3 all-gather.15.cloned.1.call-done.refs_0_
  313.9 2.8 copy-done.5
  316.7 4.7 pack_tokens.4
  324.3 51.4 %expert_layer.2 = (bf16[2816,768]{1,0:T(8,128)(2,1)}, bf16[2816,768]{1,0:T(8,128)(2,1)}, bf16[2816,128]{1,0:T(8,128)(2,1)}, bf16[768,3072]{1,0:T(8,128)(2,1)}, bf16[3072,768]{1,0:T(8,128)(2,1)}) custom-call(s32[17]{0:T(128)} %copy-done.22, s32[1]{0:T(128)} %bitcast.15.expert, bf16[2816,768]{1,0:T(8,128)(2,1)} %copy-done.6, bf16[2816,128]{1,0:T(8,128)(2,1)} %copy-done.18, ...), custom_call_target="tpu_custom_call" | custom-call | flops 1048576 | bytes 1048576 | tf_op jit(solution)/shard_map/expert_layer/pallas_call | solution.py:617
  376.4 2.2 copy-done.8
  379.7 7.8 unpack_tokens.2
  389.5 7.8 pack_tokens.7.c_ref
  399.3 4.7 pack_tokens.6
  406.8 52.6 %expert_layer.3 = (bf16[2816,768]{1,0:T(8,128)(2,1)}, bf16[2816,768]{1,0:T(8,128)(2,1)}, bf16[2816,128]{1,0:T(8,128)(2,1)}, bf16[768,3072]{1,0:T(8,128)(2,1)}, bf16[3072,768]{1,0:T(8,128)(2,1)}) custom-call(s32[17]{0:T(128)} %copy-done.24, s32[1]{0:T(128)} %bitcast.15.expert, bf16[2816,768]{1,0:T(8,128)(2,1)} %copy-done.10, bf16[2816,128]{1,0:T(8,128)(2,1)} %copy-done.17, ...), custom_call_target="tpu_custom_call" | custom-call | flops 1048576 | bytes 1048576 | tf_op jit(solution)/shard_map/expert_layer/pallas_call | solution.py:617
  460.0 2.3 copy-done.7
  463.4 7.7 unpack_tokens.3
  471.2 3.5 convert_element_type.337
  477.2 21.9 %all-to-all-start.3 = ((f32[8,1,512]{2,1,0:T(1,128)}), f32[8,1,512]{2,1,0:T(1,128)S(1)}, u32[]{:S(2)}, u32[]{:S(2)}) async-start(f32[8,1,512]{2,1,0:T(1,128)} %bitcast.21), calls=%async_computation.5 | async-start | bytes 32768 | tf_op jit(solution)/shard_map/all_to_all | solution.py:960
  500.3 2.2 copy-done.9
  502.6 7.7 window_rows.1
  510.3 2.1 copy-done.11
  513.7 5.2 all-to-all-start.2
  519.2 5.6 all-to-all-done.2
  528.3 3.2 convolution_convert_fusion.2.do_ref
  531.5 20.4 %attention_backward.4 = (bf16[512,384]{1,0:T(8,128)(2,1)}, bf16[2048,768]{1,0:T(8,128)(2,1)}, f32[6,1,2816]{2,1,0:T(1,128)}) custom-call(s32[6]{0:T(128)} %copy-done.21, bf16[1024,2304]{1,0:T(8,128)(2,1)} %copy-done.26, bf16[512,768]{1,0:T(8,128)(2,1)} %convolution_convert_fusion.2.do_ref, f32[512,384]{1,0:T(8,128)} %get-tuple-element.142.o_ref, ...), custom_call_target="tpu_custom_call" | custom-call | flops 1048576 | bytes 1048576 | tf_op jit(solution)/shard_map/attention_backward/pallas_call | solution.py:329
  552.0 20.6 %attention_backward.5 = (bf16[512,384]{1,0:T(8,128)(2,1)}, bf16[2048,768]{1,0:T(8,128)(2,1)}, f32[6,1,2816]{2,1,0:T(1,128)}) custom-call(s32[6]{0:T(128)} %copy-done.21, bf16[1024,2304]{1,0:T(8,128)(2,1)} %copy-done.26, bf16[512,768]{1,0:T(8,128)(2,1)} %convolution_convert_fusion.2.do_ref, f32[512,384]{1,0:T(8,128)} %get-tuple-element.179.o_ref, ...), custom_call_target="tpu_custom_call" | custom-call | flops 1048576 | bytes 1048576 | tf_op jit(solution)/shard_map/attention_backward/pallas_call | solution.py:329
  575.1 2.1 multiply_reduce_fusion.4
  578.8 3.2 convolution_convert_fusion.1.do_ref
  582.1 67.0 %attention_backward.6 = (bf16[512,384]{1,0:T(8,128)(2,1)}, bf16[2560,768]{1,0:T(8,128)(2,1)}, f32[6,1,2816]{2,1,0:T(1,128)}) custom-call(s32[6]{0:T(128)} %copy-done.21, bf16[1024,2304]{1,0:T(8,128)(2,1)} %copy-done.26, bf16[512,768]{1,0:T(8,128)(2,1)} %convolution_convert_fusion.1.do_ref, f32[512,384]{1,0:T(8,128)} %get-tuple-element.140.o_ref, ...), custom_call_target="tpu_custom_call" | custom-call | flops 1048576 | bytes 1048576 | tf_op jit(solution)/shard_map/attention_backward/pallas_call | solution.py:329
  649.0 3.8 slice.149
  652.8 3.6 all-to-all-start.4
  656.7 10.6 %reduce-scatter.11.cloned.1.call-done = bf16[1,192,3072]{2,1,0:T(8,128)(2,1)} async-done(((bf16[1,768,3072]{2,1,0:T(8,128)(2,1)}), bf16[1,192,3072]{2,1,0:T(8,128)(2,1)}) %reduce-scatter.11.cloned.1.call-update) | async-done | bytes 1179664 | tf_op jit(solution)/shard_map/reduce_scatter | solution.py:1088
  667.3 67.1 %attention_backward.7 = (bf16[512,384]{1,0:T(8,128)(2,1)}, bf16[2560,768]{1,0:T(8,128)(2,1)}, f32[6,1,2816]{2,1,0:T(1,128)}) custom-call(s32[6]{0:T(128)} %copy-done.21, bf16[1024,2304]{1,0:T(8,128)(2,1)} %copy-done.26, bf16[512,768]{1,0:T(8,128)(2,1)} %convolution_convert_fusion.1.do_ref, f32[512,384]{1,0:T(8,128)} %get-tuple-element.151.o_ref, ...), custom_call_target="tpu_custom_call" | custom-call | flops 1048576 | bytes 1048576 | tf_op jit(solution)/shard_map/attention_backward/pallas_call | solution.py:329
  735.7 3.8 slice.150
  739.4 4.6 all-to-all-start.5
  744.1 70.2 %reduce-scatter.15.cloned.1.call-done = bf16[512,768]{1,0:T(8,128)(2,1)} async-done(((bf16[2048,768]{1,0:T(8,128)(2,1)}), bf16[512,768]{1,0:T(8,128)(2,1)}) %reduce-scatter.15.cloned.1.call-update) | async-done | bytes 786448 | tf_op jit(solution)/shard_map/reduce_scatter | solution.py:1118
  814.4 3.8 pad_maximum_fusion.2
  821.9 4.9 fusion.13
  826.7 2.1 slice.152
  831.0 7.2 all-to-all-done.5
  838.2 13.2 %multiply_reduce_fusion.1 = (f32[768]{0:T(1024)S(1)}, f32[1024]{0:T(1024)S(1)}, f32[1024,768]{1,0:T(8,128)}) fusion(bf16[1024,768]{1,0:T(8,128)(2,1)} %param.13, f32[1024]{0:T(1024)S(1)} %copy-done.67, f32[768]{0:T(1024)S(1)} %copy-done.70, bf16[768,3200]{1,0:T(8,128)(2,1)} %all-gather.7.cloned.1.call-done, bf16[512,768]{1,0:T(8,128)(2,1)} %slice.152, ...), kind=kOutput, calls=%fused_computation.12 | convolution fusion | flops 3667130624 | bytes 12990464 | tf_op jit(solution)/shard_map/dot_general | solution.py:1139
  851.5 14.6 %fusion.55 = f32[768,2304]{1,0:T(8,128)} fusion(bf16[1024,768]{1,0:T(8,128)(2,1)} %param.13, f32[768]{0:T(1024)S(1)} %copy-done.70, f32[1024]{0:T(1024)S(1)} %copy-done.67, bf16[512,768]{1,0:T(8,128)(2,1)} %slice.152, bf16[512,768]{1,0:T(8,128)(2,1)} %reduce-scatter.15.cloned.1.call-done, bf16[512,768]{1,0:T(8,128)(2,1)S(1)} %copy-done.48, ...), kind=kOutput, calls=%fused_computation.81 | convolution fusion | flops 3664773120 | bytes 13376512 | tf_op jit(solution)/shard_map/dot_general | solution.py:1140
  866.1 75.0 %dense_sum.1 = (f32[24,3072]{1,0:T(8,128)S(1)}, f32[64,128]{1,0:T(8,128)S(1)}) custom-call(f32[16,2,24,2304]{3,2,1,0:T(8,128)} %bitcast.168, f32[16,2,24,768]{3,2,1,0:T(8,128)S(1)} %bitcast.160, f32[64,128]{1,0:T(8,128)S(1)} %pad_bitcast_fusion.s_ref), custom_call_target="tpu_custom_call" | custom-call | tf_op jit(solution)/shard_map/dense_sum/pallas_call | solution.py:754
  944.3 11.6 %collect_rows.1 = f32[1024,768]{1,0:T(8,128)S(1)} custom-call(s32[8192,128]{1,0:T(8,128)S(1)} %broadcast_in_dim.209.place_ref, bf16[4096,256]{1,0:T(8,128)(2,1)S(1)} %bitcast.158, bf16[4096,512]{1,0:T(8,128)(2,1)} %bitcast.28.refs_1_), custom_call_target="tpu_custom_call" | custom-call | flops 1048576 | bytes 1048576 | tf_op jit(solution)/shard_map/collect_rows/pallas_call | solution.py:525
  961.7 2.5 fusion.4
  964.2 2.8 convert_element_type.365
  (287 shorter events, 71.0 us)
Async XLA Ops:
  7.2 29.6 %copy-start.65 = (s32[1,512]{1,0:T(1,128)S(1)}, s32[1,512]{1,0:T(1,128)}, u32[]{:S(2)}) copy-start(s32[1,512]{1,0:T(1,128)} %param.14) | copy-start | bytes 6148
  7.2 30.0 %copy-start.68 = (f32[31,12]{0,1:T(8,128)S(1)}, f32[31,12]{0,1:T(8,128)}, u32[]{:S(2)}) copy-start(f32[31,12]{0,1:T(8,128)} %param.19) | copy-start | bytes 4468
  7.2 71.4 %all-gather.7.cloned.1.call-start = ((), (), s32[]{:S(2)}) async-start(), calls=%async_computation.12 | async-start | bytes 5068800 | tf_op jit(solution)/shard_map/all_gather | solution.py:1006
  30.2 40.9 %all-to-all-start = ((s32[8,1,1024]{2,1,0:T(1,128)}), s32[8,1,1024]{2,1,0:T(1,128)S(1)}, u32[]{:S(2)}, u32[]{:S(2)}) async-start(s32[8,1,1024]{2,1,0:T(1,128)} %copy.81), calls=%async_computation | async-start | bytes 65536 | tf_op jit(solution)/shard_map/all_to_all | solution.py:927
  34.8 96.2 %all-gather.9.cloned.1.call-start = ((), (), s32[]{:S(2)}) async-start(), calls=%async_computation.13 | async-start | bytes 3932160 | tf_op jit(solution)/shard_map/all_gather | solution.py:1023
  37.0 51.3 %copy-start.21 = (s32[6]{0:T(128)}, s32[6]{0:T(128)S(1)}, u32[]{:S(2)}) copy-start(s32[6]{0:T(128)S(1)} %pad_add_fusion.info) | copy-start | bytes 76
  37.6 29.2 %copy-start.31 = (bf16[1024,768]{1,0:T(8,128)(2,1)S(1)}, bf16[1024,768]{1,0:T(8,128)(2,1)}, u32[]{:S(2)}) copy-start(bf16[1024,768]{1,0:T(8,128)(2,1)} %param.13) | copy-start | bytes 4718596
  40.9 37.7 %copy-start.69 = (f32[768]{0:T(1024)S(1)}, f32[768]{0:T(1024)}, u32[]{:S(2)}) copy-start(f32[768]{0:T(1024)} %param.17) | copy-start | bytes 9220
  63.4 3.4 copy-start
  67.2 17.8 %copy-start.62 = (f32[1024]{0:T(1024)}, f32[1024]{0:T(1024)S(1)}, u32[]{:S(2)}) copy-start(f32[1024]{0:T(1024)S(1)} %multiply_reduce_fusion.3) | copy-start | bytes 12292
  67.3 17.8 %copy-start.66 = (f32[1024]{0:T(1024)}, f32[1024]{0:T(1024)S(1)}, u32[]{:S(2)}) copy-start(f32[1024]{0:T(1024)S(1)} %fusion.118) | copy-start | bytes 12292
  71.1 242.9 %copy-start.22 = (s32[17]{0:T(128)}, s32[17]{0:T(128)S(1)}, u32[]{:S(2)}) copy-start(s32[17]{0:T(128)S(1)} %get-tuple-element.153.info) | copy-start | bytes 208
  71.1 326.2 %copy-start.24 = (s32[17]{0:T(128)}, s32[17]{0:T(128)S(1)}, u32[]{:S(2)}) copy-start(s32[17]{0:T(128)S(1)} %get-tuple-element.121.info.later) | copy-start | bytes 208
  85.1 3.0 copy-start.26
  88.0 161.4 %all-gather.11.cloned.1.call-start = ((), (), s32[]{:S(2)}) async-start(), calls=%async_computation.14 | async-start | bytes 14155776 | tf_op jit(solution)/shard_map/all_gather | solution.py:1031
  110.8 3.4 copy-start.1
  132.9 60.6 %all-to-all-start.1 = ((bf16[4,512,768]{2,1,0:T(8,128)(2,1)}), bf16[4,512,768]{2,1,0:T(8,128)(2,1)}, u32[]{:S(2)}, u32[]{:S(2)}) async-start(bf16[4,512,768]{2,1,0:T(8,128)(2,1)} %broadcast_in_dim.194), calls=%async_computation.1 | async-start | bytes 6291456 | tf_op jit(solution)/shard_map/all_to_all | solution.py:1027
  137.6 176.4 %all-gather.15.cloned.1.call-start = ((), (), s32[]{:S(2)}) async-start(), calls=%async_computation.16 | async-start | bytes 7077888 | tf_op jit(solution)/shard_map/all_gather | solution.py:953
  140.9 12.8 %copy-start.44 = (bf16[512,768]{1,0:T(8,128)(2,1)S(1)}, bf16[512,768]{1,0:T(8,128)(2,1)}, u32[]{:S(2)}) copy-start(bf16[512,768]{1,0:T(8,128)(2,1)} %get-tuple-element.301) | copy-start | bytes 2359300
  193.5 13.8 %copy-start.41 = (f32[512,384]{1,0:T(8,128)S(1)}, f32[512,384]{1,0:T(8,128)}, u32[]{:S(2)}) copy-start(f32[512,384]{1,0:T(8,128)} %get-tuple-element.142.o_ref) | copy-start | bytes 2359300
  207.3 3.1 copy-start.51
  207.4 3.1 copy-start.52
  207.4 4.2 copy-start.55
  207.4 42.1 %copy-start.45 = (f32[512,384]{1,0:T(8,128)S(1)}, f32[512,384]{1,0:T(8,128)}, u32[]{:S(2)}) copy-start(f32[512,384]{1,0:T(8,128)} %get-tuple-element.140.o_ref) | copy-start | bytes 2359300
  210.4 39.2 %copy-start.43 = (bf16[512,768]{1,0:T(8,128)(2,1)S(1)}, bf16[512,768]{1,0:T(8,128)(2,1)}, u32[]{:S(2)}) copy-start(bf16[512,768]{1,0:T(8,128)(2,1)} %get-tuple-element.300) | copy-start | bytes 2359300
  249.4 140.0 %all-gather.13.cloned.1.call-start = ((), (), s32[]{:S(2)}) async-start(), calls=%async_computation.15 | async-start | bytes 7077888 | tf_op jit(solution)/shard_map/all_gather | solution.py:953
  249.6 41.7 %copy-start.53 = (bf16[512,384]{1,0:T(8,128)(2,1)}, bf16[512,384]{1,0:T(8,128)(2,1)S(1)}, u32[]{:S(2)}) copy-start(bf16[512,384]{1,0:T(8,128)(2,1)S(1)} %convert.12) | copy-start | bytes 1179652
  297.0 174.2 %reduce-scatter.7.cloned.1.call-start = ((), (), s32[]{:S(2)}) async-start(), calls=%async_computation.17 | async-start | bytes 7077888 | tf_op jit(solution)/shard_map/reduce_scatter | solution.py:955
  324.3 52.0 %copy-start.23 = (s32[17]{0:T(128)S(1)}, s32[17]{0:T(128)}, u32[]{:S(2)}) copy-start(s32[17]{0:T(128)} %copy-done.22) | copy-start | bytes 208
  388.9 183.7 %reduce-scatter.9.cloned.1.call-start = ((), (), s32[]{:S(2)}) async-start(), calls=%async_computation.18 | async-start | bytes 7077888 | tf_op jit(solution)/shard_map/reduce_scatter | solution.py:959
  389.4 9.8 %copy-start.4 = (bf16[4096,768]{1,0:T(8,128)(2,1)S(1)}, bf16[4096,768]{1,0:T(8,128)(2,1)}, u32[]{:S(2)}) copy-start(bf16[4096,768]{1,0:T(8,128)(2,1)} %all-gather.13.cloned.1.call-done.refs_0_) | copy-start | bytes 18874372
  389.5 9.8 %copy-start.12 = (bf16[4096,128]{1,0:T(8,128)(2,1)S(1)}, bf16[4096,128]{1,0:T(8,128)(2,1)}, u32[]{:S(2)}) copy-start(bf16[4096,128]{1,0:T(8,128)(2,1)} %get-tuple-element.166.refs_1_) | copy-start | bytes 3145732
  406.8 53.2 %copy-start.25 = (s32[17]{0:T(128)S(1)}, s32[17]{0:T(128)}, u32[]{:S(2)}) copy-start(s32[17]{0:T(128)} %copy-done.24) | copy-start | bytes 208
  471.2 3.5 copy-start.64
  471.2 3.5 copy-start.36
  471.2 4.7 copy-start.16
  477.2 36.6 %all-to-all-start.3 = ((f32[8,1,512]{2,1,0:T(1,128)}), f32[8,1,512]{2,1,0:T(1,128)S(1)}, u32[]{:S(2)}, u32[]{:S(2)}) async-start(f32[8,1,512]{2,1,0:T(1,128)} %bitcast.21), calls=%async_computation.5 | async-start | bytes 32768 | tf_op jit(solution)/shard_map/all_to_all | solution.py:960
  502.6 22.3 %copy-start.28 = (f32[512,768]{1,0:T(8,128)S(1)}, f32[512,768]{1,0:T(8,128)}, u32[]{:S(2)}) copy-start(f32[512,768]{1,0:T(8,128)} %copy-done.27) | copy-start | bytes 4718596
  502.6 22.3 %copy-start.47 = (bf16[512,768]{1,0:T(8,128)(2,1)S(1)}, bf16[512,768]{1,0:T(8,128)(2,1)}, u32[]{:S(2)}) copy-start(bf16[512,768]{1,0:T(8,128)(2,1)} %reduce-scatter.7.cloned.1.call-done) | copy-start | bytes 2359300
  513.7 11.0 %all-to-all-start.2 = ((f32[8,1,512]{2,1,0:T(1,128)}), f32[8,1,512]{2,1,0:T(1,128)S(1)}, u32[]{:S(2)}, u32[]{:S(2)}) async-start(f32[8,1,512]{2,1,0:T(1,128)} %bitcast.20), calls=%async_computation.4 | async-start | bytes 32768 | tf_op jit(solution)/shard_map/all_to_all | solution.py:960
  518.9 148.5 %reduce-scatter.11.cloned.1.call-start = ((), (), s32[]{:S(2)}) async-start(), calls=%async_computation.19 | async-start | bytes 5898240 | tf_op jit(solution)/shard_map/reduce_scatter | solution.py:1088
  528.3 23.6 %copy-start.49 = (bf16[512,768]{1,0:T(8,128)(2,1)}, bf16[512,768]{1,0:T(8,128)(2,1)S(1)}, u32[]{:S(2)}) copy-start(bf16[512,768]{1,0:T(8,128)(2,1)S(1)} %get-tuple-element.292) | copy-start | bytes 2359300
  572.6 163.1 %reduce-scatter.13.cloned.1.call-start = ((), (), s32[]{:S(2)}) async-start(), calls=%async_computation.20 | async-start | bytes 3932160 | tf_op jit(solution)/shard_map/reduce_scatter | solution.py:1118
  578.8 70.2 %copy-start.50 = (bf16[512,768]{1,0:T(8,128)(2,1)}, bf16[512,768]{1,0:T(8,128)(2,1)S(1)}, u32[]{:S(2)}) copy-start(bf16[512,768]{1,0:T(8,128)(2,1)S(1)} %get-tuple-element.288) | copy-start | bytes 2359300
  652.8 82.8 %all-to-all-start.4 = ((bf16[8,512,256]{2,1,0:T(8,128)(2,1)}), bf16[8,512,256]{2,1,0:T(8,128)(2,1)S(1)}, u32[]{:S(2)}, u32[]{:S(2)}) async-start(bf16[8,512,256]{2,1,0:T(8,128)(2,1)} %bitcast.161), calls=%async_computation.8 | async-start | bytes 4194304 | tf_op jit(solution)/shard_map/all_to_all | solution.py:1087
  656.4 157.8 %reduce-scatter.15.cloned.1.call-start = ((), (), s32[]{:S(2)}) async-start(), calls=%async_computation.21 | async-start | bytes 3932160 | tf_op jit(solution)/shard_map/reduce_scatter | solution.py:1118
  739.4 98.7 %all-to-all-start.5 = ((bf16[8,512,512]{2,1,0:T(8,128)(2,1)}), bf16[8,512,512]{2,1,0:T(8,128)(2,1)}, u32[]{:S(2)}, u32[]{:S(2)}) async-start(bf16[8,512,512]{2,1,0:T(8,128)(2,1)} %bitcast.159), calls=%async_computation.9 | async-start | bytes 8388608 | tf_op jit(solution)/shard_map/all_to_all | solution.py:1087
  744.0 70.3 %copy-start.56 = (s32[8,1,1024]{2,0,1:T(8,128)S(1)}, s32[8,1,1024]{2,0,1:T(8,128)}, u32[]{:S(2)}) copy-start(s32[8,1,1024]{2,0,1:T(8,128)} %copy.141) | copy-start | bytes 98308
  744.1 220.1 %reduce-scatter.17.cloned.1.call-start = ((), (), s32[]{:S(2)}) async-start(), calls=%async_computation.22 | async-start | bytes 5898240 | tf_op jit(solution)/shard_map/reduce_scatter | solution.py:1123
  814.3 3.9 copy-start.59
  814.4 3.9 copy-start.58
  814.4 6.6 copy-start.38
  818.2 3.6 copy-start.60
  821.8 7.0 copy-start.61
  821.8 7.0 copy-start.57
  821.8 7.5 copy-start.46
  826.7 11.4 %copy-start.67 = (f32[1024]{0:T(1024)S(1)}, f32[1024]{0:T(1024)}, u32[]{:S(2)}) copy-start(f32[1024]{0:T(1024)} %copy-done.66) | copy-start | bytes 12292
  826.7 11.4 %copy-start.70 = (f32[768]{0:T(1024)S(1)}, f32[768]{0:T(1024)}, u32[]{:S(2)}) copy-start(f32[768]{0:T(1024)} %param.17) | copy-start | bytes 9220
  838.2 13.3 %copy-start.48 = (bf16[512,768]{1,0:T(8,128)(2,1)S(1)}, bf16[512,768]{1,0:T(8,128)(2,1)}, u32[]{:S(2)}) copy-start(bf16[512,768]{1,0:T(8,128)(2,1)} %slice.151) | copy-start | bytes 2359300
  851.5 14.6 %copy-start.13 = (f32[768,768]{1,0:T(8,128)S(1)}, f32[768,768]{1,0:T(8,128)}, u32[]{:S(2)}) copy-start(f32[768,768]{1,0:T(8,128)} %fusion.13) | copy-start | bytes 7077892
  944.3 12.2 %copy-start.63 = (f32[1024]{0:T(1024)S(1)}, f32[1024]{0:T(1024)}, u32[]{:S(2)}) copy-start(f32[1024]{0:T(1024)} %copy-done.62) | copy-start | bytes 12292
  944.3 13.5 %copy-start.35 = (f32[1024,768]{1,0:T(8,128)S(1)}, f32[1024,768]{1,0:T(8,128)}, u32[]{:S(2)}) copy-start(f32[1024,768]{1,0:T(8,128)} %pad_maximum_fusion.2) | copy-start | bytes 9437188
  957.8 2.9 copy-start.40
  957.8 3.9 copy-start.42
  (25 other events, 44.2 us)
Sparse Core Ops, SparseCore 0:
  11.5 67.1 all-gather.6
  88.2 42.7 all-gather.8
  132.7 116.7 all-gather.10
  250.9 62.9 all-gather.14
  315.4 63.3 all-gather.12
  389.0 78.3 reduce-scatter.6
  471.3 88.6 reduce-scatter.8
  572.7 94.5 reduce-scatter.10
  670.9 64.7 reduce-scatter.12
  739.6 74.6 reduce-scatter.14
  817.2 57.0 reduce-scatter.16

commit v8 on v7

--- a/solution.py
+++ b/solution.py
@@ -49,7 +49,7 @@
 RUN = 256
 EARLY = pl.CostEstimate(flops=1 << 20, bytes_accessed=1 << 20, transcendentals=0)
 PARTS = 2
-ROWS = 32
+ROWS = 64
 NT = (((1,), (1,)), ((), ()))
 NN = (((1,), (0,)), ((), ()))
 
@@ -285,14 +285,16 @@
                 first = start - turn + RUN - 128 * (g // (128 // ROWS))
                 to = pl.ds(pl.multiple_of(ROWS * (g % (128 // ROWS)), ROWS), ROWS)
                 mine = (sub + ROWS * g >= start) & (sub + ROWS * g < end)
+                window = (to, pl.ds(pl.multiple_of(first, 128), PROMPT + 128))
                 before = jnp.zeros((ROWS, 128), F32)
+                moved = []
                 for b in range(PROMPT // 128 + 1):
+                    turned = jnp.zeros((ROWS, 128), F32)
                     if b < PROMPT // 128:
                         turned = pltpu.roll(jnp.where(mine, db_scr[at, 128 * b:128 * b + 128], 0.0), turn, 1)
-                    else:
-                        turned = jnp.zeros((ROWS, 128), F32)
-                    e_scr[to, pl.ds(pl.multiple_of(first + 128 * b, 128), 128)] += jnp.where(lane >= turn, turned, before)
+                    moved.append(jnp.where(lane >= turn, turned, before))
                     before = turned
+                e_scr[window] += jnp.concatenate(moved, axis=1)
                 return 0
             lax.fori_loop(start // ROWS, (end + ROWS - 1) // ROWS, fold, 0)
         for i in range(KT // 128):
@@ -958,7 +960,7 @@
     grad_later, grad_own[0] = lax.optimization_barrier((second[0], grad_own[0]))
     grad_own.append(lax.psum_scatter(grad_later, "expert", scatter_dimension=0, tiled=True))
     gate_own = [lax.all_to_all(x[1], "expert", split_axis=0, concat_axis=0, tiled=True) for x in (first, second)]
-    windows = windows_of(halves[0][0], halves[1][0], first[2], second[2], own_place.shape[0], send, (256, first[2].shape[1] - 256))
+    windows = windows_of(halves[0][0], halves[1][0], first[2], second[2], own_place.shape[0], send, (first[2].shape[1],))
     return grad_own, gate_own, windows, second[3], second[4]
 
 
@@ -1113,8 +1115,6 @@
             if c:
                 if g:
                     grad_kv[g], grad_prompts[-1] = lax.optimization_barrier((grad_kv[g], grad_prompts[-1]))
-                    if few_experts:
-                        grad_kv[g], mixed[0] = lax.optimization_barrier((grad_kv[g], mixed[0]))
                 grad_prompts.append(lax.psum_scatter(grad_kv[g][:PROMPT], "dp", scatter_dimension=0, tiled=True))
                 grad_conts.append(grad_kv[g][PROMPT:])
         grad_lines = grad_lines + jnp.concatenate(lines, axis=0)
@@ -1127,7 +1127,8 @@
         normed_ffn.T, jnp.concatenate(grad_logits, axis=0), preferred_element_type=jnp.float32
     )
     grad_out_weight = jnp.dot(attended.T, grad_branch, preferred_element_type=jnp.float32)
-    mixed, middle, grad_prompts[-1] = lax.optimization_barrier((mixed, middle, grad_prompts[-1]))
+    last = (parts - 1, 1)
+    mixed, middle, grad_queries[last] = lax.optimization_barrier((mixed, middle, grad_queries[last]))
     if few_experts:
         mixed = collect(plan[0], mixed, mixed[0].shape[0] // plan[0].shape[0])
     output = (middle + mixed).astype(jnp.bfloat16)

time: 985 us -> 950 us (0.964)
  starting transfers between devices: 46.4 us -> 23.9 us
  Pallas kernels: 556 us -> 540 us
    pallas_call x1, Pallas kernels: 75 us -> 53.3 us  [dense_sum(): pl.pallas_call(dense_kernel, in_specs=[vmem] * 3, out_specs=[vmem] * 2, o...]
    pallas_call x2, Pallas kernels: 104 us -> 123 us  [expert_layer(): pl.pallas_call(functools.partial(expert_kernel, sources, bool(before)), g...]
    all_to_all x2, starting transfers between devices: 27.1 us -> 8.36 us  [exchange_tokens(): lax.all_to_all(x[1], 'expert', split_axis=0, concat_axis=0, tiled=True)]
    unnamed x157 -> x169, local copies, waits for them, and re-layouts: 43.9 us -> 44.9 us
  transfers between devices with their start and end apart: 17 -> 16, of which waited for: 9 -> 8; matrix products, arithmetic and copies ran while one was open for 12% -> 13% of each run, Pallas kernels for 57% -> 58%
where the time goes in v8:
time: 950 us; the launch traced here: 939 us
  Pallas kernels  540 us (57%)
  waiting for transfers between devices  165 us (17%)
  local copies, waits for them, and re-layouts  72.1 us (8%)
  matrix products  53.8 us (6%)
  other arithmetic  51.9 us (5%)
  starting transfers between devices  23.9 us (3%)
  blocking collectives  15.6 us (2%)
  between operations  15.4 us (2%)
    pallas_call x4, Pallas kernels, attention_backward(): pl.pallas_call(functools.partial(bwd_kernel, 64 ** (-0.5), cont), grid_sp...  167 us
    pallas_call x2, Pallas kernels, expert_layer(): pl.pallas_call(functools.partial(expert_kernel, sources, bool(before)), g...  123 us
    pallas_call x4, Pallas kernels, attention_forward(): pl.pallas_call(functools.partial(fwd_kernel, scale2, cont), grid_spec=plt...  97.3 us
    reduce_scatter x2, waiting for transfers between devices, per_device(): lax.psum_scatter(grad_kv[g][:PROMPT], 'dp', scatter_dimension=0, tiled=True)  74.1 us
    pallas_call x1, Pallas kernels, dense_sum(): pl.pallas_call(dense_kernel, in_specs=[vmem] * 3, out_specs=[vmem] * 2, o...  53.3 us
    unnamed x169, local copies, waits for them, and re-layouts  44.9 us
    pallas_call x2, Pallas kernels, bias_tables(): pl.pallas_call(bias_kernel, grid_spec=pltpu.PrefetchScalarGridSpec(num_sc...  39.5 us
    all_gather x1, waiting for transfers between devices, per_device(): lax.all_gather(late_cotangent, 'expert', axis=0, tiled=True)  35.4 us
  transfers between devices with their start and end apart: 16, of which 8 were waited for; matrix products, arithmetic and copies ran while one was open for 13% of the time, Pallas kernels for 58%

profile of v8, /device:TPU:0, one launch (start us, length us, event | category | flops | bytes accessed | tf_op | source)
XLA Modules:
  0.0 938.7 jit_solution(7806783612451171071)
XLA Ops:
  12.1 15.6 %all-gather = s32[8192,2]{0,1:T(2,128)S(1)} all-gather(s32[1024,2]{0,1:T(2,128)S(1)} %multiply_add_fusion), channel_id=2, replica_groups=mesh['dp'=4,'expert'=8] {'expert'}, dimensions={0}, use_global_device_ids=true | all-gather | bytes 73728 | tf_op jit(solution)/shard_map/all_gather | solution.py:923
  30.2 4.6 all-to-all-start
  37.6 3.1 multiply_reduce_fusion
  41.0 19.7 %bias_tables.2 = (f32[6,128,2816]{2,1,0:T(8,128)S(1)}, f32[6,512,2560]{2,1,0:T(8,128)}) custom-call(s32[6]{0:T(128)S(1)} %pad_add_fusion.info, f32[12,8,2816]{2,1,0:T(8,128)S(1)} %broadcast_select_fusion.base_ref, s32[512,128]{1,0:T(8,128)S(1)} %broadcast_in_dim.109.row_start), custom_call_target="tpu_custom_call" | custom-call | flops 1048576 | bytes 1048576 | tf_op jit(solution)/shard_map/bias_tables/pallas_call | solution.py:106
  60.7 3.4 copy-done
  64.6 2.4 fusion.9
  69.0 9.6 %all-gather.7.cloned.1.call-done = bf16[768,3200]{1,0:T(8,128)(2,1)} async-done(((bf16[24,3200]{1,0:T(8,128)(2,1)}), bf16[768,3200]{1,0:T(8,128)(2,1)}) %all-gather.7.cloned.1.call-update) | async-done | bytes 4915216 | tf_op jit(solution)/shard_map/all_gather | solution.py:1008
  78.6 6.4 convolution_convert_fusion.q_ref
  88.1 19.8 %bias_tables.3 = (f32[6,128,2816]{2,1,0:T(8,128)S(1)}, f32[6,512,2560]{2,1,0:T(8,128)}) custom-call(s32[6]{0:T(128)S(1)} %pad_add_fusion.info, f32[12,8,2816]{2,1,0:T(8,128)S(1)} %broadcast_select_fusion.base_ref, s32[512,128]{1,0:T(8,128)S(1)} %broadcast_in_dim.109.row_start), custom_call_target="tpu_custom_call" | custom-call | flops 1048576 | bytes 1048576 | tf_op jit(solution)/shard_map/bias_tables/pallas_call | solution.py:106
  107.9 3.4 copy-done.1
  111.3 19.7 %all-gather.9.cloned.1.call-done.k_ref.v_ref = bf16[2048,768]{1,0:T(8,128)(2,1)} async-done(((bf16[512,768]{1,0:T(8,128)(2,1)}), bf16[2048,768]{1,0:T(8,128)(2,1)}) %all-gather.9.cloned.1.call-update) | async-done | bytes 3145744 | tf_op jit(solution)/shard_map/all_gather | solution.py:1025
  132.9 4.7 all-to-all-start.1
  137.8 3.4 convert_element_type.334
  141.2 13.0 %attention_forward.4 = (f32[512,384]{1,0:T(8,128)}, f32[512,128]{1,0:T(8,128)}) custom-call(s32[6]{0:T(128)} %copy-done.19, bf16[1024,2304]{1,0:T(8,128)(2,1)} %copy-done.24, bf16[2048,768]{1,0:T(8,128)(2,1)} %all-gather.9.cloned.1.call-done.k_ref.v_ref, bf16[2048,768]{1,0:T(8,128)(2,1)} %all-gather.9.cloned.1.call-done.k_ref.v_ref, f32[6,128,2816]{2,1,0:T(8,128)} %copy-done), custom_call_target="tpu_custom_call" | custom-call | flops 1048576 | bytes 1048576 | tf_op jit(solution)/shard_map/attention_forward/pallas_call | solution.py:168
  154.2 4.0 pad_maximum_fusion.k_ref.v_ref
  158.2 35.7 %attention_forward.5 = (f32[512,384]{1,0:T(8,128)}, f32[512,128]{1,0:T(8,128)}) custom-call(s32[6]{0:T(128)} %copy-done.19, bf16[1024,2304]{1,0:T(8,128)(2,1)} %copy-done.24, bf16[2560,768]{1,0:T(8,128)(2,1)} %pad_maximum_fusion.k_ref.v_ref, bf16[2560,768]{1,0:T(8,128)(2,1)} %pad_maximum_fusion.k_ref.v_ref, f32[6,512,2560]{2,1,0:T(8,128)} %get-tuple-element.131.table_ref), custom_call_target="tpu_custom_call" | custom-call | flops 1048576 | bytes 1048576 | tf_op jit(solution)/shard_map/attention_forward/pallas_call | solution.py:168
  193.9 12.4 %attention_forward.6 = (f32[512,384]{1,0:T(8,128)}, f32[512,128]{1,0:T(8,128)}) custom-call(s32[6]{0:T(128)} %copy-done.19, bf16[1024,2304]{1,0:T(8,128)(2,1)} %copy-done.24, bf16[2048,768]{1,0:T(8,128)(2,1)} %bitcast.16.k_ref.v_ref, bf16[2048,768]{1,0:T(8,128)(2,1)} %bitcast.16.k_ref.v_ref, f32[6,128,2816]{2,1,0:T(8,128)} %copy-done.1), custom_call_target="tpu_custom_call" | custom-call | flops 1048576 | bytes 1048576 | tf_op jit(solution)/shard_map/attention_forward/pallas_call | solution.py:168
  209.1 2.8 multiply_reduce_fusion.9
  214.0 35.4 %all-gather.11.cloned.1.call-done.refs_0_ = bf16[8192,768]{1,0:T(8,128)(2,1)} async-done(((bf16[1024,768]{1,0:T(8,128)(2,1)}), bf16[8192,768]{1,0:T(8,128)(2,1)}) %all-gather.11.cloned.1.call-update) | async-done | bytes 12582928 | tf_op jit(solution)/shard_map/all_gather | solution.py:1033
  249.6 4.2 pad_maximum_fusion.1.k_ref.v_ref
  253.7 36.2 %attention_forward.7 = (f32[512,384]{1,0:T(8,128)}, f32[512,128]{1,0:T(8,128)}) custom-call(s32[6]{0:T(128)} %copy-done.19, bf16[1024,2304]{1,0:T(8,128)(2,1)} %copy-done.24, bf16[2560,768]{1,0:T(8,128)(2,1)} %pad_maximum_fusion.1.k_ref.v_ref, bf16[2560,768]{1,0:T(8,128)(2,1)} %pad_maximum_fusion.1.k_ref.v_ref, f32[6,512,2560]{2,1,0:T(8,128)} %get-tuple-element.144.table_ref), custom_call_target="tpu_custom_call" | custom-call | flops 1048576 | bytes 1048576 | tf_op jit(solution)/shard_map/attention_forward/pallas_call | solution.py:168
  291.1 2.8 multiply_reduce_fusion.8
  297.0 7.5 pack_tokens.5.c_ref
  306.5 7.7 all-gather.15.cloned.1.call-done.refs_0_
  314.3 2.8 copy-done.5
  317.1 4.7 pack_tokens.4
  321.7 2.1 copy-done.6
  324.7 61.1 %expert_layer.2 = (bf16[2816,768]{1,0:T(8,128)(2,1)}, bf16[2816,768]{1,0:T(8,128)(2,1)}, bf16[2816,128]{1,0:T(8,128)(2,1)}, bf16[768,3072]{1,0:T(8,128)(2,1)}, bf16[3072,768]{1,0:T(8,128)(2,1)}) custom-call(s32[17]{0:T(128)} %copy-done.20, s32[1]{0:T(128)} %bitcast.15.expert, bf16[2816,768]{1,0:T(8,128)(2,1)} %copy-done.6, bf16[2816,128]{1,0:T(8,128)(2,1)} %copy-done.16, ...), custom_call_target="tpu_custom_call" | custom-call | flops 1048576 | bytes 1048576 | tf_op jit(solution)/shard_map/expert_layer/pallas_call | solution.py:619
  386.5 2.2 copy-done.8
  389.8 7.8 unpack_tokens.2
  399.4 7.8 pack_tokens.7.c_ref
  409.3 4.7 pack_tokens.6
  416.8 62.3 %expert_layer.3 = (bf16[2816,768]{1,0:T(8,128)(2,1)}, bf16[2816,768]{1,0:T(8,128)(2,1)}, bf16[2816,128]{1,0:T(8,128)(2,1)}, bf16[768,3072]{1,0:T(8,128)(2,1)}, bf16[3072,768]{1,0:T(8,128)(2,1)}) custom-call(s32[17]{0:T(128)} %copy-done.22, s32[1]{0:T(128)} %bitcast.15.expert, bf16[2816,768]{1,0:T(8,128)(2,1)} %copy-done.11, bf16[2816,128]{1,0:T(8,128)(2,1)} %copy-done.15, ...), custom_call_target="tpu_custom_call" | custom-call | flops 1048576 | bytes 1048576 | tf_op jit(solution)/shard_map/expert_layer/pallas_call | solution.py:619
  479.8 2.2 copy-done.7
  483.1 7.8 unpack_tokens.3
  491.0 3.5 convert_element_type.339
  496.9 3.3 all-to-all-start.3
  501.5 2.3 copy-done.9
  503.8 2.3 copy-done.10
  506.1 7.1 window_rows.1
  513.2 5.0 all-to-all-start.2
  518.5 5.6 all-to-all-done.2
  528.5 3.0 convolution_convert_fusion.2.do_ref
  531.5 20.5 %attention_backward.4 = (bf16[512,384]{1,0:T(8,128)(2,1)}, bf16[2048,768]{1,0:T(8,128)(2,1)}, f32[6,1,2816]{2,1,0:T(1,128)}) custom-call(s32[6]{0:T(128)} %copy-done.19, bf16[1024,2304]{1,0:T(8,128)(2,1)} %copy-done.24, bf16[512,768]{1,0:T(8,128)(2,1)} %convolution_convert_fusion.2.do_ref, f32[512,384]{1,0:T(8,128)} %get-tuple-element.136.o_ref, ...), custom_call_target="tpu_custom_call" | custom-call | flops 1048576 | bytes 1048576 | tf_op jit(solution)/shard_map/attention_backward/pallas_call | solution.py:331
  552.0 20.5 %attention_backward.5 = (bf16[512,384]{1,0:T(8,128)(2,1)}, bf16[2048,768]{1,0:T(8,128)(2,1)}, f32[6,1,2816]{2,1,0:T(1,128)}) custom-call(s32[6]{0:T(128)} %copy-done.19, bf16[1024,2304]{1,0:T(8,128)(2,1)} %copy-done.24, bf16[512,768]{1,0:T(8,128)(2,1)} %convolution_convert_fusion.2.do_ref, f32[512,384]{1,0:T(8,128)} %get-tuple-element.173.o_ref, ...), custom_call_target="tpu_custom_call" | custom-call | flops 1048576 | bytes 1048576 | tf_op jit(solution)/shard_map/attention_backward/pallas_call | solution.py:331
  574.4 2.1 multiply_reduce_fusion.4
  579.0 3.0 convolution_convert_fusion.1.do_ref
  581.9 63.3 %attention_backward.6 = (bf16[512,384]{1,0:T(8,128)(2,1)}, bf16[2560,768]{1,0:T(8,128)(2,1)}, f32[6,1,2816]{2,1,0:T(1,128)}) custom-call(s32[6]{0:T(128)} %copy-done.19, bf16[1024,2304]{1,0:T(8,128)(2,1)} %copy-done.24, bf16[512,768]{1,0:T(8,128)(2,1)} %convolution_convert_fusion.1.do_ref, f32[512,384]{1,0:T(8,128)} %get-tuple-element.134.o_ref, ...), custom_call_target="tpu_custom_call" | custom-call | flops 1048576 | bytes 1048576 | tf_op jit(solution)/shard_map/attention_backward/pallas_call | solution.py:331
  645.2 3.8 slice.149
  649.0 4.8 all-to-all-start.4
  654.1 13.1 %reduce-scatter.11.cloned.1.call-done = bf16[1,192,3072]{2,1,0:T(8,128)(2,1)} async-done(((bf16[1,768,3072]{2,1,0:T(8,128)(2,1)}), bf16[1,192,3072]{2,1,0:T(8,128)(2,1)}) %reduce-scatter.11.cloned.1.call-update) | async-done | bytes 1179664 | tf_op jit(solution)/shard_map/reduce_scatter | solution.py:1090
  667.2 63.2 %attention_backward.7 = (bf16[512,384]{1,0:T(8,128)(2,1)}, bf16[2560,768]{1,0:T(8,128)(2,1)}, f32[6,1,2816]{2,1,0:T(1,128)}) custom-call(s32[6]{0:T(128)} %copy-done.19, bf16[1024,2304]{1,0:T(8,128)(2,1)} %copy-done.24, bf16[512,768]{1,0:T(8,128)(2,1)} %convolution_convert_fusion.1.do_ref, f32[512,384]{1,0:T(8,128)} %get-tuple-element.145.o_ref, ...), custom_call_target="tpu_custom_call" | custom-call | flops 1048576 | bytes 1048576 | tf_op jit(solution)/shard_map/attention_backward/pallas_call | solution.py:331
  732.0 3.8 slice.151
  735.8 72.5 %reduce-scatter.15.cloned.1.call-done = bf16[512,768]{1,0:T(8,128)(2,1)} async-done(((bf16[2048,768]{1,0:T(8,128)(2,1)}), bf16[512,768]{1,0:T(8,128)(2,1)}) %reduce-scatter.15.cloned.1.call-update) | async-done | bytes 786448 | tf_op jit(solution)/shard_map/reduce_scatter | solution.py:1118
  812.8 2.1 slice.150
  816.4 3.9 fusion.13
  820.3 2.1 slice.152
  825.9 2.2 broadcast_in_dim.209.place_ref
  828.1 12.1 %collect_rows.1 = f32[1024,768]{1,0:T(8,128)S(1)} custom-call(s32[8192,128]{1,0:T(8,128)S(1)} %broadcast_in_dim.209.place_ref, bf16[4096,768]{1,0:T(8,128)(2,1)} %bitcast.24.refs_0_), custom_call_target="tpu_custom_call" | custom-call | flops 1048576 | bytes 1048576 | tf_op jit(solution)/shard_map/collect_rows/pallas_call | solution.py:527
  843.6 7.8 multiply_reduce_fusion.1
  851.5 14.9 %fusion.55 = f32[768,2304]{1,0:T(8,128)} fusion(bf16[1024,768]{1,0:T(8,128)(2,1)} %param.13, f32[768]{0:T(1024)S(1)} %copy-done.69, f32[1024]{0:T(1024)S(1)} %copy-done.66, bf16[512,768]{1,0:T(8,128)(2,1)} %slice.152, bf16[512,768]{1,0:T(8,128)(2,1)} %reduce-scatter.15.cloned.1.call-done, bf16[512,768]{1,0:T(8,128)(2,1)S(1)} %copy-done.44, ...), kind=kOutput, calls=%fused_computation.81 | convolution fusion | flops 3664773120 | bytes 13376512 | tf_op jit(solution)/shard_map/dot_general | solution.py:1141
  866.4 53.3 %dense_sum.1 = (f32[24,3072]{1,0:T(8,128)S(1)}, f32[64,128]{1,0:T(8,128)S(1)}) custom-call(f32[16,2,24,2304]{3,2,1,0:T(8,128)} %bitcast.164, f32[16,2,24,768]{3,2,1,0:T(8,128)S(1)} %bitcast.156, f32[64,128]{1,0:T(8,128)S(1)} %pad_bitcast_fusion.s_ref), custom_call_target="tpu_custom_call" | custom-call | tf_op jit(solution)/shard_map/dense_sum/pallas_call | solution.py:756
  923.6 5.3 fusion.4
  928.9 2.8 convert_element_type.365
  (297 shorter events, 71.2 us)
Async XLA Ops:
  7.2 29.6 %copy-start.64 = (s32[1,512]{1,0:T(1,128)S(1)}, s32[1,512]{1,0:T(1,128)}, u32[]{:S(2)}) copy-start(s32[1,512]{1,0:T(1,128)} %param.14) | copy-start | bytes 6148
  7.2 30.0 %copy-start.67 = (f32[31,12]{0,1:T(8,128)S(1)}, f32[31,12]{0,1:T(8,128)}, u32[]{:S(2)}) copy-start(f32[31,12]{0,1:T(8,128)} %param.19) | copy-start | bytes 4468
  7.2 71.4 %all-gather.7.cloned.1.call-start = ((), (), s32[]{:S(2)}) async-start(), calls=%async_computation.11 | async-start | bytes 5068800 | tf_op jit(solution)/shard_map/all_gather | solution.py:1008
  30.2 38.2 %all-to-all-start = ((s32[8,1,1024]{2,1,0:T(1,128)}), s32[8,1,1024]{2,1,0:T(1,128)S(1)}, u32[]{:S(2)}, u32[]{:S(2)}) async-start(s32[8,1,1024]{2,1,0:T(1,128)} %copy.81), calls=%async_computation | async-start | bytes 65536 | tf_op jit(solution)/shard_map/all_to_all | solution.py:929
  34.8 96.2 %all-gather.9.cloned.1.call-start = ((), (), s32[]{:S(2)}) async-start(), calls=%async_computation.12 | async-start | bytes 3932160 | tf_op jit(solution)/shard_map/all_gather | solution.py:1025
  37.0 51.1 %copy-start.19 = (s32[6]{0:T(128)}, s32[6]{0:T(128)S(1)}, u32[]{:S(2)}) copy-start(s32[6]{0:T(128)S(1)} %pad_add_fusion.info) | copy-start | bytes 76
  37.6 26.5 %copy-start.29 = (bf16[1024,768]{1,0:T(8,128)(2,1)S(1)}, bf16[1024,768]{1,0:T(8,128)(2,1)}, u32[]{:S(2)}) copy-start(bf16[1024,768]{1,0:T(8,128)(2,1)} %param.13) | copy-start | bytes 4718596
  40.9 37.7 %copy-start.68 = (f32[768]{0:T(1024)S(1)}, f32[768]{0:T(1024)}, u32[]{:S(2)}) copy-start(f32[768]{0:T(1024)} %param.17) | copy-start | bytes 9220
  60.7 3.4 copy-start
  64.5 20.6 %copy-start.61 = (f32[1024]{0:T(1024)}, f32[1024]{0:T(1024)S(1)}, u32[]{:S(2)}) copy-start(f32[1024]{0:T(1024)S(1)} %multiply_reduce_fusion.3) | copy-start | bytes 12292
  64.5 20.5 %copy-start.65 = (f32[1024]{0:T(1024)}, f32[1024]{0:T(1024)S(1)}, u32[]{:S(2)}) copy-start(f32[1024]{0:T(1024)S(1)} %fusion.118) | copy-start | bytes 12292
  68.4 245.9 %copy-start.20 = (s32[17]{0:T(128)}, s32[17]{0:T(128)S(1)}, u32[]{:S(2)}) copy-start(s32[17]{0:T(128)S(1)} %get-tuple-element.147.info) | copy-start | bytes 208
  68.4 338.9 %copy-start.22 = (s32[17]{0:T(128)}, s32[17]{0:T(128)S(1)}, u32[]{:S(2)}) copy-start(s32[17]{0:T(128)S(1)} %get-tuple-element.114.info.later) | copy-start | bytes 208
  85.1 3.0 copy-start.24
  88.1 161.4 %all-gather.11.cloned.1.call-start = ((), (), s32[]{:S(2)}) async-start(), calls=%async_computation.13 | async-start | bytes 14155776 | tf_op jit(solution)/shard_map/all_gather | solution.py:1033
  107.9 3.4 copy-start.1
  132.9 61.0 %all-to-all-start.1 = ((bf16[4,512,768]{2,1,0:T(8,128)(2,1)}), bf16[4,512,768]{2,1,0:T(8,128)(2,1)}, u32[]{:S(2)}, u32[]{:S(2)}) async-start(bf16[4,512,768]{2,1,0:T(8,128)(2,1)} %broadcast_in_dim.194), calls=%async_computation.1 | async-start | bytes 6291456 | tf_op jit(solution)/shard_map/all_to_all | solution.py:1029
  137.6 176.7 %all-gather.15.cloned.1.call-start = ((), (), s32[]{:S(2)}) async-start(), calls=%async_computation.15 | async-start | bytes 7077888 | tf_op jit(solution)/shard_map/all_gather | solution.py:955
  141.2 13.0 %copy-start.40 = (bf16[512,768]{1,0:T(8,128)(2,1)S(1)}, bf16[512,768]{1,0:T(8,128)(2,1)}, u32[]{:S(2)}) copy-start(bf16[512,768]{1,0:T(8,128)(2,1)} %get-tuple-element.289) | copy-start | bytes 2359300
  193.9 13.6 %copy-start.38 = (f32[512,384]{1,0:T(8,128)S(1)}, f32[512,384]{1,0:T(8,128)}, u32[]{:S(2)}) copy-start(f32[512,384]{1,0:T(8,128)} %get-tuple-element.136.o_ref) | copy-start | bytes 2359300
  209.0 3.9 copy-start.52
  209.1 40.4 %copy-start.41 = (f32[512,384]{1,0:T(8,128)S(1)}, f32[512,384]{1,0:T(8,128)}, u32[]{:S(2)}) copy-start(f32[512,384]{1,0:T(8,128)} %get-tuple-element.134.o_ref) | copy-start | bytes 2359300
  211.8 37.8 %copy-start.39 = (bf16[512,768]{1,0:T(8,128)(2,1)S(1)}, bf16[512,768]{1,0:T(8,128)(2,1)}, u32[]{:S(2)}) copy-start(bf16[512,768]{1,0:T(8,128)(2,1)} %get-tuple-element.288) | copy-start | bytes 2359300
  249.4 150.0 %all-gather.13.cloned.1.call-start = ((), (), s32[]{:S(2)}) async-start(), calls=%async_computation.14 | async-start | bytes 7077888 | tf_op jit(solution)/shard_map/all_gather | solution.py:955
  249.6 41.5 %copy-start.50 = (bf16[512,384]{1,0:T(8,128)(2,1)}, bf16[512,384]{1,0:T(8,128)(2,1)S(1)}, u32[]{:S(2)}) copy-start(bf16[512,384]{1,0:T(8,128)(2,1)S(1)} %convert.12) | copy-start | bytes 1179652
  291.1 5.1 copy-start.51
  296.2 194.7 %reduce-scatter.7.cloned.1.call-start = ((), (), s32[]{:S(2)}) async-start(), calls=%async_computation.16 | async-start | bytes 7077888 | tf_op jit(solution)/shard_map/reduce_scatter | solution.py:957
  314.3 2.8 copy-start.5
  324.7 61.8 %copy-start.21 = (s32[17]{0:T(128)S(1)}, s32[17]{0:T(128)}, u32[]{:S(2)}) copy-start(s32[17]{0:T(128)} %copy-done.20) | copy-start | bytes 208
  398.9 173.6 %reduce-scatter.9.cloned.1.call-start = ((), (), s32[]{:S(2)}) async-start(), calls=%async_computation.17 | async-start | bytes 7077888 | tf_op jit(solution)/shard_map/reduce_scatter | solution.py:961
  399.4 9.9 %copy-start.4 = (bf16[4096,768]{1,0:T(8,128)(2,1)S(1)}, bf16[4096,768]{1,0:T(8,128)(2,1)}, u32[]{:S(2)}) copy-start(bf16[4096,768]{1,0:T(8,128)(2,1)} %all-gather.13.cloned.1.call-done.refs_0_) | copy-start | bytes 18874372
  399.4 9.8 %copy-start.12 = (bf16[4096,128]{1,0:T(8,128)(2,1)S(1)}, bf16[4096,128]{1,0:T(8,128)(2,1)}, u32[]{:S(2)}) copy-start(bf16[4096,128]{1,0:T(8,128)(2,1)} %get-tuple-element.160.refs_1_) | copy-start | bytes 3145732
  416.8 62.9 %copy-start.23 = (s32[17]{0:T(128)S(1)}, s32[17]{0:T(128)}, u32[]{:S(2)}) copy-start(s32[17]{0:T(128)} %copy-done.22) | copy-start | bytes 208
  490.9 3.5 copy-start.63
  491.0 3.5 copy-start.35
  491.0 4.7 copy-start.14
  496.9 16.2 %all-to-all-start.3 = ((f32[8,1,512]{2,1,0:T(1,128)}), f32[8,1,512]{2,1,0:T(1,128)S(1)}, u32[]{:S(2)}, u32[]{:S(2)}) async-start(f32[8,1,512]{2,1,0:T(1,128)} %bitcast.21), calls=%async_computation.5 | async-start | bytes 32768 | tf_op jit(solution)/shard_map/all_to_all | solution.py:962
  506.1 18.1 %copy-start.26 = (f32[512,768]{1,0:T(8,128)S(1)}, f32[512,768]{1,0:T(8,128)}, u32[]{:S(2)}) copy-start(f32[512,768]{1,0:T(8,128)} %copy-done.25) | copy-start | bytes 4718596
  506.1 18.1 %copy-start.43 = (bf16[512,768]{1,0:T(8,128)(2,1)S(1)}, bf16[512,768]{1,0:T(8,128)(2,1)}, u32[]{:S(2)}) copy-start(bf16[512,768]{1,0:T(8,128)(2,1)} %reduce-scatter.7.cloned.1.call-done) | copy-start | bytes 2359300
  513.2 10.9 %all-to-all-start.2 = ((f32[8,1,512]{2,1,0:T(1,128)}), f32[8,1,512]{2,1,0:T(1,128)S(1)}, u32[]{:S(2)}, u32[]{:S(2)}) async-start(f32[8,1,512]{2,1,0:T(1,128)} %bitcast.20), calls=%async_computation.4 | async-start | bytes 32768 | tf_op jit(solution)/shard_map/all_to_all | solution.py:962
  518.2 149.0 %reduce-scatter.11.cloned.1.call-start = ((), (), s32[]{:S(2)}) async-start(), calls=%async_computation.18 | async-start | bytes 5898240 | tf_op jit(solution)/shard_map/reduce_scatter | solution.py:1090
  572.6 159.4 %reduce-scatter.13.cloned.1.call-start = ((), (), s32[]{:S(2)}) async-start(), calls=%async_computation.19 | async-start | bytes 3932160 | tf_op jit(solution)/shard_map/reduce_scatter | solution.py:1118
  649.0 176.9 %all-to-all-start.4 = ((bf16[8,512,768]{2,1,0:T(8,128)(2,1)}), bf16[8,512,768]{2,1,0:T(8,128)(2,1)}, u32[]{:S(2)}, u32[]{:S(2)}) async-start(bf16[8,512,768]{2,1,0:T(8,128)(2,1)} %bitcast.159), calls=%async_computation.6 | async-start | bytes 12582912 | tf_op jit(solution)/shard_map/all_to_all | solution.py:1089
  653.8 154.5 %reduce-scatter.15.cloned.1.call-start = ((), (), s32[]{:S(2)}) async-start(), calls=%async_computation.20 | async-start | bytes 3932160 | tf_op jit(solution)/shard_map/reduce_scatter | solution.py:1118
  735.8 73.2 %copy-start.53 = (s32[8,1,1024]{2,0,1:T(8,128)S(1)}, s32[8,1,1024]{2,0,1:T(8,128)}, u32[]{:S(2)}) copy-start(s32[8,1,1024]{2,0,1:T(8,128)} %copy.141) | copy-start | bytes 98308
  735.8 193.1 %reduce-scatter.17.cloned.1.call-start = ((), (), s32[]{:S(2)}) async-start(), calls=%async_computation.21 | async-start | bytes 5898240 | tf_op jit(solution)/shard_map/reduce_scatter | solution.py:1123
  809.6 5.3 copy-start.36
  809.6 5.3 copy-start.37
  811.5 4.8 copy-start.59
  816.3 6.1 copy-start.60
  816.3 6.1 copy-start.55
  816.4 6.1 copy-start.56
  816.4 6.1 copy-start.70
  816.4 7.8 copy-start.42
  828.0 12.1 %copy-start.34 = (f32[1024,768]{1,0:T(8,128)S(1)}, f32[1024,768]{1,0:T(8,128)}, u32[]{:S(2)}) copy-start(f32[1024,768]{1,0:T(8,128)} %pad_maximum_fusion.2) | copy-start | bytes 9437188
  840.2 2.7 copy-start.71
  840.2 2.9 copy-start.72
  840.2 3.0 copy-start.73
  840.3 3.1 copy-start.74
  840.3 3.2 copy-start.75
  840.3 3.3 copy-start.76
  843.6 7.8 copy-start.54
  866.4 55.8 %copy-start.62 = (f32[1024]{0:T(1024)S(1)}, f32[1024]{0:T(1024)}, u32[]{:S(2)}) copy-start(f32[1024]{0:T(1024)} %copy-done.61) | copy-start | bytes 12292
  919.7 3.8 copy-start.31
  (30 other events, 52.0 us)
Sparse Core Ops, SparseCore 0:
  11.5 67.1 all-gather.6
  88.2 42.7 all-gather.8
  132.7 116.7 all-gather.10
  250.9 63.3 all-gather.14
  315.8 63.4 all-gather.12
  399.0 68.5 reduce-scatter.6
  491.1 69.2 reduce-scatter.8
  572.7 94.4 reduce-scatter.10
  670.7 61.2 reduce-scatter.12
  735.9 72.4 reduce-scatter.14
  811.3 57.0 reduce-scatter.16
